TPU v7x, 512 devices: a whole 4x4x16 slice. The times are simulated.
512 devices in a mesh: quarter: 4 (over x), row: 8 (over z_lo), col: 16 (over y, z_hi, core).
Axes of the slice: x: 4, y: 4, z: 16 (z_hi: 2, z_lo: 8; z = z_hi * 8 + z_lo), core: 2. Of those that a mesh axis runs over, the one named last changes fastest.
Arguments:
- grad: bfloat16 [4, 4096, 4096], P('quarter', 'row', 'col'), may hold values from -6 to 6
- left_root: bfloat16 [4096, 4096], P('row', 'col'), may hold values from -1 to 3, as said below
- right_root: bfloat16 [4, 4096, 4096], P('quarter', 'row', 'col'), may hold values from -1 to 3, as said below
- momentum: float32 [4, 4096, 4096], P('quarter', 'row', 'col'), may hold values from -6 to 6
- weights: bfloat16 [4, 4096, 4096], P('quarter', 'row', 'col'), may hold values from -6 to 6
Outputs:
- momentum_new: float32 [4, 4096, 4096], P('quarter', 'row', 'col')
- new_weights: bfloat16 [4, 4096, 4096], P(None, ('row', 'quarter'), 'col')
Inputs may be any that keep to these rules, and one draw needn't show every extreme that they name: `left_root`: symmetric. `right_root`: each block symmetric.
All inputs are finite; a program needn't handle non-finite values.
Results may differ from a plain program's by a relative error of at most 0.001.
Values may be sent and summed in bfloat16 or wider, within the bound.
No kernel may reach another device: no remote copies, remote signals or barrier semaphores. Data moves between devices by JAX's collectives and lax.ppermute only.
A program may use at most 64 MiB of HBM per device.

v0:
```python
import jax
import jax.numpy as jnp
from jax import lax
from jax.sharding import PartitionSpec as P

decay_rate = 0.9
step_rate = 0.1


def per_device(grad, left_root, right_root, momentum, weights):
    right_panel = lax.all_gather(right_root, "row", axis=1, tiled=True)[0]
    mixed = jnp.dot(
        lax.all_gather(grad, "col", axis=2, tiled=True)[0],
        right_panel,
        preferred_element_type=jnp.float32,
    ).astype(jnp.bfloat16)
    left_panel = lax.all_gather(left_root, "col", axis=1, tiled=True)
    product = jnp.dot(
        left_panel,
        lax.all_gather(mixed, "row", axis=0, tiled=True),
        preferred_element_type=jnp.float32,
    )
    renewed = decay_rate * momentum[0] + (1.0 - decay_rate) * product
    updated = (weights[0].astype(jnp.float32) - step_rate * renewed).astype(jnp.bfloat16)
    spread = lax.all_to_all(updated[None], "quarter", split_axis=1, concat_axis=0, tiled=True)
    return (renewed[None], spread)


def solution(mesh):
    placed = (
        P("quarter", "row", "col"),
        P("row", "col"),
        P("quarter", "row", "col"),
        P("quarter", "row", "col"),
        P("quarter", "row", "col"),
    )
    return jax.shard_map(
        per_device,
        mesh=mesh,
        in_specs=placed,
        out_specs=(P("quarter", "row", "col"), P(None, ("row", "quarter"), "col")),
        check_vma=False,
    )
```

profile of v0, /device:TPU:8, one launch (start us, length us, event | category | flops | bytes accessed | tf_op | source)
XLA Modules:
  0.0 411.7 jit_solution(7492663751729316780)
XLA Ops:
  7.2 0.0 all-gather.7.cloned.1.call-start
  7.2 0.7 all-gather.7.cloned.1.call-update
  7.9 0.0 all-gather.5.cloned.1.call-start
  7.9 0.7 all-gather.5.cloned.1.call-update
  8.6 0.0 copy-start
  8.7 0.0 all-gather.11.cloned.1.call-start
  8.7 0.7 all-gather.11.cloned.1.call-update
  9.4 0.0 copy-start.1
  9.4 0.0 all-gather.9.cloned.1.call-start
  9.4 75.3 %all-gather.7.cloned.1.call-done = bf16[1,4096,256]{2,1,0:T(8,128)(2,1)} async-done(((bf16[1,512,256]{2,1,0:T(8,128)(2,1)}), bf16[1,4096,256]{2,1,0:T(8,128)(2,1)}) %all-gather.7.cloned.1.call-update) | async-done | bytes 2097168 | tf_op jit(solution)/shard_map/all_gather | solution.py:11
  84.7 116.1 %all-gather.5.cloned.1.call-done = bf16[1,512,4096]{2,1,0:T(8,128)(2,1)} async-done(((bf16[1,512,256]{2,1,0:T(8,128)(2,1)}), bf16[1,512,4096]{2,1,0:T(8,128)(2,1)}) %all-gather.5.cloned.1.call-update) | async-done | bytes 4194320 | tf_op jit(solution)/shard_map/all_gather | solution.py:13
  200.9 4.8 %fusion.5 = bf16[512,256]{1,0:T(8,128)(2,1)} fusion(bf16[1,4096,256]{2,1,0:T(8,128)(2,1)} %all-gather.7.cloned.1.call-done, bf16[1,512,4096]{2,1,0:T(8,128)(2,1)} %all-gather.5.cloned.1.call-done), kind=kOutput, calls=%fused_computation.6 | convolution fusion | flops 1073872896 | bytes 6553600 | tf_op jit(solution)/shard_map/dot_general | solution.py:12
  205.7 0.0 all-gather.9.cloned.1.call-update
  205.7 0.0 copy-done
  205.7 0.2 copy.15
  205.9 0.0 copy-done.1
  205.9 0.1 copy.16
  206.1 110.5 %all-gather.11.cloned.1.call-done = bf16[512,4096]{1,0:T(8,128)(2,1)} async-done(((bf16[512,256]{1,0:T(8,128)(2,1)}), bf16[512,4096]{1,0:T(8,128)(2,1)}) %all-gather.11.cloned.1.call-update) | async-done | bytes 4194320 | tf_op jit(solution)/shard_map/all_gather | solution.py:17
  316.6 68.4 %all-gather.9.cloned.1.call-done = bf16[4096,256]{1,0:T(8,128)(2,1)} async-done(((bf16[512,256]{1,0:T(8,128)(2,1)}), bf16[4096,256]{1,0:T(8,128)(2,1)}) %all-gather.9.cloned.1.call-update) | async-done | bytes 2097168 | tf_op jit(solution)/shard_map/all_gather | solution.py:20
  385.1 4.1 %fusion.4 = f32[512,256]{0,1:T(8,128)S(1)} fusion(bf16[4096,256]{1,0:T(8,128)(2,1)} %all-gather.9.cloned.1.call-done, bf16[512,4096]{1,0:T(8,128)(2,1)} %all-gather.11.cloned.1.call-done, f32[1,512,256]{1,2,0:T(8,128)S(1)} %copy.15), kind=kOutput, calls=%fused_computation.5 | convolution fusion | flops 1074135040 | bytes 7340032 | tf_op jit(solution)/shard_map/dot_general | solution.py:18
  389.2 0.1 fusion.11
  389.3 0.4 copy.17
  389.7 0.5 broadcast.13
  390.2 2.2 reduce
  392.4 0.8 reshape.12
  393.2 4.2 %all-to-all-start = ((bf16[4,2,16384]{2,1,0:T(2,128)(2,1)}), bf16[4,2,16384]{2,1,0:T(2,128)(2,1)S(1)}, u32[]{:S(2)}, u32[]{:S(2)}) async-start(bf16[4,2,16384]{2,1,0:T(2,128)(2,1)} %reshape.12), calls=%async_computation | async-start | bytes 524288 | tf_op jit(solution)/shard_map/all_to_all | solution.py:25
  397.4 1.0 copy.18
  398.4 5.7 %all-to-all-done = bf16[4,2,16384]{2,1,0:T(2,128)(2,1)S(1)} async-done(((bf16[4,2,16384]{2,1,0:T(2,128)(2,1)}), bf16[4,2,16384]{2,1,0:T(2,128)(2,1)S(1)}, u32[]{:S(2)}, u32[]{:S(2)}) %all-to-all-start) | async-done | bytes 262176 | tf_op jit(solution)/shard_map/all_to_all | solution.py:25
  404.1 0.3 reshape.13
  404.4 0.7 copy.19
Async XLA Ops:
  7.2 77.6 %all-gather.7.cloned.1.call-start = ((), (), s32[]{:S(2)}) async-start(), calls=%async_computation.2 | async-start | bytes 2359296 | tf_op jit(solution)/shard_map/all_gather | solution.py:11
  7.9 193.0 %all-gather.5.cloned.1.call-start = ((), (), s32[]{:S(2)}) async-start(), calls=%async_computation.1 | async-start | bytes 4456448 | tf_op jit(solution)/shard_map/all_gather | solution.py:13
  8.6 197.1 %copy-start = (f32[1,512,256]{2,1,0:T(8,128)S(1)}, f32[1,512,256]{2,1,0:T(8,128)}, u32[]{:S(2)}) copy-start(f32[1,512,256]{2,1,0:T(8,128)} %param.8) | copy-start | bytes 1572868
  8.7 307.9 %all-gather.11.cloned.1.call-start = ((), (), s32[]{:S(2)}) async-start(), calls=%async_computation.4 | async-start | bytes 4456448 | tf_op jit(solution)/shard_map/all_gather | solution.py:17
  9.4 196.5 %copy-start.1 = (bf16[1,512,256]{2,1,0:T(8,128)(2,1)S(1)}, bf16[1,512,256]{2,1,0:T(8,128)(2,1)}, u32[]{:S(2)}) copy-start(bf16[1,512,256]{2,1,0:T(8,128)(2,1)} %param.9) | copy-start | bytes 786436
  9.4 375.6 %all-gather.9.cloned.1.call-start = ((), (), s32[]{:S(2)}) async-start(), calls=%async_computation.3 | async-start | bytes 2359296 | tf_op jit(solution)/shard_map/all_gather | solution.py:20
  393.2 10.9 %all-to-all-start = ((bf16[4,2,16384]{2,1,0:T(2,128)(2,1)}), bf16[4,2,16384]{2,1,0:T(2,128)(2,1)S(1)}, u32[]{:S(2)}, u32[]{:S(2)}) async-start(bf16[4,2,16384]{2,1,0:T(2,128)(2,1)} %reshape.12), calls=%async_computation | async-start | bytes 524288 | tf_op jit(solution)/shard_map/all_to_all | solution.py:25
Sparse Core Ops, SparseCore 0:
  10.1 74.6 all-gather.6
  87.8 112.9 all-gather.4
  204.0 112.5 all-gather.10
  319.1 65.8 all-gather.8
where the time goes:
time: 412 us
  waiting for transfers between devices  378 us (92%)
  between operations  13.9 us (3%)
  matrix products  8.94 us (2%)
  starting transfers between devices  4.4 us (1%)
    all_gather x1, waiting for transfers between devices, per_device(): lax.all_gather(grad, 'col', axis=2, tiled=True)[0]  116 us
    all_gather x1, waiting for transfers between devices, per_device(): left_panel = lax.all_gather(left_root, 'col', axis=1, tiled=True)  111 us
    all_gather x1, waiting for transfers between devices, per_device(): right_panel = lax.all_gather(right_root, 'row', axis=1, tiled=True)[0]  75.3 us
    all_gather x1, waiting for transfers between devices, per_device(): lax.all_gather(mixed, 'row', axis=0, tiled=True)  68.4 us
  transfers between devices with their start and end apart: 5, of which 5 were waited for; matrix products, arithmetic and copies ran while one was open for 1% of the time, Pallas kernels for 0%

commit v1 on v0

v1 whole, which is shorter than its diff:
```python
import jax
import jax.numpy as jnp
from jax import lax
from jax.experimental import pallas as pl
from jax.experimental.pallas import tpu as pltpu
from jax.sharding import Mesh, PartitionSpec as P

decay_rate = 0.9
step_rate = 0.1
AXES = ("quarter", "row", "y", "z_hi", "core")
SWAP = [(0, 1), (1, 0)]


def copies_to_all(piece, axis):
    n = lax.axis_size(axis)
    spread = jnp.broadcast_to(piece[None], (n, *piece.shape))
    return lax.all_to_all(spread, axis, 0, 0, tiled=True)


def row_panel(own, other):
    pieces = []
    for piece in (own, other):
        mine = copies_to_all(piece, "y")
        pieces += [mine, lax.ppermute(mine, "core", SWAP)]
    return pieces


def accumulate(place, pieces, b_ref, acc_ref):
    depth = pieces[0].shape[-1]
    half, core = place[0], place[1]

    @pl.when(pl.program_id(0) == 0)
    def _():
        acc_ref[...] = jnp.zeros_like(acc_ref)

    total = acc_ref[...]
    for n, piece in enumerate(pieces):
        at = 2 * (half if n < 2 else 1 - half) + (core if n % 2 == 0 else 1 - core)
        rows = b_ref[pl.ds(pl.multiple_of(at * depth, depth), depth), :]
        total += jnp.dot(piece[0], rows, preferred_element_type=jnp.float32)
    acc_ref[...] = total


def first_kernel(place, a0, a1, a2, a3, b_ref, o_ref, acc_ref):
    accumulate(place, (a0, a1, a2, a3), b_ref, acc_ref)

    @pl.when(pl.program_id(0) == pl.num_programs(0) - 1)
    def _():
        o_ref[...] = acc_ref[...].astype(o_ref.dtype)


def second_kernel(place, a0, a1, a2, a3, b_ref, m_ref, w_ref, mo_ref, wo_ref, acc_ref):
    accumulate(place, (a0, a1, a2, a3), b_ref, acc_ref)

    @pl.when(pl.program_id(0) == pl.num_programs(0) - 1)
    def _():
        renewed = decay_rate * m_ref[...] + (1.0 - decay_rate) * acc_ref[...]
        mo_ref[...] = renewed
        wo_ref[...] = (w_ref[...].astype(jnp.float32) - step_rate * renewed).astype(wo_ref.dtype)


def call(body, name, place, pieces, right, extra, types):
    steps, rows, depth = pieces[0].shape
    columns = right.shape[1]
    whole = pl.BlockSpec((rows, columns), lambda i, place: (0, 0))
    a = pl.BlockSpec((1, rows, depth), lambda i, place: (i, 0, 0))
    b = pl.BlockSpec((4 * depth, columns), lambda i, place: (i, 0))
    moved = 2 * (4 * steps * rows * depth + right.size) + 6 * rows * columns
    return pl.pallas_call(
        body,
        out_shape=[jax.ShapeDtypeStruct((rows, columns), t) for t in types],
        grid_spec=pltpu.PrefetchScalarGridSpec(
            num_scalar_prefetch=1,
            grid=(steps,),
            in_specs=[a] * 4 + [b] + [whole] * len(extra),
            out_specs=[whole] * len(types),
            scratch_shapes=[pltpu.VMEM((rows, columns), jnp.float32)],
        ),
        cost_estimate=pl.CostEstimate(flops=2 * rows * right.size, bytes_accessed=moved, transcendentals=0),
        name=name,
    )(place, *pieces, right, *extra)


def per_device(grad, left_root, right_root, momentum, weights):
    place = jnp.stack((lax.axis_index("z_hi"), lax.axis_index("core"))).astype(jnp.int32)
    quarter = lax.axis_index("quarter")
    quarters = lax.axis_size("quarter")
    rows, depth = left_root.shape
    part = rows // quarters

    right_panel = lax.all_gather(right_root[0], "row", axis=0, tiled=True)
    grad_other = lax.ppermute(grad[0], "z_hi", SWAP)
    left_part = lax.ppermute(lax.dynamic_slice_in_dim(left_root, quarter * part, part, 0), "z_hi", SWAP)
    (mixed,) = call(first_kernel, "mix", place, row_panel(grad[0], grad_other), right_panel, (), (jnp.bfloat16,))

    mixed, left_own, left_part = lax.optimization_barrier((mixed, left_root, left_part))
    mixed_panel = lax.all_gather(mixed, "row", axis=0, tiled=True)
    left_other = copies_to_all(left_part, "quarter").reshape(rows, depth)
    renewed, updated = call(
        second_kernel,
        "update",
        place,
        row_panel(left_own, left_other),
        mixed_panel,
        (momentum[0], weights[0]),
        (jnp.float32, jnp.bfloat16),
    )
    spread = lax.all_to_all(updated.reshape(quarters, part, depth), "quarter", 0, 0, tiled=True)
    return renewed[None], spread


def solution(mesh):
    fine = Mesh(mesh.devices.reshape(4, 8, 4, 2, 2), AXES)
    placed = P("quarter", "row", ("y", "z_hi", "core"))
    return jax.shard_map(
        per_device,
        mesh=fine,
        in_specs=(placed, P("row", ("y", "z_hi", "core")), placed, placed, placed),
        out_specs=(placed, P(None, ("row", "quarter"), ("y", "z_hi", "core"))),
        check_vma=False,
    )
```

time: 412 us -> 198 us (0.48)
  waiting for transfers between devices: 378 us -> 75.6 us
  starting transfers between devices: 4.4 us -> 52.7 us
  blocking collectives: 0 us -> 36.9 us
  Pallas kernels: 0 us -> 12 us
  matrix products: 8.94 us -> 0 us
    all_gather x4 -> x2, waiting for transfers between devices: 370 us -> 36.2 us  [the longest x1 19.8 us: per_device(): mixed_panel = lax.all_gather(mixed, 'row', axis=0, tiled=True)]
    all_to_all x0 -> x3, blocking collectives: none -> 36.9 us  [the longest x2 26 us: copies_to_all(): return lax.all_to_all(spread, axis, 0, 0, tiled=True)]
    ppermute x0 -> x6, starting transfers between devices: none -> 33.6 us  [the longest x1 14.5 us: per_device(): lax.ppermute(lax.dynamic_slice_in_dim(left_root, quarter * part, part, 0)...]
    ppermute x0 -> x6, waiting for transfers between devices: none -> 23.7 us  [the longest x1 20.9 us: per_device(): grad_other = lax.ppermute(grad[0], 'z_hi', SWAP)]
    all_to_all x1 -> x3, starting transfers between devices: 4.25 us -> 19 us  [copies_to_all(): return lax.all_to_all(spread, axis, 0, 0, tiled=True)]
    pallas_call x0 -> x2, Pallas kernels: none -> 12 us  [call(): pl.pallas_call(body, out_shape=[jax.ShapeDtypeStruct((rows, columns), t)...]
    all_to_all x1 -> x3, waiting for transfers between devices: 5.68 us -> 15 us  [copies_to_all(): return lax.all_to_all(spread, axis, 0, 0, tiled=True)]
    dot_general x2 -> x0, matrix products: 8.94 us -> none  [the longest x1 4.82 us: per_device(): jnp.dot(lax.all_gather(grad, 'col', axis=2, tiled=True)[0], right_panel,...]
  transfers between devices with their start and end apart: 5 -> 11, of which waited for: 5 -> 6; matrix products, arithmetic and copies ran while one was open for 1% -> 3% of each run, Pallas kernels for 0% -> 3%
where the time goes in v1:
time: 198 us; the launch traced here: 197 us
  waiting for transfers between devices  75.6 us (38%)
  starting transfers between devices  52.7 us (27%)
  blocking collectives  36.9 us (19%)
  between operations  14.2 us (7%)
  Pallas kernels  12 us (6%)
  local copies, waits for them, and re-layouts  5.04 us (3%)
    all_to_all x2, blocking collectives, copies_to_all(): return lax.all_to_all(spread, axis, 0, 0, tiled=True)  26 us
    ppermute x1, waiting for transfers between devices, per_device(): grad_other = lax.ppermute(grad[0], 'z_hi', SWAP)  20.9 us
    all_gather x1, waiting for transfers between devices, per_device(): mixed_panel = lax.all_gather(mixed, 'row', axis=0, tiled=True)  19.8 us
    all_to_all x3, starting transfers between devices, copies_to_all(): return lax.all_to_all(spread, axis, 0, 0, tiled=True)  19 us
    all_gather x1, waiting for transfers between devices, per_device(): right_panel = lax.all_gather(right_root[0], 'row', axis=0, tiled=True)  16.4 us
    all_to_all x3, waiting for transfers between devices, copies_to_all(): return lax.all_to_all(spread, axis, 0, 0, tiled=True)  15 us
    ppermute x1, starting transfers between devices, per_device(): lax.ppermute(lax.dynamic_slice_in_dim(left_root, quarter * part, part, 0)...  14.5 us
    pallas_call x2, Pallas kernels, call(): pl.pallas_call(body, out_shape=[jax.ShapeDtypeStruct((rows, columns), t)...  12 us
  transfers between devices with their start and end apart: 11, of which 6 were waited for; matrix products, arithmetic and copies ran while one was open for 3% of the time, Pallas kernels for 3%

profile of v1, /device:TPU:8, one launch (start us, length us, event | category | flops | bytes accessed | tf_op | source)
XLA Modules:
  0.0 197.0 jit_solution(10987960748990838645)
XLA Ops:
  7.2 0.0 copy-start.7
  7.2 0.0 all-gather.6.cloned.1.call-start
  7.2 0.7 all-gather.6.cloned.1.call-update
  7.9 2.0 %broadcast_in_dim.17 = bf16[4,512,256]{2,1,0:T(8,128)(2,1)} broadcast(bf16[512,256]{1,0:T(8,128)(2,1)} %bitcast.13), dimensions={1,2} | broadcast | bytes 1310720 | tf_op jit(solution)/shard_map/broadcast_in_dim | solution.py:16
  9.9 9.3 %all-to-all-start = ((bf16[4,512,256]{2,1,0:T(8,128)(2,1)}), bf16[4,512,256]{2,1,0:T(8,128)(2,1)S(1)}, u32[]{:S(2)}, u32[]{:S(2)}) async-start(bf16[4,512,256]{2,1,0:T(8,128)(2,1)} %broadcast_in_dim.17), calls=%async_computation | async-start | bytes 2097152 | tf_op jit(solution)/shard_map/all_to_all | solution.py:17
  19.2 0.0 copy-done.7
  19.2 0.0 copy-start.6
  19.2 11.5 %collective-permute-start.1 = (bf16[512,256]{1,0:T(8,128)(2,1)S(1)}, bf16[512,256]{1,0:T(8,128)(2,1)S(1)}, u32[]{:S(2)}, u32[]{:S(2)}) collective-permute-start(bf16[512,256]{1,0:T(8,128)(2,1)S(1)} %bitcast.14), channel_id=1, source_target_pairs={{0,2},{2,0},{1,3},{3,1},{4,6},{6,4},{5,7},{7,5},{8,10},{10,8},{9,1... | collective-permute-start | bytes 786440 | tf_op jit(solution)/shard_map/ppermute | solution.py:92
  30.7 20.9 %collective-permute-done.1 = bf16[512,256]{1,0:T(8,128)(2,1)S(1)} collective-permute-done((bf16[512,256]{1,0:T(8,128)(2,1)S(1)}, bf16[512,256]{1,0:T(8,128)(2,1)S(1)}, u32[]{:S(2)}, u32[]{:S(2)}) %collective-permute-start.1) | collective-permute-done | bytes 262176 | tf_op jit(solution)/shard_map/ppermute | solution.py:92
  51.6 0.0 all-to-all-done.a0
  51.6 0.0 copy-start.2
  51.6 1.1 broadcast_in_dim.18
  52.7 4.8 %all-to-all-start.1 = ((bf16[4,512,256]{2,1,0:T(8,128)(2,1)}), bf16[4,512,256]{2,1,0:T(8,128)(2,1)S(1)}, u32[]{:S(2)}, u32[]{:S(2)}) async-start(bf16[4,512,256]{2,1,0:T(8,128)(2,1)} %broadcast_in_dim.18), calls=%async_computation.1 | async-start | bytes 2097152 | tf_op jit(solution)/shard_map/all_to_all | solution.py:17
  57.4 0.0 all-gather.4.cloned.1.call-start
  57.4 1.9 collective-permute-start
  59.4 7.5 %all-to-all-done.1.a2 = bf16[4,512,256]{2,1,0:T(8,128)(2,1)S(1)} async-done(((bf16[4,512,256]{2,1,0:T(8,128)(2,1)}), bf16[4,512,256]{2,1,0:T(8,128)(2,1)S(1)}, u32[]{:S(2)}, u32[]{:S(2)}) %all-to-all-start.1) | async-done | bytes 1048608 | tf_op jit(solution)/shard_map/all_to_all | solution.py:17
  66.9 0.0 copy-start.3
  66.9 1.9 collective-permute-start.2
  68.8 0.0 copy-done.6
  68.8 14.5 %collective-permute-start.3 = (bf16[128,256]{1,0:T(8,128)(2,1)S(1)}, bf16[128,256]{1,0:T(8,128)(2,1)S(1)}, u32[]{:S(2)}, u32[]{:S(2)}) collective-permute-start(bf16[128,256]{1,0:T(8,128)(2,1)S(1)} %constant_dynamic-slice_fusion), channel_id=1, source_target_pairs={{0,2},{2,0},{1,3},{3,1},{4,6},{6,4},{5,7},{7,5},{8,10},{10,8},{9,1... | collective-permute-start | bytes 196616 | tf_op jit(solution)/shard_map/ppermute | solution.py:93
  83.4 0.7 pad_add_fusion.place
  84.0 0.0 collective-permute-done.a1
  84.0 0.0 collective-permute-done.2.a3
  84.0 16.4 %all-gather.6.cloned.1.call-done = bf16[1,4096,256]{2,1,0:T(8,128)(2,1)} async-done(((bf16[1,512,256]{2,1,0:T(8,128)(2,1)}), bf16[1,4096,256]{2,1,0:T(8,128)(2,1)}) %all-gather.6.cloned.1.call-update) | async-done | bytes 2097168 | tf_op jit(solution)/shard_map/all_gather | solution.py:91
  100.4 0.0 copy-done.2
  100.4 0.0 copy-done.3
  100.4 0.0 copy-done.5
  100.4 5.6 %mix.1 = bf16[512,256]{1,0:T(8,128)(2,1)} custom-call(s32[2]{0:T(128)} %pad_add_fusion.place, bf16[4,512,256]{2,1,0:T(8,128)(2,1)} %copy-done.2, bf16[4,512,256]{2,1,0:T(8,128)(2,1)} %copy-done.5, bf16[4,512,256]{2,1,0:T(8,128)(2,1)} %copy-done.3, bf16[4,512,256]{2,1,0:T(8,128)(2,1)} %collective-permute-done.2.a3, bf16[4096,256]{1,0:T(8,128)(2,1)} %bitcast.9), custom_call_target="tpu_custom_call" | custom-call | flops 1073741824 | bytes 7077888 | tf_op jit(solution)/shard_map/mix/pallas_call | solution.py:69
  106.1 0.0 collective-permute-done.3
  106.1 0.0 all-gather.4.cloned.1.call-update
  106.1 10.8 %all_to_all.30 = bf16[4,128,256]{2,1,0:T(8,128)(2,1)S(1)} all-to-all(bf16[4,128,256]{2,1,0:T(8,128)(2,1)S(1)} %broadcast_in_dim.39), channel_id=1, replica_groups=mesh['quarter'=4,'row'=8,'y'=4,'z_hi'=2,'core'=2] {'quarter'}, dimensions={0} | all-to-all | bytes 524288 | tf_op jit(solution)/shard_map/all_to_all | solution.py:17
  116.9 0.1 broadcast_in_dim.38
  117.0 15.2 %all_to_all.31.a0 = bf16[4,512,256]{2,1,0:T(8,128)(2,1)S(1)} all-to-all(bf16[4,512,256]{2,1,0:T(8,128)(2,1)S(1)} %broadcast_in_dim.38), channel_id=1, replica_groups=mesh['quarter'=4,'row'=8,'y'=4,'z_hi'=2,'core'=2] {'y'}, dimensions={0} | all-to-all | bytes 2097152 | tf_op jit(solution)/shard_map/all_to_all | solution.py:17
  132.2 1.1 broadcast_in_dim.41
  133.3 4.9 %all-to-all-start.4 = ((bf16[4,512,256]{2,1,0:T(8,128)(2,1)}), bf16[4,512,256]{2,1,0:T(8,128)(2,1)S(1)}, u32[]{:S(2)}, u32[]{:S(2)}) async-start(bf16[4,512,256]{2,1,0:T(8,128)(2,1)} %broadcast_in_dim.41), calls=%async_computation.4 | async-start | bytes 2097152 | tf_op jit(solution)/shard_map/all_to_all | solution.py:17
  138.2 1.9 collective-permute-start.4
  140.2 7.5 %all-to-all-done.4.a2 = bf16[4,512,256]{2,1,0:T(8,128)(2,1)S(1)} async-done(((bf16[4,512,256]{2,1,0:T(8,128)(2,1)}), bf16[4,512,256]{2,1,0:T(8,128)(2,1)S(1)}, u32[]{:S(2)}, u32[]{:S(2)}) %all-to-all-start.4) | async-done | bytes 1048608 | tf_op jit(solution)/shard_map/all_to_all | solution.py:17
  147.7 1.9 collective-permute-start.5
  149.6 0.0 collective-permute-done.4.a1
  149.6 0.0 copy-start.4
  149.6 2.7 %collective-permute-done.5.a3 = bf16[4,512,256]{2,1,0:T(8,128)(2,1)} collective-permute-done((bf16[4,512,256]{2,1,0:T(8,128)(2,1)S(1)}, bf16[4,512,256]{2,1,0:T(8,128)(2,1)}, u32[]{:S(2)}, u32[]{:S(2)}) %collective-permute-start.5) | collective-permute-done | bytes 1048608 | tf_op jit(solution)/shard_map/ppermute | solution.py:24
  152.4 19.8 %all-gather.4.cloned.1.call-done.b_ref = bf16[4096,256]{1,0:T(8,128)(2,1)} async-done(((bf16[512,256]{1,0:T(8,128)(2,1)}), bf16[4096,256]{1,0:T(8,128)(2,1)}) %all-gather.4.cloned.1.call-update) | async-done | bytes 2097168 | tf_op jit(solution)/shard_map/all_gather | solution.py:97
  172.2 0.0 copy-done
  172.2 0.0 copy-done.1
  172.2 0.0 copy-done.4
  172.2 6.4 %update.1 = (f32[512,256]{1,0:T(8,128)}, bf16[512,256]{1,0:T(8,128)(2,1)}) custom-call(s32[2]{0:T(128)} %pad_add_fusion.place, bf16[4,512,256]{2,1,0:T(8,128)(2,1)} %copy-done, bf16[4,512,256]{2,1,0:T(8,128)(2,1)} %copy-done.4, bf16[4,512,256]{2,1,0:T(8,128)(2,1)} %copy-done.1, bf16[4,512,256]{2,1,0:T(8,128)(2,1)} %collective-permute-done.5.a3, ...), custom_call_target="tpu_custom_call" | custom-call | flops 1073741824 | bytes 7077888 | tf_op jit(solution)/shard_map/update/pallas_call | solution.py:69
  178.6 10.9 %all_to_all.32 = bf16[4,128,256]{2,1,0:T(8,128)(2,1)S(1)} all-to-all(bf16[4,128,256]{2,1,0:T(8,128)(2,1)} %bitcast.15), channel_id=1, replica_groups=mesh['quarter'=4,'row'=8,'y'=4,'z_hi'=2,'core'=2] {'quarter'}, dimensions={0} | all-to-all | bytes 524288 | tf_op jit(solution)/shard_map/all_to_all | solution.py:108
  189.5 0.7 copy.8
  (5 shorter events, 0.0 us)
Async XLA Ops:
  7.2 12.0 %copy-start.7 = (bf16[1,512,256]{2,1,0:T(8,128)(2,1)S(1)}, bf16[1,512,256]{2,1,0:T(8,128)(2,1)}, u32[]{:S(2)}) copy-start(bf16[1,512,256]{2,1,0:T(8,128)(2,1)} %param.5) | copy-start | bytes 786436
  7.2 93.3 %all-gather.6.cloned.1.call-start = ((), (), s32[]{:S(2)}) async-start(), calls=%async_computation.7 | async-start | bytes 2359296 | tf_op jit(solution)/shard_map/all_gather | solution.py:91
  9.9 41.7 %all-to-all-start = ((bf16[4,512,256]{2,1,0:T(8,128)(2,1)}), bf16[4,512,256]{2,1,0:T(8,128)(2,1)S(1)}, u32[]{:S(2)}, u32[]{:S(2)}) async-start(bf16[4,512,256]{2,1,0:T(8,128)(2,1)} %broadcast_in_dim.17), calls=%async_computation | async-start | bytes 2097152 | tf_op jit(solution)/shard_map/all_to_all | solution.py:17
  19.2 49.6 %copy-start.6 = (bf16[512,256]{1,0:T(8,128)(2,1)S(1)}, bf16[512,256]{1,0:T(8,128)(2,1)}, u32[]{:S(2)}) copy-start(bf16[512,256]{1,0:T(8,128)(2,1)} %param.6) | copy-start | bytes 786436
  19.2 32.4 %collective-permute-start.1 = (bf16[512,256]{1,0:T(8,128)(2,1)S(1)}, bf16[512,256]{1,0:T(8,128)(2,1)S(1)}, u32[]{:S(2)}, u32[]{:S(2)}) collective-permute-start(bf16[512,256]{1,0:T(8,128)(2,1)S(1)} %bitcast.14), channel_id=1, source_target_pairs={{0,2},{2,0},{1,3},{3,1},{4,6},{6,4},{5,7},{7,5},{8,10},{10,8},{9,1... | collective-permute-start | bytes 786440 | tf_op jit(solution)/shard_map/ppermute | solution.py:92
  51.6 48.9 %copy-start.2 = (bf16[4,512,256]{2,1,0:T(8,128)(2,1)}, bf16[4,512,256]{2,1,0:T(8,128)(2,1)S(1)}, u32[]{:S(2)}) copy-start(bf16[4,512,256]{2,1,0:T(8,128)(2,1)S(1)} %all-to-all-done.a0) | copy-start | bytes 3145732
  52.7 14.2 %all-to-all-start.1 = ((bf16[4,512,256]{2,1,0:T(8,128)(2,1)}), bf16[4,512,256]{2,1,0:T(8,128)(2,1)S(1)}, u32[]{:S(2)}, u32[]{:S(2)}) async-start(bf16[4,512,256]{2,1,0:T(8,128)(2,1)} %broadcast_in_dim.18), calls=%async_computation.1 | async-start | bytes 2097152 | tf_op jit(solution)/shard_map/all_to_all | solution.py:17
  57.4 114.7 %all-gather.4.cloned.1.call-start = ((), (), s32[]{:S(2)}) async-start(), calls=%async_computation.6 | async-start | bytes 2359296 | tf_op jit(solution)/shard_map/all_gather | solution.py:97
  57.4 26.6 %collective-permute-start = (bf16[4,512,256]{2,1,0:T(8,128)(2,1)S(1)}, bf16[4,512,256]{2,1,0:T(8,128)(2,1)S(1)}, u32[]{:S(2)}, u32[]{:S(2)}) collective-permute-start(bf16[4,512,256]{2,1,0:T(8,128)(2,1)S(1)} %all-to-all-done.a0), channel_id=1, source_target_pairs={{0,1},{1,0},{2,3},{3,2},{4,5},{5,4},{6,7},{7,6},{8,9},{9,8},{10,11... | collective-permute-start | bytes 3145736 | tf_op jit(solution)/shard_map/ppermute | solution.py:24
  66.9 33.6 %copy-start.3 = (bf16[4,512,256]{2,1,0:T(8,128)(2,1)}, bf16[4,512,256]{2,1,0:T(8,128)(2,1)S(1)}, u32[]{:S(2)}) copy-start(bf16[4,512,256]{2,1,0:T(8,128)(2,1)S(1)} %all-to-all-done.1.a2) | copy-start | bytes 3145732
  66.9 17.2 %collective-permute-start.2 = (bf16[4,512,256]{2,1,0:T(8,128)(2,1)S(1)}, bf16[4,512,256]{2,1,0:T(8,128)(2,1)}, u32[]{:S(2)}, u32[]{:S(2)}) collective-permute-start(bf16[4,512,256]{2,1,0:T(8,128)(2,1)S(1)} %all-to-all-done.1.a2), channel_id=1, source_target_pairs={{0,1},{1,0},{2,3},{3,2},{4,5},{5,4},{6,7},{7,6},{8,9},{9,8},{10,11... | collective-permute-start | bytes 3145736 | tf_op jit(solution)/shard_map/ppermute | solution.py:24
  68.8 37.2 %collective-permute-start.3 = (bf16[128,256]{1,0:T(8,128)(2,1)S(1)}, bf16[128,256]{1,0:T(8,128)(2,1)S(1)}, u32[]{:S(2)}, u32[]{:S(2)}) collective-permute-start(bf16[128,256]{1,0:T(8,128)(2,1)S(1)} %constant_dynamic-slice_fusion), channel_id=1, source_target_pairs={{0,2},{2,0},{1,3},{3,1},{4,6},{6,4},{5,7},{7,5},{8,10},{10,8},{9,1... | collective-permute-start | bytes 196616 | tf_op jit(solution)/shard_map/ppermute | solution.py:93
  84.0 16.4 %copy-start.5 = (bf16[4,512,256]{2,1,0:T(8,128)(2,1)}, bf16[4,512,256]{2,1,0:T(8,128)(2,1)S(1)}, u32[]{:S(2)}) copy-start(bf16[4,512,256]{2,1,0:T(8,128)(2,1)S(1)} %collective-permute-done.a1) | copy-start | bytes 3145732
  132.2 40.0 %copy-start = (bf16[4,512,256]{2,1,0:T(8,128)(2,1)}, bf16[4,512,256]{2,1,0:T(8,128)(2,1)S(1)}, u32[]{:S(2)}) copy-start(bf16[4,512,256]{2,1,0:T(8,128)(2,1)S(1)} %all_to_all.31.a0) | copy-start | bytes 3145732
  133.3 14.4 %all-to-all-start.4 = ((bf16[4,512,256]{2,1,0:T(8,128)(2,1)}), bf16[4,512,256]{2,1,0:T(8,128)(2,1)S(1)}, u32[]{:S(2)}, u32[]{:S(2)}) async-start(bf16[4,512,256]{2,1,0:T(8,128)(2,1)} %broadcast_in_dim.41), calls=%async_computation.4 | async-start | bytes 2097152 | tf_op jit(solution)/shard_map/all_to_all | solution.py:17
  138.2 11.4 %collective-permute-start.4 = (bf16[4,512,256]{2,1,0:T(8,128)(2,1)S(1)}, bf16[4,512,256]{2,1,0:T(8,128)(2,1)S(1)}, u32[]{:S(2)}, u32[]{:S(2)}) collective-permute-start(bf16[4,512,256]{2,1,0:T(8,128)(2,1)S(1)} %all_to_all.31.a0), channel_id=1, source_target_pairs={{0,1},{1,0},{2,3},{3,2},{4,5},{5,4},{6,7},{7,6},{8,9},{9,8},{10,11... | collective-permute-start | bytes 3145736 | tf_op jit(solution)/shard_map/ppermute | solution.py:24
  147.7 24.5 %copy-start.1 = (bf16[4,512,256]{2,1,0:T(8,128)(2,1)}, bf16[4,512,256]{2,1,0:T(8,128)(2,1)S(1)}, u32[]{:S(2)}) copy-start(bf16[4,512,256]{2,1,0:T(8,128)(2,1)S(1)} %all-to-all-done.4.a2) | copy-start | bytes 3145732
  147.7 4.7 %collective-permute-start.5 = (bf16[4,512,256]{2,1,0:T(8,128)(2,1)S(1)}, bf16[4,512,256]{2,1,0:T(8,128)(2,1)}, u32[]{:S(2)}, u32[]{:S(2)}) collective-permute-start(bf16[4,512,256]{2,1,0:T(8,128)(2,1)S(1)} %all-to-all-done.4.a2), channel_id=1, source_target_pairs={{0,1},{1,0},{2,3},{3,2},{4,5},{5,4},{6,7},{7,6},{8,9},{9,8},{10,11... | collective-permute-start | bytes 3145736 | tf_op jit(solution)/shard_map/ppermute | solution.py:24
  149.6 22.6 %copy-start.4 = (bf16[4,512,256]{2,1,0:T(8,128)(2,1)}, bf16[4,512,256]{2,1,0:T(8,128)(2,1)S(1)}, u32[]{:S(2)}) copy-start(bf16[4,512,256]{2,1,0:T(8,128)(2,1)S(1)} %collective-permute-done.4.a1) | copy-start | bytes 3145732
Sparse Core Ops, SparseCore 0:
  10.1 90.3 all-gather.5
  106.2 65.9 all-gather.3

commit v2 on v1

v2 whole, which is shorter than its diff:
```python
import jax
import jax.numpy as jnp
from jax import lax
from jax.experimental import pallas as pl
from jax.experimental.pallas import tpu as pltpu
from jax.sharding import Mesh, PartitionSpec as P

decay_rate = 0.9
step_rate = 0.1
AXES = ("quarter", "row", "y", "z_hi", "core")
SWAP = [(0, 1), (1, 0)]
CUBE = 4


def copies_to_all(piece, axis):
    n = lax.axis_size(axis)
    spread = jnp.broadcast_to(piece[None], (n, *piece.shape))
    return lax.all_to_all(spread, axis, 0, 0, tiled=True)


def turn(piece, by):
    rows = lax.axis_size("row")
    pairs = [(i, i // CUBE * CUBE + (i + by) % CUBE) for i in range(rows)]
    return lax.ppermute(piece, "row", pairs)


def across(piece):
    rows = lax.axis_size("row")
    return lax.ppermute(piece, "row", [(i, i ^ CUBE) for i in range(rows)])


def cube_slots(piece):
    return [piece] + [turn(piece, by) for by in range(1, CUBE)]


def accumulate(place, pieces, slots, panel_ref, sems):
    half, core, turned = place[0], place[1], place[2]
    depth = pieces[0].shape[-1]

    @pl.when(pl.program_id(0) == 0)
    def _():
        loads = [
            pltpu.make_async_copy(slot, panel_ref.at[lax.rem(turned + CUBE - s, CUBE)], sems.at[s])
            for s, slot in enumerate(slots)
        ]
        for load in loads:
            load.start()
        for load in loads:
            load.wait()

    total = None
    for n, piece in enumerate(pieces):
        at = 2 * pl.program_id(0) + (half if n < 2 else 1 - half)
        first = depth * (core if n % 2 == 0 else 1 - core)
        rows = panel_ref[at, pl.ds(pl.multiple_of(first, depth), depth), :]
        part = jnp.dot(piece[0], rows, preferred_element_type=jnp.float32)
        total = part if total is None else total + part
    return total


def split(refs, extra, outs):
    refs = list(refs)
    pieces, slots, refs = refs[:4], refs[4 : 4 + CUBE], refs[4 + CUBE :]
    return pieces, slots, refs[:extra], refs[extra : extra + outs], refs[extra + outs :]


def half_kernel(place, *refs):
    pieces, slots, _, (o_ref,), (panel_ref, sems) = split(refs, 0, 1)
    total = accumulate(place, pieces, slots, panel_ref, sems)

    @pl.when(pl.program_id(0) == 0)
    def _():
        o_ref[...] = total

    @pl.when(pl.program_id(0) == 1)
    def _():
        o_ref[...] += total


def mix_kernel(place, *refs):
    pieces, slots, (p_ref,), (o_ref,), (panel_ref, sems, acc_ref) = split(refs, 1, 1)
    total = accumulate(place, pieces, slots, panel_ref, sems)

    @pl.when(pl.program_id(0) == 0)
    def _():
        acc_ref[...] = p_ref[...] + total

    @pl.when(pl.program_id(0) == 1)
    def _():
        o_ref[...] = (acc_ref[...] + total).astype(o_ref.dtype)


def update_kernel(place, *refs):
    pieces, slots, (p_ref, m_ref, w_ref), (mo_ref, wo_ref), (panel_ref, sems, acc_ref) = split(refs, 3, 2)
    total = accumulate(place, pieces, slots, panel_ref, sems)

    @pl.when(pl.program_id(0) == 0)
    def _():
        acc_ref[...] = p_ref[...] + total

    @pl.when(pl.program_id(0) == 1)
    def _():
        renewed = decay_rate * m_ref[...] + (1.0 - decay_rate) * (acc_ref[...] + total)
        mo_ref[...] = renewed
        wo_ref[...] = (w_ref[...].astype(jnp.float32) - step_rate * renewed).astype(wo_ref.dtype)


def call(body, place, pieces, slots, extra, types):
    _, rows, depth = pieces[0].shape
    own_rows, columns = slots[0].shape
    whole = pl.BlockSpec((rows, columns), lambda i, place: (0, 0))
    a = pl.BlockSpec((1, rows, depth), lambda i, place: (place[3] + i, 0, 0))
    scratch = [pltpu.VMEM((CUBE, own_rows, columns), jnp.bfloat16), pltpu.SemaphoreType.DMA((CUBE,))]
    if extra:
        scratch.append(pltpu.VMEM((rows, columns), jnp.float32))
    moved = 4 * CUBE * rows * depth + 2 * CUBE * own_rows * columns + 8 * rows * columns
    return pl.pallas_call(
        body,
        out_shape=[jax.ShapeDtypeStruct((rows, columns), t) for t in types],
        grid_spec=pltpu.PrefetchScalarGridSpec(
            num_scalar_prefetch=1,
            grid=(2,),
            in_specs=[a] * 4 + [pl.BlockSpec(memory_space=pl.ANY)] * CUBE + [whole] * len(extra),
            out_specs=[whole] * len(types),
            scratch_shapes=scratch,
        ),
        cost_estimate=pl.CostEstimate(
            flops=2 * rows * CUBE * own_rows * columns, bytes_accessed=moved, transcendentals=0
        ),
    )(place, *pieces, *slots, *extra)


def with_partner(mine):
    return [mine, lax.ppermute(mine, "core", SWAP)]


def per_device(grad, left_root, right_root, momentum, weights):
    half, core, row = (lax.axis_index(a).astype(jnp.int32) for a in ("z_hi", "core", "row"))
    upper = row // CUBE
    near = jnp.stack((half, core, row % CUBE, 2 * upper))
    far = jnp.stack((half, core, row % CUBE, 2 - 2 * upper))
    quarter = lax.axis_index("quarter")
    quarters = lax.axis_size("quarter")
    rows, depth = left_root.shape
    part = rows // quarters
    grad, right_root = grad[0], right_root[0]

    left_part = lax.dynamic_slice_in_dim(left_root, quarter * part, part, 0)
    crossed = lax.ppermute(jnp.concatenate((grad, left_part)), "z_hi", SWAP)
    right_far = across(right_root)
    near_slots = cube_slots(right_root)
    grad_mine = copies_to_all(grad, "y")
    grad_theirs = copies_to_all(crossed[:rows], "y")
    panel = with_partner(grad_mine) + with_partner(grad_theirs)
    far_slots = cube_slots(right_far)
    (begun,) = call(half_kernel, near, panel, near_slots, (), (jnp.float32,))
    (mixed,) = call(mix_kernel, far, panel, far_slots, (begun,), (jnp.bfloat16,))
    left_mine = with_partner(copies_to_all(left_root, "y"))

    mixed, left_part = lax.optimization_barrier((mixed, crossed[rows:]))
    mixed_far = across(mixed)
    near_slots = cube_slots(mixed)
    left_other = copies_to_all(left_part, "quarter").reshape(rows, depth)
    left_theirs = copies_to_all(left_other, "y")
    panel = left_mine + with_partner(left_theirs)
    far_slots = cube_slots(mixed_far)
    (begun,) = call(half_kernel, near, panel, near_slots, (), (jnp.float32,))
    renewed, updated = call(
        update_kernel,
        far,
        panel,
        far_slots,
        (begun, momentum[0], weights[0]),
        (jnp.float32, jnp.bfloat16),
    )
    spread = lax.all_to_all(updated.reshape(quarters, part, depth), "quarter", 0, 0, tiled=True)
    return renewed[None], spread


def solution(mesh):
    fine = Mesh(mesh.devices.reshape(4, 8, 4, 2, 2), AXES)
    placed = P("quarter", "row", ("y", "z_hi", "core"))
    return jax.shard_map(
        per_device,
        mesh=fine,
        in_specs=(placed, P("row", ("y", "z_hi", "core")), placed, placed, placed),
        out_specs=(placed, P(None, ("row", "quarter"), ("y", "z_hi", "core"))),
        check_vma=False,
    )
```

time: 198 us -> 261 us (1.32)
  the two profiles are of different devices: /device:TPU:8 before, /device:TPU:32 now
where the time goes in v2:
time: 261 us; the launch traced here: 259 us
  starting transfers between devices  108 us (41%)
  waiting for transfers between devices  99.2 us (38%)
  blocking collectives  21.5 us (8%)
  Pallas kernels  20.8 us (8%)
  local copies, waits for them, and re-layouts  7.5 us (3%)
    ppermute x12, starting transfers between devices, turn(): return lax.ppermute(piece, 'row', pairs)  60.8 us
    ppermute x1, waiting for transfers between devices, per_device(): crossed = lax.ppermute(jnp.concatenate((grad, left_part)), 'z_hi', SWAP)  28.3 us
    ppermute x12, waiting for transfers between devices, turn(): return lax.ppermute(piece, 'row', pairs)  24.3 us
    all_to_all x4, waiting for transfers between devices, copies_to_all(): return lax.all_to_all(spread, axis, 0, 0, tiled=True)  24.1 us
    ppermute x2, waiting for transfers between devices, across(): return lax.ppermute(piece, 'row', [(i, i ^ CUBE) for i in range(rows)])  22.5 us
    pallas_call x4, Pallas kernels, call(): pl.pallas_call(body, out_shape=[jax.ShapeDtypeStruct((rows, columns), t)...  20.8 us
    all_to_all x4, starting transfers between devices, copies_to_all(): return lax.all_to_all(spread, axis, 0, 0, tiled=True)  17.2 us
    ppermute x1, starting transfers between devices, per_device(): crossed = lax.ppermute(jnp.concatenate((grad, left_part)), 'z_hi', SWAP)  14.8 us
  transfers between devices with their start and end apart: 23, of which 12 were waited for; matrix products, arithmetic and copies ran while one was open for 1% of the time, Pallas kernels for 6%

profile of v2, /device:TPU:32, one launch (start us, length us, event | category | flops | bytes accessed | tf_op | source)
XLA Modules:
  0.0 259.4 jit_solution(14599135044733041463)
XLA Ops:
  0.6 2.0 broadcast_in_dim.18
  2.7 4.6 %all-to-all-start.1 = ((bf16[4,512,256]{2,1,0:T(8,128)(2,1)}), bf16[4,512,256]{2,1,0:T(8,128)(2,1)S(1)}, u32[]{:S(2)}, u32[]{:S(2)}) async-start(bf16[4,512,256]{2,1,0:T(8,128)(2,1)} %broadcast_in_dim.18), calls=%async_computation.1 | async-start | bytes 2097152 | tf_op jit(solution)/shard_map/all_to_all | solution.py:18
  7.3 14.8 %collective-permute-start.2 = (bf16[640,256]{1,0:T(8,128)(2,1)S(1)}, bf16[640,256]{1,0:T(8,128)(2,1)S(1)}, u32[]{:S(2)}, u32[]{:S(2)}) collective-permute-start(bf16[640,256]{1,0:T(8,128)(2,1)S(1)} %pad_maximum_fusion), channel_id=1, source_target_pairs={{0,2},{2,0},{1,3},{3,1},{4,6},{6,4},{5,7},{7,5},{8,10},{10,8},{9,1... | collective-permute-start | bytes 983048 | tf_op jit(solution)/shard_map/ppermute | solution.py:149
  22.1 28.3 %collective-permute-done.2 = bf16[640,256]{1,0:T(8,128)(2,1)S(1)} collective-permute-done((bf16[640,256]{1,0:T(8,128)(2,1)S(1)}, bf16[640,256]{1,0:T(8,128)(2,1)S(1)}, u32[]{:S(2)}, u32[]{:S(2)}) %collective-permute-start.2) | collective-permute-done | bytes 327712 | tf_op jit(solution)/shard_map/ppermute | solution.py:149
  50.4 1.2 broadcast_in_dim.38
  51.6 4.5 %all-to-all-start.2 = ((bf16[4,512,256]{2,1,0:T(8,128)(2,1)}), bf16[4,512,256]{2,1,0:T(8,128)(2,1)S(1)}, u32[]{:S(2)}, u32[]{:S(2)}) async-start(bf16[4,512,256]{2,1,0:T(8,128)(2,1)} %broadcast_in_dim.38), calls=%async_computation.2 | async-start | bytes 2097152 | tf_op jit(solution)/shard_map/all_to_all | solution.py:18
  56.1 1.9 collective-permute-start.1
  58.0 12.1 %all-to-all-done.2.refs_2_ = bf16[4,512,256]{2,1,0:T(8,128)(2,1)S(1)} async-done(((bf16[4,512,256]{2,1,0:T(8,128)(2,1)}), bf16[4,512,256]{2,1,0:T(8,128)(2,1)S(1)}, u32[]{:S(2)}, u32[]{:S(2)}) %all-to-all-start.2) | async-done | bytes 1048608 | tf_op jit(solution)/shard_map/all_to_all | solution.py:18
  70.2 1.9 collective-permute-start.3
  72.1 1.9 collective-permute-start.10
  74.0 1.1 broadcast_in_dim.16
  75.1 3.5 %all-to-all-start = ((bf16[4,512,256]{2,1,0:T(8,128)(2,1)}), bf16[4,512,256]{2,1,0:T(8,128)(2,1)S(1)}, u32[]{:S(2)}, u32[]{:S(2)}) async-start(bf16[4,512,256]{2,1,0:T(8,128)(2,1)} %broadcast_in_dim.16), calls=%async_computation | async-start | bytes 2097152 | tf_op jit(solution)/shard_map/all_to_all | solution.py:18
  78.6 2.7 %collective-permute-start.4 = (bf16[512,256]{1,0:T(8,128)(2,1)}, bf16[512,256]{1,0:T(8,128)(2,1)}, u32[]{:S(2)}, u32[]{:S(2)}) collective-permute-start(bf16[512,256]{1,0:T(8,128)(2,1)} %bitcast.5.refs_4_), channel_id=1, source_target_pairs={{0,64},{16,80},{32,96},{48,112},{64,0},{80,16},{96,32},{112,48},{1... | collective-permute-start | bytes 786440 | tf_op jit(solution)/shard_map/ppermute | solution.py:29
  81.3 8.3 %collective-permute-start.8 = (bf16[512,256]{1,0:T(8,128)(2,1)}, bf16[512,256]{1,0:T(8,128)(2,1)}, u32[]{:S(2)}, u32[]{:S(2)}) collective-permute-start(bf16[512,256]{1,0:T(8,128)(2,1)} %bitcast.5.refs_4_), channel_id=1, source_target_pairs={{0,16},{16,32},{32,48},{48,0},{64,80},{80,96},{96,112},{112,64},{1... | collective-permute-start | bytes 786440 | tf_op jit(solution)/shard_map/ppermute | solution.py:24
  89.6 3.4 %collective-permute-start.9 = (bf16[512,256]{1,0:T(8,128)(2,1)}, bf16[512,256]{1,0:T(8,128)(2,1)}, u32[]{:S(2)}, u32[]{:S(2)}) collective-permute-start(bf16[512,256]{1,0:T(8,128)(2,1)} %bitcast.5.refs_4_), channel_id=1, source_target_pairs={{0,32},{16,48},{32,0},{48,16},{64,96},{80,112},{96,64},{112,80},{1... | collective-permute-start | bytes 786440 | tf_op jit(solution)/shard_map/ppermute | solution.py:24
  93.0 0.7 pad_add_fusion.2
  93.7 12.2 %collective-permute-done.4.refs_4_ = bf16[512,256]{1,0:T(8,128)(2,1)} collective-permute-done((bf16[512,256]{1,0:T(8,128)(2,1)}, bf16[512,256]{1,0:T(8,128)(2,1)}, u32[]{:S(2)}, u32[]{:S(2)}) %collective-permute-start.4) | collective-permute-done | bytes 262176 | tf_op jit(solution)/shard_map/ppermute | solution.py:29
  105.9 8.8 %collective-permute-start.5 = (bf16[512,256]{1,0:T(8,128)(2,1)}, bf16[512,256]{1,0:T(8,128)(2,1)}, u32[]{:S(2)}, u32[]{:S(2)}) collective-permute-start(bf16[512,256]{1,0:T(8,128)(2,1)} %collective-permute-done.4.refs_4_), channel_id=1, source_target_pairs={{0,16},{16,32},{32,48},{48,0},{64,80},{80,96},{96,112},{112,64},{1... | collective-permute-start | bytes 786440 | tf_op jit(solution)/shard_map/ppermute | solution.py:24
  114.7 1.9 collective-permute-start.6
  116.7 12.4 %collective-permute-start.7 = (bf16[512,256]{1,0:T(8,128)(2,1)}, bf16[512,256]{1,0:T(8,128)(2,1)}, u32[]{:S(2)}, u32[]{:S(2)}) collective-permute-start(bf16[512,256]{1,0:T(8,128)(2,1)} %collective-permute-done.4.refs_4_), channel_id=1, source_target_pairs={{0,48},{16,0},{32,16},{48,32},{64,112},{80,64},{96,80},{112,96},{1... | collective-permute-start | bytes 786440 | tf_op jit(solution)/shard_map/ppermute | solution.py:24
  129.1 0.6 pad_add_fusion.place
  129.7 5.0 %shard_map.68.refs_8_ = f32[512,256]{1,0:T(8,128)} custom-call(s32[4]{0:T(128)} %get-tuple-element.10.place, bf16[4,512,256]{2,1,0:T(8,128)(2,1)} %copy-done.1, bf16[4,512,256]{2,1,0:T(8,128)(2,1)} %collective-permute-done.1.refs_1_, bf16[4,512,256]{2,1,0:T(8,128)(2,1)} %copy-done.2, bf16[4,512,256]{2,1,0:T(8,128)(2,1)} %collective-permute-done.3.refs_3_, ...), custom_call_target="tpu_custom_call" | custom-call | flops 536870912 | bytes 4194304 | tf_op jit(solution)/shard_map/pallas_call | solution.py:117
  134.7 1.5 collective-permute-done.6.refs_6_
  136.2 0.7 collective-permute-done.7.refs_7_
  136.9 5.1 %shard_map.69.refs_4_ = bf16[512,256]{1,0:T(8,128)(2,1)} custom-call(s32[4]{0:T(128)} %pad_add_fusion.place, bf16[4,512,256]{2,1,0:T(8,128)(2,1)} %copy-done.1, bf16[4,512,256]{2,1,0:T(8,128)(2,1)} %collective-permute-done.1.refs_1_, bf16[4,512,256]{2,1,0:T(8,128)(2,1)} %copy-done.2, bf16[4,512,256]{2,1,0:T(8,128)(2,1)} %collective-permute-done.3.refs_3_, ...), custom_call_target="tpu_custom_call" | custom-call | flops 536870912 | bytes 4194304 | tf_op jit(solution)/shard_map/pallas_call | solution.py:117
  142.1 10.9 %all_to_all.30 = bf16[4,128,256]{2,1,0:T(8,128)(2,1)S(1)} all-to-all(bf16[4,128,256]{2,1,0:T(8,128)(2,1)S(1)} %broadcast_in_dim.39), channel_id=1, replica_groups=mesh['quarter'=4,'row'=8,'y'=4,'z_hi'=2,'core'=2] {'quarter'}, dimensions={0} | all-to-all | bytes 524288 | tf_op jit(solution)/shard_map/all_to_all | solution.py:18
  153.1 1.0 broadcast_in_dim.41
  154.1 4.6 %all-to-all-start.4 = ((bf16[4,512,256]{2,1,0:T(8,128)(2,1)}), bf16[4,512,256]{2,1,0:T(8,128)(2,1)S(1)}, u32[]{:S(2)}, u32[]{:S(2)}) async-start(bf16[4,512,256]{2,1,0:T(8,128)(2,1)} %broadcast_in_dim.41), calls=%async_computation.4 | async-start | bytes 2097152 | tf_op jit(solution)/shard_map/all_to_all | solution.py:18
  158.7 1.9 collective-permute-start
  160.6 11.9 %all-to-all-done.4.refs_2_ = bf16[4,512,256]{2,1,0:T(8,128)(2,1)S(1)} async-done(((bf16[4,512,256]{2,1,0:T(8,128)(2,1)}), bf16[4,512,256]{2,1,0:T(8,128)(2,1)S(1)}, u32[]{:S(2)}, u32[]{:S(2)}) %all-to-all-start.4) | async-done | bytes 1048608 | tf_op jit(solution)/shard_map/all_to_all | solution.py:18
  172.6 1.9 collective-permute-start.11
  174.5 4.9 %collective-permute-start.12 = (bf16[512,256]{1,0:T(8,128)(2,1)S(1)}, bf16[512,256]{1,0:T(8,128)(2,1)}, u32[]{:S(2)}, u32[]{:S(2)}) collective-permute-start(bf16[512,256]{1,0:T(8,128)(2,1)S(1)} %copy-done.5), channel_id=1, source_target_pairs={{0,64},{16,80},{32,96},{48,112},{64,0},{80,16},{96,32},{112,48},{1... | collective-permute-start | bytes 786440 | tf_op jit(solution)/shard_map/ppermute | solution.py:29
  179.4 1.9 collective-permute-start.16
  181.3 5.3 %collective-permute-start.17 = (bf16[512,256]{1,0:T(8,128)(2,1)S(1)}, bf16[512,256]{1,0:T(8,128)(2,1)S(1)}, u32[]{:S(2)}, u32[]{:S(2)}) collective-permute-start(bf16[512,256]{1,0:T(8,128)(2,1)S(1)} %copy-done.5), channel_id=1, source_target_pairs={{0,32},{16,48},{32,0},{48,16},{64,96},{80,112},{96,64},{112,80},{1... | collective-permute-start | bytes 786440 | tf_op jit(solution)/shard_map/ppermute | solution.py:24
  186.6 3.9 %collective-permute-start.18 = (bf16[512,256]{1,0:T(8,128)(2,1)S(1)}, bf16[512,256]{1,0:T(8,128)(2,1)S(1)}, u32[]{:S(2)}, u32[]{:S(2)}) collective-permute-start(bf16[512,256]{1,0:T(8,128)(2,1)S(1)} %copy-done.5), channel_id=1, source_target_pairs={{0,48},{16,0},{32,16},{48,32},{64,112},{80,64},{96,80},{112,96},{1... | collective-permute-start | bytes 786440 | tf_op jit(solution)/shard_map/ppermute | solution.py:24
  190.6 10.3 %collective-permute-done.12.refs_4_ = bf16[512,256]{1,0:T(8,128)(2,1)} collective-permute-done((bf16[512,256]{1,0:T(8,128)(2,1)S(1)}, bf16[512,256]{1,0:T(8,128)(2,1)}, u32[]{:S(2)}, u32[]{:S(2)}) %collective-permute-start.12) | collective-permute-done | bytes 262176 | tf_op jit(solution)/shard_map/ppermute | solution.py:29
  200.9 7.2 %collective-permute-start.13 = (bf16[512,256]{1,0:T(8,128)(2,1)}, bf16[512,256]{1,0:T(8,128)(2,1)S(1)}, u32[]{:S(2)}, u32[]{:S(2)}) collective-permute-start(bf16[512,256]{1,0:T(8,128)(2,1)} %collective-permute-done.12.refs_4_), channel_id=1, source_target_pairs={{0,16},{16,32},{32,48},{48,0},{64,80},{80,96},{96,112},{112,64},{1... | collective-permute-start | bytes 786440 | tf_op jit(solution)/shard_map/ppermute | solution.py:24
  208.2 2.5 collective-permute-start.14
  210.7 3.1 %collective-permute-done.17.refs_6_ = bf16[512,256]{1,0:T(8,128)(2,1)S(1)} collective-permute-done((bf16[512,256]{1,0:T(8,128)(2,1)S(1)}, bf16[512,256]{1,0:T(8,128)(2,1)S(1)}, u32[]{:S(2)}, u32[]{:S(2)}) %collective-permute-start.17) | collective-permute-done | bytes 262176 | tf_op jit(solution)/shard_map/ppermute | solution.py:24
  213.9 3.2 %collective-permute-start.15 = (bf16[512,256]{1,0:T(8,128)(2,1)}, bf16[512,256]{1,0:T(8,128)(2,1)S(1)}, u32[]{:S(2)}, u32[]{:S(2)}) collective-permute-start(bf16[512,256]{1,0:T(8,128)(2,1)} %collective-permute-done.12.refs_4_), channel_id=1, source_target_pairs={{0,48},{16,0},{32,16},{48,32},{64,112},{80,64},{96,80},{112,96},{1... | collective-permute-start | bytes 786440 | tf_op jit(solution)/shard_map/ppermute | solution.py:24
  217.1 13.5 %collective-permute-done.18.refs_7_ = bf16[512,256]{1,0:T(8,128)(2,1)S(1)} collective-permute-done((bf16[512,256]{1,0:T(8,128)(2,1)S(1)}, bf16[512,256]{1,0:T(8,128)(2,1)S(1)}, u32[]{:S(2)}, u32[]{:S(2)}) %collective-permute-start.18) | collective-permute-done | bytes 262176 | tf_op jit(solution)/shard_map/ppermute | solution.py:24
  230.6 0.7 copy-done.11
  231.3 5.0 %shard_map.70.refs_8_ = f32[512,256]{1,0:T(8,128)} custom-call(s32[4]{0:T(128)} %get-tuple-element.10.place, bf16[4,512,256]{2,1,0:T(8,128)(2,1)} %copy-done, bf16[4,512,256]{2,1,0:T(8,128)(2,1)} %copy-done.4, bf16[4,512,256]{2,1,0:T(8,128)(2,1)} %copy-done.3, bf16[4,512,256]{2,1,0:T(8,128)(2,1)} %collective-permute-done.11.refs_3_, ...), custom_call_target="tpu_custom_call" | custom-call | flops 536870912 | bytes 4194304 | tf_op jit(solution)/shard_map/pallas_call | solution.py:117
  236.4 5.4 %collective-permute-done.15.refs_7_ = bf16[512,256]{1,0:T(8,128)(2,1)S(1)} collective-permute-done((bf16[512,256]{1,0:T(8,128)(2,1)}, bf16[512,256]{1,0:T(8,128)(2,1)S(1)}, u32[]{:S(2)}, u32[]{:S(2)}) %collective-permute-start.15) | collective-permute-done | bytes 262176 | tf_op jit(solution)/shard_map/ppermute | solution.py:24
  241.8 0.7 copy-done.14
  242.5 5.7 %shard_map.71 = (f32[512,256]{1,0:T(8,128)}, bf16[512,256]{1,0:T(8,128)(2,1)}) custom-call(s32[4]{0:T(128)} %pad_add_fusion.place, bf16[4,512,256]{2,1,0:T(8,128)(2,1)} %copy-done, bf16[4,512,256]{2,1,0:T(8,128)(2,1)} %copy-done.4, bf16[4,512,256]{2,1,0:T(8,128)(2,1)} %copy-done.3, bf16[4,512,256]{2,1,0:T(8,128)(2,1)} %collective-permute-done.11.refs_3_, ...), custom_call_target="tpu_custom_call" | custom-call | flops 536870912 | bytes 4194304 | tf_op jit(solution)/shard_map/pallas_call | solution.py:117
  248.2 10.5 %all_to_all.31 = bf16[4,128,256]{2,1,0:T(8,128)(2,1)S(1)} all-to-all(bf16[4,128,256]{2,1,0:T(8,128)(2,1)} %bitcast.16), channel_id=1, replica_groups=mesh['quarter'=4,'row'=8,'y'=4,'z_hi'=2,'core'=2] {'quarter'}, dimensions={0} | all-to-all | bytes 524288 | tf_op jit(solution)/shard_map/all_to_all | solution.py:176
  258.7 0.7 copy.8
  (47 shorter events, 0.3 us)
Async XLA Ops:
  2.6 4.6 %copy-start.7 = (bf16[512,256]{1,0:T(8,128)(2,1)S(1)}, bf16[512,256]{1,0:T(8,128)(2,1)}, u32[]{:S(2)}) copy-start(bf16[512,256]{1,0:T(8,128)(2,1)} %param.6) | copy-start | bytes 786436
  2.6 4.6 %copy-start.6 = (bf16[1,512,256]{2,1,0:T(8,128)(2,1)S(1)}, bf16[1,512,256]{2,1,0:T(8,128)(2,1)}, u32[]{:S(2)}) copy-start(bf16[1,512,256]{2,1,0:T(8,128)(2,1)} %param.5) | copy-start | bytes 786436
  2.7 47.8 %all-to-all-start.1 = ((bf16[4,512,256]{2,1,0:T(8,128)(2,1)}), bf16[4,512,256]{2,1,0:T(8,128)(2,1)S(1)}, u32[]{:S(2)}, u32[]{:S(2)}) async-start(bf16[4,512,256]{2,1,0:T(8,128)(2,1)} %broadcast_in_dim.18), calls=%async_computation.1 | async-start | bytes 2097152 | tf_op jit(solution)/shard_map/all_to_all | solution.py:18
  7.3 43.1 %collective-permute-start.2 = (bf16[640,256]{1,0:T(8,128)(2,1)S(1)}, bf16[640,256]{1,0:T(8,128)(2,1)S(1)}, u32[]{:S(2)}, u32[]{:S(2)}) collective-permute-start(bf16[640,256]{1,0:T(8,128)(2,1)S(1)} %pad_maximum_fusion), channel_id=1, source_target_pairs={{0,2},{2,0},{1,3},{3,1},{4,6},{6,4},{5,7},{7,5},{8,10},{10,8},{9,1... | collective-permute-start | bytes 983048 | tf_op jit(solution)/shard_map/ppermute | solution.py:149
  50.4 79.3 %copy-start.8 = (bf16[640,256]{1,0:T(8,128)(2,1)}, bf16[640,256]{1,0:T(8,128)(2,1)S(1)}, u32[]{:S(2)}) copy-start(bf16[640,256]{1,0:T(8,128)(2,1)S(1)} %collective-permute-done.2) | copy-start | bytes 983044
  50.4 5.7 %copy-start.1 = (bf16[4,512,256]{2,1,0:T(8,128)(2,1)}, bf16[4,512,256]{2,1,0:T(8,128)(2,1)S(1)}, u32[]{:S(2)}) copy-start(bf16[4,512,256]{2,1,0:T(8,128)(2,1)S(1)} %all-to-all-done.1.refs_0_) | copy-start | bytes 3145732
  51.6 18.6 %all-to-all-start.2 = ((bf16[4,512,256]{2,1,0:T(8,128)(2,1)}), bf16[4,512,256]{2,1,0:T(8,128)(2,1)S(1)}, u32[]{:S(2)}, u32[]{:S(2)}) async-start(bf16[4,512,256]{2,1,0:T(8,128)(2,1)} %broadcast_in_dim.38), calls=%async_computation.2 | async-start | bytes 2097152 | tf_op jit(solution)/shard_map/all_to_all | solution.py:18
  56.1 73.6 %collective-permute-start.1 = (bf16[4,512,256]{2,1,0:T(8,128)(2,1)S(1)}, bf16[4,512,256]{2,1,0:T(8,128)(2,1)}, u32[]{:S(2)}, u32[]{:S(2)}) collective-permute-start(bf16[4,512,256]{2,1,0:T(8,128)(2,1)S(1)} %all-to-all-done.1.refs_0_), channel_id=1, source_target_pairs={{0,1},{1,0},{2,3},{3,2},{4,5},{5,4},{6,7},{7,6},{8,9},{9,8},{10,11... | collective-permute-start | bytes 3145736 | tf_op jit(solution)/shard_map/ppermute | solution.py:134
  70.2 4.9 %copy-start.2 = (bf16[4,512,256]{2,1,0:T(8,128)(2,1)}, bf16[4,512,256]{2,1,0:T(8,128)(2,1)S(1)}, u32[]{:S(2)}) copy-start(bf16[4,512,256]{2,1,0:T(8,128)(2,1)S(1)} %all-to-all-done.2.refs_2_) | copy-start | bytes 3145732
  70.2 59.6 %collective-permute-start.3 = (bf16[4,512,256]{2,1,0:T(8,128)(2,1)S(1)}, bf16[4,512,256]{2,1,0:T(8,128)(2,1)}, u32[]{:S(2)}, u32[]{:S(2)}) collective-permute-start(bf16[4,512,256]{2,1,0:T(8,128)(2,1)S(1)} %all-to-all-done.2.refs_2_), channel_id=1, source_target_pairs={{0,1},{1,0},{2,3},{3,2},{4,5},{5,4},{6,7},{7,6},{8,9},{9,8},{10,11... | collective-permute-start | bytes 3145736 | tf_op jit(solution)/shard_map/ppermute | solution.py:134
  72.1 17.5 %collective-permute-start.10 = (bf16[512,256]{1,0:T(8,128)(2,1)}, bf16[512,256]{1,0:T(8,128)(2,1)}, u32[]{:S(2)}, u32[]{:S(2)}) collective-permute-start(bf16[512,256]{1,0:T(8,128)(2,1)} %bitcast.5.refs_4_), channel_id=1, source_target_pairs={{0,48},{16,0},{32,16},{48,32},{64,112},{80,64},{96,80},{112,96},{1... | collective-permute-start | bytes 786440 | tf_op jit(solution)/shard_map/ppermute | solution.py:24
  75.1 67.0 %all-to-all-start = ((bf16[4,512,256]{2,1,0:T(8,128)(2,1)}), bf16[4,512,256]{2,1,0:T(8,128)(2,1)S(1)}, u32[]{:S(2)}, u32[]{:S(2)}) async-start(bf16[4,512,256]{2,1,0:T(8,128)(2,1)} %broadcast_in_dim.16), calls=%async_computation | async-start | bytes 2097152 | tf_op jit(solution)/shard_map/all_to_all | solution.py:18
  78.6 27.3 %collective-permute-start.4 = (bf16[512,256]{1,0:T(8,128)(2,1)}, bf16[512,256]{1,0:T(8,128)(2,1)}, u32[]{:S(2)}, u32[]{:S(2)}) collective-permute-start(bf16[512,256]{1,0:T(8,128)(2,1)} %bitcast.5.refs_4_), channel_id=1, source_target_pairs={{0,64},{16,80},{32,96},{48,112},{64,0},{80,16},{96,32},{112,48},{1... | collective-permute-start | bytes 786440 | tf_op jit(solution)/shard_map/ppermute | solution.py:29
  81.3 33.4 %collective-permute-start.8 = (bf16[512,256]{1,0:T(8,128)(2,1)}, bf16[512,256]{1,0:T(8,128)(2,1)}, u32[]{:S(2)}, u32[]{:S(2)}) collective-permute-start(bf16[512,256]{1,0:T(8,128)(2,1)} %bitcast.5.refs_4_), channel_id=1, source_target_pairs={{0,16},{16,32},{32,48},{48,0},{64,80},{80,96},{96,112},{112,64},{1... | collective-permute-start | bytes 786440 | tf_op jit(solution)/shard_map/ppermute | solution.py:24
  89.6 27.0 %collective-permute-start.9 = (bf16[512,256]{1,0:T(8,128)(2,1)}, bf16[512,256]{1,0:T(8,128)(2,1)}, u32[]{:S(2)}, u32[]{:S(2)}) collective-permute-start(bf16[512,256]{1,0:T(8,128)(2,1)} %bitcast.5.refs_4_), channel_id=1, source_target_pairs={{0,32},{16,48},{32,0},{48,16},{64,96},{80,112},{96,64},{112,80},{1... | collective-permute-start | bytes 786440 | tf_op jit(solution)/shard_map/ppermute | solution.py:24
  105.9 28.8 %collective-permute-start.5 = (bf16[512,256]{1,0:T(8,128)(2,1)}, bf16[512,256]{1,0:T(8,128)(2,1)}, u32[]{:S(2)}, u32[]{:S(2)}) collective-permute-start(bf16[512,256]{1,0:T(8,128)(2,1)} %collective-permute-done.4.refs_4_), channel_id=1, source_target_pairs={{0,16},{16,32},{32,48},{48,0},{64,80},{80,96},{96,112},{112,64},{1... | collective-permute-start | bytes 786440 | tf_op jit(solution)/shard_map/ppermute | solution.py:24
  114.7 21.5 %collective-permute-start.6 = (bf16[512,256]{1,0:T(8,128)(2,1)}, bf16[512,256]{1,0:T(8,128)(2,1)}, u32[]{:S(2)}, u32[]{:S(2)}) collective-permute-start(bf16[512,256]{1,0:T(8,128)(2,1)} %collective-permute-done.4.refs_4_), channel_id=1, source_target_pairs={{0,32},{16,48},{32,0},{48,16},{64,96},{80,112},{96,64},{112,80},{1... | collective-permute-start | bytes 786440 | tf_op jit(solution)/shard_map/ppermute | solution.py:24
  116.7 20.2 %collective-permute-start.7 = (bf16[512,256]{1,0:T(8,128)(2,1)}, bf16[512,256]{1,0:T(8,128)(2,1)}, u32[]{:S(2)}, u32[]{:S(2)}) collective-permute-start(bf16[512,256]{1,0:T(8,128)(2,1)} %collective-permute-done.4.refs_4_), channel_id=1, source_target_pairs={{0,48},{16,0},{32,16},{48,32},{64,112},{80,64},{96,80},{112,96},{1... | collective-permute-start | bytes 786440 | tf_op jit(solution)/shard_map/ppermute | solution.py:24
  134.7 7.4 %slice-start = ((bf16[640,256]{1,0:T(8,128)(2,1)}), bf16[128,256]{1,0:T(8,128)(2,1)S(1)}, s32[]{:S(2)}) async-start(bf16[640,256]{1,0:T(8,128)(2,1)} %copy-done.8), calls=%async_computation.6 | async-start | bytes 131072 | tf_op jit(solution)/shard_map/slice | solution.py:160
  142.1 16.6 %copy-start = (bf16[4,512,256]{2,1,0:T(8,128)(2,1)}, bf16[4,512,256]{2,1,0:T(8,128)(2,1)S(1)}, u32[]{:S(2)}) copy-start(bf16[4,512,256]{2,1,0:T(8,128)(2,1)S(1)} %all-to-all-done.refs_0_) | copy-start | bytes 3145732
  154.1 20.4 %copy-start.5 = (bf16[512,256]{1,0:T(8,128)(2,1)S(1)}, bf16[512,256]{1,0:T(8,128)(2,1)}, u32[]{:S(2)}) copy-start(bf16[512,256]{1,0:T(8,128)(2,1)} %shard_map.69.refs_4_) | copy-start | bytes 786436
  154.1 18.5 %all-to-all-start.4 = ((bf16[4,512,256]{2,1,0:T(8,128)(2,1)}), bf16[4,512,256]{2,1,0:T(8,128)(2,1)S(1)}, u32[]{:S(2)}, u32[]{:S(2)}) async-start(bf16[4,512,256]{2,1,0:T(8,128)(2,1)} %broadcast_in_dim.41), calls=%async_computation.4 | async-start | bytes 2097152 | tf_op jit(solution)/shard_map/all_to_all | solution.py:18
  158.7 27.9 %collective-permute-start = (bf16[4,512,256]{2,1,0:T(8,128)(2,1)S(1)}, bf16[4,512,256]{2,1,0:T(8,128)(2,1)S(1)}, u32[]{:S(2)}, u32[]{:S(2)}) collective-permute-start(bf16[4,512,256]{2,1,0:T(8,128)(2,1)S(1)} %all-to-all-done.refs_0_), channel_id=1, source_target_pairs={{0,1},{1,0},{2,3},{3,2},{4,5},{5,4},{6,7},{7,6},{8,9},{9,8},{10,11... | collective-permute-start | bytes 3145736 | tf_op jit(solution)/shard_map/ppermute | solution.py:134
  172.6 58.0 %copy-start.3 = (bf16[4,512,256]{2,1,0:T(8,128)(2,1)}, bf16[4,512,256]{2,1,0:T(8,128)(2,1)S(1)}, u32[]{:S(2)}) copy-start(bf16[4,512,256]{2,1,0:T(8,128)(2,1)S(1)} %all-to-all-done.4.refs_2_) | copy-start | bytes 3145732
  172.6 58.0 %collective-permute-start.11 = (bf16[4,512,256]{2,1,0:T(8,128)(2,1)S(1)}, bf16[4,512,256]{2,1,0:T(8,128)(2,1)}, u32[]{:S(2)}, u32[]{:S(2)}) collective-permute-start(bf16[4,512,256]{2,1,0:T(8,128)(2,1)S(1)} %all-to-all-done.4.refs_2_), channel_id=1, source_target_pairs={{0,1},{1,0},{2,3},{3,2},{4,5},{5,4},{6,7},{7,6},{8,9},{9,8},{10,11... | collective-permute-start | bytes 3145736 | tf_op jit(solution)/shard_map/ppermute | solution.py:134
  174.5 26.4 %collective-permute-start.12 = (bf16[512,256]{1,0:T(8,128)(2,1)S(1)}, bf16[512,256]{1,0:T(8,128)(2,1)}, u32[]{:S(2)}, u32[]{:S(2)}) collective-permute-start(bf16[512,256]{1,0:T(8,128)(2,1)S(1)} %copy-done.5), channel_id=1, source_target_pairs={{0,64},{16,80},{32,96},{48,112},{64,0},{80,16},{96,32},{112,48},{1... | collective-permute-start | bytes 786440 | tf_op jit(solution)/shard_map/ppermute | solution.py:29
  179.4 28.8 %collective-permute-start.16 = (bf16[512,256]{1,0:T(8,128)(2,1)S(1)}, bf16[512,256]{1,0:T(8,128)(2,1)S(1)}, u32[]{:S(2)}, u32[]{:S(2)}) collective-permute-start(bf16[512,256]{1,0:T(8,128)(2,1)S(1)} %copy-done.5), channel_id=1, source_target_pairs={{0,16},{16,32},{32,48},{48,0},{64,80},{80,96},{96,112},{112,64},{1... | collective-permute-start | bytes 786440 | tf_op jit(solution)/shard_map/ppermute | solution.py:24
  181.3 32.5 %collective-permute-start.17 = (bf16[512,256]{1,0:T(8,128)(2,1)S(1)}, bf16[512,256]{1,0:T(8,128)(2,1)S(1)}, u32[]{:S(2)}, u32[]{:S(2)}) collective-permute-start(bf16[512,256]{1,0:T(8,128)(2,1)S(1)} %copy-done.5), channel_id=1, source_target_pairs={{0,32},{16,48},{32,0},{48,16},{64,96},{80,112},{96,64},{112,80},{1... | collective-permute-start | bytes 786440 | tf_op jit(solution)/shard_map/ppermute | solution.py:24
  186.6 44.0 %copy-start.4 = (bf16[4,512,256]{2,1,0:T(8,128)(2,1)}, bf16[4,512,256]{2,1,0:T(8,128)(2,1)S(1)}, u32[]{:S(2)}) copy-start(bf16[4,512,256]{2,1,0:T(8,128)(2,1)S(1)} %collective-permute-done.refs_1_) | copy-start | bytes 3145732
  186.6 44.0 %collective-permute-start.18 = (bf16[512,256]{1,0:T(8,128)(2,1)S(1)}, bf16[512,256]{1,0:T(8,128)(2,1)S(1)}, u32[]{:S(2)}, u32[]{:S(2)}) collective-permute-start(bf16[512,256]{1,0:T(8,128)(2,1)S(1)} %copy-done.5), channel_id=1, source_target_pairs={{0,48},{16,0},{32,16},{48,32},{64,112},{80,64},{96,80},{112,96},{1... | collective-permute-start | bytes 786440 | tf_op jit(solution)/shard_map/ppermute | solution.py:24
  200.9 35.5 %collective-permute-start.13 = (bf16[512,256]{1,0:T(8,128)(2,1)}, bf16[512,256]{1,0:T(8,128)(2,1)S(1)}, u32[]{:S(2)}, u32[]{:S(2)}) collective-permute-start(bf16[512,256]{1,0:T(8,128)(2,1)} %collective-permute-done.12.refs_4_), channel_id=1, source_target_pairs={{0,16},{16,32},{32,48},{48,0},{64,80},{80,96},{96,112},{112,64},{1... | collective-permute-start | bytes 786440 | tf_op jit(solution)/shard_map/ppermute | solution.py:24
  208.2 22.4 %copy-start.9 = (bf16[512,256]{1,0:T(8,128)(2,1)}, bf16[512,256]{1,0:T(8,128)(2,1)S(1)}, u32[]{:S(2)}) copy-start(bf16[512,256]{1,0:T(8,128)(2,1)S(1)} %collective-permute-done.16.refs_5_) | copy-start | bytes 786436
  208.2 28.2 %collective-permute-start.14 = (bf16[512,256]{1,0:T(8,128)(2,1)}, bf16[512,256]{1,0:T(8,128)(2,1)S(1)}, u32[]{:S(2)}, u32[]{:S(2)}) collective-permute-start(bf16[512,256]{1,0:T(8,128)(2,1)} %collective-permute-done.12.refs_4_), channel_id=1, source_target_pairs={{0,32},{16,48},{32,0},{48,16},{64,96},{80,112},{96,64},{112,80},{1... | collective-permute-start | bytes 786440 | tf_op jit(solution)/shard_map/ppermute | solution.py:24
  213.9 16.7 %copy-start.10 = (bf16[512,256]{1,0:T(8,128)(2,1)}, bf16[512,256]{1,0:T(8,128)(2,1)S(1)}, u32[]{:S(2)}) copy-start(bf16[512,256]{1,0:T(8,128)(2,1)S(1)} %collective-permute-done.17.refs_6_) | copy-start | bytes 786436
  213.9 27.9 %collective-permute-start.15 = (bf16[512,256]{1,0:T(8,128)(2,1)}, bf16[512,256]{1,0:T(8,128)(2,1)S(1)}, u32[]{:S(2)}, u32[]{:S(2)}) collective-permute-start(bf16[512,256]{1,0:T(8,128)(2,1)} %collective-permute-done.12.refs_4_), channel_id=1, source_target_pairs={{0,48},{16,0},{32,16},{48,32},{64,112},{80,64},{96,80},{112,96},{1... | collective-permute-start | bytes 786440 | tf_op jit(solution)/shard_map/ppermute | solution.py:24
  230.6 0.7 copy-start.11
  236.3 5.5 %copy-start.12 = (bf16[512,256]{1,0:T(8,128)(2,1)}, bf16[512,256]{1,0:T(8,128)(2,1)S(1)}, u32[]{:S(2)}) copy-start(bf16[512,256]{1,0:T(8,128)(2,1)S(1)} %collective-permute-done.13.refs_5_) | copy-start | bytes 786436
  236.4 5.4 %copy-start.13 = (bf16[512,256]{1,0:T(8,128)(2,1)}, bf16[512,256]{1,0:T(8,128)(2,1)S(1)}, u32[]{:S(2)}) copy-start(bf16[512,256]{1,0:T(8,128)(2,1)S(1)} %collective-permute-done.14.refs_6_) | copy-start | bytes 786436
  241.8 0.7 copy-start.14

commit v3 on v2

v3 whole, which is shorter than its diff:
```python
import jax
import jax.numpy as jnp
from jax import lax
from jax.experimental import pallas as pl
from jax.experimental.pallas import tpu as pltpu
from jax.sharding import Mesh, PartitionSpec as P

decay_rate = 0.9
step_rate = 0.1
AXES = ("quarter", "row", "y", "z_hi", "core")
SWAP = [(0, 1), (1, 0)]
CUBE = 4


def copies_to_all(piece, axis):
    n = lax.axis_size(axis)
    spread = jnp.broadcast_to(piece[None], (n, *piece.shape))
    return lax.all_to_all(spread, axis, 0, 0, tiled=True)


def turn(piece, by):
    rows = lax.axis_size("row")
    pairs = [(i, i // CUBE * CUBE + (i + by) % CUBE) for i in range(rows)]
    return lax.ppermute(piece, "row", pairs)


def across(piece):
    rows = lax.axis_size("row")
    return lax.ppermute(piece, "row", [(i, i ^ CUBE) for i in range(rows)])


def cube_slots(piece):
    return [piece] + [turn(piece, by) for by in range(1, CUBE)]


def accumulate(place, step, pieces, slots):
    half, core, turned = place[0], place[1], place[2]
    depth = pieces[0].shape[-1]
    odd = (turned + half) % 2
    total = None
    for n, piece in enumerate(pieces):
        first = pl.multiple_of(depth * (core if n % 2 == 0 else 1 - core), depth)
        even, other = (slot[pl.ds(first, depth), :] for slot in slots[2 * step : 2 * step + 2])
        rows = jnp.where(odd == n // 2, even, other)
        part = jnp.dot(piece[0], rows, preferred_element_type=jnp.float32)
        total = part if total is None else total + part
    return total


def split(refs, extra, outs):
    refs = list(refs)
    pieces, slots, refs = refs[:4], refs[4 : 4 + CUBE], refs[4 + CUBE :]
    return pieces, slots, refs[:extra], refs[extra : extra + outs], refs[extra + outs :]


def half_kernel(place, *refs):
    pieces, slots, _, (o_ref,), _ = split(refs, 0, 1)

    @pl.when(pl.program_id(0) == 0)
    def _():
        o_ref[...] = accumulate(place, 0, pieces, slots)

    @pl.when(pl.program_id(0) == 1)
    def _():
        o_ref[...] += accumulate(place, 1, pieces, slots)


def mix_kernel(place, *refs):
    pieces, slots, (p_ref,), (o_ref,), (acc_ref,) = split(refs, 1, 1)

    @pl.when(pl.program_id(0) == 0)
    def _():
        acc_ref[...] = p_ref[...] + accumulate(place, 0, pieces, slots)

    @pl.when(pl.program_id(0) == 1)
    def _():
        o_ref[...] = (acc_ref[...] + accumulate(place, 1, pieces, slots)).astype(o_ref.dtype)


def update_kernel(place, *refs):
    pieces, slots, (p_ref, m_ref, w_ref), (mo_ref, wo_ref), (acc_ref,) = split(refs, 3, 2)

    @pl.when(pl.program_id(0) == 0)
    def _():
        acc_ref[...] = p_ref[...] + accumulate(place, 0, pieces, slots)

    @pl.when(pl.program_id(0) == 1)
    def _():
        product = acc_ref[...] + accumulate(place, 1, pieces, slots)
        renewed = decay_rate * m_ref[...] + (1.0 - decay_rate) * product
        mo_ref[...] = renewed
        wo_ref[...] = (w_ref[...].astype(jnp.float32) - step_rate * renewed).astype(wo_ref.dtype)


def call(body, place, pieces, at_rows, slots, extra, types):
    depth = pieces[0].shape[-1]
    rows, columns = own_rows, _ = slots[0].shape
    whole = pl.BlockSpec((rows, columns), lambda i, place: (0, 0))

    def piece_spec(theirs, block):
        def at(i, place):
            odd = (place[2] + place[0]) % 2
            back = 2 * i + (1 - odd if theirs else odd)
            return place[3] + (place[2] + 2 * CUBE - back) % CUBE // 2, block, 0

        return pl.BlockSpec((1, rows, depth), at)

    slot_spec = pl.BlockSpec((own_rows, columns), lambda i, place: (0, 0))
    moved = 4 * CUBE * rows * depth + 2 * CUBE * own_rows * columns + 8 * rows * columns
    return pl.pallas_call(
        body,
        out_shape=[jax.ShapeDtypeStruct((rows, columns), t) for t in types],
        grid_spec=pltpu.PrefetchScalarGridSpec(
            num_scalar_prefetch=1,
            grid=(2,),
            in_specs=[piece_spec(n >= 2, at_rows[n]) for n in range(4)] + [slot_spec] * CUBE + [whole] * len(extra),
            out_specs=[whole] * len(types),
            scratch_shapes=[pltpu.VMEM((rows, columns), jnp.float32)] if extra else [],
        ),
        cost_estimate=pl.CostEstimate(
            flops=2 * rows * CUBE * own_rows * columns, bytes_accessed=moved, transcendentals=0
        ),
    )(place, *pieces, *slots, *extra)


def with_partner(mine):
    return [mine, lax.ppermute(mine, "core", SWAP)]


def per_device(grad, left_root, right_root, momentum, weights):
    half, core, row = (lax.axis_index(a).astype(jnp.int32) for a in ("z_hi", "core", "row"))
    upper = row // CUBE
    near = jnp.stack((half, core, row % CUBE, 2 * upper))
    far = jnp.stack((half, core, row % CUBE, 2 - 2 * upper))
    quarter = lax.axis_index("quarter")
    quarters = lax.axis_size("quarter")
    rows, depth = left_root.shape
    part = rows // quarters
    grad, right_root = grad[0], right_root[0]

    left_part = lax.dynamic_slice_in_dim(left_root, quarter * part, part, 0)
    crossed = lax.ppermute(jnp.concatenate((grad, left_part)), "z_hi", SWAP)
    right_far = across(right_root)
    near_slots = cube_slots(right_root)
    mine = with_partner(copies_to_all(jnp.concatenate((grad, left_root)), "y"))
    grad_theirs = copies_to_all(crossed[:rows], "y")
    panel = mine + with_partner(grad_theirs)
    far_slots = cube_slots(right_far)
    (begun,) = call(half_kernel, near, panel, (0, 0, 0, 0), near_slots, (), (jnp.float32,))
    (mixed,) = call(mix_kernel, far, panel, (0, 0, 0, 0), far_slots, (begun,), (jnp.bfloat16,))

    mixed, left_part = lax.optimization_barrier((mixed, crossed[rows:]))
    mixed_far = across(mixed)
    near_slots = cube_slots(mixed)
    left_other = copies_to_all(left_part, "quarter").reshape(rows, depth)
    left_theirs = copies_to_all(left_other, "y")
    panel = mine + with_partner(left_theirs)
    far_slots = cube_slots(mixed_far)
    (begun,) = call(half_kernel, near, panel, (1, 1, 0, 0), near_slots, (), (jnp.float32,))
    renewed, updated = call(
        update_kernel,
        far,
        panel,
        (1, 1, 0, 0),
        far_slots,
        (begun, momentum[0], weights[0]),
        (jnp.float32, jnp.bfloat16),
    )
    spread = lax.all_to_all(updated.reshape(quarters, part, depth), "quarter", 0, 0, tiled=True)
    return renewed[None], spread


def solution(mesh):
    fine = Mesh(mesh.devices.reshape(4, 8, 4, 2, 2), AXES)
    placed = P("quarter", "row", ("y", "z_hi", "core"))
    return jax.shard_map(
        per_device,
        mesh=fine,
        in_specs=(placed, P("row", ("y", "z_hi", "core")), placed, placed, placed),
        out_specs=(placed, P(None, ("row", "quarter"), ("y", "z_hi", "core"))),
        check_vma=False,
    )
```

time: 261 us -> 249 us (0.954)
  the two profiles are of different devices: /device:TPU:32 before, /device:TPU:480 now
where the time goes in v3:
time: 249 us; the launch traced here: 248 us
  starting transfers between devices  93.8 us (38%)
  waiting for transfers between devices  72.1 us (29%)
  blocking collectives  56.3 us (23%)
  Pallas kernels  16.9 us (7%)
  local copies, waits for them, and re-layouts  5.66 us (2%)
    ppermute x12, starting transfers between devices, turn(): return lax.ppermute(piece, 'row', pairs)  69.3 us
    all_to_all x3, blocking collectives, copies_to_all(): return lax.all_to_all(spread, axis, 0, 0, tiled=True)  46.2 us
    ppermute x12, waiting for transfers between devices, turn(): return lax.ppermute(piece, 'row', pairs)  28.4 us
    all_to_all x1, waiting for transfers between devices, copies_to_all(): return lax.all_to_all(spread, axis, 0, 0, tiled=True)  19.1 us
    pallas_call x4, Pallas kernels, call(): pl.pallas_call(body, out_shape=[jax.ShapeDtypeStruct((rows, columns), t)...  16.9 us
    ppermute x2, waiting for transfers between devices, across(): return lax.ppermute(piece, 'row', [(i, i ^ CUBE) for i in range(rows)])  13.8 us
    ppermute x1, waiting for transfers between devices, per_device(): crossed = lax.ppermute(jnp.concatenate((grad, left_part)), 'z_hi', SWAP)  10.8 us
    all_to_all x1, blocking collectives, per_device(): lax.all_to_all(updated.reshape(quarters, part, depth), 'quarter', 0, 0, t...  10.1 us
  transfers between devices with their start and end apart: 19, of which 8 were waited for; matrix products, arithmetic and copies ran while one was open for 1% of the time, Pallas kernels for 3%

profile of v3, /device:TPU:480, one launch (start us, length us, event | category | flops | bytes accessed | tf_op | source)
XLA Modules:
  0.0 248.0 jit_solution(7985639420833583849)
XLA Ops:
  0.6 1.1 pad_maximum_fusion
  1.7 1.5 broadcast_in_dim.12
  3.2 4.6 %all-to-all-start = ((bf16[4,1024,256]{2,1,0:T(8,128)(2,1)}), bf16[4,1024,256]{2,1,0:T(8,128)(2,1)S(1)}, u32[]{:S(2)}, u32[]{:S(2)}) async-start(bf16[4,1024,256]{2,1,0:T(8,128)(2,1)} %broadcast_in_dim.12), calls=%async_computation | async-start | bytes 4194304 | tf_op jit(solution)/shard_map/all_to_all | solution.py:18
  7.8 0.8 constant_dynamic-slice_fusion
  8.6 6.3 %collective-permute-start.1 = (bf16[640,256]{1,0:T(8,128)(2,1)S(1)}, bf16[640,256]{1,0:T(8,128)(2,1)S(1)}, u32[]{:S(2)}, u32[]{:S(2)}) collective-permute-start(bf16[640,256]{1,0:T(8,128)(2,1)S(1)} %pad_maximum_fusion.1), channel_id=1, source_target_pairs={{0,2},{2,0},{1,3},{3,1},{4,6},{6,4},{5,7},{7,5},{8,10},{10,8},{9,1... | collective-permute-start | bytes 983048 | tf_op jit(solution)/shard_map/ppermute | solution.py:142
  15.0 19.1 %all-to-all-done.refs_0_ = bf16[4,1024,256]{2,1,0:T(8,128)(2,1)S(1)} async-done(((bf16[4,1024,256]{2,1,0:T(8,128)(2,1)}), bf16[4,1024,256]{2,1,0:T(8,128)(2,1)S(1)}, u32[]{:S(2)}, u32[]{:S(2)}) %all-to-all-start) | async-done | bytes 2097184 | tf_op jit(solution)/shard_map/all_to_all | solution.py:18
  34.1 1.9 collective-permute-start
  36.0 10.8 %collective-permute-done.1 = bf16[640,256]{1,0:T(8,128)(2,1)S(1)} collective-permute-done((bf16[640,256]{1,0:T(8,128)(2,1)S(1)}, bf16[640,256]{1,0:T(8,128)(2,1)S(1)}, u32[]{:S(2)}, u32[]{:S(2)}) %collective-permute-start.1) | collective-permute-done | bytes 327712 | tf_op jit(solution)/shard_map/ppermute | solution.py:142
  46.8 0.1 broadcast_in_dim.13
  46.9 19.3 %all_to_all.25.refs_2_ = bf16[4,512,256]{2,1,0:T(8,128)(2,1)S(1)} all-to-all(bf16[4,512,256]{2,1,0:T(8,128)(2,1)S(1)} %broadcast_in_dim.13), channel_id=1, replica_groups=mesh['quarter'=4,'row'=8,'y'=4,'z_hi'=2,'core'=2] {'y'}, dimensions={0} | all-to-all | bytes 2097152 | tf_op jit(solution)/shard_map/all_to_all | solution.py:18
  66.2 1.9 collective-permute-start.2
  68.1 1.9 collective-permute-start.7
  70.1 3.2 %collective-permute-start.3 = (bf16[512,256]{1,0:T(8,128)(2,1)}, bf16[512,256]{1,0:T(8,128)(2,1)}, u32[]{:S(2)}, u32[]{:S(2)}) collective-permute-start(bf16[512,256]{1,0:T(8,128)(2,1)} %bitcast.17), channel_id=1, source_target_pairs={{0,64},{16,80},{32,96},{48,112},{64,0},{80,16},{96,32},{112,48},{1... | collective-permute-start | bytes 786440 | tf_op jit(solution)/shard_map/ppermute | solution.py:29
  73.3 7.1 %collective-permute-start.8 = (bf16[512,256]{1,0:T(8,128)(2,1)}, bf16[512,256]{1,0:T(8,128)(2,1)}, u32[]{:S(2)}, u32[]{:S(2)}) collective-permute-start(bf16[512,256]{1,0:T(8,128)(2,1)} %bitcast.18), channel_id=1, source_target_pairs={{0,32},{16,48},{32,0},{48,16},{64,96},{80,112},{96,64},{112,80},{1... | collective-permute-start | bytes 786440 | tf_op jit(solution)/shard_map/ppermute | solution.py:24
  80.4 2.5 %collective-permute-done.7.refs_5_ = bf16[512,256]{1,0:T(8,128)(2,1)} collective-permute-done((bf16[512,256]{1,0:T(8,128)(2,1)}, bf16[512,256]{1,0:T(8,128)(2,1)}, u32[]{:S(2)}, u32[]{:S(2)}) %collective-permute-start.7) | collective-permute-done | bytes 262176 | tf_op jit(solution)/shard_map/ppermute | solution.py:24
  82.9 22.5 %collective-permute-start.9 = (bf16[512,256]{1,0:T(8,128)(2,1)}, bf16[512,256]{1,0:T(8,128)(2,1)}, u32[]{:S(2)}, u32[]{:S(2)}) collective-permute-start(bf16[512,256]{1,0:T(8,128)(2,1)} %bitcast.19), channel_id=1, source_target_pairs={{0,48},{16,0},{32,16},{48,32},{64,112},{80,64},{96,80},{112,96},{1... | collective-permute-start | bytes 786440 | tf_op jit(solution)/shard_map/ppermute | solution.py:24
  105.5 0.6 pad_add_fusion.2
  106.0 1.9 collective-permute-start.4
  107.9 1.9 collective-permute-done.8.refs_6_
  109.8 1.9 collective-permute-start.5
  111.7 0.7 collective-permute-done.9.refs_7_
  112.4 4.4 %collective-permute-start.6 = (bf16[512,256]{1,0:T(8,128)(2,1)}, bf16[512,256]{1,0:T(8,128)(2,1)}, u32[]{:S(2)}, u32[]{:S(2)}) collective-permute-start(bf16[512,256]{1,0:T(8,128)(2,1)} %collective-permute-done.3.refs_4_), channel_id=1, source_target_pairs={{0,48},{16,0},{32,16},{48,32},{64,112},{80,64},{96,80},{112,96},{1... | collective-permute-start | bytes 786440 | tf_op jit(solution)/shard_map/ppermute | solution.py:24
  116.8 0.6 pad_add_fusion.place
  117.4 0.0 collective-permute-done.2.refs_3_
  117.4 4.1 %shard_map.68.refs_8_ = f32[512,256]{1,0:T(8,128)} custom-call(s32[4]{0:T(128)} %get-tuple-element.10.place, bf16[4,1024,256]{2,1,0:T(8,128)(2,1)} %copy-done, bf16[4,1024,256]{2,1,0:T(8,128)(2,1)} %collective-permute-done.refs_1_, bf16[4,512,256]{2,1,0:T(8,128)(2,1)} %copy-done.2, bf16[4,512,256]{2,1,0:T(8,128)(2,1)} %collective-permute-done.2.refs_3_, ...), custom_call_target="tpu_custom_call" | custom-call | flops 536870912 | bytes 4194304 | tf_op jit(solution)/shard_map/pallas_call | solution.py:110
  121.5 10.6 %collective-permute-done.5.refs_6_ = bf16[512,256]{1,0:T(8,128)(2,1)} collective-permute-done((bf16[512,256]{1,0:T(8,128)(2,1)}, bf16[512,256]{1,0:T(8,128)(2,1)}, u32[]{:S(2)}, u32[]{:S(2)}) %collective-permute-start.5) | collective-permute-done | bytes 262176 | tf_op jit(solution)/shard_map/ppermute | solution.py:24
  132.1 4.2 %shard_map.69.refs_4_ = bf16[512,256]{1,0:T(8,128)(2,1)} custom-call(s32[4]{0:T(128)} %pad_add_fusion.place, bf16[4,1024,256]{2,1,0:T(8,128)(2,1)} %copy-done, bf16[4,1024,256]{2,1,0:T(8,128)(2,1)} %collective-permute-done.refs_1_, bf16[4,512,256]{2,1,0:T(8,128)(2,1)} %copy-done.2, bf16[4,512,256]{2,1,0:T(8,128)(2,1)} %collective-permute-done.2.refs_3_, ...), custom_call_target="tpu_custom_call" | custom-call | flops 536870912 | bytes 4194304 | tf_op jit(solution)/shard_map/pallas_call | solution.py:110
  136.3 10.9 %all_to_all.26 = bf16[4,128,256]{2,1,0:T(8,128)(2,1)S(1)} all-to-all(bf16[4,128,256]{2,1,0:T(8,128)(2,1)S(1)} %broadcast_in_dim.14), channel_id=1, replica_groups=mesh['quarter'=4,'row'=8,'y'=4,'z_hi'=2,'core'=2] {'quarter'}, dimensions={0} | all-to-all | bytes 524288 | tf_op jit(solution)/shard_map/all_to_all | solution.py:18
  147.2 0.1 broadcast_in_dim.32
  147.3 16.0 %all_to_all.27.refs_2_ = bf16[4,512,256]{2,1,0:T(8,128)(2,1)S(1)} all-to-all(bf16[4,512,256]{2,1,0:T(8,128)(2,1)S(1)} %broadcast_in_dim.32), channel_id=1, replica_groups=mesh['quarter'=4,'row'=8,'y'=4,'z_hi'=2,'core'=2] {'y'}, dimensions={0} | all-to-all | bytes 2097152 | tf_op jit(solution)/shard_map/all_to_all | solution.py:18
  163.3 1.9 collective-permute-start.10
  165.2 4.6 %collective-permute-start.11 = (bf16[512,256]{1,0:T(8,128)(2,1)S(1)}, bf16[512,256]{1,0:T(8,128)(2,1)S(1)}, u32[]{:S(2)}, u32[]{:S(2)}) collective-permute-start(bf16[512,256]{1,0:T(8,128)(2,1)S(1)} %copy-done.4), channel_id=1, source_target_pairs={{0,64},{16,80},{32,96},{48,112},{64,0},{80,16},{96,32},{112,48},{1... | collective-permute-start | bytes 786440 | tf_op jit(solution)/shard_map/ppermute | solution.py:29
  169.8 1.9 collective-permute-start.15
  171.7 5.1 %collective-permute-start.16 = (bf16[512,256]{1,0:T(8,128)(2,1)S(1)}, bf16[512,256]{1,0:T(8,128)(2,1)S(1)}, u32[]{:S(2)}, u32[]{:S(2)}) collective-permute-start(bf16[512,256]{1,0:T(8,128)(2,1)S(1)} %copy-done.4), channel_id=1, source_target_pairs={{0,32},{16,48},{32,0},{48,16},{64,96},{80,112},{96,64},{112,80},{1... | collective-permute-start | bytes 786440 | tf_op jit(solution)/shard_map/ppermute | solution.py:24
  176.9 3.9 %collective-permute-start.17 = (bf16[512,256]{1,0:T(8,128)(2,1)S(1)}, bf16[512,256]{1,0:T(8,128)(2,1)S(1)}, u32[]{:S(2)}, u32[]{:S(2)}) collective-permute-start(bf16[512,256]{1,0:T(8,128)(2,1)S(1)} %copy-done.4), channel_id=1, source_target_pairs={{0,48},{16,0},{32,16},{48,32},{64,112},{80,64},{96,80},{112,96},{1... | collective-permute-start | bytes 786440 | tf_op jit(solution)/shard_map/ppermute | solution.py:24
  180.8 13.8 %collective-permute-done.11.refs_4_ = bf16[512,256]{1,0:T(8,128)(2,1)S(1)} collective-permute-done((bf16[512,256]{1,0:T(8,128)(2,1)S(1)}, bf16[512,256]{1,0:T(8,128)(2,1)S(1)}, u32[]{:S(2)}, u32[]{:S(2)}) %collective-permute-start.11) | collective-permute-done | bytes 262176 | tf_op jit(solution)/shard_map/ppermute | solution.py:29
  194.6 1.9 collective-permute-start.12
  196.5 0.0 copy-start.9
  196.6 6.0 %collective-permute-start.13 = (bf16[512,256]{1,0:T(8,128)(2,1)S(1)}, bf16[512,256]{1,0:T(8,128)(2,1)S(1)}, u32[]{:S(2)}, u32[]{:S(2)}) collective-permute-start(bf16[512,256]{1,0:T(8,128)(2,1)S(1)} %collective-permute-done.11.refs_4_), channel_id=1, source_target_pairs={{0,32},{16,48},{32,0},{48,16},{64,96},{80,112},{96,64},{112,80},{1... | collective-permute-start | bytes 786440 | tf_op jit(solution)/shard_map/ppermute | solution.py:24
  202.6 10.8 %collective-permute-start.14 = (bf16[512,256]{1,0:T(8,128)(2,1)S(1)}, bf16[512,256]{1,0:T(8,128)(2,1)}, u32[]{:S(2)}, u32[]{:S(2)}) collective-permute-start(bf16[512,256]{1,0:T(8,128)(2,1)S(1)} %collective-permute-done.11.refs_4_), channel_id=1, source_target_pairs={{0,48},{16,0},{32,16},{48,32},{64,112},{80,64},{96,80},{112,96},{1... | collective-permute-start | bytes 786440 | tf_op jit(solution)/shard_map/ppermute | solution.py:24
  213.3 0.7 copy-done.12
  214.1 1.0 copy-done.3
  215.1 4.1 %shard_map.70.refs_8_ = f32[512,256]{1,0:T(8,128)} custom-call(s32[4]{0:T(128)} %get-tuple-element.10.place, bf16[4,1024,256]{2,1,0:T(8,128)(2,1)} %copy-done, bf16[4,1024,256]{2,1,0:T(8,128)(2,1)} %collective-permute-done.refs_1_, bf16[4,512,256]{2,1,0:T(8,128)(2,1)} %copy-done.1, bf16[4,512,256]{2,1,0:T(8,128)(2,1)} %copy-done.3, ...), custom_call_target="tpu_custom_call" | custom-call | flops 536870912 | bytes 4194304 | tf_op jit(solution)/shard_map/pallas_call | solution.py:110
  219.2 12.8 %collective-permute-done.13.refs_6_ = bf16[512,256]{1,0:T(8,128)(2,1)S(1)} collective-permute-done((bf16[512,256]{1,0:T(8,128)(2,1)S(1)}, bf16[512,256]{1,0:T(8,128)(2,1)S(1)}, u32[]{:S(2)}, u32[]{:S(2)}) %collective-permute-start.13) | collective-permute-done | bytes 262176 | tf_op jit(solution)/shard_map/ppermute | solution.py:24
  232.0 0.7 copy-done.10
  232.7 4.6 %shard_map.71 = (f32[512,256]{1,0:T(8,128)}, bf16[512,256]{1,0:T(8,128)(2,1)}) custom-call(s32[4]{0:T(128)} %pad_add_fusion.place, bf16[4,1024,256]{2,1,0:T(8,128)(2,1)} %copy-done, bf16[4,1024,256]{2,1,0:T(8,128)(2,1)} %collective-permute-done.refs_1_, bf16[4,512,256]{2,1,0:T(8,128)(2,1)} %copy-done.1, bf16[4,512,256]{2,1,0:T(8,128)(2,1)} %copy-done.3, ...), custom_call_target="tpu_custom_call" | custom-call | flops 536870912 | bytes 4194304 | tf_op jit(solution)/shard_map/pallas_call | solution.py:110
  237.3 10.1 %all_to_all.28 = bf16[4,128,256]{2,1,0:T(8,128)(2,1)S(1)} all-to-all(bf16[4,128,256]{2,1,0:T(8,128)(2,1)} %bitcast.22), channel_id=1, replica_groups=mesh['quarter'=4,'row'=8,'y'=4,'z_hi'=2,'core'=2] {'quarter'}, dimensions={0} | all-to-all | bytes 524288 | tf_op jit(solution)/shard_map/all_to_all | solution.py:169
  247.3 0.7 copy.8
  (37 shorter events, 0.1 us)
Async XLA Ops:
  3.2 5.4 %copy-start.5 = (bf16[1,512,256]{2,1,0:T(8,128)(2,1)S(1)}, bf16[1,512,256]{2,1,0:T(8,128)(2,1)}, u32[]{:S(2)}) copy-start(bf16[1,512,256]{2,1,0:T(8,128)(2,1)} %param.5) | copy-start | bytes 786436
  3.2 30.9 %all-to-all-start = ((bf16[4,1024,256]{2,1,0:T(8,128)(2,1)}), bf16[4,1024,256]{2,1,0:T(8,128)(2,1)S(1)}, u32[]{:S(2)}, u32[]{:S(2)}) async-start(bf16[4,1024,256]{2,1,0:T(8,128)(2,1)} %broadcast_in_dim.12), calls=%async_computation | async-start | bytes 4194304 | tf_op jit(solution)/shard_map/all_to_all | solution.py:18
  8.6 38.1 %collective-permute-start.1 = (bf16[640,256]{1,0:T(8,128)(2,1)S(1)}, bf16[640,256]{1,0:T(8,128)(2,1)S(1)}, u32[]{:S(2)}, u32[]{:S(2)}) collective-permute-start(bf16[640,256]{1,0:T(8,128)(2,1)S(1)} %pad_maximum_fusion.1), channel_id=1, source_target_pairs={{0,2},{2,0},{1,3},{3,1},{4,6},{6,4},{5,7},{7,5},{8,10},{10,8},{9,1... | collective-permute-start | bytes 983048 | tf_op jit(solution)/shard_map/ppermute | solution.py:142
  34.1 83.3 %copy-start = (bf16[4,1024,256]{2,1,0:T(8,128)(2,1)}, bf16[4,1024,256]{2,1,0:T(8,128)(2,1)S(1)}, u32[]{:S(2)}) copy-start(bf16[4,1024,256]{2,1,0:T(8,128)(2,1)S(1)} %all-to-all-done.refs_0_) | copy-start | bytes 6291460
  34.1 83.3 %collective-permute-start = (bf16[4,1024,256]{2,1,0:T(8,128)(2,1)S(1)}, bf16[4,1024,256]{2,1,0:T(8,128)(2,1)}, u32[]{:S(2)}, u32[]{:S(2)}) collective-permute-start(bf16[4,1024,256]{2,1,0:T(8,128)(2,1)S(1)} %all-to-all-done.refs_0_), channel_id=1, source_target_pairs={{0,1},{1,0},{2,3},{3,2},{4,5},{5,4},{6,7},{7,6},{8,9},{9,8},{10,11... | collective-permute-start | bytes 6291464 | tf_op jit(solution)/shard_map/ppermute | solution.py:127
  46.8 74.7 %copy-start.6 = (bf16[640,256]{1,0:T(8,128)(2,1)}, bf16[640,256]{1,0:T(8,128)(2,1)S(1)}, u32[]{:S(2)}) copy-start(bf16[640,256]{1,0:T(8,128)(2,1)S(1)} %collective-permute-done.1) | copy-start | bytes 983044
  66.2 51.2 %copy-start.2 = (bf16[4,512,256]{2,1,0:T(8,128)(2,1)}, bf16[4,512,256]{2,1,0:T(8,128)(2,1)S(1)}, u32[]{:S(2)}) copy-start(bf16[4,512,256]{2,1,0:T(8,128)(2,1)S(1)} %all_to_all.25.refs_2_) | copy-start | bytes 3145732
  66.2 51.2 %collective-permute-start.2 = (bf16[4,512,256]{2,1,0:T(8,128)(2,1)S(1)}, bf16[4,512,256]{2,1,0:T(8,128)(2,1)}, u32[]{:S(2)}, u32[]{:S(2)}) collective-permute-start(bf16[4,512,256]{2,1,0:T(8,128)(2,1)S(1)} %all_to_all.25.refs_2_), channel_id=1, source_target_pairs={{0,1},{1,0},{2,3},{3,2},{4,5},{5,4},{6,7},{7,6},{8,9},{9,8},{10,11... | collective-permute-start | bytes 3145736 | tf_op jit(solution)/shard_map/ppermute | solution.py:127
  68.1 14.8 %collective-permute-start.7 = (bf16[512,256]{1,0:T(8,128)(2,1)}, bf16[512,256]{1,0:T(8,128)(2,1)}, u32[]{:S(2)}, u32[]{:S(2)}) collective-permute-start(bf16[512,256]{1,0:T(8,128)(2,1)} %bitcast.16), channel_id=1, source_target_pairs={{0,16},{16,32},{32,48},{48,0},{64,80},{80,96},{96,112},{112,64},{1... | collective-permute-start | bytes 786440 | tf_op jit(solution)/shard_map/ppermute | solution.py:24
  70.1 36.0 %collective-permute-start.3 = (bf16[512,256]{1,0:T(8,128)(2,1)}, bf16[512,256]{1,0:T(8,128)(2,1)}, u32[]{:S(2)}, u32[]{:S(2)}) collective-permute-start(bf16[512,256]{1,0:T(8,128)(2,1)} %bitcast.17), channel_id=1, source_target_pairs={{0,64},{16,80},{32,96},{48,112},{64,0},{80,16},{96,32},{112,48},{1... | collective-permute-start | bytes 786440 | tf_op jit(solution)/shard_map/ppermute | solution.py:29
  73.3 36.5 %collective-permute-start.8 = (bf16[512,256]{1,0:T(8,128)(2,1)}, bf16[512,256]{1,0:T(8,128)(2,1)}, u32[]{:S(2)}, u32[]{:S(2)}) collective-permute-start(bf16[512,256]{1,0:T(8,128)(2,1)} %bitcast.18), channel_id=1, source_target_pairs={{0,32},{16,48},{32,0},{48,16},{64,96},{80,112},{96,64},{112,80},{1... | collective-permute-start | bytes 786440 | tf_op jit(solution)/shard_map/ppermute | solution.py:24
  82.9 29.5 %collective-permute-start.9 = (bf16[512,256]{1,0:T(8,128)(2,1)}, bf16[512,256]{1,0:T(8,128)(2,1)}, u32[]{:S(2)}, u32[]{:S(2)}) collective-permute-start(bf16[512,256]{1,0:T(8,128)(2,1)} %bitcast.19), channel_id=1, source_target_pairs={{0,48},{16,0},{32,16},{48,32},{64,112},{80,64},{96,80},{112,96},{1... | collective-permute-start | bytes 786440 | tf_op jit(solution)/shard_map/ppermute | solution.py:24
  106.0 15.5 %collective-permute-start.4 = (bf16[512,256]{1,0:T(8,128)(2,1)}, bf16[512,256]{1,0:T(8,128)(2,1)}, u32[]{:S(2)}, u32[]{:S(2)}) collective-permute-start(bf16[512,256]{1,0:T(8,128)(2,1)} %collective-permute-done.3.refs_4_), channel_id=1, source_target_pairs={{0,16},{16,32},{32,48},{48,0},{64,80},{80,96},{96,112},{112,64},{1... | collective-permute-start | bytes 786440 | tf_op jit(solution)/shard_map/ppermute | solution.py:24
  109.8 22.3 %collective-permute-start.5 = (bf16[512,256]{1,0:T(8,128)(2,1)}, bf16[512,256]{1,0:T(8,128)(2,1)}, u32[]{:S(2)}, u32[]{:S(2)}) collective-permute-start(bf16[512,256]{1,0:T(8,128)(2,1)} %collective-permute-done.3.refs_4_), channel_id=1, source_target_pairs={{0,32},{16,48},{32,0},{48,16},{64,96},{80,112},{96,64},{112,80},{1... | collective-permute-start | bytes 786440 | tf_op jit(solution)/shard_map/ppermute | solution.py:24
  112.4 19.7 %collective-permute-start.6 = (bf16[512,256]{1,0:T(8,128)(2,1)}, bf16[512,256]{1,0:T(8,128)(2,1)}, u32[]{:S(2)}, u32[]{:S(2)}) collective-permute-start(bf16[512,256]{1,0:T(8,128)(2,1)} %collective-permute-done.3.refs_4_), channel_id=1, source_target_pairs={{0,48},{16,0},{32,16},{48,32},{64,112},{80,64},{96,80},{112,96},{1... | collective-permute-start | bytes 786440 | tf_op jit(solution)/shard_map/ppermute | solution.py:24
  121.5 14.8 %slice-start = ((bf16[640,256]{1,0:T(8,128)(2,1)}), bf16[128,256]{1,0:T(8,128)(2,1)S(1)}, s32[]{:S(2)}) async-start(bf16[640,256]{1,0:T(8,128)(2,1)} %copy-done.6), calls=%async_computation.5 | async-start | bytes 131072 | tf_op jit(solution)/shard_map/slice | solution.py:152
  136.2 28.9 %copy-start.4 = (bf16[512,256]{1,0:T(8,128)(2,1)S(1)}, bf16[512,256]{1,0:T(8,128)(2,1)}, u32[]{:S(2)}) copy-start(bf16[512,256]{1,0:T(8,128)(2,1)} %shard_map.69.refs_4_) | copy-start | bytes 786436
  163.3 50.8 %copy-start.1 = (bf16[4,512,256]{2,1,0:T(8,128)(2,1)}, bf16[4,512,256]{2,1,0:T(8,128)(2,1)S(1)}, u32[]{:S(2)}) copy-start(bf16[4,512,256]{2,1,0:T(8,128)(2,1)S(1)} %all_to_all.27.refs_2_) | copy-start | bytes 3145732
  163.3 50.8 %collective-permute-start.10 = (bf16[4,512,256]{2,1,0:T(8,128)(2,1)S(1)}, bf16[4,512,256]{2,1,0:T(8,128)(2,1)S(1)}, u32[]{:S(2)}, u32[]{:S(2)}) collective-permute-start(bf16[4,512,256]{2,1,0:T(8,128)(2,1)S(1)} %all_to_all.27.refs_2_), channel_id=1, source_target_pairs={{0,1},{1,0},{2,3},{3,2},{4,5},{5,4},{6,7},{7,6},{8,9},{9,8},{10,11... | collective-permute-start | bytes 3145736 | tf_op jit(solution)/shard_map/ppermute | solution.py:127
  165.2 29.4 %collective-permute-start.11 = (bf16[512,256]{1,0:T(8,128)(2,1)S(1)}, bf16[512,256]{1,0:T(8,128)(2,1)S(1)}, u32[]{:S(2)}, u32[]{:S(2)}) collective-permute-start(bf16[512,256]{1,0:T(8,128)(2,1)S(1)} %copy-done.4), channel_id=1, source_target_pairs={{0,64},{16,80},{32,96},{48,112},{64,0},{80,16},{96,32},{112,48},{1... | collective-permute-start | bytes 786440 | tf_op jit(solution)/shard_map/ppermute | solution.py:29
  169.8 26.7 %collective-permute-start.15 = (bf16[512,256]{1,0:T(8,128)(2,1)S(1)}, bf16[512,256]{1,0:T(8,128)(2,1)S(1)}, u32[]{:S(2)}, u32[]{:S(2)}) collective-permute-start(bf16[512,256]{1,0:T(8,128)(2,1)S(1)} %copy-done.4), channel_id=1, source_target_pairs={{0,16},{16,32},{32,48},{48,0},{64,80},{80,96},{96,112},{112,64},{1... | collective-permute-start | bytes 786440 | tf_op jit(solution)/shard_map/ppermute | solution.py:24
  171.7 30.8 %collective-permute-start.16 = (bf16[512,256]{1,0:T(8,128)(2,1)S(1)}, bf16[512,256]{1,0:T(8,128)(2,1)S(1)}, u32[]{:S(2)}, u32[]{:S(2)}) collective-permute-start(bf16[512,256]{1,0:T(8,128)(2,1)S(1)} %copy-done.4), channel_id=1, source_target_pairs={{0,32},{16,48},{32,0},{48,16},{64,96},{80,112},{96,64},{112,80},{1... | collective-permute-start | bytes 786440 | tf_op jit(solution)/shard_map/ppermute | solution.py:24
  176.9 36.5 %collective-permute-start.17 = (bf16[512,256]{1,0:T(8,128)(2,1)S(1)}, bf16[512,256]{1,0:T(8,128)(2,1)S(1)}, u32[]{:S(2)}, u32[]{:S(2)}) collective-permute-start(bf16[512,256]{1,0:T(8,128)(2,1)S(1)} %copy-done.4), channel_id=1, source_target_pairs={{0,48},{16,0},{32,16},{48,32},{64,112},{80,64},{96,80},{112,96},{1... | collective-permute-start | bytes 786440 | tf_op jit(solution)/shard_map/ppermute | solution.py:24
  194.6 37.4 %copy-start.7 = (bf16[512,256]{1,0:T(8,128)(2,1)}, bf16[512,256]{1,0:T(8,128)(2,1)S(1)}, u32[]{:S(2)}) copy-start(bf16[512,256]{1,0:T(8,128)(2,1)S(1)} %collective-permute-done.11.refs_4_) | copy-start | bytes 786436
  194.6 24.6 %collective-permute-start.12 = (bf16[512,256]{1,0:T(8,128)(2,1)S(1)}, bf16[512,256]{1,0:T(8,128)(2,1)S(1)}, u32[]{:S(2)}, u32[]{:S(2)}) collective-permute-start(bf16[512,256]{1,0:T(8,128)(2,1)S(1)} %collective-permute-done.11.refs_4_), channel_id=1, source_target_pairs={{0,16},{16,32},{32,48},{48,0},{64,80},{80,96},{96,112},{112,64},{1... | collective-permute-start | bytes 786440 | tf_op jit(solution)/shard_map/ppermute | solution.py:24
  196.5 17.5 %copy-start.9 = (bf16[512,256]{1,0:T(8,128)(2,1)}, bf16[512,256]{1,0:T(8,128)(2,1)S(1)}, u32[]{:S(2)}) copy-start(bf16[512,256]{1,0:T(8,128)(2,1)S(1)} %collective-permute-done.15.refs_5_) | copy-start | bytes 786436
  196.6 35.4 %collective-permute-start.13 = (bf16[512,256]{1,0:T(8,128)(2,1)S(1)}, bf16[512,256]{1,0:T(8,128)(2,1)S(1)}, u32[]{:S(2)}, u32[]{:S(2)}) collective-permute-start(bf16[512,256]{1,0:T(8,128)(2,1)S(1)} %collective-permute-done.11.refs_4_), channel_id=1, source_target_pairs={{0,32},{16,48},{32,0},{48,16},{64,96},{80,112},{96,64},{112,80},{1... | collective-permute-start | bytes 786440 | tf_op jit(solution)/shard_map/ppermute | solution.py:24
  202.5 10.8 %copy-start.11 = (bf16[512,256]{1,0:T(8,128)(2,1)}, bf16[512,256]{1,0:T(8,128)(2,1)S(1)}, u32[]{:S(2)}) copy-start(bf16[512,256]{1,0:T(8,128)(2,1)S(1)} %collective-permute-done.16.refs_6_) | copy-start | bytes 786436
  202.6 29.4 %collective-permute-start.14 = (bf16[512,256]{1,0:T(8,128)(2,1)S(1)}, bf16[512,256]{1,0:T(8,128)(2,1)}, u32[]{:S(2)}, u32[]{:S(2)}) collective-permute-start(bf16[512,256]{1,0:T(8,128)(2,1)S(1)} %collective-permute-done.11.refs_4_), channel_id=1, source_target_pairs={{0,48},{16,0},{32,16},{48,32},{64,112},{80,64},{96,80},{112,96},{1... | collective-permute-start | bytes 786440 | tf_op jit(solution)/shard_map/ppermute | solution.py:24
  213.3 0.7 copy-start.12
  214.1 1.0 copy-start.3
  219.2 12.8 %copy-start.8 = (bf16[512,256]{1,0:T(8,128)(2,1)}, bf16[512,256]{1,0:T(8,128)(2,1)S(1)}, u32[]{:S(2)}) copy-start(bf16[512,256]{1,0:T(8,128)(2,1)S(1)} %collective-permute-done.12.refs_5_) | copy-start | bytes 786436
  232.0 0.7 copy-start.10

commit v4 on v3

--- a/solution.py
+++ b/solution.py
@@ -65,18 +65,6 @@
         o_ref[...] += accumulate(place, 1, pieces, slots)
 
 
-def mix_kernel(place, *refs):
-    pieces, slots, (p_ref,), (o_ref,), (acc_ref,) = split(refs, 1, 1)
-
-    @pl.when(pl.program_id(0) == 0)
-    def _():
-        acc_ref[...] = p_ref[...] + accumulate(place, 0, pieces, slots)
-
-    @pl.when(pl.program_id(0) == 1)
-    def _():
-        o_ref[...] = (acc_ref[...] + accumulate(place, 1, pieces, slots)).astype(o_ref.dtype)
-
-
 def update_kernel(place, *refs):
     pieces, slots, (p_ref, m_ref, w_ref), (mo_ref, wo_ref), (acc_ref,) = split(refs, 3, 2)
 
@@ -123,6 +111,54 @@
     )(place, *pieces, *slots, *extra)
 
 
+def mix_kernel(place, a0, a1, a2, a3, b_ref, o_ref, acc_ref):
+    half, core = place[0], place[1]
+    depth = a0.shape[-1]
+    total = None
+    for n, piece in enumerate((a0, a1, a2, a3)):
+        at = 2 * (half if n < 2 else 1 - half) + (core if n % 2 == 0 else 1 - core)
+        rows = b_ref[pl.ds(pl.multiple_of(at * depth, depth), depth), :]
+        part = jnp.dot(piece[0], rows, preferred_element_type=jnp.float32)
+        total = part if total is None else total + part
+
+    @pl.when(pl.program_id(0) == 0)
+    def _():
+        acc_ref[...] = total
+
+    @pl.when(pl.program_id(0) > 0)
+    def _():
+        acc_ref[...] += total
+
+    @pl.when(pl.program_id(0) == pl.num_programs(0) - 1)
+    def _():
+        o_ref[...] = acc_ref[...].astype(o_ref.dtype)
+
+
+def mix(place, pieces, right):
+    steps, rows, depth = pieces[2].shape
+    columns = right.shape[1]
+    whole = pl.BlockSpec((rows, columns), lambda i, place: (0, 0))
+    a = pl.BlockSpec((1, rows, depth), lambda i, place: (i, 0, 0))
+    b = pl.BlockSpec((4 * depth, columns), lambda i, place: (i, 0))
+    return pl.pallas_call(
+        mix_kernel,
+        out_shape=jax.ShapeDtypeStruct((rows, columns), jnp.bfloat16),
+        grid_spec=pltpu.PrefetchScalarGridSpec(
+            num_scalar_prefetch=1,
+            grid=(steps,),
+            in_specs=[a] * 4 + [b],
+            out_specs=whole,
+            scratch_shapes=[pltpu.VMEM((rows, columns), jnp.float32)],
+        ),
+        cost_estimate=pl.CostEstimate(
+            flops=2 * rows * right.size,
+            bytes_accessed=2 * (4 * steps * rows * depth + right.size),
+            transcendentals=0,
+        ),
+        name="mix",
+    )(place, *pieces, right)
+
+
 def with_partner(mine):
     return [mine, lax.ppermute(mine, "core", SWAP)]
 
@@ -138,21 +174,19 @@
     part = rows // quarters
     grad, right_root = grad[0], right_root[0]
 
+    right_panel = lax.all_gather(right_root, "row", axis=0, tiled=True)
     left_part = lax.dynamic_slice_in_dim(left_root, quarter * part, part, 0)
     crossed = lax.ppermute(jnp.concatenate((grad, left_part)), "z_hi", SWAP)
-    right_far = across(right_root)
-    near_slots = cube_slots(right_root)
     mine = with_partner(copies_to_all(jnp.concatenate((grad, left_root)), "y"))
     grad_theirs = copies_to_all(crossed[:rows], "y")
     panel = mine + with_partner(grad_theirs)
-    far_slots = cube_slots(right_far)
-    (begun,) = call(half_kernel, near, panel, (0, 0, 0, 0), near_slots, (), (jnp.float32,))
-    (mixed,) = call(mix_kernel, far, panel, (0, 0, 0, 0), far_slots, (begun,), (jnp.bfloat16,))
-
-    mixed, left_part = lax.optimization_barrier((mixed, crossed[rows:]))
+    mixed = mix(near, panel, right_panel)
+    _, left_part = lax.optimization_barrier((grad_theirs, crossed[rows:]))
+    left_other = copies_to_all(left_part, "quarter").reshape(rows, depth)
+
+    mixed, left_other = lax.optimization_barrier((mixed, left_other))
     mixed_far = across(mixed)
     near_slots = cube_slots(mixed)
-    left_other = copies_to_all(left_part, "quarter").reshape(rows, depth)
     left_theirs = copies_to_all(left_other, "y")
     panel = mine + with_partner(left_theirs)
     far_slots = cube_slots(mixed_far)

time: 249 us -> 217 us (0.87)
  the two profiles are of different devices: /device:TPU:480 before, /device:TPU:1 now
where the time goes in v4:
time: 217 us; the launch traced here: 216 us
  waiting for transfers between devices  70.5 us (32%)
  starting transfers between devices  68.6 us (32%)
  blocking collectives  40.9 us (19%)
  Pallas kernels  14.4 us (7%)
  between operations  14.3 us (7%)
  local copies, waits for them, and re-layouts  4.91 us (2%)
  other arithmetic  2.4 us (1%)
    all_to_all x2, blocking collectives, copies_to_all(): return lax.all_to_all(spread, axis, 0, 0, tiled=True)  31.1 us
    ppermute x3, starting transfers between devices, with_partner(): return [mine, lax.ppermute(mine, 'core', SWAP)]  22.2 us
    all_gather x1, waiting for transfers between devices, per_device(): right_panel = lax.all_gather(right_root, 'row', axis=0, tiled=True)  21.1 us
    ppermute x6, waiting for transfers between devices, turn(): return lax.ppermute(piece, 'row', pairs)  20.4 us
    ppermute x6, starting transfers between devices, turn(): return lax.ppermute(piece, 'row', pairs)  19.9 us
    ppermute x1, starting transfers between devices, per_device(): crossed = lax.ppermute(jnp.concatenate((grad, left_part)), 'z_hi', SWAP)  15.4 us
    ppermute x1, waiting for transfers between devices, across(): return lax.ppermute(piece, 'row', [(i, i ^ CUBE) for i in range(rows)])  15.4 us
    all_to_all x1, blocking collectives, per_device(): lax.all_to_all(updated.reshape(quarters, part, depth), 'quarter', 0, 0, t...  9.83 us
  transfers between devices with their start and end apart: 14, of which 6 were waited for; matrix products, arithmetic and copies ran while one was open for 3% of the time, Pallas kernels for 5%

profile of v4, /device:TPU:1, one launch (start us, length us, event | category | flops | bytes accessed | tf_op | source)
XLA Modules:
  0.0 216.0 jit_solution(6973761028310688068)
XLA Ops:
  7.2 0.0 all-gather.3.cloned.1.call-start
  7.2 0.7 all-gather.3.cloned.1.call-update
  7.9 1.1 pad_maximum_fusion
  9.0 1.5 broadcast_in_dim.10
  10.4 5.1 %all-to-all-start = ((bf16[4,1024,256]{2,1,0:T(8,128)(2,1)}), bf16[4,1024,256]{2,1,0:T(8,128)(2,1)S(1)}, u32[]{:S(2)}, u32[]{:S(2)}) async-start(bf16[4,1024,256]{2,1,0:T(8,128)(2,1)} %broadcast_in_dim.10), calls=%async_computation | async-start | bytes 4194304 | tf_op jit(solution)/shard_map/all_to_all | solution.py:18
  15.6 0.8 constant_dynamic-slice_fusion
  16.4 0.0 copy-done.5
  16.4 15.4 %collective-permute-start.1 = (bf16[640,256]{1,0:T(8,128)(2,1)S(1)}, bf16[640,256]{1,0:T(8,128)(2,1)S(1)}, u32[]{:S(2)}, u32[]{:S(2)}) collective-permute-start(bf16[640,256]{1,0:T(8,128)(2,1)S(1)} %pad_maximum_fusion.1), channel_id=1, source_target_pairs={{0,2},{2,0},{1,3},{3,1},{4,6},{6,4},{5,7},{7,5},{8,10},{10,8},{9,1... | collective-permute-start | bytes 983048 | tf_op jit(solution)/shard_map/ppermute | solution.py:179
  31.9 4.7 %all-to-all-done.a0.refs_0_ = bf16[4,1024,256]{2,1,0:T(8,128)(2,1)S(1)} async-done(((bf16[4,1024,256]{2,1,0:T(8,128)(2,1)}), bf16[4,1024,256]{2,1,0:T(8,128)(2,1)S(1)}, u32[]{:S(2)}, u32[]{:S(2)}) %all-to-all-start) | async-done | bytes 2097184 | tf_op jit(solution)/shard_map/all_to_all | solution.py:18
  36.6 8.2 %collective-permute-start = (bf16[4,1024,256]{2,1,0:T(8,128)(2,1)S(1)}, bf16[4,1024,256]{2,1,0:T(8,128)(2,1)}, u32[]{:S(2)}, u32[]{:S(2)}) collective-permute-start(bf16[4,1024,256]{2,1,0:T(8,128)(2,1)S(1)} %all-to-all-done.a0.refs_0_), channel_id=1, source_target_pairs={{0,1},{1,0},{2,3},{3,2},{4,5},{5,4},{6,7},{7,6},{8,9},{9,8},{10,11... | collective-permute-start | bytes 6291464 | tf_op jit(solution)/shard_map/ppermute | solution.py:163
  44.8 8.3 %collective-permute-done.1 = bf16[640,256]{1,0:T(8,128)(2,1)S(1)} collective-permute-done((bf16[640,256]{1,0:T(8,128)(2,1)S(1)}, bf16[640,256]{1,0:T(8,128)(2,1)S(1)}, u32[]{:S(2)}, u32[]{:S(2)}) %collective-permute-start.1) | collective-permute-done | bytes 327712 | tf_op jit(solution)/shard_map/ppermute | solution.py:179
  53.1 0.1 broadcast_in_dim.11
  53.1 15.8 %all_to_all.25.a2 = bf16[4,512,256]{2,1,0:T(8,128)(2,1)S(1)} all-to-all(bf16[4,512,256]{2,1,0:T(8,128)(2,1)S(1)} %broadcast_in_dim.11), channel_id=1, replica_groups=mesh['quarter'=4,'row'=8,'y'=4,'z_hi'=2,'core'=2] {'y'}, dimensions={0} | all-to-all | bytes 2097152 | tf_op jit(solution)/shard_map/all_to_all | solution.py:18
  69.0 7.2 %collective-permute-start.2 = (bf16[4,512,256]{2,1,0:T(8,128)(2,1)S(1)}, bf16[4,512,256]{2,1,0:T(8,128)(2,1)}, u32[]{:S(2)}, u32[]{:S(2)}) collective-permute-start(bf16[4,512,256]{2,1,0:T(8,128)(2,1)S(1)} %all_to_all.25.a2), channel_id=1, source_target_pairs={{0,1},{1,0},{2,3},{3,2},{4,5},{5,4},{6,7},{7,6},{8,9},{9,8},{10,11... | collective-permute-start | bytes 3145736 | tf_op jit(solution)/shard_map/ppermute | solution.py:163
  76.2 0.7 broadcast_in_dim.12
  76.9 4.0 %all-to-all-start.2 = ((bf16[4,128,256]{2,1,0:T(8,128)(2,1)}), bf16[4,128,256]{2,1,0:T(8,128)(2,1)S(1)}, u32[]{:S(2)}, u32[]{:S(2)}) async-start(bf16[4,128,256]{2,1,0:T(8,128)(2,1)} %broadcast_in_dim.12), calls=%async_computation.2 | async-start | bytes 524288 | tf_op jit(solution)/shard_map/all_to_all | solution.py:18
  80.9 0.7 pad_add_fusion.2
  81.6 0.0 collective-permute-done.2.a3
  81.6 21.1 %all-gather.3.cloned.1.call-done = bf16[1,4096,256]{2,1,0:T(8,128)(2,1)} async-done(((bf16[1,512,256]{2,1,0:T(8,128)(2,1)}), bf16[1,4096,256]{2,1,0:T(8,128)(2,1)}) %all-gather.3.cloned.1.call-update) | async-done | bytes 2097168 | tf_op jit(solution)/shard_map/all_gather | solution.py:177
  102.7 0.0 collective-permute-done.a1.refs_1_
  102.7 5.7 %mix.1.refs_4_ = bf16[512,256]{1,0:T(8,128)(2,1)} custom-call(s32[4]{0:T(128)} %get-tuple-element.12.place, bf16[4,1024,256]{2,1,0:T(8,128)(2,1)} %copy-done, bf16[4,1024,256]{2,1,0:T(8,128)(2,1)} %collective-permute-done.a1.refs_1_, bf16[4,512,256]{2,1,0:T(8,128)(2,1)} %copy-done.3, bf16[4,512,256]{2,1,0:T(8,128)(2,1)} %collective-permute-done.2.a3, ...), custom_call_target="tpu_custom_call" | custom-call | flops 1073741824 | bytes 6291456 | tf_op jit(solution)/shard_map/mix/pallas_call | solution.py:143
  108.4 0.0 all-to-all-done.2
  108.4 0.1 broadcast_in_dim.13
  108.5 15.2 %all_to_all.26.refs_2_ = bf16[4,512,256]{2,1,0:T(8,128)(2,1)S(1)} all-to-all(bf16[4,512,256]{2,1,0:T(8,128)(2,1)S(1)} %broadcast_in_dim.13), channel_id=1, replica_groups=mesh['quarter'=4,'row'=8,'y'=4,'z_hi'=2,'core'=2] {'y'}, dimensions={0} | all-to-all | bytes 2097152 | tf_op jit(solution)/shard_map/all_to_all | solution.py:18
  123.7 6.8 %collective-permute-start.3 = (bf16[4,512,256]{2,1,0:T(8,128)(2,1)S(1)}, bf16[4,512,256]{2,1,0:T(8,128)(2,1)S(1)}, u32[]{:S(2)}, u32[]{:S(2)}) collective-permute-start(bf16[4,512,256]{2,1,0:T(8,128)(2,1)S(1)} %all_to_all.26.refs_2_), channel_id=1, source_target_pairs={{0,1},{1,0},{2,3},{3,2},{4,5},{5,4},{6,7},{7,6},{8,9},{9,8},{10,11... | collective-permute-start | bytes 3145736 | tf_op jit(solution)/shard_map/ppermute | solution.py:163
  130.5 1.9 collective-permute-start.4
  132.5 6.5 %collective-permute-start.10 = (bf16[512,256]{1,0:T(8,128)(2,1)S(1)}, bf16[512,256]{1,0:T(8,128)(2,1)S(1)}, u32[]{:S(2)}, u32[]{:S(2)}) collective-permute-start(bf16[512,256]{1,0:T(8,128)(2,1)S(1)} %copy-done.4), channel_id=1, source_target_pairs={{0,48},{16,0},{32,16},{48,32},{64,112},{80,64},{96,80},{112,96},{1... | collective-permute-start | bytes 786440 | tf_op jit(solution)/shard_map/ppermute | solution.py:24
  138.9 1.9 collective-permute-start.9
  140.9 2.4 %collective-permute-start.8 = (bf16[512,256]{1,0:T(8,128)(2,1)S(1)}, bf16[512,256]{1,0:T(8,128)(2,1)}, u32[]{:S(2)}, u32[]{:S(2)}) collective-permute-start(bf16[512,256]{1,0:T(8,128)(2,1)S(1)} %copy-done.4), channel_id=1, source_target_pairs={{0,16},{16,32},{32,48},{48,0},{64,80},{80,96},{96,112},{112,64},{1... | collective-permute-start | bytes 786440 | tf_op jit(solution)/shard_map/ppermute | solution.py:24
  143.3 15.4 %collective-permute-done.4.refs_4_ = bf16[512,256]{1,0:T(8,128)(2,1)S(1)} collective-permute-done((bf16[512,256]{1,0:T(8,128)(2,1)S(1)}, bf16[512,256]{1,0:T(8,128)(2,1)S(1)}, u32[]{:S(2)}, u32[]{:S(2)}) %collective-permute-start.4) | collective-permute-done | bytes 262176 | tf_op jit(solution)/shard_map/ppermute | solution.py:29
  158.7 1.9 collective-permute-start.7
  160.6 0.0 collective-permute-done.10.refs_7_
  160.6 1.9 collective-permute-start.6
  162.5 0.0 collective-permute-done.9.refs_6_
  162.6 5.3 %collective-permute-start.5 = (bf16[512,256]{1,0:T(8,128)(2,1)S(1)}, bf16[512,256]{1,0:T(8,128)(2,1)}, u32[]{:S(2)}, u32[]{:S(2)}) collective-permute-start(bf16[512,256]{1,0:T(8,128)(2,1)S(1)} %collective-permute-done.4.refs_4_), channel_id=1, source_target_pairs={{0,16},{16,32},{32,48},{48,0},{64,80},{80,96},{96,112},{112,64},{1... | collective-permute-start | bytes 786440 | tf_op jit(solution)/shard_map/ppermute | solution.py:24
  167.8 0.6 pad_add_fusion.place
  168.5 2.9 %collective-permute-done.8.refs_5_ = bf16[512,256]{1,0:T(8,128)(2,1)} collective-permute-done((bf16[512,256]{1,0:T(8,128)(2,1)S(1)}, bf16[512,256]{1,0:T(8,128)(2,1)}, u32[]{:S(2)}, u32[]{:S(2)}) %collective-permute-start.8) | collective-permute-done | bytes 262176 | tf_op jit(solution)/shard_map/ppermute | solution.py:24
  171.4 0.0 collective-permute-done.3.refs_3_
  171.4 0.0 copy-done.1
  171.4 1.0 copy-done.2
  172.4 4.1 %shard_map.68.refs_8_ = f32[512,256]{1,0:T(8,128)} custom-call(s32[4]{0:T(128)} %get-tuple-element.12.place, bf16[4,1024,256]{2,1,0:T(8,128)(2,1)} %copy-done, bf16[4,1024,256]{2,1,0:T(8,128)(2,1)} %collective-permute-done.a1.refs_1_, bf16[4,512,256]{2,1,0:T(8,128)(2,1)} %copy-done.1, bf16[4,512,256]{2,1,0:T(8,128)(2,1)} %copy-done.2, ...), custom_call_target="tpu_custom_call" | custom-call | flops 536870912 | bytes 4194304 | tf_op jit(solution)/shard_map/pallas_call | solution.py:98
  176.5 0.0 collective-permute-done.7.refs_7_
  176.5 17.5 %collective-permute-done.6.refs_6_ = bf16[512,256]{1,0:T(8,128)(2,1)} collective-permute-done((bf16[512,256]{1,0:T(8,128)(2,1)S(1)}, bf16[512,256]{1,0:T(8,128)(2,1)}, u32[]{:S(2)}, u32[]{:S(2)}) %collective-permute-start.6) | collective-permute-done | bytes 262176 | tf_op jit(solution)/shard_map/ppermute | solution.py:24
  194.0 0.0 collective-permute-done.5.refs_5_
  194.0 0.0 copy-done.6
  194.0 4.6 %shard_map.69 = (f32[512,256]{1,0:T(8,128)}, bf16[512,256]{1,0:T(8,128)(2,1)}) custom-call(s32[4]{0:T(128)} %pad_add_fusion.place, bf16[4,1024,256]{2,1,0:T(8,128)(2,1)} %copy-done, bf16[4,1024,256]{2,1,0:T(8,128)(2,1)} %collective-permute-done.a1.refs_1_, bf16[4,512,256]{2,1,0:T(8,128)(2,1)} %copy-done.1, bf16[4,512,256]{2,1,0:T(8,128)(2,1)} %copy-done.2, ...), custom_call_target="tpu_custom_call" | custom-call | flops 536870912 | bytes 4194304 | tf_op jit(solution)/shard_map/pallas_call | solution.py:98
  198.6 9.8 %all_to_all.27 = bf16[4,128,256]{2,1,0:T(8,128)(2,1)S(1)} all-to-all(bf16[4,128,256]{2,1,0:T(8,128)(2,1)} %bitcast.18), channel_id=1, replica_groups=mesh['quarter'=4,'row'=8,'y'=4,'z_hi'=2,'core'=2] {'quarter'}, dimensions={0} | all-to-all | bytes 524288 | tf_op jit(solution)/shard_map/all_to_all | solution.py:203
  208.4 0.7 copy.8
  (19 shorter events, 0.1 us)
Async XLA Ops:
  7.2 95.5 %all-gather.3.cloned.1.call-start = ((), (), s32[]{:S(2)}) async-start(), calls=%async_computation.5 | async-start | bytes 2359296 | tf_op jit(solution)/shard_map/all_gather | solution.py:177
  10.4 6.0 %copy-start.5 = (bf16[1,512,256]{2,1,0:T(8,128)(2,1)S(1)}, bf16[1,512,256]{2,1,0:T(8,128)(2,1)}, u32[]{:S(2)}) copy-start(bf16[1,512,256]{2,1,0:T(8,128)(2,1)} %param.5) | copy-start | bytes 786436
  10.4 26.1 %all-to-all-start = ((bf16[4,1024,256]{2,1,0:T(8,128)(2,1)}), bf16[4,1024,256]{2,1,0:T(8,128)(2,1)S(1)}, u32[]{:S(2)}, u32[]{:S(2)}) async-start(bf16[4,1024,256]{2,1,0:T(8,128)(2,1)} %broadcast_in_dim.10), calls=%async_computation | async-start | bytes 4194304 | tf_op jit(solution)/shard_map/all_to_all | solution.py:18
  16.4 36.6 %collective-permute-start.1 = (bf16[640,256]{1,0:T(8,128)(2,1)S(1)}, bf16[640,256]{1,0:T(8,128)(2,1)S(1)}, u32[]{:S(2)}, u32[]{:S(2)}) collective-permute-start(bf16[640,256]{1,0:T(8,128)(2,1)S(1)} %pad_maximum_fusion.1), channel_id=1, source_target_pairs={{0,2},{2,0},{1,3},{3,1},{4,6},{6,4},{5,7},{7,5},{8,10},{10,8},{9,1... | collective-permute-start | bytes 983048 | tf_op jit(solution)/shard_map/ppermute | solution.py:179
  36.6 40.3 %copy-start = (bf16[4,1024,256]{2,1,0:T(8,128)(2,1)}, bf16[4,1024,256]{2,1,0:T(8,128)(2,1)S(1)}, u32[]{:S(2)}) copy-start(bf16[4,1024,256]{2,1,0:T(8,128)(2,1)S(1)} %all-to-all-done.a0.refs_0_) | copy-start | bytes 6291460
  36.6 66.1 %collective-permute-start = (bf16[4,1024,256]{2,1,0:T(8,128)(2,1)S(1)}, bf16[4,1024,256]{2,1,0:T(8,128)(2,1)}, u32[]{:S(2)}, u32[]{:S(2)}) collective-permute-start(bf16[4,1024,256]{2,1,0:T(8,128)(2,1)S(1)} %all-to-all-done.a0.refs_0_), channel_id=1, source_target_pairs={{0,1},{1,0},{2,3},{3,2},{4,5},{5,4},{6,7},{7,6},{8,9},{9,8},{10,11... | collective-permute-start | bytes 6291464 | tf_op jit(solution)/shard_map/ppermute | solution.py:163
  69.0 33.7 %copy-start.3 = (bf16[4,512,256]{2,1,0:T(8,128)(2,1)}, bf16[4,512,256]{2,1,0:T(8,128)(2,1)S(1)}, u32[]{:S(2)}) copy-start(bf16[4,512,256]{2,1,0:T(8,128)(2,1)S(1)} %all_to_all.25.a2) | copy-start | bytes 3145732
  69.0 12.6 %collective-permute-start.2 = (bf16[4,512,256]{2,1,0:T(8,128)(2,1)S(1)}, bf16[4,512,256]{2,1,0:T(8,128)(2,1)}, u32[]{:S(2)}, u32[]{:S(2)}) collective-permute-start(bf16[4,512,256]{2,1,0:T(8,128)(2,1)S(1)} %all_to_all.25.a2), channel_id=1, source_target_pairs={{0,1},{1,0},{2,3},{3,2},{4,5},{5,4},{6,7},{7,6},{8,9},{9,8},{10,11... | collective-permute-start | bytes 3145736 | tf_op jit(solution)/shard_map/ppermute | solution.py:163
  76.9 31.5 %all-to-all-start.2 = ((bf16[4,128,256]{2,1,0:T(8,128)(2,1)}), bf16[4,128,256]{2,1,0:T(8,128)(2,1)S(1)}, u32[]{:S(2)}, u32[]{:S(2)}) async-start(bf16[4,128,256]{2,1,0:T(8,128)(2,1)} %broadcast_in_dim.12), calls=%async_computation.2 | async-start | bytes 524288 | tf_op jit(solution)/shard_map/all_to_all | solution.py:18
  108.4 22.1 %copy-start.4 = (bf16[512,256]{1,0:T(8,128)(2,1)S(1)}, bf16[512,256]{1,0:T(8,128)(2,1)}, u32[]{:S(2)}) copy-start(bf16[512,256]{1,0:T(8,128)(2,1)} %mix.1.refs_4_) | copy-start | bytes 786436
  123.7 47.7 %copy-start.1 = (bf16[4,512,256]{2,1,0:T(8,128)(2,1)}, bf16[4,512,256]{2,1,0:T(8,128)(2,1)S(1)}, u32[]{:S(2)}) copy-start(bf16[4,512,256]{2,1,0:T(8,128)(2,1)S(1)} %all_to_all.26.refs_2_) | copy-start | bytes 3145732
  123.7 47.7 %collective-permute-start.3 = (bf16[4,512,256]{2,1,0:T(8,128)(2,1)S(1)}, bf16[4,512,256]{2,1,0:T(8,128)(2,1)S(1)}, u32[]{:S(2)}, u32[]{:S(2)}) collective-permute-start(bf16[4,512,256]{2,1,0:T(8,128)(2,1)S(1)} %all_to_all.26.refs_2_), channel_id=1, source_target_pairs={{0,1},{1,0},{2,3},{3,2},{4,5},{5,4},{6,7},{7,6},{8,9},{9,8},{10,11... | collective-permute-start | bytes 3145736 | tf_op jit(solution)/shard_map/ppermute | solution.py:163
  130.5 28.1 %collective-permute-start.4 = (bf16[512,256]{1,0:T(8,128)(2,1)S(1)}, bf16[512,256]{1,0:T(8,128)(2,1)S(1)}, u32[]{:S(2)}, u32[]{:S(2)}) collective-permute-start(bf16[512,256]{1,0:T(8,128)(2,1)S(1)} %copy-done.4), channel_id=1, source_target_pairs={{0,64},{16,80},{32,96},{48,112},{64,0},{80,16},{96,32},{112,48},{1... | collective-permute-start | bytes 786440 | tf_op jit(solution)/shard_map/ppermute | solution.py:29
  132.5 28.1 %collective-permute-start.10 = (bf16[512,256]{1,0:T(8,128)(2,1)S(1)}, bf16[512,256]{1,0:T(8,128)(2,1)S(1)}, u32[]{:S(2)}, u32[]{:S(2)}) collective-permute-start(bf16[512,256]{1,0:T(8,128)(2,1)S(1)} %copy-done.4), channel_id=1, source_target_pairs={{0,48},{16,0},{32,16},{48,32},{64,112},{80,64},{96,80},{112,96},{1... | collective-permute-start | bytes 786440 | tf_op jit(solution)/shard_map/ppermute | solution.py:24
  138.9 23.6 %collective-permute-start.9 = (bf16[512,256]{1,0:T(8,128)(2,1)S(1)}, bf16[512,256]{1,0:T(8,128)(2,1)S(1)}, u32[]{:S(2)}, u32[]{:S(2)}) collective-permute-start(bf16[512,256]{1,0:T(8,128)(2,1)S(1)} %copy-done.4), channel_id=1, source_target_pairs={{0,32},{16,48},{32,0},{48,16},{64,96},{80,112},{96,64},{112,80},{1... | collective-permute-start | bytes 786440 | tf_op jit(solution)/shard_map/ppermute | solution.py:24
  140.9 30.5 %collective-permute-start.8 = (bf16[512,256]{1,0:T(8,128)(2,1)S(1)}, bf16[512,256]{1,0:T(8,128)(2,1)}, u32[]{:S(2)}, u32[]{:S(2)}) collective-permute-start(bf16[512,256]{1,0:T(8,128)(2,1)S(1)} %copy-done.4), channel_id=1, source_target_pairs={{0,16},{16,32},{32,48},{48,0},{64,80},{80,96},{96,112},{112,64},{1... | collective-permute-start | bytes 786440 | tf_op jit(solution)/shard_map/ppermute | solution.py:24
  158.7 35.3 %copy-start.6 = (bf16[512,256]{1,0:T(8,128)(2,1)}, bf16[512,256]{1,0:T(8,128)(2,1)S(1)}, u32[]{:S(2)}) copy-start(bf16[512,256]{1,0:T(8,128)(2,1)S(1)} %collective-permute-done.4.refs_4_) | copy-start | bytes 786436
  158.7 17.8 %collective-permute-start.7 = (bf16[512,256]{1,0:T(8,128)(2,1)S(1)}, bf16[512,256]{1,0:T(8,128)(2,1)S(1)}, u32[]{:S(2)}, u32[]{:S(2)}) collective-permute-start(bf16[512,256]{1,0:T(8,128)(2,1)S(1)} %collective-permute-done.4.refs_4_), channel_id=1, source_target_pairs={{0,48},{16,0},{32,16},{48,32},{64,112},{80,64},{96,80},{112,96},{1... | collective-permute-start | bytes 786440 | tf_op jit(solution)/shard_map/ppermute | solution.py:24
  160.6 10.8 %copy-start.8 = (bf16[512,256]{1,0:T(8,128)(2,1)}, bf16[512,256]{1,0:T(8,128)(2,1)S(1)}, u32[]{:S(2)}) copy-start(bf16[512,256]{1,0:T(8,128)(2,1)S(1)} %collective-permute-done.10.refs_7_) | copy-start | bytes 786436
  160.6 33.4 %collective-permute-start.6 = (bf16[512,256]{1,0:T(8,128)(2,1)S(1)}, bf16[512,256]{1,0:T(8,128)(2,1)}, u32[]{:S(2)}, u32[]{:S(2)}) collective-permute-start(bf16[512,256]{1,0:T(8,128)(2,1)S(1)} %collective-permute-done.4.refs_4_), channel_id=1, source_target_pairs={{0,32},{16,48},{32,0},{48,16},{64,96},{80,112},{96,64},{112,80},{1... | collective-permute-start | bytes 786440 | tf_op jit(solution)/shard_map/ppermute | solution.py:24
  162.5 8.9 %copy-start.9 = (bf16[512,256]{1,0:T(8,128)(2,1)}, bf16[512,256]{1,0:T(8,128)(2,1)S(1)}, u32[]{:S(2)}) copy-start(bf16[512,256]{1,0:T(8,128)(2,1)S(1)} %collective-permute-done.9.refs_6_) | copy-start | bytes 786436
  162.6 31.4 %collective-permute-start.5 = (bf16[512,256]{1,0:T(8,128)(2,1)S(1)}, bf16[512,256]{1,0:T(8,128)(2,1)}, u32[]{:S(2)}, u32[]{:S(2)}) collective-permute-start(bf16[512,256]{1,0:T(8,128)(2,1)S(1)} %collective-permute-done.4.refs_4_), channel_id=1, source_target_pairs={{0,16},{16,32},{32,48},{48,0},{64,80},{80,96},{96,112},{112,64},{1... | collective-permute-start | bytes 786440 | tf_op jit(solution)/shard_map/ppermute | solution.py:24
  171.4 1.0 copy-start.2
  176.5 17.5 %copy-start.7 = (bf16[512,256]{1,0:T(8,128)(2,1)}, bf16[512,256]{1,0:T(8,128)(2,1)S(1)}, u32[]{:S(2)}) copy-start(bf16[512,256]{1,0:T(8,128)(2,1)S(1)} %collective-permute-done.7.refs_7_) | copy-start | bytes 786436
Sparse Core Ops, SparseCore 0:
  10.0 92.5 all-gather.2

commit v5 on v4

v5 whole, which is shorter than its diff:
```python
import jax
import jax.numpy as jnp
from jax import lax
from jax.experimental import pallas as pl
from jax.experimental.pallas import tpu as pltpu
from jax.sharding import Mesh, PartitionSpec as P

decay_rate = 0.9
step_rate = 0.1
AXES = ("quarter", "row", "y", "z_hi", "core")
SWAP = [(0, 1), (1, 0)]
CUBE = 4


def copies_to_all(piece, axis):
    n = lax.axis_size(axis)
    spread = jnp.broadcast_to(piece[None], (n, *piece.shape))
    return lax.all_to_all(spread, axis, 0, 0, tiled=True)


def turn(piece, by):
    rows = lax.axis_size("row")
    pairs = [(i, i // CUBE * CUBE + (i + by) % CUBE) for i in range(rows)]
    return lax.ppermute(piece, "row", pairs)


def across(piece):
    rows = lax.axis_size("row")
    return lax.ppermute(piece, "row", [(i, i ^ CUBE) for i in range(rows)])


def far_slots(piece):
    return [piece] + [turn(piece, by) for by in range(1, CUBE)]


def accumulate(place, step, pieces, slots):
    half, core, turned = place[0], place[1], place[2]
    depth = pieces[0].shape[-1]
    odd = (turned + half) % 2
    total = None
    for n, piece in enumerate(pieces):
        first = pl.multiple_of(depth * (core if n % 2 == 0 else 1 - core), depth)
        even, other = (
            jnp.concatenate([part[pl.ds(first, depth), :] for part in slot], axis=1)
            for slot in slots[2 * step : 2 * step + 2]
        )
        rows = jnp.where(odd == n // 2, even, other)
        part = jnp.dot(piece[0], rows, preferred_element_type=jnp.float32)
        total = part if total is None else total + part
    return total


def update_kernel(place, *refs):
    pieces, parts, (p_ref, m_ref, w_ref, mo_ref, wo_ref, acc_ref) = refs[:4], refs[4 : 4 + 2 * CUBE], refs[4 + 2 * CUBE :]
    slots = list(zip(parts[:CUBE], parts[CUBE:], strict=True))

    @pl.when(pl.program_id(0) == 0)
    def _():
        acc_ref[...] = p_ref[...] + accumulate(place, 0, pieces, slots)

    @pl.when(pl.program_id(0) == 1)
    def _():
        product = acc_ref[...] + accumulate(place, 1, pieces, slots)
        renewed = decay_rate * m_ref[...] + (1.0 - decay_rate) * product
        mo_ref[...] = renewed
        wo_ref[...] = (w_ref[...].astype(jnp.float32) - step_rate * renewed).astype(wo_ref.dtype)


def update(place, pieces, at_rows, low, high, begun, momentum, weights):
    depth = pieces[0].shape[-1]
    rows, columns = momentum.shape
    whole = pl.BlockSpec((rows, columns), lambda i, place: (0, 0))

    def piece_spec(theirs, block):
        def at(i, place):
            odd = (place[2] + place[0]) % 2
            back = 2 * i + (1 - odd if theirs else odd)
            return place[3] + (place[2] + 2 * CUBE - back) % CUBE // 2, block, 0

        return pl.BlockSpec((1, rows, depth), at)

    slot_spec = pl.BlockSpec(memory_space=pltpu.MemorySpace.VMEM)
    moved = 4 * CUBE * rows * depth + 2 * CUBE * rows * columns + 14 * rows * columns
    return pl.pallas_call(
        update_kernel,
        out_shape=[jax.ShapeDtypeStruct((rows, columns), t) for t in (jnp.float32, jnp.bfloat16)],
        grid_spec=pltpu.PrefetchScalarGridSpec(
            num_scalar_prefetch=1,
            grid=(2,),
            in_specs=[piece_spec(n >= 2, at_rows[n]) for n in range(4)] + [slot_spec] * (2 * CUBE) + [whole] * 3,
            out_specs=[whole, whole],
            scratch_shapes=[pltpu.VMEM((rows, columns), jnp.float32)],
        ),
        cost_estimate=pl.CostEstimate(
            flops=2 * rows * CUBE * rows * columns, bytes_accessed=moved, transcendentals=0
        ),
        name="update",
    )(place, *pieces, *[pltpu.with_memory_space_constraint(v, pltpu.MemorySpace.VMEM) for v in (*low, *high)], begun, momentum, weights)


def mix_kernel(place, a0, a1, a2, a3, b_ref, o_ref, *refs):
    half, core = place[0], place[1]
    depth = a0.shape[-1]
    parts, acc_ref = refs[:-1], refs[-1]
    total = None
    for n, piece in enumerate((a0, a1, a2, a3)):
        at = 2 * (half if n < 2 else 1 - half) + (core if n % 2 == 0 else 1 - core)
        rows = b_ref[pl.ds(pl.multiple_of(at * depth, depth), depth), :]
        part = jnp.dot(piece[0], rows, preferred_element_type=jnp.float32)
        total = part if total is None else total + part

    @pl.when(pl.program_id(0) == 0)
    def _():
        acc_ref[...] = total

    @pl.when(pl.program_id(0) > 0)
    def _():
        acc_ref[...] += total

    @pl.when(pl.program_id(0) == pl.num_programs(0) - 1)
    def _():
        done = acc_ref[...].astype(o_ref.dtype)
        o_ref[...] = done
        for n, part_ref in enumerate(parts):
            width = part_ref.shape[1]
            part_ref[...] = done[:, n * width : (n + 1) * width]


def mix(place, pieces, at_rows, right, kind, split):
    depth = pieces[0].shape[-1]
    columns = right.shape[1]
    steps, rows = right.shape[0] // (4 * depth), 2 * depth
    whole = pl.BlockSpec((rows, columns), lambda i, place: (0, 0))
    block = pl.BlockSpec((rows, columns // max(split, 1)), lambda i, place: (0, 0))
    b = pl.BlockSpec((4 * depth, columns), lambda i, place: (i, 0))

    def piece_spec(at):
        return pl.BlockSpec((1, rows, depth), lambda i, place: (place[3] + i, at, 0))

    return pl.pallas_call(
        mix_kernel,
        out_shape=[jax.ShapeDtypeStruct((rows, columns), kind)]
        + [jax.ShapeDtypeStruct((rows, columns // split), kind) for _ in range(split)],
        grid_spec=pltpu.PrefetchScalarGridSpec(
            num_scalar_prefetch=1,
            grid=(steps,),
            in_specs=[piece_spec(at) for at in at_rows] + [b],
            out_specs=[whole] + [block] * split,
            scratch_shapes=[pltpu.VMEM((rows, columns), jnp.float32)],
        ),
        cost_estimate=pl.CostEstimate(
            flops=2 * rows * right.size,
            bytes_accessed=2 * (4 * steps * rows * depth + right.size),
            transcendentals=0,
        ),
    )(place, *pieces, right)


def with_partner(mine):
    return [mine, lax.ppermute(mine, "core", SWAP)]


def per_device(grad, left_root, right_root, momentum, weights):
    half, core, row = (lax.axis_index(a).astype(jnp.int32) for a in ("z_hi", "core", "row"))
    upper = row // CUBE
    every = jnp.stack((half, core, row % CUBE, 0 * upper))
    near = jnp.stack((half, core, row % CUBE, 2 * upper))
    far = jnp.stack((half, core, row % CUBE, 2 - 2 * upper))
    quarter = lax.axis_index("quarter")
    quarters = lax.axis_size("quarter")
    rows, depth = left_root.shape
    part = rows // quarters
    grad, right_root = grad[0], right_root[0]

    right_panel = lax.all_gather(right_root, "row", axis=0, tiled=True)
    left_part = lax.dynamic_slice_in_dim(left_root, quarter * part, part, 0)
    crossed = lax.ppermute(jnp.concatenate((grad, left_part)), "z_hi", SWAP)
    mine = with_partner(copies_to_all(jnp.concatenate((grad, left_root)), "y"))
    grad_theirs = copies_to_all(crossed[:rows], "y")
    panel = mine + with_partner(grad_theirs)
    mixed, *parts = mix(every, panel, (0, 0, 0, 0), right_panel, jnp.bfloat16, 2)
    _, left_part = lax.optimization_barrier((grad_theirs, crossed[rows:]))
    left_other = copies_to_all(left_part, "quarter").reshape(rows, depth)

    mixed, parts, left_other = lax.optimization_barrier((mixed, parts, left_other))
    runs = [list(range(i, i + CUBE)) for i in range(0, lax.axis_size("row"), CUBE)]
    near_panel = lax.all_gather(mixed, "row", axis=0, tiled=True, axis_index_groups=runs)
    others = []
    for piece in parts:
        others.append(across(piece))
    left_theirs = copies_to_all(left_other, "y")
    panel = mine + with_partner(left_theirs)
    slots = []
    for piece in others:
        slots.append(far_slots(piece))
    (begun,) = mix(near, panel, (1, 1, 0, 0), near_panel, jnp.float32, 0)
    renewed, updated = update(far, panel, (1, 1, 0, 0), *slots, begun, momentum[0], weights[0])
    spread = lax.all_to_all(updated.reshape(quarters, part, depth), "quarter", 0, 0, tiled=True)
    return renewed[None], spread


def solution(mesh):
    fine = Mesh(mesh.devices.reshape(4, 8, 4, 2, 2), AXES)
    placed = P("quarter", "row", ("y", "z_hi", "core"))
    return jax.shard_map(
        per_device,
        mesh=fine,
        in_specs=(placed, P("row", ("y", "z_hi", "core")), placed, placed, placed),
        out_specs=(placed, P(None, ("row", "quarter"), ("y", "z_hi", "core"))),
        check_vma=False,
    )
```

time: 217 us -> 214 us (0.986)
  the two profiles are of different devices: /device:TPU:1 before, /device:TPU:8 now
where the time goes in v5:
time: 214 us; the launch traced here: 213 us
  waiting for transfers between devices  81.8 us (38%)
  starting transfers between devices  70.2 us (33%)
  blocking collectives  25.8 us (12%)
  between operations  14.2 us (7%)
  Pallas kernels  14 us (7%)
  local copies, waits for them, and re-layouts  4.98 us (2%)
  other arithmetic  2.28 us (1%)
    all_gather x1, waiting for transfers between devices, per_device(): right_panel = lax.all_gather(right_root, 'row', axis=0, tiled=True)  25.3 us
    ppermute x6, starting transfers between devices, turn(): return lax.ppermute(piece, 'row', pairs)  24.9 us
    all_to_all x3, starting transfers between devices, copies_to_all(): return lax.all_to_all(spread, axis, 0, 0, tiled=True)  18.6 us
    all_to_all x3, waiting for transfers between devices, copies_to_all(): return lax.all_to_all(spread, axis, 0, 0, tiled=True)  18 us
    ppermute x1, waiting for transfers between devices, per_device(): crossed = lax.ppermute(jnp.concatenate((grad, left_part)), 'z_hi', SWAP)  14.7 us
    all_to_all x1, blocking collectives, copies_to_all(): return lax.all_to_all(spread, axis, 0, 0, tiled=True)  14.7 us
    ppermute x1, starting transfers between devices, per_device(): crossed = lax.ppermute(jnp.concatenate((grad, left_part)), 'z_hi', SWAP)  11.3 us
    all_to_all x1, blocking collectives, per_device(): lax.all_to_all(updated.reshape(quarters, part, depth), 'quarter', 0, 0, t...  11.1 us
  transfers between devices with their start and end apart: 17, of which 7 were waited for; matrix products, arithmetic and copies ran while one was open for 3% of the time, Pallas kernels for 5%

profile of v5, /device:TPU:8, one launch (start us, length us, event | category | flops | bytes accessed | tf_op | source)
XLA Modules:
  0.0 213.4 jit_solution(16041394232904457388)
XLA Ops:
  7.2 0.0 all-gather.6.cloned.1.call-start
  7.2 0.7 all-gather.6.cloned.1.call-update
  7.9 1.1 pad_maximum_fusion
  9.0 1.5 broadcast_in_dim.10
  10.5 9.5 %all-to-all-start = ((bf16[4,1024,256]{2,1,0:T(8,128)(2,1)}), bf16[4,1024,256]{2,1,0:T(8,128)(2,1)S(1)}, u32[]{:S(2)}, u32[]{:S(2)}) async-start(bf16[4,1024,256]{2,1,0:T(8,128)(2,1)} %broadcast_in_dim.10), calls=%async_computation | async-start | bytes 4194304 | tf_op jit(solution)/shard_map/all_to_all | solution.py:18
  20.0 0.8 constant_dynamic-slice_fusion
  20.8 11.3 %collective-permute-start.1 = (bf16[640,256]{1,0:T(8,128)(2,1)S(1)}, bf16[640,256]{1,0:T(8,128)(2,1)S(1)}, u32[]{:S(2)}, u32[]{:S(2)}) collective-permute-start(bf16[640,256]{1,0:T(8,128)(2,1)S(1)} %pad_maximum_fusion.1), channel_id=1, source_target_pairs={{0,2},{2,0},{1,3},{3,1},{4,6},{6,4},{5,7},{7,5},{8,10},{10,8},{9,1... | collective-permute-start | bytes 983048 | tf_op jit(solution)/shard_map/ppermute | solution.py:177
  32.1 8.3 %all-to-all-done.a0.refs_0_ = bf16[4,1024,256]{2,1,0:T(8,128)(2,1)S(1)} async-done(((bf16[4,1024,256]{2,1,0:T(8,128)(2,1)}), bf16[4,1024,256]{2,1,0:T(8,128)(2,1)S(1)}, u32[]{:S(2)}, u32[]{:S(2)}) %all-to-all-start) | async-done | bytes 2097184 | tf_op jit(solution)/shard_map/all_to_all | solution.py:18
  40.4 1.9 collective-permute-start
  42.3 14.7 %collective-permute-done.1 = bf16[640,256]{1,0:T(8,128)(2,1)S(1)} collective-permute-done((bf16[640,256]{1,0:T(8,128)(2,1)S(1)}, bf16[640,256]{1,0:T(8,128)(2,1)S(1)}, u32[]{:S(2)}, u32[]{:S(2)}) %collective-permute-start.1) | collective-permute-done | bytes 327712 | tf_op jit(solution)/shard_map/ppermute | solution.py:177
  57.0 0.1 broadcast_in_dim.11
  57.1 14.7 %all_to_all.25.a2 = bf16[4,512,256]{2,1,0:T(8,128)(2,1)S(1)} all-to-all(bf16[4,512,256]{2,1,0:T(8,128)(2,1)S(1)} %broadcast_in_dim.11), channel_id=1, replica_groups=mesh['quarter'=4,'row'=8,'y'=4,'z_hi'=2,'core'=2] {'y'}, dimensions={0} | all-to-all | bytes 2097152 | tf_op jit(solution)/shard_map/all_to_all | solution.py:18
  71.8 1.9 collective-permute-start.2
  73.7 0.6 pad_add_fusion.3
  74.3 0.7 broadcast_in_dim.12
  75.0 4.3 %all-to-all-start.2 = ((bf16[4,128,256]{2,1,0:T(8,128)(2,1)}), bf16[4,128,256]{2,1,0:T(8,128)(2,1)S(1)}, u32[]{:S(2)}, u32[]{:S(2)}) async-start(bf16[4,128,256]{2,1,0:T(8,128)(2,1)} %broadcast_in_dim.12), calls=%async_computation.2 | async-start | bytes 524288 | tf_op jit(solution)/shard_map/all_to_all | solution.py:18
  79.3 0.6 pad_add_fusion.2
  79.9 0.0 collective-permute-done.2.a3
  79.9 25.3 %all-gather.6.cloned.1.call-done = bf16[1,4096,256]{2,1,0:T(8,128)(2,1)} async-done(((bf16[1,512,256]{2,1,0:T(8,128)(2,1)}), bf16[1,4096,256]{2,1,0:T(8,128)(2,1)}) %all-gather.6.cloned.1.call-update) | async-done | bytes 2097168 | tf_op jit(solution)/shard_map/all_gather | solution.py:175
  105.2 0.0 collective-permute-done.a1.refs_1_
  105.2 5.9 %shard_map.68 = (bf16[512,256]{1,0:T(8,128)(2,1)}, bf16[512,128]{1,0:T(8,128)(2,1)}, bf16[512,128]{1,0:T(8,128)(2,1)}) custom-call(s32[4]{0:T(128)} %get-tuple-element.24.place, bf16[4,1024,256]{2,1,0:T(8,128)(2,1)} %copy-done, bf16[4,1024,256]{2,1,0:T(8,128)(2,1)} %collective-permute-done.a1.refs_1_, bf16[4,512,256]{2,1,0:T(8,128)(2,1)} %copy-done.3, ...), custom_call_target="tpu_custom_call" | custom-call | flops 1073741824 | bytes 6291456 | tf_op jit(solution)/shard_map/pallas_call | solution.py:140
  111.0 0.0 all-to-all-done.2
  111.0 1.1 broadcast_in_dim.13
  112.1 4.8 %all-to-all-start.3 = ((bf16[4,512,256]{2,1,0:T(8,128)(2,1)}), bf16[4,512,256]{2,1,0:T(8,128)(2,1)S(1)}, u32[]{:S(2)}, u32[]{:S(2)}) async-start(bf16[4,512,256]{2,1,0:T(8,128)(2,1)} %broadcast_in_dim.13), calls=%async_computation.3 | async-start | bytes 2097152 | tf_op jit(solution)/shard_map/all_to_all | solution.py:18
  117.0 0.7 all-gather.4.cloned.1.call-update
  117.7 9.7 %all-to-all-done.3.a2.refs_2_ = bf16[4,512,256]{2,1,0:T(8,128)(2,1)S(1)} async-done(((bf16[4,512,256]{2,1,0:T(8,128)(2,1)}), bf16[4,512,256]{2,1,0:T(8,128)(2,1)S(1)}, u32[]{:S(2)}, u32[]{:S(2)}) %all-to-all-start.3) | async-done | bytes 1048608 | tf_op jit(solution)/shard_map/all_to_all | solution.py:18
  127.4 1.9 collective-permute-start.3
  129.3 2.3 %collective-permute-start.4 = (bf16[512,128]{1,0:T(8,128)(2,1)S(1)}, bf16[512,128]{1,0:T(8,128)(2,1)S(1)}, u32[]{:S(2)}, u32[]{:S(2)}) collective-permute-start(bf16[512,128]{1,0:T(8,128)(2,1)S(1)} %copy-done.6), channel_id=1, source_target_pairs={{0,64},{16,80},{32,96},{48,112},{64,0},{80,16},{96,32},{112,48},{1... | collective-permute-start | bytes 393224 | tf_op jit(solution)/shard_map/ppermute | solution.py:29
  131.7 7.4 %collective-permute-start.8 = (bf16[512,128]{1,0:T(8,128)(2,1)S(1)}, bf16[512,128]{1,0:T(8,128)(2,1)S(1)}, u32[]{:S(2)}, u32[]{:S(2)}) collective-permute-start(bf16[512,128]{1,0:T(8,128)(2,1)S(1)} %copy-done.5), channel_id=1, source_target_pairs={{0,64},{16,80},{32,96},{48,112},{64,0},{80,16},{96,32},{112,48},{1... | collective-permute-start | bytes 393224 | tf_op jit(solution)/shard_map/ppermute | solution.py:29
  139.1 10.4 %collective-permute-done.4.refs_4_ = bf16[512,128]{1,0:T(8,128)(2,1)S(1)} collective-permute-done((bf16[512,128]{1,0:T(8,128)(2,1)S(1)}, bf16[512,128]{1,0:T(8,128)(2,1)S(1)}, u32[]{:S(2)}, u32[]{:S(2)}) %collective-permute-start.4) | collective-permute-done | bytes 131104 | tf_op jit(solution)/shard_map/ppermute | solution.py:29
  149.5 1.9 collective-permute-start.7
  151.5 10.7 %collective-permute-start.6 = (bf16[512,128]{1,0:T(8,128)(2,1)S(1)}, bf16[512,128]{1,0:T(8,128)(2,1)S(1)}, u32[]{:S(2)}, u32[]{:S(2)}) collective-permute-start(bf16[512,128]{1,0:T(8,128)(2,1)S(1)} %collective-permute-done.4.refs_4_), channel_id=1, source_target_pairs={{0,32},{16,48},{32,0},{48,16},{64,96},{80,112},{96,64},{112,80},{1... | collective-permute-start | bytes 393224 | tf_op jit(solution)/shard_map/ppermute | solution.py:24
  162.2 3.9 %collective-permute-start.5 = (bf16[512,128]{1,0:T(8,128)(2,1)S(1)}, bf16[512,128]{1,0:T(8,128)(2,1)S(1)}, u32[]{:S(2)}, u32[]{:S(2)}) collective-permute-start(bf16[512,128]{1,0:T(8,128)(2,1)S(1)} %collective-permute-done.4.refs_4_), channel_id=1, source_target_pairs={{0,16},{16,32},{32,48},{48,0},{64,80},{80,96},{96,112},{112,64},{1... | collective-permute-start | bytes 393224 | tf_op jit(solution)/shard_map/ppermute | solution.py:24
  166.1 0.0 collective-permute-done.8.refs_8_
  166.1 3.7 %collective-permute-start.11 = (bf16[512,128]{1,0:T(8,128)(2,1)S(1)}, bf16[512,128]{1,0:T(8,128)(2,1)S(1)}, u32[]{:S(2)}, u32[]{:S(2)}) collective-permute-start(bf16[512,128]{1,0:T(8,128)(2,1)S(1)} %collective-permute-done.8.refs_8_), channel_id=1, source_target_pairs={{0,48},{16,0},{32,16},{48,32},{64,112},{80,64},{96,80},{112,96},{1... | collective-permute-start | bytes 393224 | tf_op jit(solution)/shard_map/ppermute | solution.py:24
  169.8 0.0 collective-permute-done.7.refs_7_
  169.8 1.9 collective-permute-start.10
  171.8 0.0 collective-permute-done.3.a3.refs_3_
  171.8 2.7 %collective-permute-start.9 = (bf16[512,128]{1,0:T(8,128)(2,1)S(1)}, bf16[512,128]{1,0:T(8,128)(2,1)S(1)}, u32[]{:S(2)}, u32[]{:S(2)}) collective-permute-start(bf16[512,128]{1,0:T(8,128)(2,1)S(1)} %collective-permute-done.8.refs_8_), channel_id=1, source_target_pairs={{0,16},{16,32},{32,48},{48,0},{64,80},{80,96},{96,112},{112,64},{1... | collective-permute-start | bytes 393224 | tf_op jit(solution)/shard_map/ppermute | solution.py:24
  174.5 2.5 %all-gather.4.cloned.1.call-done.b_ref = bf16[2048,256]{1,0:T(8,128)(2,1)} async-done(((bf16[512,256]{1,0:T(8,128)(2,1)}), bf16[2048,256]{1,0:T(8,128)(2,1)}) %all-gather.4.cloned.1.call-update) | async-done | bytes 1048592 | tf_op jit(solution)/shard_map/all_gather | solution.py:187
  177.0 3.9 %shard_map.69.refs_12_ = f32[512,256]{1,0:T(8,128)} custom-call(s32[4]{0:T(128)} %get-tuple-element.22.place, bf16[4,1024,256]{2,1,0:T(8,128)(2,1)} %copy-done, bf16[4,1024,256]{2,1,0:T(8,128)(2,1)} %collective-permute-done.a1.refs_1_, bf16[4,512,256]{2,1,0:T(8,128)(2,1)} %copy-done.1, bf16[4,512,256]{2,1,0:T(8,128)(2,1)} %copy-done.2, ...), custom_call_target="tpu_custom_call" | custom-call | flops 536870912 | bytes 3145728 | tf_op jit(solution)/shard_map/pallas_call | solution.py:140
  181.0 0.0 collective-permute-done.6.refs_6_
  181.0 0.0 collective-permute-done.5.refs_5_
  181.0 0.0 collective-permute-done.11.refs_11_
  181.0 9.5 %collective-permute-done.10.refs_10_ = bf16[512,128]{1,0:T(8,128)(2,1)S(1)} collective-permute-done((bf16[512,128]{1,0:T(8,128)(2,1)S(1)}, bf16[512,128]{1,0:T(8,128)(2,1)S(1)}, u32[]{:S(2)}, u32[]{:S(2)}) %collective-permute-start.10) | collective-permute-done | bytes 131104 | tf_op jit(solution)/shard_map/ppermute | solution.py:24
  190.4 4.3 %update.1 = (f32[512,256]{1,0:T(8,128)}, bf16[512,256]{1,0:T(8,128)(2,1)}) custom-call(s32[4]{0:T(128)} %get-tuple-element.25.place, bf16[4,1024,256]{2,1,0:T(8,128)(2,1)} %copy-done, bf16[4,1024,256]{2,1,0:T(8,128)(2,1)} %collective-permute-done.a1.refs_1_, bf16[4,512,256]{2,1,0:T(8,128)(2,1)} %copy-done.1, bf16[4,512,256]{2,1,0:T(8,128)(2,1)} %copy-done.2, ...), custom_call_target="tpu_custom_call" | custom-call | flops 536870912 | bytes 4980736 | tf_op jit(solution)/shard_map/update/pallas_call | solution.py:84
  194.7 11.1 %all_to_all.26 = bf16[4,128,256]{2,1,0:T(8,128)(2,1)S(1)} all-to-all(bf16[4,128,256]{2,1,0:T(8,128)(2,1)} %bitcast.18), channel_id=1, replica_groups=mesh['quarter'=4,'row'=8,'y'=4,'z_hi'=2,'core'=2] {'quarter'}, dimensions={0} | all-to-all | bytes 524288 | tf_op jit(solution)/shard_map/all_to_all | solution.py:198
  205.8 0.7 copy.8
  (19 shorter events, 0.1 us)
Async XLA Ops:
  7.2 98.0 %all-gather.6.cloned.1.call-start = ((), (), s32[]{:S(2)}) async-start(), calls=%async_computation.6 | async-start | bytes 2359296 | tf_op jit(solution)/shard_map/all_gather | solution.py:175
  10.5 10.3 %copy-start.4 = (bf16[1,512,256]{2,1,0:T(8,128)(2,1)S(1)}, bf16[1,512,256]{2,1,0:T(8,128)(2,1)}, u32[]{:S(2)}) copy-start(bf16[1,512,256]{2,1,0:T(8,128)(2,1)} %param.5) | copy-start | bytes 786436
  10.5 29.9 %all-to-all-start = ((bf16[4,1024,256]{2,1,0:T(8,128)(2,1)}), bf16[4,1024,256]{2,1,0:T(8,128)(2,1)S(1)}, u32[]{:S(2)}, u32[]{:S(2)}) async-start(bf16[4,1024,256]{2,1,0:T(8,128)(2,1)} %broadcast_in_dim.10), calls=%async_computation | async-start | bytes 4194304 | tf_op jit(solution)/shard_map/all_to_all | solution.py:18
  20.8 36.2 %collective-permute-start.1 = (bf16[640,256]{1,0:T(8,128)(2,1)S(1)}, bf16[640,256]{1,0:T(8,128)(2,1)S(1)}, u32[]{:S(2)}, u32[]{:S(2)}) collective-permute-start(bf16[640,256]{1,0:T(8,128)(2,1)S(1)} %pad_maximum_fusion.1), channel_id=1, source_target_pairs={{0,2},{2,0},{1,3},{3,1},{4,6},{6,4},{5,7},{7,5},{8,10},{10,8},{9,1... | collective-permute-start | bytes 983048 | tf_op jit(solution)/shard_map/ppermute | solution.py:177
  40.4 34.7 %copy-start = (bf16[4,1024,256]{2,1,0:T(8,128)(2,1)}, bf16[4,1024,256]{2,1,0:T(8,128)(2,1)S(1)}, u32[]{:S(2)}) copy-start(bf16[4,1024,256]{2,1,0:T(8,128)(2,1)S(1)} %all-to-all-done.a0.refs_0_) | copy-start | bytes 6291460
  40.4 64.8 %collective-permute-start = (bf16[4,1024,256]{2,1,0:T(8,128)(2,1)S(1)}, bf16[4,1024,256]{2,1,0:T(8,128)(2,1)}, u32[]{:S(2)}, u32[]{:S(2)}) collective-permute-start(bf16[4,1024,256]{2,1,0:T(8,128)(2,1)S(1)} %all-to-all-done.a0.refs_0_), channel_id=1, source_target_pairs={{0,1},{1,0},{2,3},{3,2},{4,5},{5,4},{6,7},{7,6},{8,9},{9,8},{10,11... | collective-permute-start | bytes 6291464 | tf_op jit(solution)/shard_map/ppermute | solution.py:160
  71.8 33.4 %copy-start.3 = (bf16[4,512,256]{2,1,0:T(8,128)(2,1)}, bf16[4,512,256]{2,1,0:T(8,128)(2,1)S(1)}, u32[]{:S(2)}) copy-start(bf16[4,512,256]{2,1,0:T(8,128)(2,1)S(1)} %all_to_all.25.a2) | copy-start | bytes 3145732
  71.8 8.1 %collective-permute-start.2 = (bf16[4,512,256]{2,1,0:T(8,128)(2,1)S(1)}, bf16[4,512,256]{2,1,0:T(8,128)(2,1)}, u32[]{:S(2)}, u32[]{:S(2)}) collective-permute-start(bf16[4,512,256]{2,1,0:T(8,128)(2,1)S(1)} %all_to_all.25.a2), channel_id=1, source_target_pairs={{0,1},{1,0},{2,3},{3,2},{4,5},{5,4},{6,7},{7,6},{8,9},{9,8},{10,11... | collective-permute-start | bytes 3145736 | tf_op jit(solution)/shard_map/ppermute | solution.py:160
  75.0 36.0 %all-to-all-start.2 = ((bf16[4,128,256]{2,1,0:T(8,128)(2,1)}), bf16[4,128,256]{2,1,0:T(8,128)(2,1)S(1)}, u32[]{:S(2)}, u32[]{:S(2)}) async-start(bf16[4,128,256]{2,1,0:T(8,128)(2,1)} %broadcast_in_dim.12), calls=%async_computation.2 | async-start | bytes 524288 | tf_op jit(solution)/shard_map/all_to_all | solution.py:18
  111.0 18.3 %copy-start.6 = (bf16[512,128]{1,0:T(8,128)(2,1)S(1)}, bf16[512,128]{1,0:T(8,128)(2,1)}, u32[]{:S(2)}) copy-start(bf16[512,128]{1,0:T(8,128)(2,1)} %get-tuple-element.17) | copy-start | bytes 393220
  111.0 20.7 %copy-start.5 = (bf16[512,128]{1,0:T(8,128)(2,1)S(1)}, bf16[512,128]{1,0:T(8,128)(2,1)}, u32[]{:S(2)}) copy-start(bf16[512,128]{1,0:T(8,128)(2,1)} %get-tuple-element.18) | copy-start | bytes 393220
  112.1 15.3 %all-to-all-start.3 = ((bf16[4,512,256]{2,1,0:T(8,128)(2,1)}), bf16[4,512,256]{2,1,0:T(8,128)(2,1)S(1)}, u32[]{:S(2)}, u32[]{:S(2)}) async-start(bf16[4,512,256]{2,1,0:T(8,128)(2,1)} %broadcast_in_dim.13), calls=%async_computation.3 | async-start | bytes 2097152 | tf_op jit(solution)/shard_map/all_to_all | solution.py:18
  117.0 60.1 %all-gather.4.cloned.1.call-start = ((), (), s32[]{:S(2)}) async-start(), calls=%async_computation.5 | async-start | bytes 1310720 | tf_op jit(solution)/shard_map/all_gather | solution.py:187
  127.4 49.6 %copy-start.1 = (bf16[4,512,256]{2,1,0:T(8,128)(2,1)}, bf16[4,512,256]{2,1,0:T(8,128)(2,1)S(1)}, u32[]{:S(2)}) copy-start(bf16[4,512,256]{2,1,0:T(8,128)(2,1)S(1)} %all-to-all-done.3.a2.refs_2_) | copy-start | bytes 3145732
  127.4 44.4 %collective-permute-start.3 = (bf16[4,512,256]{2,1,0:T(8,128)(2,1)S(1)}, bf16[4,512,256]{2,1,0:T(8,128)(2,1)S(1)}, u32[]{:S(2)}, u32[]{:S(2)}) collective-permute-start(bf16[4,512,256]{2,1,0:T(8,128)(2,1)S(1)} %all-to-all-done.3.a2.refs_2_), channel_id=1, source_target_pairs={{0,1},{1,0},{2,3},{3,2},{4,5},{5,4},{6,7},{7,6},{8,9},{9,8},{10,11... | collective-permute-start | bytes 3145736 | tf_op jit(solution)/shard_map/ppermute | solution.py:160
  129.3 20.2 %collective-permute-start.4 = (bf16[512,128]{1,0:T(8,128)(2,1)S(1)}, bf16[512,128]{1,0:T(8,128)(2,1)S(1)}, u32[]{:S(2)}, u32[]{:S(2)}) collective-permute-start(bf16[512,128]{1,0:T(8,128)(2,1)S(1)} %copy-done.6), channel_id=1, source_target_pairs={{0,64},{16,80},{32,96},{48,112},{64,0},{80,16},{96,32},{112,48},{1... | collective-permute-start | bytes 393224 | tf_op jit(solution)/shard_map/ppermute | solution.py:29
  131.7 34.4 %collective-permute-start.8 = (bf16[512,128]{1,0:T(8,128)(2,1)S(1)}, bf16[512,128]{1,0:T(8,128)(2,1)S(1)}, u32[]{:S(2)}, u32[]{:S(2)}) collective-permute-start(bf16[512,128]{1,0:T(8,128)(2,1)S(1)} %copy-done.5), channel_id=1, source_target_pairs={{0,64},{16,80},{32,96},{48,112},{64,0},{80,16},{96,32},{112,48},{1... | collective-permute-start | bytes 393224 | tf_op jit(solution)/shard_map/ppermute | solution.py:29
  149.5 20.3 %collective-permute-start.7 = (bf16[512,128]{1,0:T(8,128)(2,1)S(1)}, bf16[512,128]{1,0:T(8,128)(2,1)S(1)}, u32[]{:S(2)}, u32[]{:S(2)}) collective-permute-start(bf16[512,128]{1,0:T(8,128)(2,1)S(1)} %collective-permute-done.4.refs_4_), channel_id=1, source_target_pairs={{0,48},{16,0},{32,16},{48,32},{64,112},{80,64},{96,80},{112,96},{1... | collective-permute-start | bytes 393224 | tf_op jit(solution)/shard_map/ppermute | solution.py:24
  151.5 29.5 %collective-permute-start.6 = (bf16[512,128]{1,0:T(8,128)(2,1)S(1)}, bf16[512,128]{1,0:T(8,128)(2,1)S(1)}, u32[]{:S(2)}, u32[]{:S(2)}) collective-permute-start(bf16[512,128]{1,0:T(8,128)(2,1)S(1)} %collective-permute-done.4.refs_4_), channel_id=1, source_target_pairs={{0,32},{16,48},{32,0},{48,16},{64,96},{80,112},{96,64},{112,80},{1... | collective-permute-start | bytes 393224 | tf_op jit(solution)/shard_map/ppermute | solution.py:24
  162.2 18.8 %collective-permute-start.5 = (bf16[512,128]{1,0:T(8,128)(2,1)S(1)}, bf16[512,128]{1,0:T(8,128)(2,1)S(1)}, u32[]{:S(2)}, u32[]{:S(2)}) collective-permute-start(bf16[512,128]{1,0:T(8,128)(2,1)S(1)} %collective-permute-done.4.refs_4_), channel_id=1, source_target_pairs={{0,16},{16,32},{32,48},{48,0},{64,80},{80,96},{96,112},{112,64},{1... | collective-permute-start | bytes 393224 | tf_op jit(solution)/shard_map/ppermute | solution.py:24
  166.1 14.9 %collective-permute-start.11 = (bf16[512,128]{1,0:T(8,128)(2,1)S(1)}, bf16[512,128]{1,0:T(8,128)(2,1)S(1)}, u32[]{:S(2)}, u32[]{:S(2)}) collective-permute-start(bf16[512,128]{1,0:T(8,128)(2,1)S(1)} %collective-permute-done.8.refs_8_), channel_id=1, source_target_pairs={{0,48},{16,0},{32,16},{48,32},{64,112},{80,64},{96,80},{112,96},{1... | collective-permute-start | bytes 393224 | tf_op jit(solution)/shard_map/ppermute | solution.py:24
  169.8 20.6 %collective-permute-start.10 = (bf16[512,128]{1,0:T(8,128)(2,1)S(1)}, bf16[512,128]{1,0:T(8,128)(2,1)S(1)}, u32[]{:S(2)}, u32[]{:S(2)}) collective-permute-start(bf16[512,128]{1,0:T(8,128)(2,1)S(1)} %collective-permute-done.8.refs_8_), channel_id=1, source_target_pairs={{0,32},{16,48},{32,0},{48,16},{64,96},{80,112},{96,64},{112,80},{1... | collective-permute-start | bytes 393224 | tf_op jit(solution)/shard_map/ppermute | solution.py:24
  171.8 5.2 %copy-start.2 = (bf16[4,512,256]{2,1,0:T(8,128)(2,1)}, bf16[4,512,256]{2,1,0:T(8,128)(2,1)S(1)}, u32[]{:S(2)}) copy-start(bf16[4,512,256]{2,1,0:T(8,128)(2,1)S(1)} %collective-permute-done.3.a3.refs_3_) | copy-start | bytes 3145732
  171.8 18.7 %collective-permute-start.9 = (bf16[512,128]{1,0:T(8,128)(2,1)S(1)}, bf16[512,128]{1,0:T(8,128)(2,1)S(1)}, u32[]{:S(2)}, u32[]{:S(2)}) collective-permute-start(bf16[512,128]{1,0:T(8,128)(2,1)S(1)} %collective-permute-done.8.refs_8_), channel_id=1, source_target_pairs={{0,16},{16,32},{32,48},{48,0},{64,80},{80,96},{96,112},{112,64},{1... | collective-permute-start | bytes 393224 | tf_op jit(solution)/shard_map/ppermute | solution.py:24
Sparse Core Ops, SparseCore 0:
  10.0 95.0 all-gather.5
  120.4 56.5 all-gather.3

commit v6 on v5

v6 whole, which is shorter than its diff:
```python
import functools

import jax
import jax.numpy as jnp
from jax import lax
from jax.experimental import pallas as pl
from jax.experimental.pallas import tpu as pltpu
from jax.sharding import Mesh, PartitionSpec as P

decay_rate = 0.9
step_rate = 0.1
AXES = ("quarter", "row", "y", "z_hi", "core")
SWAP = [(0, 1), (1, 0)]
CUBE = 4
KERNEL_VMEM = 16 * 2**20


def copies_to_all(piece, axis):
    n = lax.axis_size(axis)
    spread = jnp.broadcast_to(piece[None], (n, *piece.shape))
    return lax.all_to_all(spread, axis, 0, 0, tiled=True)


def turn(piece, by):
    rows = lax.axis_size("row")
    pairs = [(i, i // CUBE * CUBE + (i + by) % CUBE) for i in range(rows)]
    return lax.ppermute(piece, "row", pairs)


def across(piece):
    rows = lax.axis_size("row")
    return lax.ppermute(piece, "row", [(i, i ^ CUBE) for i in range(rows)])


def far_slots(piece):
    return [piece] + [turn(piece, by) for by in range(1, CUBE)]


def accumulate(place, step, pieces, at_rows, slots):
    half, core, turned = place[0], place[1], place[2]
    depth = pieces[0].shape[-1]
    odd = (turned + half) % 2
    total = None
    for n, piece in enumerate(pieces):
        first = pl.multiple_of(depth * (core if n % 2 == 0 else 1 - core), depth)
        even, other = (
            jnp.concatenate([part[pl.ds(first, depth), :] for part in slot], axis=1)
            for slot in slots[2 * step : 2 * step + 2]
        )
        rows = jnp.where(odd == n // 2, even, other)
        back = 2 * step + (odd if n < 2 else 1 - odd)
        at = place[3] + (turned + 2 * CUBE - back) % CUBE // 2
        block = piece[at, at_rows[n] * 2 * depth : (at_rows[n] + 1) * 2 * depth, :]
        part = jnp.dot(block, rows, preferred_element_type=jnp.float32)
        total = part if total is None else total + part
    return total


def update_kernel(at_rows, place, *refs):
    pieces, parts, (p_ref, m_ref, w_ref, mo_ref, wo_ref) = refs[:4], refs[4 : 4 + 2 * CUBE], refs[4 + 2 * CUBE :]
    slots = list(zip(parts[:CUBE], parts[CUBE:], strict=True))
    product = p_ref[...]
    for step in range(CUBE // 2):
        product += accumulate(place, step, pieces, at_rows, slots)
    renewed = decay_rate * m_ref[...] + (1.0 - decay_rate) * product
    mo_ref[...] = renewed
    wo_ref[...] = (w_ref[...].astype(jnp.float32) - step_rate * renewed).astype(wo_ref.dtype)


def update(place, pieces, at_rows, low, high, begun, momentum, weights):
    depth = pieces[0].shape[-1]
    rows, columns = momentum.shape
    given = in_vmem([*pieces, *low, *high, begun, momentum, weights])
    moved = 4 * CUBE * rows * depth + 2 * CUBE * rows * columns + 14 * rows * columns
    return pl.pallas_call(
        functools.partial(update_kernel, at_rows),
        out_shape=[jax.ShapeDtypeStruct((rows, columns), t) for t in (jnp.float32, jnp.bfloat16)],
        grid_spec=pltpu.PrefetchScalarGridSpec(
            num_scalar_prefetch=1,
            grid=(1,),
            in_specs=[pl.BlockSpec(memory_space=pltpu.MemorySpace.VMEM)] * len(given),
            out_specs=[pl.BlockSpec((rows, columns), lambda i, place: (0, 0))] * 2,
        ),
        cost_estimate=pl.CostEstimate(
            flops=2 * rows * CUBE * rows * columns, bytes_accessed=moved, transcendentals=0
        ),
        compiler_params=pltpu.CompilerParams(vmem_limit_bytes=KERNEL_VMEM),
        name="update",
    )(place, *given)


def mix_kernel(at_rows, place, a0, a1, a2, a3, b_ref, o_ref, acc_ref):
    half, core = place[0], place[1]
    depth = a0.shape[-1]
    at = place[3] + pl.program_id(0)
    total = None
    for n, piece in enumerate((a0, a1, a2, a3)):
        first = 2 * (half if n < 2 else 1 - half) + (core if n % 2 == 0 else 1 - core)
        rows = b_ref[pl.ds(pl.multiple_of(first * depth, depth), depth), :]
        block = piece[at, at_rows[n] * 2 * depth : (at_rows[n] + 1) * 2 * depth, :]
        part = jnp.dot(block, rows, preferred_element_type=jnp.float32)
        total = part if total is None else total + part

    @pl.when(pl.program_id(0) == 0)
    def _():
        acc_ref[...] = total

    @pl.when(pl.program_id(0) > 0)
    def _():
        acc_ref[...] += total

    @pl.when(pl.program_id(0) == pl.num_programs(0) - 1)
    def _():
        o_ref[...] = acc_ref[...].astype(o_ref.dtype)


def mix(place, pieces, at_rows, right, kind, first=0, columns=None):
    depth = pieces[0].shape[-1]
    columns = columns or right.shape[1]
    steps, rows = right.shape[0] // (4 * depth), 2 * depth
    return pl.pallas_call(
        functools.partial(mix_kernel, at_rows),
        out_shape=jax.ShapeDtypeStruct((rows, columns), kind),
        grid_spec=pltpu.PrefetchScalarGridSpec(
            num_scalar_prefetch=1,
            grid=(steps,),
            in_specs=[pl.BlockSpec(memory_space=pltpu.MemorySpace.VMEM)] * 4
            + [pl.BlockSpec((4 * depth, columns), lambda i, place: (i, first))],
            out_specs=pl.BlockSpec((rows, columns), lambda i, place: (0, 0)),
            scratch_shapes=[pltpu.VMEM((rows, columns), jnp.float32)],
        ),
        cost_estimate=pl.CostEstimate(
            flops=2 * rows * right.shape[0] * columns,
            bytes_accessed=2 * (4 * steps * rows * depth + right.shape[0] * columns),
            transcendentals=0,
        ),
        compiler_params=pltpu.CompilerParams(vmem_limit_bytes=KERNEL_VMEM),
    )(place, *in_vmem(pieces), pltpu.with_memory_space_constraint(right, pltpu.MemorySpace.HBM))


def in_vmem(values):
    return [pltpu.with_memory_space_constraint(value, pltpu.MemorySpace.VMEM) for value in values]


def with_partner(mine):
    return [mine, lax.ppermute(mine, "core", SWAP)]


def per_device(grad, left_root, right_root, momentum, weights):
    half, core, row = (lax.axis_index(a).astype(jnp.int32) for a in ("z_hi", "core", "row"))
    upper = row // CUBE
    every = jnp.stack((half, core, row % CUBE, 0 * upper))
    near = jnp.stack((half, core, row % CUBE, 2 * upper))
    far = jnp.stack((half, core, row % CUBE, 2 - 2 * upper))
    quarter = lax.axis_index("quarter")
    quarters = lax.axis_size("quarter")
    rows, depth = left_root.shape
    part = rows // quarters
    grad, right_root = grad[0], right_root[0]

    right_panel = lax.all_gather(right_root, "row", axis=0, tiled=True)
    left_part = lax.dynamic_slice_in_dim(left_root, quarter * part, part, 0)
    crossed = lax.ppermute(jnp.concatenate((grad, left_part)), "z_hi", SWAP)
    mine = with_partner(copies_to_all(jnp.concatenate((grad, left_root)), "y"))
    grad_theirs = copies_to_all(crossed[:rows], "y")
    panel = mine + with_partner(grad_theirs)
    _, left_part = lax.optimization_barrier((grad_theirs, crossed[rows:]))
    left_other = copies_to_all(left_part, "quarter").reshape(rows, depth)

    half_columns = depth // 2
    parts = []
    for n in range(2):
        parts.append(mix(every, panel, (0, 0, 0, 0), right_panel, jnp.bfloat16, n, half_columns))
    parts[0], left_other = lax.optimization_barrier((parts[0], left_other))
    runs = [list(range(i, i + CUBE)) for i in range(0, lax.axis_size("row"), CUBE)]
    near_panel = lax.all_gather(
        jnp.concatenate(parts, axis=1), "row", axis=0, tiled=True, axis_index_groups=runs
    )
    others = []
    for piece in parts:
        others.append(across(piece))
    left_theirs = copies_to_all(left_other, "y")
    panel = mine + with_partner(left_theirs)
    slots = []
    for piece in others:
        slots.append(far_slots(piece))
    begun = mix(near, panel, (1, 1, 0, 0), near_panel, jnp.float32)
    renewed, updated = update(far, panel, (1, 1, 0, 0), *slots, begun, momentum[0], weights[0])
    spread = lax.all_to_all(updated.reshape(quarters, part, depth), "quarter", 0, 0, tiled=True)
    return renewed[None], spread


def solution(mesh):
    fine = Mesh(mesh.devices.reshape(4, 8, 4, 2, 2), AXES)
    placed = P("quarter", "row", ("y", "z_hi", "core"))
    return jax.shard_map(
        per_device,
        mesh=fine,
        in_specs=(placed, P("row", ("y", "z_hi", "core")), placed, placed, placed),
        out_specs=(placed, P(None, ("row", "quarter"), ("y", "z_hi", "core"))),
        check_vma=False,
    )
```

time: 214 us -> 214 us (level)
  starting transfers between devices: 70.2 us -> 66.2 us
  Pallas kernels: 14 us -> 17.6 us
    all_gather x1, waiting for transfers between devices: 2.52 us -> 11.7 us  [per_device(): lax.all_gather(jnp.concatenate(parts, axis=1), 'row', axis=0, tiled=True,...]
    ppermute x6, waiting for transfers between devices: 9.48 us -> 4.57 us  [turn(): return lax.ppermute(piece, 'row', pairs)]
    all_to_all x3, waiting for transfers between devices: 18 us -> 13.6 us  [copies_to_all(): return lax.all_to_all(spread, axis, 0, 0, tiled=True)]
    ppermute x6, starting transfers between devices: 24.9 us -> 21.2 us  [turn(): return lax.ppermute(piece, 'row', pairs)]
    pallas_call x3 -> x4, Pallas kernels: 14 us -> 17.6 us  [the longest x3 13.5 us: mix(): pl.pallas_call(functools.partial(mix_kernel, at_rows), out_shape=jax.Shap...]
  transfers between devices with their start and end apart: 17 -> 17, of which waited for: 7 -> 7; matrix products, arithmetic and copies ran while one was open for 3% -> 2% of each run, Pallas kernels for 5% -> 6%
where the time goes in v6:
time: 214 us; the launch traced here: 213 us
  waiting for transfers between devices  83.2 us (39%)
  starting transfers between devices  66.2 us (31%)
  blocking collectives  25.1 us (12%)
  Pallas kernels  17.6 us (8%)
  between operations  14.3 us (7%)
  local copies, waits for them, and re-layouts  4.87 us (2%)
    all_gather x1, waiting for transfers between devices, per_device(): right_panel = lax.all_gather(right_root, 'row', axis=0, tiled=True)  26.3 us
    ppermute x6, starting transfers between devices, turn(): return lax.ppermute(piece, 'row', pairs)  21.2 us
    all_to_all x3, starting transfers between devices, copies_to_all(): return lax.all_to_all(spread, axis, 0, 0, tiled=True)  18.2 us
    ppermute x1, waiting for transfers between devices, per_device(): crossed = lax.ppermute(jnp.concatenate((grad, left_part)), 'z_hi', SWAP)  14.7 us
    all_to_all x1, blocking collectives, copies_to_all(): return lax.all_to_all(spread, axis, 0, 0, tiled=True)  14.7 us
    all_to_all x3, waiting for transfers between devices, copies_to_all(): return lax.all_to_all(spread, axis, 0, 0, tiled=True)  13.6 us
    pallas_call x3, Pallas kernels, mix(): pl.pallas_call(functools.partial(mix_kernel, at_rows), out_shape=jax.Shap...  13.5 us
    all_gather x1, waiting for transfers between devices, per_device(): lax.all_gather(jnp.concatenate(parts, axis=1), 'row', axis=0, tiled=True,...  11.7 us
  transfers between devices with their start and end apart: 17, of which 7 were waited for; matrix products, arithmetic and copies ran while one was open for 2% of the time, Pallas kernels for 6%

profile of v6, /device:TPU:8, one launch (start us, length us, event | category | flops | bytes accessed | tf_op | source)
XLA Modules:
  0.0 213.2 jit_solution(18065344232380412741)
XLA Ops:
  7.2 0.0 all-gather.6.cloned.1.call-start
  7.2 0.7 all-gather.6.cloned.1.call-update
  7.9 1.1 pad_maximum_fusion
  9.0 1.5 broadcast_in_dim.10
  10.4 9.5 %all-to-all-start = ((bf16[4,1024,256]{2,1,0:T(8,128)(2,1)}), bf16[4,1024,256]{2,1,0:T(8,128)(2,1)S(1)}, u32[]{:S(2)}, u32[]{:S(2)}) async-start(bf16[4,1024,256]{2,1,0:T(8,128)(2,1)} %broadcast_in_dim.10), calls=%async_computation | async-start | bytes 4194304 | tf_op jit(solution)/shard_map/all_to_all | solution.py:21
  19.9 0.8 constant_dynamic-slice_fusion
  20.8 11.3 %collective-permute-start.1 = (bf16[640,256]{1,0:T(8,128)(2,1)S(1)}, bf16[640,256]{1,0:T(8,128)(2,1)S(1)}, u32[]{:S(2)}, u32[]{:S(2)}) collective-permute-start(bf16[640,256]{1,0:T(8,128)(2,1)S(1)} %pad_maximum_fusion.1), channel_id=1, source_target_pairs={{0,2},{2,0},{1,3},{3,1},{4,6},{6,4},{5,7},{7,5},{8,10},{10,8},{9,1... | collective-permute-start | bytes 983048 | tf_op jit(solution)/shard_map/ppermute | solution.py:163
  32.1 8.3 %all-to-all-done.a0.refs_0_ = bf16[4,1024,256]{2,1,0:T(8,128)(2,1)S(1)} async-done(((bf16[4,1024,256]{2,1,0:T(8,128)(2,1)}), bf16[4,1024,256]{2,1,0:T(8,128)(2,1)S(1)}, u32[]{:S(2)}, u32[]{:S(2)}) %all-to-all-start) | async-done | bytes 2097184 | tf_op jit(solution)/shard_map/all_to_all | solution.py:21
  40.4 1.9 collective-permute-start
  42.3 14.7 %collective-permute-done.1 = bf16[640,256]{1,0:T(8,128)(2,1)S(1)} collective-permute-done((bf16[640,256]{1,0:T(8,128)(2,1)S(1)}, bf16[640,256]{1,0:T(8,128)(2,1)S(1)}, u32[]{:S(2)}, u32[]{:S(2)}) %collective-permute-start.1) | collective-permute-done | bytes 327712 | tf_op jit(solution)/shard_map/ppermute | solution.py:163
  57.0 0.1 broadcast_in_dim.11
  57.1 14.7 %all_to_all.25.a2 = bf16[4,512,256]{2,1,0:T(8,128)(2,1)S(1)} all-to-all(bf16[4,512,256]{2,1,0:T(8,128)(2,1)S(1)} %broadcast_in_dim.11), channel_id=1, replica_groups=mesh['quarter'=4,'row'=8,'y'=4,'z_hi'=2,'core'=2] {'y'}, dimensions={0} | all-to-all | bytes 2097152 | tf_op jit(solution)/shard_map/all_to_all | solution.py:21
  71.8 1.9 collective-permute-start.2
  73.7 0.1 pad_add_fusion.3
  73.8 0.7 broadcast_in_dim.12
  74.5 4.3 %all-to-all-start.2 = ((bf16[4,128,256]{2,1,0:T(8,128)(2,1)}), bf16[4,128,256]{2,1,0:T(8,128)(2,1)S(1)}, u32[]{:S(2)}, u32[]{:S(2)}) async-start(bf16[4,128,256]{2,1,0:T(8,128)(2,1)} %broadcast_in_dim.12), calls=%async_computation.2 | async-start | bytes 524288 | tf_op jit(solution)/shard_map/all_to_all | solution.py:21
  78.8 0.1 pad_add_fusion.2
  78.8 0.0 collective-permute-done.2.a3
  78.8 26.3 %all-gather.6.cloned.1.call-done = bf16[1,4096,256]{2,1,0:T(8,128)(2,1)} async-done(((bf16[1,512,256]{2,1,0:T(8,128)(2,1)}), bf16[1,4096,256]{2,1,0:T(8,128)(2,1)}) %all-gather.6.cloned.1.call-update) | async-done | bytes 2097168 | tf_op jit(solution)/shard_map/all_gather | solution.py:161
  105.2 0.0 collective-permute-done.a1.refs_1_
  105.2 4.9 %shard_map.68 = bf16[512,128]{1,0:T(8,128)(2,1)S(1)} custom-call(s32[4]{0:T(128)S(1)} %get-tuple-element.14.place, bf16[4,1024,256]{2,1,0:T(8,128)(2,1)S(1)} %all-to-all-done.a0.refs_0_, bf16[4,1024,256]{2,1,0:T(8,128)(2,1)} %collective-permute-done.a1.refs_1_, bf16[4,512,256]{2,1,0:T(8,128)(2,1)S(1)} %all_to_all.25.a2, ...), custom_call_target="tpu_custom_call" | custom-call | flops 536870912 | bytes 5242880 | tf_op jit(solution)/shard_map/pallas_call | solution.py:121
  110.1 1.0 broadcast_in_dim.13
  111.1 4.5 %all-to-all-start.3 = ((bf16[4,512,256]{2,1,0:T(8,128)(2,1)}), bf16[4,512,256]{2,1,0:T(8,128)(2,1)}, u32[]{:S(2)}, u32[]{:S(2)}) async-start(bf16[4,512,256]{2,1,0:T(8,128)(2,1)} %broadcast_in_dim.13), calls=%async_computation.3 | async-start | bytes 2097152 | tf_op jit(solution)/shard_map/all_to_all | solution.py:21
  115.6 4.9 %shard_map.69 = bf16[512,128]{1,0:T(8,128)(2,1)S(1)} custom-call(s32[4]{0:T(128)S(1)} %get-tuple-element.14.place, bf16[4,1024,256]{2,1,0:T(8,128)(2,1)S(1)} %all-to-all-done.a0.refs_0_, bf16[4,1024,256]{2,1,0:T(8,128)(2,1)} %collective-permute-done.a1.refs_1_, bf16[4,512,256]{2,1,0:T(8,128)(2,1)S(1)} %all_to_all.25.a2, ...), custom_call_target="tpu_custom_call" | custom-call | flops 536870912 | bytes 5242880 | tf_op jit(solution)/shard_map/pallas_call | solution.py:121
  120.6 0.7 pad_maximum_fusion.2
  121.3 0.0 all-gather.4.cloned.1.call-update
  121.3 5.3 %all-to-all-done.3.a2.refs_2_ = bf16[4,512,256]{2,1,0:T(8,128)(2,1)} async-done(((bf16[4,512,256]{2,1,0:T(8,128)(2,1)}), bf16[4,512,256]{2,1,0:T(8,128)(2,1)}, u32[]{:S(2)}, u32[]{:S(2)}) %all-to-all-start.3) | async-done | bytes 1048608 | tf_op jit(solution)/shard_map/all_to_all | solution.py:21
  126.7 1.9 collective-permute-start.3
  128.6 2.6 %collective-permute-start.4 = (bf16[512,128]{1,0:T(8,128)(2,1)S(1)}, bf16[512,128]{1,0:T(8,128)(2,1)S(1)}, u32[]{:S(2)}, u32[]{:S(2)}) collective-permute-start(bf16[512,128]{1,0:T(8,128)(2,1)S(1)} %shard_map.68), channel_id=1, source_target_pairs={{0,64},{16,80},{32,96},{48,112},{64,0},{80,16},{96,32},{112,48},{1... | collective-permute-start | bytes 393224 | tf_op jit(solution)/shard_map/ppermute | solution.py:32
  131.2 7.1 %collective-permute-start.8 = (bf16[512,128]{1,0:T(8,128)(2,1)S(1)}, bf16[512,128]{1,0:T(8,128)(2,1)}, u32[]{:S(2)}, u32[]{:S(2)}) collective-permute-start(bf16[512,128]{1,0:T(8,128)(2,1)S(1)} %shard_map.69), channel_id=1, source_target_pairs={{0,64},{16,80},{32,96},{48,112},{64,0},{80,16},{96,32},{112,48},{1... | collective-permute-start | bytes 393224 | tf_op jit(solution)/shard_map/ppermute | solution.py:32
  138.3 11.6 %collective-permute-done.4.refs_4_ = bf16[512,128]{1,0:T(8,128)(2,1)S(1)} collective-permute-done((bf16[512,128]{1,0:T(8,128)(2,1)S(1)}, bf16[512,128]{1,0:T(8,128)(2,1)S(1)}, u32[]{:S(2)}, u32[]{:S(2)}) %collective-permute-start.4) | collective-permute-done | bytes 131104 | tf_op jit(solution)/shard_map/ppermute | solution.py:32
  149.9 1.9 collective-permute-start.7
  151.8 7.2 %collective-permute-start.6 = (bf16[512,128]{1,0:T(8,128)(2,1)S(1)}, bf16[512,128]{1,0:T(8,128)(2,1)}, u32[]{:S(2)}, u32[]{:S(2)}) collective-permute-start(bf16[512,128]{1,0:T(8,128)(2,1)S(1)} %collective-permute-done.4.refs_4_), channel_id=1, source_target_pairs={{0,32},{16,48},{32,0},{48,16},{64,96},{80,112},{96,64},{112,80},{1... | collective-permute-start | bytes 393224 | tf_op jit(solution)/shard_map/ppermute | solution.py:27
  159.1 2.1 collective-permute-start.5
  161.2 0.0 collective-permute-done.8.refs_8_
  161.2 5.5 %collective-permute-start.11 = (bf16[512,128]{1,0:T(8,128)(2,1)}, bf16[512,128]{1,0:T(8,128)(2,1)S(1)}, u32[]{:S(2)}, u32[]{:S(2)}) collective-permute-start(bf16[512,128]{1,0:T(8,128)(2,1)} %collective-permute-done.8.refs_8_), channel_id=1, source_target_pairs={{0,48},{16,0},{32,16},{48,32},{64,112},{80,64},{96,80},{112,96},{1... | collective-permute-start | bytes 393224 | tf_op jit(solution)/shard_map/ppermute | solution.py:27
  166.7 0.0 collective-permute-done.7.refs_7_
  166.7 1.9 collective-permute-start.10
  168.7 0.0 collective-permute-done.3.a3.refs_3_
  168.7 2.5 %collective-permute-start.9 = (bf16[512,128]{1,0:T(8,128)(2,1)}, bf16[512,128]{1,0:T(8,128)(2,1)}, u32[]{:S(2)}, u32[]{:S(2)}) collective-permute-start(bf16[512,128]{1,0:T(8,128)(2,1)} %collective-permute-done.8.refs_8_), channel_id=1, source_target_pairs={{0,16},{16,32},{32,48},{48,0},{64,80},{80,96},{96,112},{112,64},{1... | collective-permute-start | bytes 393224 | tf_op jit(solution)/shard_map/ppermute | solution.py:27
  171.1 11.7 %all-gather.4.cloned.1.call-done.b_ref = bf16[2048,256]{1,0:T(8,128)(2,1)} async-done(((bf16[512,256]{1,0:T(8,128)(2,1)}), bf16[2048,256]{1,0:T(8,128)(2,1)}) %all-gather.4.cloned.1.call-update) | async-done | bytes 1048592 | tf_op jit(solution)/shard_map/all_gather | solution.py:176
  182.8 3.6 %shard_map.70.refs_12_ = f32[512,256]{1,0:T(8,128)S(1)} custom-call(s32[4]{0:T(128)S(1)} %get-tuple-element.12.place, bf16[4,1024,256]{2,1,0:T(8,128)(2,1)S(1)} %all-to-all-done.a0.refs_0_, bf16[4,1024,256]{2,1,0:T(8,128)(2,1)} %collective-permute-done.a1.refs_1_, bf16[4,512,256]{2,1,0:T(8,128)(2,1)} %all-to-all-done.3.a2.refs_2_, ...), custom_call_target="tpu_custom_call" | custom-call | flops 536870912 | bytes 3145728 | tf_op jit(solution)/shard_map/pallas_call | solution.py:121
  186.4 0.0 collective-permute-done.6.refs_6_
  186.5 0.0 collective-permute-done.5.refs_5_
  186.5 4.6 %collective-permute-done.10.refs_10_ = bf16[512,128]{1,0:T(8,128)(2,1)} collective-permute-done((bf16[512,128]{1,0:T(8,128)(2,1)}, bf16[512,128]{1,0:T(8,128)(2,1)}, u32[]{:S(2)}, u32[]{:S(2)}) %collective-permute-start.10) | collective-permute-done | bytes 131104 | tf_op jit(solution)/shard_map/ppermute | solution.py:27
  191.0 4.1 %update.1 = (f32[512,256]{1,0:T(8,128)}, bf16[512,256]{1,0:T(8,128)(2,1)S(1)}) custom-call(s32[4]{0:T(128)S(1)} %get-tuple-element.15.place, bf16[4,1024,256]{2,1,0:T(8,128)(2,1)S(1)} %all-to-all-done.a0.refs_0_, bf16[4,1024,256]{2,1,0:T(8,128)(2,1)} %collective-permute-done.a1.refs_1_, bf16[4,512,256]{2,1,0:T(8,128)(2,1)} %all-to-all-done.3.a2.refs_2_, ...), custom_call_target="tpu_custom_call" | custom-call | flops 536870912 | bytes 4980736 | tf_op jit(solution)/shard_map/update/pallas_call | solution.py:75
  195.2 10.5 %all_to_all.26 = bf16[4,128,256]{2,1,0:T(8,128)(2,1)S(1)} all-to-all(bf16[4,128,256]{2,1,0:T(8,128)(2,1)S(1)} %bitcast.14), channel_id=1, replica_groups=mesh['quarter'=4,'row'=8,'y'=4,'z_hi'=2,'core'=2] {'quarter'}, dimensions={0} | all-to-all | bytes 524288 | tf_op jit(solution)/shard_map/all_to_all | solution.py:189
  205.6 0.7 copy.8
  (13 shorter events, 0.1 us)
Async XLA Ops:
  7.2 98.0 %all-gather.6.cloned.1.call-start = ((), (), s32[]{:S(2)}) async-start(), calls=%async_computation.6 | async-start | bytes 2359296 | tf_op jit(solution)/shard_map/all_gather | solution.py:161
  10.4 10.3 %copy-start.2 = (bf16[1,512,256]{2,1,0:T(8,128)(2,1)S(1)}, bf16[1,512,256]{2,1,0:T(8,128)(2,1)}, u32[]{:S(2)}) copy-start(bf16[1,512,256]{2,1,0:T(8,128)(2,1)} %param.5) | copy-start | bytes 786436
  10.4 29.9 %all-to-all-start = ((bf16[4,1024,256]{2,1,0:T(8,128)(2,1)}), bf16[4,1024,256]{2,1,0:T(8,128)(2,1)S(1)}, u32[]{:S(2)}, u32[]{:S(2)}) async-start(bf16[4,1024,256]{2,1,0:T(8,128)(2,1)} %broadcast_in_dim.10), calls=%async_computation | async-start | bytes 4194304 | tf_op jit(solution)/shard_map/all_to_all | solution.py:21
  20.8 36.2 %collective-permute-start.1 = (bf16[640,256]{1,0:T(8,128)(2,1)S(1)}, bf16[640,256]{1,0:T(8,128)(2,1)S(1)}, u32[]{:S(2)}, u32[]{:S(2)}) collective-permute-start(bf16[640,256]{1,0:T(8,128)(2,1)S(1)} %pad_maximum_fusion.1), channel_id=1, source_target_pairs={{0,2},{2,0},{1,3},{3,1},{4,6},{6,4},{5,7},{7,5},{8,10},{10,8},{9,1... | collective-permute-start | bytes 983048 | tf_op jit(solution)/shard_map/ppermute | solution.py:163
  40.4 64.8 %collective-permute-start = (bf16[4,1024,256]{2,1,0:T(8,128)(2,1)S(1)}, bf16[4,1024,256]{2,1,0:T(8,128)(2,1)}, u32[]{:S(2)}, u32[]{:S(2)}) collective-permute-start(bf16[4,1024,256]{2,1,0:T(8,128)(2,1)S(1)} %all-to-all-done.a0.refs_0_), channel_id=1, source_target_pairs={{0,1},{1,0},{2,3},{3,2},{4,5},{5,4},{6,7},{7,6},{8,9},{9,8},{10,11... | collective-permute-start | bytes 6291464 | tf_op jit(solution)/shard_map/ppermute | solution.py:146
  71.8 7.1 %collective-permute-start.2 = (bf16[4,512,256]{2,1,0:T(8,128)(2,1)S(1)}, bf16[4,512,256]{2,1,0:T(8,128)(2,1)}, u32[]{:S(2)}, u32[]{:S(2)}) collective-permute-start(bf16[4,512,256]{2,1,0:T(8,128)(2,1)S(1)} %all_to_all.25.a2), channel_id=1, source_target_pairs={{0,1},{1,0},{2,3},{3,2},{4,5},{5,4},{6,7},{7,6},{8,9},{9,8},{10,11... | collective-permute-start | bytes 3145736 | tf_op jit(solution)/shard_map/ppermute | solution.py:146
  74.5 35.6 %all-to-all-start.2 = ((bf16[4,128,256]{2,1,0:T(8,128)(2,1)}), bf16[4,128,256]{2,1,0:T(8,128)(2,1)S(1)}, u32[]{:S(2)}, u32[]{:S(2)}) async-start(bf16[4,128,256]{2,1,0:T(8,128)(2,1)} %broadcast_in_dim.12), calls=%async_computation.2 | async-start | bytes 524288 | tf_op jit(solution)/shard_map/all_to_all | solution.py:21
  111.1 15.5 %all-to-all-start.3 = ((bf16[4,512,256]{2,1,0:T(8,128)(2,1)}), bf16[4,512,256]{2,1,0:T(8,128)(2,1)}, u32[]{:S(2)}, u32[]{:S(2)}) async-start(bf16[4,512,256]{2,1,0:T(8,128)(2,1)} %broadcast_in_dim.13), calls=%async_computation.3 | async-start | bytes 2097152 | tf_op jit(solution)/shard_map/all_to_all | solution.py:21
  115.6 67.2 %all-gather.4.cloned.1.call-start = ((), (), s32[]{:S(2)}) async-start(), calls=%async_computation.5 | async-start | bytes 1310720 | tf_op jit(solution)/shard_map/all_gather | solution.py:176
  126.7 42.0 %collective-permute-start.3 = (bf16[4,512,256]{2,1,0:T(8,128)(2,1)}, bf16[4,512,256]{2,1,0:T(8,128)(2,1)S(1)}, u32[]{:S(2)}, u32[]{:S(2)}) collective-permute-start(bf16[4,512,256]{2,1,0:T(8,128)(2,1)} %all-to-all-done.3.a2.refs_2_), channel_id=1, source_target_pairs={{0,1},{1,0},{2,3},{3,2},{4,5},{5,4},{6,7},{7,6},{8,9},{9,8},{10,11... | collective-permute-start | bytes 3145736 | tf_op jit(solution)/shard_map/ppermute | solution.py:146
  128.6 21.3 %collective-permute-start.4 = (bf16[512,128]{1,0:T(8,128)(2,1)S(1)}, bf16[512,128]{1,0:T(8,128)(2,1)S(1)}, u32[]{:S(2)}, u32[]{:S(2)}) collective-permute-start(bf16[512,128]{1,0:T(8,128)(2,1)S(1)} %shard_map.68), channel_id=1, source_target_pairs={{0,64},{16,80},{32,96},{48,112},{64,0},{80,16},{96,32},{112,48},{1... | collective-permute-start | bytes 393224 | tf_op jit(solution)/shard_map/ppermute | solution.py:32
  131.2 30.0 %collective-permute-start.8 = (bf16[512,128]{1,0:T(8,128)(2,1)S(1)}, bf16[512,128]{1,0:T(8,128)(2,1)}, u32[]{:S(2)}, u32[]{:S(2)}) collective-permute-start(bf16[512,128]{1,0:T(8,128)(2,1)S(1)} %shard_map.69), channel_id=1, source_target_pairs={{0,64},{16,80},{32,96},{48,112},{64,0},{80,16},{96,32},{112,48},{1... | collective-permute-start | bytes 393224 | tf_op jit(solution)/shard_map/ppermute | solution.py:32
  149.9 16.8 %collective-permute-start.7 = (bf16[512,128]{1,0:T(8,128)(2,1)S(1)}, bf16[512,128]{1,0:T(8,128)(2,1)S(1)}, u32[]{:S(2)}, u32[]{:S(2)}) collective-permute-start(bf16[512,128]{1,0:T(8,128)(2,1)S(1)} %collective-permute-done.4.refs_4_), channel_id=1, source_target_pairs={{0,48},{16,0},{32,16},{48,32},{64,112},{80,64},{96,80},{112,96},{1... | collective-permute-start | bytes 393224 | tf_op jit(solution)/shard_map/ppermute | solution.py:27
  151.8 34.6 %collective-permute-start.6 = (bf16[512,128]{1,0:T(8,128)(2,1)S(1)}, bf16[512,128]{1,0:T(8,128)(2,1)}, u32[]{:S(2)}, u32[]{:S(2)}) collective-permute-start(bf16[512,128]{1,0:T(8,128)(2,1)S(1)} %collective-permute-done.4.refs_4_), channel_id=1, source_target_pairs={{0,32},{16,48},{32,0},{48,16},{64,96},{80,112},{96,64},{112,80},{1... | collective-permute-start | bytes 393224 | tf_op jit(solution)/shard_map/ppermute | solution.py:27
  159.1 27.4 %collective-permute-start.5 = (bf16[512,128]{1,0:T(8,128)(2,1)S(1)}, bf16[512,128]{1,0:T(8,128)(2,1)}, u32[]{:S(2)}, u32[]{:S(2)}) collective-permute-start(bf16[512,128]{1,0:T(8,128)(2,1)S(1)} %collective-permute-done.4.refs_4_), channel_id=1, source_target_pairs={{0,16},{16,32},{32,48},{48,0},{64,80},{80,96},{96,112},{112,64},{1... | collective-permute-start | bytes 393224 | tf_op jit(solution)/shard_map/ppermute | solution.py:27
  161.2 25.3 %collective-permute-start.11 = (bf16[512,128]{1,0:T(8,128)(2,1)}, bf16[512,128]{1,0:T(8,128)(2,1)S(1)}, u32[]{:S(2)}, u32[]{:S(2)}) collective-permute-start(bf16[512,128]{1,0:T(8,128)(2,1)} %collective-permute-done.8.refs_8_), channel_id=1, source_target_pairs={{0,48},{16,0},{32,16},{48,32},{64,112},{80,64},{96,80},{112,96},{1... | collective-permute-start | bytes 393224 | tf_op jit(solution)/shard_map/ppermute | solution.py:27
  166.7 24.3 %collective-permute-start.10 = (bf16[512,128]{1,0:T(8,128)(2,1)}, bf16[512,128]{1,0:T(8,128)(2,1)}, u32[]{:S(2)}, u32[]{:S(2)}) collective-permute-start(bf16[512,128]{1,0:T(8,128)(2,1)} %collective-permute-done.8.refs_8_), channel_id=1, source_target_pairs={{0,32},{16,48},{32,0},{48,16},{64,96},{80,112},{96,64},{112,80},{1... | collective-permute-start | bytes 393224 | tf_op jit(solution)/shard_map/ppermute | solution.py:27
  168.7 22.4 %collective-permute-start.9 = (bf16[512,128]{1,0:T(8,128)(2,1)}, bf16[512,128]{1,0:T(8,128)(2,1)}, u32[]{:S(2)}, u32[]{:S(2)}) collective-permute-start(bf16[512,128]{1,0:T(8,128)(2,1)} %collective-permute-done.8.refs_8_), channel_id=1, source_target_pairs={{0,16},{16,32},{32,48},{48,0},{64,80},{80,96},{96,112},{112,64},{1... | collective-permute-start | bytes 393224 | tf_op jit(solution)/shard_map/ppermute | solution.py:27
  182.8 8.2 %copy-start = (f32[1,512,256]{2,1,0:T(8,128)S(1)}, f32[1,512,256]{2,1,0:T(8,128)}, u32[]{:S(2)}) copy-start(f32[1,512,256]{2,1,0:T(8,128)} %param.8) | copy-start | bytes 1572868
  182.8 8.2 %copy-start.1 = (bf16[1,512,256]{2,1,0:T(8,128)(2,1)S(1)}, bf16[1,512,256]{2,1,0:T(8,128)(2,1)}, u32[]{:S(2)}) copy-start(bf16[1,512,256]{2,1,0:T(8,128)(2,1)} %param.9) | copy-start | bytes 786436
Sparse Core Ops, SparseCore 0:
  10.0 95.0 all-gather.5
  121.4 61.3 all-gather.3

commit v7 on v6

--- a/solution.py
+++ b/solution.py
@@ -89,17 +89,20 @@
     )(place, *given)
 
 
-def mix_kernel(at_rows, place, a0, a1, a2, a3, b_ref, o_ref, acc_ref):
+def mix_kernel(at_rows, place, a0, a1, a2, a3, b_ref, o_ref, *refs):
     half, core = place[0], place[1]
     depth = a0.shape[-1]
-    at = place[3] + pl.program_id(0)
-    total = None
+    parts, acc_ref = refs[:-1], refs[-1]
+    lefts, rights = [], []
     for n, piece in enumerate((a0, a1, a2, a3)):
         first = 2 * (half if n < 2 else 1 - half) + (core if n % 2 == 0 else 1 - core)
-        rows = b_ref[pl.ds(pl.multiple_of(first * depth, depth), depth), :]
-        block = piece[at, at_rows[n] * 2 * depth : (at_rows[n] + 1) * 2 * depth, :]
-        part = jnp.dot(block, rows, preferred_element_type=jnp.float32)
-        total = part if total is None else total + part
+        rights.append(b_ref[pl.ds(pl.multiple_of(first * depth, depth), depth), :])
+        at = place[3] + pl.program_id(0) if piece.shape[0] > 1 else 0
+        start = at_rows[n] * 2 * depth if piece.shape[1] > 2 * depth else 0
+        lefts.append(piece[at, start : start + 2 * depth, :])
+    total = jnp.dot(
+        jnp.concatenate(lefts, axis=1), jnp.concatenate(rights, axis=0), preferred_element_type=jnp.float32
+    )
 
     @pl.when(pl.program_id(0) == 0)
     def _():
@@ -111,31 +114,42 @@
 
     @pl.when(pl.program_id(0) == pl.num_programs(0) - 1)
     def _():
-        o_ref[...] = acc_ref[...].astype(o_ref.dtype)
-
-
-def mix(place, pieces, at_rows, right, kind, first=0, columns=None):
+        done = acc_ref[...].astype(o_ref.dtype)
+        o_ref[...] = done
+        for n, part_ref in enumerate(parts):
+            width = part_ref.shape[1]
+            part_ref[...] = done[:, n * width : (n + 1) * width]
+
+
+def mix(place, pieces, at_rows, right, kind, split, streamed=()):
     depth = pieces[0].shape[-1]
-    columns = columns or right.shape[1]
+    columns = right.shape[1]
     steps, rows = right.shape[0] // (4 * depth), 2 * depth
+
+    def piece_spec(n):
+        if n in streamed:
+            return pl.BlockSpec((1, rows, depth), lambda i, place: (place[3] + i, at_rows[n], 0))
+        return pl.BlockSpec(memory_space=pltpu.MemorySpace.VMEM)
+
+    kept = [piece if n in streamed else in_vmem([piece])[0] for n, piece in enumerate(pieces)]
+    widths = [columns] + [columns // split] * split if split else [columns]
     return pl.pallas_call(
         functools.partial(mix_kernel, at_rows),
-        out_shape=jax.ShapeDtypeStruct((rows, columns), kind),
+        out_shape=[jax.ShapeDtypeStruct((rows, width), kind) for width in widths],
         grid_spec=pltpu.PrefetchScalarGridSpec(
             num_scalar_prefetch=1,
             grid=(steps,),
-            in_specs=[pl.BlockSpec(memory_space=pltpu.MemorySpace.VMEM)] * 4
-            + [pl.BlockSpec((4 * depth, columns), lambda i, place: (i, first))],
-            out_specs=pl.BlockSpec((rows, columns), lambda i, place: (0, 0)),
+            in_specs=[piece_spec(n) for n in range(4)] + [pl.BlockSpec((4 * depth, columns), lambda i, place: (i, 0))],
+            out_specs=[pl.BlockSpec((rows, width), lambda i, place: (0, 0)) for width in widths],
             scratch_shapes=[pltpu.VMEM((rows, columns), jnp.float32)],
         ),
         cost_estimate=pl.CostEstimate(
-            flops=2 * rows * right.shape[0] * columns,
-            bytes_accessed=2 * (4 * steps * rows * depth + right.shape[0] * columns),
+            flops=2 * rows * right.size,
+            bytes_accessed=2 * (4 * steps * rows * depth + right.size),
             transcendentals=0,
         ),
         compiler_params=pltpu.CompilerParams(vmem_limit_bytes=KERNEL_VMEM),
-    )(place, *in_vmem(pieces), pltpu.with_memory_space_constraint(right, pltpu.MemorySpace.HBM))
+    )(place, *kept, pltpu.with_memory_space_constraint(right, pltpu.MemorySpace.HBM))
 
 
 def in_vmem(values):
@@ -160,22 +174,19 @@
 
     right_panel = lax.all_gather(right_root, "row", axis=0, tiled=True)
     left_part = lax.dynamic_slice_in_dim(left_root, quarter * part, part, 0)
-    crossed = lax.ppermute(jnp.concatenate((grad, left_part)), "z_hi", SWAP)
+    cut = (rows + part) // 2
+    top = lax.ppermute(grad[:cut], "z_hi", SWAP)
+    bottom = lax.ppermute(jnp.concatenate((grad[cut:], left_part)), "z_hi", SWAP)
     mine = with_partner(copies_to_all(jnp.concatenate((grad, left_root)), "y"))
-    grad_theirs = copies_to_all(crossed[:rows], "y")
+    grad_theirs = copies_to_all(jnp.concatenate((top, bottom[: rows - cut])), "y")
     panel = mine + with_partner(grad_theirs)
-    _, left_part = lax.optimization_barrier((grad_theirs, crossed[rows:]))
+    _, left_part = lax.optimization_barrier((grad_theirs, bottom[rows - cut :]))
     left_other = copies_to_all(left_part, "quarter").reshape(rows, depth)
 
-    half_columns = depth // 2
-    parts = []
-    for n in range(2):
-        parts.append(mix(every, panel, (0, 0, 0, 0), right_panel, jnp.bfloat16, n, half_columns))
-    parts[0], left_other = lax.optimization_barrier((parts[0], left_other))
+    mixed, *parts = mix(every, panel, (0, 0, 0, 0), right_panel, jnp.bfloat16, 2)
+    mixed, parts, left_other = lax.optimization_barrier((mixed, parts, left_other))
     runs = [list(range(i, i + CUBE)) for i in range(0, lax.axis_size("row"), CUBE)]
-    near_panel = lax.all_gather(
-        jnp.concatenate(parts, axis=1), "row", axis=0, tiled=True, axis_index_groups=runs
-    )
+    near_panel = lax.all_gather(mixed, "row", axis=0, tiled=True, axis_index_groups=runs)
     others = []
     for piece in parts:
         others.append(across(piece))
@@ -184,7 +195,7 @@
     slots = []
     for piece in others:
         slots.append(far_slots(piece))
-    begun = mix(near, panel, (1, 1, 0, 0), near_panel, jnp.float32)
+    (begun,) = mix(near, panel, (1, 1, 0, 0), near_panel, jnp.float32, 0, (3,))
     renewed, updated = update(far, panel, (1, 1, 0, 0), *slots, begun, momentum[0], weights[0])
     spread = lax.all_to_all(updated.reshape(quarters, part, depth), "quarter", 0, 0, tiled=True)
     return renewed[None], spread

time: 214 us -> 212 us (level)
  the two profiles are of different devices: /device:TPU:8 before, /device:TPU:32 now
where the time goes in v7:
time: 212 us; the launch traced here: 211 us
  waiting for transfers between devices  79.6 us (38%)
  starting transfers between devices  69.5 us (33%)
  blocking collectives  26.6 us (13%)
  between operations  14.3 us (7%)
  Pallas kernels  13.2 us (6%)
  local copies, waits for them, and re-layouts  7.1 us (3%)
    ppermute x6, starting transfers between devices, turn(): return lax.ppermute(piece, 'row', pairs)  23.8 us
    all_to_all x3, waiting for transfers between devices, copies_to_all(): return lax.all_to_all(spread, axis, 0, 0, tiled=True)  19.9 us
    ppermute x2, waiting for transfers between devices, across(): return lax.ppermute(piece, 'row', [(i, i ^ CUBE) for i in range(rows)])  19.8 us
    ppermute x1, waiting for transfers between devices, per_device(): top = lax.ppermute(grad[:cut], 'z_hi', SWAP)  15.4 us
    all_to_all x1, blocking collectives, copies_to_all(): return lax.all_to_all(spread, axis, 0, 0, tiled=True)  15.2 us
    ppermute x1, starting transfers between devices, per_device(): lax.ppermute(jnp.concatenate((grad[cut:], left_part)), 'z_hi', SWAP)  14.8 us
    ppermute x1, waiting for transfers between devices, per_device(): lax.ppermute(jnp.concatenate((grad[cut:], left_part)), 'z_hi', SWAP)  13.6 us
    all_to_all x3, starting transfers between devices, copies_to_all(): return lax.all_to_all(spread, axis, 0, 0, tiled=True)  13.4 us
  transfers between devices with their start and end apart: 18, of which 8 were waited for; matrix products, arithmetic and copies ran while one was open for 1% of the time, Pallas kernels for 4%

profile of v7, /device:TPU:32, one launch (start us, length us, event | category | flops | bytes accessed | tf_op | source)
XLA Modules:
  0.0 211.4 jit_solution(12660007399185239468)
XLA Ops:
  7.2 1.1 pad_maximum_fusion
  8.2 1.5 broadcast_in_dim.10
  9.7 4.6 %all-to-all-start = ((bf16[4,1024,256]{2,1,0:T(8,128)(2,1)}), bf16[4,1024,256]{2,1,0:T(8,128)(2,1)S(1)}, u32[]{:S(2)}, u32[]{:S(2)}) async-start(bf16[4,1024,256]{2,1,0:T(8,128)(2,1)} %broadcast_in_dim.10), calls=%async_computation | async-start | bytes 4194304 | tf_op jit(solution)/shard_map/all_to_all | solution.py:21
  14.3 0.7 all-gather.6.cloned.1.call-update
  15.0 0.8 constant_dynamic-slice_fusion
  15.9 14.8 %collective-permute-start.2 = (bf16[320,256]{1,0:T(8,128)(2,1)S(1)}, bf16[320,256]{1,0:T(8,128)(2,1)S(1)}, u32[]{:S(2)}, u32[]{:S(2)}) collective-permute-start(bf16[320,256]{1,0:T(8,128)(2,1)S(1)} %pad_maximum_fusion.2), channel_id=1, source_target_pairs={{0,2},{2,0},{1,3},{3,1},{4,6},{6,4},{5,7},{7,5},{8,10},{10,8},{9,1... | collective-permute-start | bytes 491528 | tf_op jit(solution)/shard_map/ppermute | solution.py:179
  30.8 1.9 collective-permute-start.1
  32.7 7.9 %all-to-all-done.a0.refs_0_ = bf16[4,1024,256]{2,1,0:T(8,128)(2,1)S(1)} async-done(((bf16[4,1024,256]{2,1,0:T(8,128)(2,1)}), bf16[4,1024,256]{2,1,0:T(8,128)(2,1)S(1)}, u32[]{:S(2)}, u32[]{:S(2)}) %all-to-all-start) | async-done | bytes 2097184 | tf_op jit(solution)/shard_map/all_to_all | solution.py:21
  40.7 1.9 collective-permute-start
  42.6 13.6 %collective-permute-done.2 = bf16[320,256]{1,0:T(8,128)(2,1)S(1)} collective-permute-done((bf16[320,256]{1,0:T(8,128)(2,1)S(1)}, bf16[320,256]{1,0:T(8,128)(2,1)S(1)}, u32[]{:S(2)}, u32[]{:S(2)}) %collective-permute-start.2) | collective-permute-done | bytes 163872 | tf_op jit(solution)/shard_map/ppermute | solution.py:179
  56.2 15.4 %collective-permute-done.1 = bf16[320,256]{1,0:T(8,128)(2,1)S(1)} collective-permute-done((bf16[320,256]{1,0:T(8,128)(2,1)S(1)}, bf16[320,256]{1,0:T(8,128)(2,1)S(1)}, u32[]{:S(2)}, u32[]{:S(2)}) %collective-permute-start.1) | collective-permute-done | bytes 163872 | tf_op jit(solution)/shard_map/ppermute | solution.py:178
  71.5 0.1 broadcast_in_dim.11
  71.6 15.2 %all_to_all.25.a2 = bf16[4,512,256]{2,1,0:T(8,128)(2,1)S(1)} all-to-all(bf16[4,512,256]{2,1,0:T(8,128)(2,1)S(1)} %broadcast_in_dim.11), channel_id=1, replica_groups=mesh['quarter'=4,'row'=8,'y'=4,'z_hi'=2,'core'=2] {'y'}, dimensions={0} | all-to-all | bytes 2097152 | tf_op jit(solution)/shard_map/all_to_all | solution.py:21
  86.8 1.9 collective-permute-start.3
  88.8 0.1 pad_add_fusion.3
  88.8 0.7 broadcast_in_dim.12
  89.6 4.3 %all-to-all-start.2 = ((bf16[4,128,256]{2,1,0:T(8,128)(2,1)}), bf16[4,128,256]{2,1,0:T(8,128)(2,1)S(1)}, u32[]{:S(2)}, u32[]{:S(2)}) async-start(bf16[4,128,256]{2,1,0:T(8,128)(2,1)} %broadcast_in_dim.12), calls=%async_computation.2 | async-start | bytes 524288 | tf_op jit(solution)/shard_map/all_to_all | solution.py:21
  93.9 0.1 pad_add_fusion.2
  93.9 0.0 collective-permute-done.3.a3
  93.9 0.0 collective-permute-done.a1.refs_1_
  93.9 6.9 %all-gather.6.cloned.1.call-done = bf16[1,4096,256]{2,1,0:T(8,128)(2,1)} async-done(((bf16[1,512,256]{2,1,0:T(8,128)(2,1)}), bf16[1,4096,256]{2,1,0:T(8,128)(2,1)}) %all-gather.6.cloned.1.call-update) | async-done | bytes 2097168 | tf_op jit(solution)/shard_map/all_gather | solution.py:175
  100.8 6.0 %shard_map.68 = (bf16[512,256]{1,0:T(8,128)(2,1)}, bf16[512,128]{1,0:T(8,128)(2,1)S(1)}, bf16[512,128]{1,0:T(8,128)(2,1)}) custom-call(s32[4]{0:T(128)S(1)} %get-tuple-element.24.place, bf16[4,1024,256]{2,1,0:T(8,128)(2,1)S(1)} %all-to-all-done.a0.refs_0_, bf16[4,1024,256]{2,1,0:T(8,128)(2,1)} %collective-permute-done.a1.refs_1_, ...), custom_call_target="tpu_custom_call" | custom-call | flops 1073741824 | bytes 6291456 | tf_op jit(solution)/shard_map/pallas_call | solution.py:136
  106.8 0.0 all-to-all-done.2
  106.8 1.0 broadcast_in_dim.13
  107.8 4.5 %all-to-all-start.3 = ((bf16[4,512,256]{2,1,0:T(8,128)(2,1)}), bf16[4,512,256]{2,1,0:T(8,128)(2,1)S(1)}, u32[]{:S(2)}, u32[]{:S(2)}) async-start(bf16[4,512,256]{2,1,0:T(8,128)(2,1)} %broadcast_in_dim.13), calls=%async_computation.3 | async-start | bytes 2097152 | tf_op jit(solution)/shard_map/all_to_all | solution.py:21
  112.4 0.7 all-gather.4.cloned.1.call-update
  113.1 12.0 %all-to-all-done.3.a2.refs_2_ = bf16[4,512,256]{2,1,0:T(8,128)(2,1)S(1)} async-done(((bf16[4,512,256]{2,1,0:T(8,128)(2,1)}), bf16[4,512,256]{2,1,0:T(8,128)(2,1)S(1)}, u32[]{:S(2)}, u32[]{:S(2)}) %all-to-all-start.3) | async-done | bytes 1048608 | tf_op jit(solution)/shard_map/all_to_all | solution.py:21
  125.1 1.9 collective-permute-start.4
  127.0 3.6 %collective-permute-start.5 = (bf16[512,128]{1,0:T(8,128)(2,1)S(1)}, bf16[512,128]{1,0:T(8,128)(2,1)S(1)}, u32[]{:S(2)}, u32[]{:S(2)}) collective-permute-start(bf16[512,128]{1,0:T(8,128)(2,1)S(1)} %get-tuple-element.17), channel_id=1, source_target_pairs={{0,64},{16,80},{32,96},{48,112},{64,0},{80,16},{96,32},{112,48},{1... | collective-permute-start | bytes 393224 | tf_op jit(solution)/shard_map/ppermute | solution.py:32
  130.5 6.2 %collective-permute-start.9 = (bf16[512,128]{1,0:T(8,128)(2,1)}, bf16[512,128]{1,0:T(8,128)(2,1)S(1)}, u32[]{:S(2)}, u32[]{:S(2)}) collective-permute-start(bf16[512,128]{1,0:T(8,128)(2,1)} %get-tuple-element.18), channel_id=1, source_target_pairs={{0,64},{16,80},{32,96},{48,112},{64,0},{80,16},{96,32},{112,48},{1... | collective-permute-start | bytes 393224 | tf_op jit(solution)/shard_map/ppermute | solution.py:32
  136.7 19.4 %collective-permute-done.5.refs_4_ = bf16[512,128]{1,0:T(8,128)(2,1)S(1)} collective-permute-done((bf16[512,128]{1,0:T(8,128)(2,1)S(1)}, bf16[512,128]{1,0:T(8,128)(2,1)S(1)}, u32[]{:S(2)}, u32[]{:S(2)}) %collective-permute-start.5) | collective-permute-done | bytes 131104 | tf_op jit(solution)/shard_map/ppermute | solution.py:32
  156.2 1.9 collective-permute-start.6
  158.1 1.9 collective-permute-start.7
  160.0 3.9 %collective-permute-start.8 = (bf16[512,128]{1,0:T(8,128)(2,1)S(1)}, bf16[512,128]{1,0:T(8,128)(2,1)}, u32[]{:S(2)}, u32[]{:S(2)}) collective-permute-start(bf16[512,128]{1,0:T(8,128)(2,1)S(1)} %collective-permute-done.5.refs_4_), channel_id=1, source_target_pairs={{0,48},{16,0},{32,16},{48,32},{64,112},{80,64},{96,80},{112,96},{1... | collective-permute-start | bytes 393224 | tf_op jit(solution)/shard_map/ppermute | solution.py:27
  164.0 0.4 collective-permute-done.9.refs_8_
  164.3 3.0 %collective-permute-start.10 = (bf16[512,128]{1,0:T(8,128)(2,1)S(1)}, bf16[512,128]{1,0:T(8,128)(2,1)}, u32[]{:S(2)}, u32[]{:S(2)}) collective-permute-start(bf16[512,128]{1,0:T(8,128)(2,1)S(1)} %collective-permute-done.9.refs_8_), channel_id=1, source_target_pairs={{0,16},{16,32},{32,48},{48,0},{64,80},{80,96},{96,112},{112,64},{1... | collective-permute-start | bytes 393224 | tf_op jit(solution)/shard_map/ppermute | solution.py:27
  167.4 11.2 %collective-permute-start.11 = (bf16[512,128]{1,0:T(8,128)(2,1)S(1)}, bf16[512,128]{1,0:T(8,128)(2,1)}, u32[]{:S(2)}, u32[]{:S(2)}) collective-permute-start(bf16[512,128]{1,0:T(8,128)(2,1)S(1)} %collective-permute-done.9.refs_8_), channel_id=1, source_target_pairs={{0,32},{16,48},{32,0},{48,16},{64,96},{80,112},{96,64},{112,80},{1... | collective-permute-start | bytes 393224 | tf_op jit(solution)/shard_map/ppermute | solution.py:27
  178.5 1.0 copy-done
  179.5 1.9 collective-permute-start.12
  181.4 0.0 all-gather.4.cloned.1.call-done.b_ref
  181.5 1.2 copy-done.1
  182.7 3.4 %shard_map.69.refs_12_ = f32[512,256]{1,0:T(8,128)S(1)} custom-call(s32[4]{0:T(128)S(1)} %get-tuple-element.22.place, bf16[4,1024,256]{2,1,0:T(8,128)(2,1)S(1)} %all-to-all-done.a0.refs_0_, bf16[4,1024,256]{2,1,0:T(8,128)(2,1)} %collective-permute-done.a1.refs_1_, bf16[4,512,256]{2,1,0:T(8,128)(2,1)S(1)} %all-to-all-done.3.a2.refs_2_, ...), custom_call_target="tpu_custom_call" | custom-call | flops 536870912 | bytes 3145728 | tf_op jit(solution)/shard_map/pallas_call | solution.py:136
  186.1 0.0 collective-permute-done.7.refs_6_
  186.1 0.0 collective-permute-done.8.refs_7_
  186.1 2.6 %collective-permute-done.12.refs_11_ = bf16[512,128]{1,0:T(8,128)(2,1)} collective-permute-done((bf16[512,128]{1,0:T(8,128)(2,1)S(1)}, bf16[512,128]{1,0:T(8,128)(2,1)}, u32[]{:S(2)}, u32[]{:S(2)}) %collective-permute-start.12) | collective-permute-done | bytes 131104 | tf_op jit(solution)/shard_map/ppermute | solution.py:27
  188.7 3.8 %update.1 = (f32[512,256]{1,0:T(8,128)}, bf16[512,256]{1,0:T(8,128)(2,1)S(1)}) custom-call(s32[4]{0:T(128)S(1)} %get-tuple-element.25.place, bf16[4,1024,256]{2,1,0:T(8,128)(2,1)S(1)} %all-to-all-done.a0.refs_0_, bf16[4,1024,256]{2,1,0:T(8,128)(2,1)} %collective-permute-done.a1.refs_1_, bf16[4,512,256]{2,1,0:T(8,128)(2,1)S(1)} %all-to-all-done.3.a2.refs_2_, ...), custom_call_target="tpu_custom_call" | custom-call | flops 536870912 | bytes 4980736 | tf_op jit(solution)/shard_map/update/pallas_call | solution.py:75
  192.5 11.4 %all_to_all.26 = bf16[4,128,256]{2,1,0:T(8,128)(2,1)S(1)} all-to-all(bf16[4,128,256]{2,1,0:T(8,128)(2,1)S(1)} %bitcast.18), channel_id=1, replica_groups=mesh['quarter'=4,'row'=8,'y'=4,'z_hi'=2,'core'=2] {'quarter'}, dimensions={0} | all-to-all | bytes 524288 | tf_op jit(solution)/shard_map/all_to_all | solution.py:200
  203.9 0.7 copy.8
  (20 shorter events, 0.1 us)
Async XLA Ops:
  9.7 6.2 %copy-start.4 = (bf16[1,512,256]{2,1,0:T(8,128)(2,1)S(1)}, bf16[1,512,256]{2,1,0:T(8,128)(2,1)}, u32[]{:S(2)}) copy-start(bf16[1,512,256]{2,1,0:T(8,128)(2,1)} %param.5) | copy-start | bytes 786436
  9.7 30.9 %all-to-all-start = ((bf16[4,1024,256]{2,1,0:T(8,128)(2,1)}), bf16[4,1024,256]{2,1,0:T(8,128)(2,1)S(1)}, u32[]{:S(2)}, u32[]{:S(2)}) async-start(bf16[4,1024,256]{2,1,0:T(8,128)(2,1)} %broadcast_in_dim.10), calls=%async_computation | async-start | bytes 4194304 | tf_op jit(solution)/shard_map/all_to_all | solution.py:21
  14.3 86.5 %all-gather.6.cloned.1.call-start = ((), (), s32[]{:S(2)}) async-start(), calls=%async_computation.6 | async-start | bytes 2359296 | tf_op jit(solution)/shard_map/all_gather | solution.py:175
  15.9 40.2 %collective-permute-start.2 = (bf16[320,256]{1,0:T(8,128)(2,1)S(1)}, bf16[320,256]{1,0:T(8,128)(2,1)S(1)}, u32[]{:S(2)}, u32[]{:S(2)}) collective-permute-start(bf16[320,256]{1,0:T(8,128)(2,1)S(1)} %pad_maximum_fusion.2), channel_id=1, source_target_pairs={{0,2},{2,0},{1,3},{3,1},{4,6},{6,4},{5,7},{7,5},{8,10},{10,8},{9,1... | collective-permute-start | bytes 491528 | tf_op jit(solution)/shard_map/ppermute | solution.py:179
  30.8 40.7 %collective-permute-start.1 = (bf16[320,256]{1,0:T(8,128)(2,1)S(1)}, bf16[320,256]{1,0:T(8,128)(2,1)S(1)}, u32[]{:S(2)}, u32[]{:S(2)}) collective-permute-start(bf16[320,256]{1,0:T(8,128)(2,1)S(1)} %slice_bitcast_fusion), channel_id=1, source_target_pairs={{0,2},{2,0},{1,3},{3,1},{4,6},{6,4},{5,7},{7,5},{8,10},{10,8},{9,1... | collective-permute-start | bytes 491528 | tf_op jit(solution)/shard_map/ppermute | solution.py:178
  40.7 53.3 %collective-permute-start = (bf16[4,1024,256]{2,1,0:T(8,128)(2,1)S(1)}, bf16[4,1024,256]{2,1,0:T(8,128)(2,1)}, u32[]{:S(2)}, u32[]{:S(2)}) collective-permute-start(bf16[4,1024,256]{2,1,0:T(8,128)(2,1)S(1)} %all-to-all-done.a0.refs_0_), channel_id=1, source_target_pairs={{0,1},{1,0},{2,3},{3,2},{4,5},{5,4},{6,7},{7,6},{8,9},{9,8},{10,11... | collective-permute-start | bytes 6291464 | tf_op jit(solution)/shard_map/ppermute | solution.py:160
  86.8 7.1 %collective-permute-start.3 = (bf16[4,512,256]{2,1,0:T(8,128)(2,1)S(1)}, bf16[4,512,256]{2,1,0:T(8,128)(2,1)}, u32[]{:S(2)}, u32[]{:S(2)}) collective-permute-start(bf16[4,512,256]{2,1,0:T(8,128)(2,1)S(1)} %all_to_all.25.a2), channel_id=1, source_target_pairs={{0,1},{1,0},{2,3},{3,2},{4,5},{5,4},{6,7},{7,6},{8,9},{9,8},{10,11... | collective-permute-start | bytes 3145736 | tf_op jit(solution)/shard_map/ppermute | solution.py:160
  89.6 17.2 %all-to-all-start.2 = ((bf16[4,128,256]{2,1,0:T(8,128)(2,1)}), bf16[4,128,256]{2,1,0:T(8,128)(2,1)S(1)}, u32[]{:S(2)}, u32[]{:S(2)}) async-start(bf16[4,128,256]{2,1,0:T(8,128)(2,1)} %broadcast_in_dim.12), calls=%async_computation.2 | async-start | bytes 524288 | tf_op jit(solution)/shard_map/all_to_all | solution.py:21
  107.8 17.2 %all-to-all-start.3 = ((bf16[4,512,256]{2,1,0:T(8,128)(2,1)}), bf16[4,512,256]{2,1,0:T(8,128)(2,1)S(1)}, u32[]{:S(2)}, u32[]{:S(2)}) async-start(bf16[4,512,256]{2,1,0:T(8,128)(2,1)} %broadcast_in_dim.13), calls=%async_computation.3 | async-start | bytes 2097152 | tf_op jit(solution)/shard_map/all_to_all | solution.py:21
  112.4 69.1 %all-gather.4.cloned.1.call-start = ((), (), s32[]{:S(2)}) async-start(), calls=%async_computation.5 | async-start | bytes 1310720 | tf_op jit(solution)/shard_map/all_gather | solution.py:189
  125.1 53.5 %collective-permute-start.4 = (bf16[4,512,256]{2,1,0:T(8,128)(2,1)S(1)}, bf16[4,512,256]{2,1,0:T(8,128)(2,1)S(1)}, u32[]{:S(2)}, u32[]{:S(2)}) collective-permute-start(bf16[4,512,256]{2,1,0:T(8,128)(2,1)S(1)} %all-to-all-done.3.a2.refs_2_), channel_id=1, source_target_pairs={{0,1},{1,0},{2,3},{3,2},{4,5},{5,4},{6,7},{7,6},{8,9},{9,8},{10,11... | collective-permute-start | bytes 3145736 | tf_op jit(solution)/shard_map/ppermute | solution.py:160
  127.0 29.2 %collective-permute-start.5 = (bf16[512,128]{1,0:T(8,128)(2,1)S(1)}, bf16[512,128]{1,0:T(8,128)(2,1)S(1)}, u32[]{:S(2)}, u32[]{:S(2)}) collective-permute-start(bf16[512,128]{1,0:T(8,128)(2,1)S(1)} %get-tuple-element.17), channel_id=1, source_target_pairs={{0,64},{16,80},{32,96},{48,112},{64,0},{80,16},{96,32},{112,48},{1... | collective-permute-start | bytes 393224 | tf_op jit(solution)/shard_map/ppermute | solution.py:32
  130.5 33.8 %collective-permute-start.9 = (bf16[512,128]{1,0:T(8,128)(2,1)}, bf16[512,128]{1,0:T(8,128)(2,1)S(1)}, u32[]{:S(2)}, u32[]{:S(2)}) collective-permute-start(bf16[512,128]{1,0:T(8,128)(2,1)} %get-tuple-element.18), channel_id=1, source_target_pairs={{0,64},{16,80},{32,96},{48,112},{64,0},{80,16},{96,32},{112,48},{1... | collective-permute-start | bytes 393224 | tf_op jit(solution)/shard_map/ppermute | solution.py:32
  156.2 11.2 %collective-permute-start.6 = (bf16[512,128]{1,0:T(8,128)(2,1)S(1)}, bf16[512,128]{1,0:T(8,128)(2,1)S(1)}, u32[]{:S(2)}, u32[]{:S(2)}) collective-permute-start(bf16[512,128]{1,0:T(8,128)(2,1)S(1)} %collective-permute-done.5.refs_4_), channel_id=1, source_target_pairs={{0,16},{16,32},{32,48},{48,0},{64,80},{80,96},{96,112},{112,64},{1... | collective-permute-start | bytes 393224 | tf_op jit(solution)/shard_map/ppermute | solution.py:27
  158.1 28.0 %collective-permute-start.7 = (bf16[512,128]{1,0:T(8,128)(2,1)S(1)}, bf16[512,128]{1,0:T(8,128)(2,1)}, u32[]{:S(2)}, u32[]{:S(2)}) collective-permute-start(bf16[512,128]{1,0:T(8,128)(2,1)S(1)} %collective-permute-done.5.refs_4_), channel_id=1, source_target_pairs={{0,32},{16,48},{32,0},{48,16},{64,96},{80,112},{96,64},{112,80},{1... | collective-permute-start | bytes 393224 | tf_op jit(solution)/shard_map/ppermute | solution.py:27
  160.0 26.0 %collective-permute-start.8 = (bf16[512,128]{1,0:T(8,128)(2,1)S(1)}, bf16[512,128]{1,0:T(8,128)(2,1)}, u32[]{:S(2)}, u32[]{:S(2)}) collective-permute-start(bf16[512,128]{1,0:T(8,128)(2,1)S(1)} %collective-permute-done.5.refs_4_), channel_id=1, source_target_pairs={{0,48},{16,0},{32,16},{48,32},{64,112},{80,64},{96,80},{112,96},{1... | collective-permute-start | bytes 393224 | tf_op jit(solution)/shard_map/ppermute | solution.py:27
  164.3 21.8 %collective-permute-start.10 = (bf16[512,128]{1,0:T(8,128)(2,1)S(1)}, bf16[512,128]{1,0:T(8,128)(2,1)}, u32[]{:S(2)}, u32[]{:S(2)}) collective-permute-start(bf16[512,128]{1,0:T(8,128)(2,1)S(1)} %collective-permute-done.9.refs_8_), channel_id=1, source_target_pairs={{0,16},{16,32},{32,48},{48,0},{64,80},{80,96},{96,112},{112,64},{1... | collective-permute-start | bytes 393224 | tf_op jit(solution)/shard_map/ppermute | solution.py:27
  167.4 18.7 %collective-permute-start.11 = (bf16[512,128]{1,0:T(8,128)(2,1)S(1)}, bf16[512,128]{1,0:T(8,128)(2,1)}, u32[]{:S(2)}, u32[]{:S(2)}) collective-permute-start(bf16[512,128]{1,0:T(8,128)(2,1)S(1)} %collective-permute-done.9.refs_8_), channel_id=1, source_target_pairs={{0,32},{16,48},{32,0},{48,16},{64,96},{80,112},{96,64},{112,80},{1... | collective-permute-start | bytes 393224 | tf_op jit(solution)/shard_map/ppermute | solution.py:27
  178.5 1.0 copy-start
  179.5 9.2 %collective-permute-start.12 = (bf16[512,128]{1,0:T(8,128)(2,1)S(1)}, bf16[512,128]{1,0:T(8,128)(2,1)}, u32[]{:S(2)}, u32[]{:S(2)}) collective-permute-start(bf16[512,128]{1,0:T(8,128)(2,1)S(1)} %collective-permute-done.9.refs_8_), channel_id=1, source_target_pairs={{0,48},{16,0},{32,16},{48,32},{64,112},{80,64},{96,80},{112,96},{1... | collective-permute-start | bytes 393224 | tf_op jit(solution)/shard_map/ppermute | solution.py:27
  181.4 1.2 copy-start.1
  182.7 6.0 %copy-start.2 = (f32[1,512,256]{2,1,0:T(8,128)S(1)}, f32[1,512,256]{2,1,0:T(8,128)}, u32[]{:S(2)}) copy-start(f32[1,512,256]{2,1,0:T(8,128)} %param.8) | copy-start | bytes 1572868
  182.7 6.0 %copy-start.3 = (bf16[1,512,256]{2,1,0:T(8,128)(2,1)S(1)}, bf16[1,512,256]{2,1,0:T(8,128)(2,1)}, u32[]{:S(2)}) copy-start(bf16[1,512,256]{2,1,0:T(8,128)(2,1)} %param.9) | copy-start | bytes 786436
Sparse Core Ops, SparseCore 0:
  17.2 83.5 all-gather.5
  115.8 56.3 all-gather.3

commit v8 on v6

--- a/solution.py
+++ b/solution.py
@@ -21,6 +21,13 @@
     return lax.all_to_all(spread, axis, 0, 0, tiled=True)
 
 
+def y_slots(piece):
+    n = lax.axis_size("y")
+    return jnp.stack(
+        [piece] + [lax.ppermute(piece, "y", [(i, (i + by) % n) for i in range(n)]) for by in range(1, n)]
+    )
+
+
 def turn(piece, by):
     rows = lax.axis_size("row")
     pairs = [(i, i // CUBE * CUBE + (i + by) % CUBE) for i in range(rows)]
@@ -32,8 +39,17 @@
     return lax.ppermute(piece, "row", [(i, i ^ CUBE) for i in range(rows)])
 
 
-def far_slots(piece):
+def cube_slots(piece):
     return [piece] + [turn(piece, by) for by in range(1, CUBE)]
+
+
+def line_slots(piece):
+    rows = lax.axis_size("row")
+    up, down = [piece], [piece]
+    for _ in range(1, rows):
+        up.append(lax.ppermute(up[-1], "row", [(i, i + 1) for i in range(rows - 1)]))
+        down.append(lax.ppermute(down[-1], "row", [(i + 1, i) for i in range(rows - 1)]))
+    return up + down[1:]
 
 
 def accumulate(place, step, pieces, at_rows, slots):
@@ -50,6 +66,8 @@
         rows = jnp.where(odd == n // 2, even, other)
         back = 2 * step + (odd if n < 2 else 1 - odd)
         at = place[3] + (turned + 2 * CUBE - back) % CUBE // 2
+        if n < 2:
+            at = (place[4] + CUBE - at) % CUBE
         block = piece[at, at_rows[n] * 2 * depth : (at_rows[n] + 1) * 2 * depth, :]
         part = jnp.dot(block, rows, preferred_element_type=jnp.float32)
         total = part if total is None else total + part
@@ -89,53 +107,93 @@
     )(place, *given)
 
 
-def mix_kernel(at_rows, place, a0, a1, a2, a3, b_ref, o_ref, acc_ref):
-    half, core = place[0], place[1]
-    depth = a0.shape[-1]
-    at = place[3] + pl.program_id(0)
+def mix_kernel(n_rows, place, *refs):
+    pieces, slots, outs, panel_ref, sems = refs[:4], refs[4 : 3 + 2 * n_rows], refs[3 + 2 * n_rows : -2], refs[-2], refs[-1]
+    half, core, row, y = place[0], place[1], place[2], place[3]
+    depth = pieces[0].shape[-1]
+    rows = 2 * depth
+    for back in range(n_rows):
+
+        @pl.when(row >= back)
+        def _():
+            pltpu.make_async_copy(slots[back], panel_ref.at[back], sems.at[back]).start()
+
+        if back:
+
+            @pl.when(row < back)
+            def _():
+                source = slots[2 * n_rows - 1 - back]
+                pltpu.make_async_copy(source, panel_ref.at[back], sems.at[back]).start()
+
     total = None
-    for n, piece in enumerate((a0, a1, a2, a3)):
-        first = 2 * (half if n < 2 else 1 - half) + (core if n % 2 == 0 else 1 - core)
-        rows = b_ref[pl.ds(pl.multiple_of(first * depth, depth), depth), :]
-        block = piece[at, at_rows[n] * 2 * depth : (at_rows[n] + 1) * 2 * depth, :]
-        part = jnp.dot(block, rows, preferred_element_type=jnp.float32)
+    for back in range(n_rows):
+        pltpu.make_async_copy(slots[back], panel_ref.at[back], sems.at[back]).wait()
+        at = (row + n_rows - back) % n_rows
+        theirs = (at + half) % 2 == 1
+        turned = (y + CUBE - at // 2) % CUBE
+        lefts, rights = [], []
+        for n in range(2):
+            first = pl.multiple_of(depth * (core if n == 0 else 1 - core), depth)
+            lefts.append(jnp.where(theirs, pieces[2 + n][turned, :rows, :], pieces[n][turned, :rows, :]))
+            rights.append(panel_ref[back, pl.ds(first, depth), :])
+        part = jnp.dot(
+            jnp.concatenate(lefts, axis=1), jnp.concatenate(rights, axis=0), preferred_element_type=jnp.float32
+        )
         total = part if total is None else total + part
-
-    @pl.when(pl.program_id(0) == 0)
-    def _():
-        acc_ref[...] = total
-
-    @pl.when(pl.program_id(0) > 0)
-    def _():
-        acc_ref[...] += total
-
-    @pl.when(pl.program_id(0) == pl.num_programs(0) - 1)
-    def _():
-        o_ref[...] = acc_ref[...].astype(o_ref.dtype)
-
-
-def mix(place, pieces, at_rows, right, kind, first=0, columns=None):
-    depth = pieces[0].shape[-1]
-    columns = columns or right.shape[1]
-    steps, rows = right.shape[0] // (4 * depth), 2 * depth
+    done = total.astype(outs[0].dtype)
+    outs[0][...] = done
+    for n, part_ref in enumerate(outs[1:]):
+        width = part_ref.shape[1]
+        part_ref[...] = done[:, n * width : (n + 1) * width]
+
+
+def mix(place, pieces, slots):
+    n_rows = (len(slots) + 1) // 2
+    rows, columns = slots[0].shape
+    widths = (columns, columns // 2, columns // 2)
+    kept = [pltpu.with_memory_space_constraint(slot, pltpu.MemorySpace.HBM) for slot in slots]
     return pl.pallas_call(
-        functools.partial(mix_kernel, at_rows),
-        out_shape=jax.ShapeDtypeStruct((rows, columns), kind),
+        functools.partial(mix_kernel, n_rows),
+        out_shape=[jax.ShapeDtypeStruct((rows, width), jnp.bfloat16) for width in widths],
         grid_spec=pltpu.PrefetchScalarGridSpec(
             num_scalar_prefetch=1,
-            grid=(steps,),
+            grid=(1,),
             in_specs=[pl.BlockSpec(memory_space=pltpu.MemorySpace.VMEM)] * 4
-            + [pl.BlockSpec((4 * depth, columns), lambda i, place: (i, first))],
-            out_specs=pl.BlockSpec((rows, columns), lambda i, place: (0, 0)),
-            scratch_shapes=[pltpu.VMEM((rows, columns), jnp.float32)],
+            + [pl.BlockSpec(memory_space=pl.ANY)] * len(slots),
+            out_specs=[pl.BlockSpec((rows, width), lambda i, place: (0, 0)) for width in widths],
+            scratch_shapes=[pltpu.VMEM((n_rows, rows, columns), jnp.bfloat16), pltpu.SemaphoreType.DMA((n_rows,))],
         ),
         cost_estimate=pl.CostEstimate(
-            flops=2 * rows * right.shape[0] * columns,
-            bytes_accessed=2 * (4 * steps * rows * depth + right.shape[0] * columns),
-            transcendentals=0,
+            flops=2 * n_rows * rows * rows * columns, bytes_accessed=2 * n_rows * rows * columns, transcendentals=0
         ),
         compiler_params=pltpu.CompilerParams(vmem_limit_bytes=KERNEL_VMEM),
-    )(place, *in_vmem(pieces), pltpu.with_memory_space_constraint(right, pltpu.MemorySpace.HBM))
+        name="mix",
+    )(place, *in_vmem(pieces), *kept)
+
+
+def near_kernel(at_rows, place, *refs):
+    pieces, slots, o_ref = refs[:4], [(slot,) for slot in refs[4:-1]], refs[-1]
+    total = None
+    for step in range(CUBE // 2):
+        part = accumulate(place, step, pieces, at_rows, slots)
+        total = part if total is None else total + part
+    o_ref[...] = total
+
+
+def call(body, place, given, widths, kind, flops):
+    rows = given[-1].shape[0]
+    return pl.pallas_call(
+        body,
+        out_shape=[jax.ShapeDtypeStruct((rows, width), kind) for width in widths],
+        grid_spec=pltpu.PrefetchScalarGridSpec(
+            num_scalar_prefetch=1,
+            grid=(1,),
+            in_specs=[pl.BlockSpec(memory_space=pltpu.MemorySpace.VMEM)] * len(given),
+            out_specs=[pl.BlockSpec((rows, width), lambda i, place: (0, 0)) for width in widths],
+        ),
+        cost_estimate=pl.CostEstimate(flops=flops, bytes_accessed=4 * rows * sum(widths), transcendentals=0),
+        compiler_params=pltpu.CompilerParams(vmem_limit_bytes=KERNEL_VMEM),
+    )(place, *in_vmem(given))
 
 
 def in_vmem(values):
@@ -149,42 +207,41 @@
 def per_device(grad, left_root, right_root, momentum, weights):
     half, core, row = (lax.axis_index(a).astype(jnp.int32) for a in ("z_hi", "core", "row"))
     upper = row // CUBE
-    every = jnp.stack((half, core, row % CUBE, 0 * upper))
-    near = jnp.stack((half, core, row % CUBE, 2 * upper))
-    far = jnp.stack((half, core, row % CUBE, 2 - 2 * upper))
+    y = lax.axis_index("y").astype(jnp.int32)
+    line = jnp.stack((half, core, row, y))
+    near = jnp.stack((half, core, row % CUBE, 2 * upper, y))
+    far = jnp.stack((half, core, row % CUBE, 2 - 2 * upper, y))
     quarter = lax.axis_index("quarter")
     quarters = lax.axis_size("quarter")
     rows, depth = left_root.shape
     part = rows // quarters
     grad, right_root = grad[0], right_root[0]
 
-    right_panel = lax.all_gather(right_root, "row", axis=0, tiled=True)
+    right_slots = line_slots(right_root)
     left_part = lax.dynamic_slice_in_dim(left_root, quarter * part, part, 0)
     crossed = lax.ppermute(jnp.concatenate((grad, left_part)), "z_hi", SWAP)
-    mine = with_partner(copies_to_all(jnp.concatenate((grad, left_root)), "y"))
-    grad_theirs = copies_to_all(crossed[:rows], "y")
+    mine = y_slots(jnp.concatenate((grad, left_root)))
+    mine = with_partner(mine)
+    grad_theirs = y_slots(crossed[:rows])
     panel = mine + with_partner(grad_theirs)
     _, left_part = lax.optimization_barrier((grad_theirs, crossed[rows:]))
     left_other = copies_to_all(left_part, "quarter").reshape(rows, depth)
 
-    half_columns = depth // 2
-    parts = []
-    for n in range(2):
-        parts.append(mix(every, panel, (0, 0, 0, 0), right_panel, jnp.bfloat16, n, half_columns))
-    parts[0], left_other = lax.optimization_barrier((parts[0], left_other))
-    runs = [list(range(i, i + CUBE)) for i in range(0, lax.axis_size("row"), CUBE)]
-    near_panel = lax.all_gather(
-        jnp.concatenate(parts, axis=1), "row", axis=0, tiled=True, axis_index_groups=runs
-    )
+    flops = 2 * rows * rows * CUBE * depth
+    mixed, *parts = mix(line, panel, right_slots)
+    mixed, parts, left_other = lax.optimization_barrier((mixed, parts, left_other))
     others = []
     for piece in parts:
         others.append(across(piece))
+    near_slots = cube_slots(mixed)
     left_theirs = copies_to_all(left_other, "y")
     panel = mine + with_partner(left_theirs)
     slots = []
     for piece in others:
-        slots.append(far_slots(piece))
-    begun = mix(near, panel, (1, 1, 0, 0), near_panel, jnp.float32)
+        slots.append(cube_slots(piece))
+    (begun,) = call(
+        functools.partial(near_kernel, (1, 1, 0, 0)), near, panel + near_slots, (depth,), jnp.float32, flops
+    )
     renewed, updated = update(far, panel, (1, 1, 0, 0), *slots, begun, momentum[0], weights[0])
     spread = lax.all_to_all(updated.reshape(quarters, part, depth), "quarter", 0, 0, tiled=True)
     return renewed[None], spread

time: 214 us -> 252 us (1.18)
  the two profiles are of different devices: /device:TPU:8 before, /device:TPU:32 now
where the time goes in v8:
time: 252 us; the launch traced here: 250 us
  starting transfers between devices  134 us (53%)
  waiting for transfers between devices  57 us (23%)
  blocking collectives  27.4 us (11%)
  local copies, waits for them, and re-layouts  13.6 us (5%)
  Pallas kernels  12.9 us (5%)
  other arithmetic  3.79 us (2%)
    ppermute x7, waiting for transfers between devices, line_slots(): lax.ppermute(down[-1], 'row', [(i + 1, i) for i in range(rows - 1)])  33.5 us
    ppermute x9, starting transfers between devices, turn(): return lax.ppermute(piece, 'row', pairs)  29.8 us
    ppermute x7, starting transfers between devices, line_slots(): lax.ppermute(up[-1], 'row', [(i, i + 1) for i in range(rows - 1)])  23.1 us
    ppermute x2, waiting for transfers between devices, across(): return lax.ppermute(piece, 'row', [(i, i ^ CUBE) for i in range(rows)])  21.6 us
    ppermute x6, starting transfers between devices, y_slots(): lax.ppermute(piece, 'y', [(i, (i + by) % n) for i in range(n)])  21.1 us
    ppermute x7, starting transfers between devices, line_slots(): lax.ppermute(down[-1], 'row', [(i + 1, i) for i in range(rows - 1)])  19.3 us
    all_to_all x1, blocking collectives, copies_to_all(): return lax.all_to_all(spread, axis, 0, 0, tiled=True)  16.5 us
    ppermute x2, starting transfers between devices, across(): return lax.ppermute(piece, 'row', [(i, i ^ CUBE) for i in range(rows)])  16 us
  transfers between devices with their start and end apart: 36, of which 10 were waited for; matrix products, arithmetic and copies ran while one was open for 2% of the time, Pallas kernels for 4%

profile of v8, /device:TPU:32, one launch (start us, length us, event | category | flops | bytes accessed | tf_op | source)
XLA Modules:
  0.0 250.3 jit_solution(1554516717539664330)
XLA Ops:
  1.7 5.1 %collective-permute-start.1 = (bf16[1024,256]{1,0:T(8,128)(2,1)S(1)}, bf16[1024,256]{1,0:T(8,128)(2,1)S(1)}, u32[]{:S(2)}, u32[]{:S(2)}) collective-permute-start(bf16[1024,256]{1,0:T(8,128)(2,1)S(1)} %get-tuple-element.23), channel_id=1, source_target_pairs={{0,8},{4,12},{8,0},{12,4},{1,9},{5,13},{9,1},{13,5},{2,10},{6,14},... | collective-permute-start | bytes 1572872 | tf_op jit(solution)/shard_map/ppermute | solution.py:27
  6.8 2.6 %collective-permute-start = (bf16[1024,256]{1,0:T(8,128)(2,1)S(1)}, bf16[1024,256]{1,0:T(8,128)(2,1)S(1)}, u32[]{:S(2)}, u32[]{:S(2)}) collective-permute-start(bf16[1024,256]{1,0:T(8,128)(2,1)S(1)} %get-tuple-element.23), channel_id=1, source_target_pairs={{0,4},{4,8},{8,12},{12,0},{1,5},{5,9},{9,13},{13,1},{2,6},{6,10},{... | collective-permute-start | bytes 1572872 | tf_op jit(solution)/shard_map/ppermute | solution.py:27
  9.4 4.5 %collective-permute-start.2 = (bf16[1024,256]{1,0:T(8,128)(2,1)S(1)}, bf16[1024,256]{1,0:T(8,128)(2,1)S(1)}, u32[]{:S(2)}, u32[]{:S(2)}) collective-permute-start(bf16[1024,256]{1,0:T(8,128)(2,1)S(1)} %get-tuple-element.23), channel_id=1, source_target_pairs={{0,12},{4,0},{8,4},{12,8},{1,13},{5,1},{9,5},{13,9},{2,14},{6,2},{... | collective-permute-start | bytes 1572872 | tf_op jit(solution)/shard_map/ppermute | solution.py:27
  15.7 14.8 %collective-permute-start.4 = (bf16[640,256]{1,0:T(8,128)(2,1)S(1)}, bf16[640,256]{1,0:T(8,128)(2,1)S(1)}, u32[]{:S(2)}, u32[]{:S(2)}) collective-permute-start(bf16[640,256]{1,0:T(8,128)(2,1)S(1)} %pad_maximum_fusion.3), channel_id=1, source_target_pairs={{0,2},{2,0},{1,3},{3,1},{4,6},{6,4},{5,7},{7,5},{8,10},{10,8},{9,1... | collective-permute-start | bytes 983048 | tf_op jit(solution)/shard_map/ppermute | solution.py:222
  31.6 1.5 pad_maximum_fusion.refs_0_
  33.1 1.9 collective-permute-start.3
  35.0 2.9 %collective-permute-start.16 = (bf16[512,256]{1,0:T(8,128)(2,1)S(1)}, bf16[512,256]{1,0:T(8,128)(2,1)S(1)}, u32[]{:S(2)}, u32[]{:S(2)}) collective-permute-start(bf16[512,256]{1,0:T(8,128)(2,1)S(1)} %bitcast.33), channel_id=1, source_target_pairs={{16,0},{32,16},{48,32},{64,48},{80,64},{96,80},{112,96},{17,1},{33... | collective-permute-start | bytes 786440 | tf_op jit(solution)/shard_map/ppermute | solution.py:51
  37.9 2.9 %collective-permute-start.9 = (bf16[512,256]{1,0:T(8,128)(2,1)S(1)}, bf16[512,256]{1,0:T(8,128)(2,1)S(1)}, u32[]{:S(2)}, u32[]{:S(2)}) collective-permute-start(bf16[512,256]{1,0:T(8,128)(2,1)S(1)} %bitcast.34), channel_id=1, source_target_pairs={{0,16},{16,32},{32,48},{48,64},{64,80},{80,96},{96,112},{1,17},{17... | collective-permute-start | bytes 786440 | tf_op jit(solution)/shard_map/ppermute | solution.py:50
  40.9 23.5 %collective-permute-done.16.refs_12_ = bf16[512,256]{1,0:T(8,128)(2,1)S(1)} collective-permute-done((bf16[512,256]{1,0:T(8,128)(2,1)S(1)}, bf16[512,256]{1,0:T(8,128)(2,1)S(1)}, u32[]{:S(2)}, u32[]{:S(2)}) %collective-permute-start.16) | collective-permute-done | bytes 262176 | tf_op jit(solution)/shard_map/ppermute | solution.py:51
  64.3 3.4 %collective-permute-start.17 = (bf16[512,256]{1,0:T(8,128)(2,1)S(1)}, bf16[512,256]{1,0:T(8,128)(2,1)S(1)}, u32[]{:S(2)}, u32[]{:S(2)}) collective-permute-start(bf16[512,256]{1,0:T(8,128)(2,1)S(1)} %collective-permute-done.16.refs_12_), channel_id=1, source_target_pairs={{16,0},{32,16},{48,32},{64,48},{80,64},{96,80},{112,96},{17,1},{33... | collective-permute-start | bytes 786440 | tf_op jit(solution)/shard_map/ppermute | solution.py:51
  67.8 2.4 collective-permute-start.10
  70.3 1.9 collective-permute-start.6
  72.2 3.0 %collective-permute-start.5 = (bf16[512,256]{1,0:T(8,128)(2,1)S(1)}, bf16[512,256]{1,0:T(8,128)(2,1)S(1)}, u32[]{:S(2)}, u32[]{:S(2)}) collective-permute-start(bf16[512,256]{1,0:T(8,128)(2,1)S(1)} %get-tuple-element.25), channel_id=1, source_target_pairs={{0,4},{4,8},{8,12},{12,0},{1,5},{5,9},{9,13},{13,1},{2,6},{6,10},{... | collective-permute-start | bytes 786440 | tf_op jit(solution)/shard_map/ppermute | solution.py:27
  75.3 4.0 %collective-permute-start.7 = (bf16[512,256]{1,0:T(8,128)(2,1)S(1)}, bf16[512,256]{1,0:T(8,128)(2,1)S(1)}, u32[]{:S(2)}, u32[]{:S(2)}) collective-permute-start(bf16[512,256]{1,0:T(8,128)(2,1)S(1)} %get-tuple-element.25), channel_id=1, source_target_pairs={{0,12},{4,0},{8,4},{12,8},{1,13},{5,1},{9,5},{13,9},{2,14},{6,2},{... | collective-permute-start | bytes 786440 | tf_op jit(solution)/shard_map/ppermute | solution.py:27
  79.3 3.5 %collective-permute-start.18 = (bf16[512,256]{1,0:T(8,128)(2,1)S(1)}, bf16[512,256]{1,0:T(8,128)(2,1)S(1)}, u32[]{:S(2)}, u32[]{:S(2)}) collective-permute-start(bf16[512,256]{1,0:T(8,128)(2,1)S(1)} %collective-permute-done.17.refs_13_), channel_id=1, source_target_pairs={{16,0},{32,16},{48,32},{64,48},{80,64},{96,80},{112,96},{17,1},{33... | collective-permute-start | bytes 786440 | tf_op jit(solution)/shard_map/ppermute | solution.py:51
  82.9 2.5 %collective-permute-start.11 = (bf16[512,256]{1,0:T(8,128)(2,1)S(1)}, bf16[512,256]{1,0:T(8,128)(2,1)S(1)}, u32[]{:S(2)}, u32[]{:S(2)}) collective-permute-start(bf16[512,256]{1,0:T(8,128)(2,1)S(1)} %collective-permute-done.10.refs_6_), channel_id=1, source_target_pairs={{0,16},{16,32},{32,48},{48,64},{64,80},{80,96},{96,112},{1,17},{17... | collective-permute-start | bytes 786440 | tf_op jit(solution)/shard_map/ppermute | solution.py:50
  85.4 1.6 collective-permute-done.5
  88.4 2.7 %collective-permute-start.19 = (bf16[512,256]{1,0:T(8,128)(2,1)S(1)}, bf16[512,256]{1,0:T(8,128)(2,1)S(1)}, u32[]{:S(2)}, u32[]{:S(2)}) collective-permute-start(bf16[512,256]{1,0:T(8,128)(2,1)S(1)} %collective-permute-done.18.refs_14_), channel_id=1, source_target_pairs={{16,0},{32,16},{48,32},{64,48},{80,64},{96,80},{112,96},{17,1},{33... | collective-permute-start | bytes 786440 | tf_op jit(solution)/shard_map/ppermute | solution.py:51
  91.1 3.1 %collective-permute-start.12 = (bf16[512,256]{1,0:T(8,128)(2,1)S(1)}, bf16[512,256]{1,0:T(8,128)(2,1)S(1)}, u32[]{:S(2)}, u32[]{:S(2)}) collective-permute-start(bf16[512,256]{1,0:T(8,128)(2,1)S(1)} %collective-permute-done.11.refs_7_), channel_id=1, source_target_pairs={{0,16},{16,32},{32,48},{48,64},{64,80},{80,96},{96,112},{1,17},{17... | collective-permute-start | bytes 786440 | tf_op jit(solution)/shard_map/ppermute | solution.py:50
  94.2 1.9 collective-permute-start.8
  97.3 2.2 collective-permute-start.20
  99.5 3.6 %collective-permute-start.13 = (bf16[512,256]{1,0:T(8,128)(2,1)S(1)}, bf16[512,256]{1,0:T(8,128)(2,1)S(1)}, u32[]{:S(2)}, u32[]{:S(2)}) collective-permute-start(bf16[512,256]{1,0:T(8,128)(2,1)S(1)} %collective-permute-done.12.refs_8_), channel_id=1, source_target_pairs={{0,16},{16,32},{32,48},{48,64},{64,80},{80,96},{96,112},{1,17},{17... | collective-permute-start | bytes 786440 | tf_op jit(solution)/shard_map/ppermute | solution.py:50
  103.2 3.6 %collective-permute-done.20.refs_16_ = bf16[512,256]{1,0:T(8,128)(2,1)S(1)} collective-permute-done((bf16[512,256]{1,0:T(8,128)(2,1)S(1)}, bf16[512,256]{1,0:T(8,128)(2,1)S(1)}, u32[]{:S(2)}, u32[]{:S(2)}) %collective-permute-start.20) | collective-permute-done | bytes 262176 | tf_op jit(solution)/shard_map/ppermute | solution.py:51
  106.8 2.7 %collective-permute-start.21 = (bf16[512,256]{1,0:T(8,128)(2,1)S(1)}, bf16[512,256]{1,0:T(8,128)(2,1)}, u32[]{:S(2)}, u32[]{:S(2)}) collective-permute-start(bf16[512,256]{1,0:T(8,128)(2,1)S(1)} %collective-permute-done.20.refs_16_), channel_id=1, source_target_pairs={{16,0},{32,16},{48,32},{64,48},{80,64},{96,80},{112,96},{17,1},{33... | collective-permute-start | bytes 786440 | tf_op jit(solution)/shard_map/ppermute | solution.py:51
  109.6 3.9 %collective-permute-start.14 = (bf16[512,256]{1,0:T(8,128)(2,1)S(1)}, bf16[512,256]{1,0:T(8,128)(2,1)}, u32[]{:S(2)}, u32[]{:S(2)}) collective-permute-start(bf16[512,256]{1,0:T(8,128)(2,1)S(1)} %collective-permute-done.13.refs_9_), channel_id=1, source_target_pairs={{0,16},{16,32},{32,48},{48,64},{64,80},{80,96},{96,112},{1,17},{17... | collective-permute-start | bytes 786440 | tf_op jit(solution)/shard_map/ppermute | solution.py:50
  113.6 4.1 %collective-permute-done.21.refs_17_ = bf16[512,256]{1,0:T(8,128)(2,1)} collective-permute-done((bf16[512,256]{1,0:T(8,128)(2,1)S(1)}, bf16[512,256]{1,0:T(8,128)(2,1)}, u32[]{:S(2)}, u32[]{:S(2)}) %collective-permute-start.21) | collective-permute-done | bytes 262176 | tf_op jit(solution)/shard_map/ppermute | solution.py:51
  117.7 1.9 collective-permute-start.22
  119.6 4.6 %collective-permute-start.15 = (bf16[512,256]{1,0:T(8,128)(2,1)}, bf16[512,256]{1,0:T(8,128)(2,1)}, u32[]{:S(2)}, u32[]{:S(2)}) collective-permute-start(bf16[512,256]{1,0:T(8,128)(2,1)} %collective-permute-done.14.refs_10_), channel_id=1, source_target_pairs={{0,16},{16,32},{32,48},{48,64},{64,80},{80,96},{96,112},{1,17},{17... | collective-permute-start | bytes 786440 | tf_op jit(solution)/shard_map/ppermute | solution.py:50
  124.9 4.3 %all-to-all-start = ((bf16[4,128,256]{2,1,0:T(8,128)(2,1)}), bf16[4,128,256]{2,1,0:T(8,128)(2,1)}, u32[]{:S(2)}, u32[]{:S(2)}) async-start(bf16[4,128,256]{2,1,0:T(8,128)(2,1)} %broadcast_in_dim.6), calls=%async_computation | async-start | bytes 524288 | tf_op jit(solution)/shard_map/all_to_all | solution.py:21
  129.3 6.1 %mix.1 = (bf16[512,256]{1,0:T(8,128)(2,1)S(1)}, bf16[512,128]{1,0:T(8,128)(2,1)S(1)}, bf16[512,128]{1,0:T(8,128)(2,1)S(1)}) custom-call(s32[4]{0:T(128)S(1)} %pad_add_fusion.place, bf16[4,1024,256]{2,1,0:T(8,128)(2,1)S(1)} %pad_maximum_fusion.refs_0_, bf16[4,1024,256]{2,1,0:T(8,128)(2,1)} %collective-permute-done.3.refs_1_, ...), custom_call_target="tpu_custom_call" | custom-call | flops 1073741824 | bytes 2097152 | tf_op jit(solution)/shard_map/mix/pallas_call | solution.py:155
  137.9 16.5 %all_to_all.15.refs_2_ = bf16[4,512,256]{2,1,0:T(8,128)(2,1)S(1)} all-to-all(bf16[4,512,256]{2,1,0:T(8,128)(2,1)S(1)} %broadcast_in_dim.7), channel_id=1, replica_groups=mesh['quarter'=4,'row'=8,'y'=4,'z_hi'=2,'core'=2] {'y'}, dimensions={0} | all-to-all | bytes 2097152 | tf_op jit(solution)/shard_map/all_to_all | solution.py:21
  154.4 1.9 collective-permute-start.23
  156.3 7.5 %collective-permute-start.24 = (bf16[512,128]{1,0:T(8,128)(2,1)S(1)}, bf16[512,128]{1,0:T(8,128)(2,1)S(1)}, u32[]{:S(2)}, u32[]{:S(2)}) collective-permute-start(bf16[512,128]{1,0:T(8,128)(2,1)S(1)} %copy-done.15), channel_id=1, source_target_pairs={{0,64},{16,80},{32,96},{48,112},{64,0},{80,16},{96,32},{112,48},{1... | collective-permute-start | bytes 393224 | tf_op jit(solution)/shard_map/ppermute | solution.py:39
  163.8 4.3 %collective-permute-start.34 = (bf16[512,256]{1,0:T(8,128)(2,1)S(1)}, bf16[512,256]{1,0:T(8,128)(2,1)S(1)}, u32[]{:S(2)}, u32[]{:S(2)}) collective-permute-start(bf16[512,256]{1,0:T(8,128)(2,1)S(1)} %get-tuple-element.19.refs_4_), channel_id=1, source_target_pairs={{0,48},{16,0},{32,16},{48,32},{64,112},{80,64},{96,80},{112,96},{1... | collective-permute-start | bytes 786440 | tf_op jit(solution)/shard_map/ppermute | solution.py:34
  168.2 1.9 collective-permute-start.33
  170.1 3.4 %collective-permute-start.32 = (bf16[512,256]{1,0:T(8,128)(2,1)S(1)}, bf16[512,256]{1,0:T(8,128)(2,1)S(1)}, u32[]{:S(2)}, u32[]{:S(2)}) collective-permute-start(bf16[512,256]{1,0:T(8,128)(2,1)S(1)} %get-tuple-element.19.refs_4_), channel_id=1, source_target_pairs={{0,16},{16,32},{32,48},{48,0},{64,80},{80,96},{96,112},{112,64},{1... | collective-permute-start | bytes 786440 | tf_op jit(solution)/shard_map/ppermute | solution.py:34
  173.5 8.3 %collective-permute-done.24.refs_4_ = bf16[512,128]{1,0:T(8,128)(2,1)S(1)} collective-permute-done((bf16[512,128]{1,0:T(8,128)(2,1)S(1)}, bf16[512,128]{1,0:T(8,128)(2,1)S(1)}, u32[]{:S(2)}, u32[]{:S(2)}) %collective-permute-start.24) | collective-permute-done | bytes 131104 | tf_op jit(solution)/shard_map/ppermute | solution.py:39
  181.8 8.5 %collective-permute-start.28 = (bf16[512,128]{1,0:T(8,128)(2,1)S(1)}, bf16[512,128]{1,0:T(8,128)(2,1)}, u32[]{:S(2)}, u32[]{:S(2)}) collective-permute-start(bf16[512,128]{1,0:T(8,128)(2,1)S(1)} %copy-done.13), channel_id=1, source_target_pairs={{0,64},{16,80},{32,96},{48,112},{64,0},{80,16},{96,32},{112,48},{1... | collective-permute-start | bytes 393224 | tf_op jit(solution)/shard_map/ppermute | solution.py:39
  190.3 13.3 %collective-permute-done.28.refs_8_ = bf16[512,128]{1,0:T(8,128)(2,1)} collective-permute-done((bf16[512,128]{1,0:T(8,128)(2,1)S(1)}, bf16[512,128]{1,0:T(8,128)(2,1)}, u32[]{:S(2)}, u32[]{:S(2)}) %collective-permute-start.28) | collective-permute-done | bytes 131104 | tf_op jit(solution)/shard_map/ppermute | solution.py:39
  203.6 1.9 collective-permute-start.27
  206.2 1.9 collective-permute-start.26
  208.8 3.9 %collective-permute-start.25 = (bf16[512,128]{1,0:T(8,128)(2,1)S(1)}, bf16[512,128]{1,0:T(8,128)(2,1)}, u32[]{:S(2)}, u32[]{:S(2)}) collective-permute-start(bf16[512,128]{1,0:T(8,128)(2,1)S(1)} %collective-permute-done.24.refs_4_), channel_id=1, source_target_pairs={{0,16},{16,32},{32,48},{48,0},{64,80},{80,96},{96,112},{112,64},{1... | collective-permute-start | bytes 393224 | tf_op jit(solution)/shard_map/ppermute | solution.py:34
  213.5 3.4 %collective-permute-start.31 = (bf16[512,128]{1,0:T(8,128)(2,1)}, bf16[512,128]{1,0:T(8,128)(2,1)}, u32[]{:S(2)}, u32[]{:S(2)}) collective-permute-start(bf16[512,128]{1,0:T(8,128)(2,1)} %collective-permute-done.28.refs_8_), channel_id=1, source_target_pairs={{0,48},{16,0},{32,16},{48,32},{64,112},{80,64},{96,80},{112,96},{1... | collective-permute-start | bytes 393224 | tf_op jit(solution)/shard_map/ppermute | solution.py:34
  217.5 4.3 %collective-permute-start.30 = (bf16[512,128]{1,0:T(8,128)(2,1)}, bf16[512,128]{1,0:T(8,128)(2,1)}, u32[]{:S(2)}, u32[]{:S(2)}) collective-permute-start(bf16[512,128]{1,0:T(8,128)(2,1)} %collective-permute-done.28.refs_8_), channel_id=1, source_target_pairs={{0,32},{16,48},{32,0},{48,16},{64,96},{80,112},{96,64},{112,80},{1... | collective-permute-start | bytes 393224 | tf_op jit(solution)/shard_map/ppermute | solution.py:34
  222.7 4.8 %collective-permute-start.29 = (bf16[512,128]{1,0:T(8,128)(2,1)}, bf16[512,128]{1,0:T(8,128)(2,1)}, u32[]{:S(2)}, u32[]{:S(2)}) collective-permute-start(bf16[512,128]{1,0:T(8,128)(2,1)} %collective-permute-done.28.refs_8_), channel_id=1, source_target_pairs={{0,16},{16,32},{32,48},{48,0},{64,80},{80,96},{96,112},{112,64},{1... | collective-permute-start | bytes 393224 | tf_op jit(solution)/shard_map/ppermute | solution.py:34
  231.8 2.8 %shard_map.68.refs_12_ = f32[512,256]{1,0:T(8,128)S(1)} custom-call(s32[5]{0:T(128)S(1)} %stack.86.place, bf16[4,1024,256]{2,1,0:T(8,128)(2,1)S(1)} %pad_maximum_fusion.refs_0_, bf16[4,1024,256]{2,1,0:T(8,128)(2,1)} %collective-permute-done.3.refs_1_, bf16[4,512,256]{2,1,0:T(8,128)(2,1)S(1)} %all_to_all.15.refs_2_, bf16[4,512,256]{2,1,0:T(8,128)(2,1)S(1)} %copy-done.1, ...), custom_call_target="tpu_custom_call" | custom-call | flops 536870912 | bytes 524288 | tf_op jit(solution)/shard_map/pallas_call | solution.py:185
  234.8 3.9 %update.1 = (f32[512,256]{1,0:T(8,128)}, bf16[512,256]{1,0:T(8,128)(2,1)S(1)}) custom-call(s32[5]{0:T(128)S(1)} %stack.72.place, bf16[4,1024,256]{2,1,0:T(8,128)(2,1)S(1)} %pad_maximum_fusion.refs_0_, bf16[4,1024,256]{2,1,0:T(8,128)(2,1)} %collective-permute-done.3.refs_1_, bf16[4,512,256]{2,1,0:T(8,128)(2,1)S(1)} %all_to_all.15.refs_2_, ...), custom_call_target="tpu_custom_call" | custom-call | flops 536870912 | bytes 4980736 | tf_op jit(solution)/shard_map/update/pallas_call | solution.py:93
  238.7 10.9 %all_to_all.16 = bf16[4,128,256]{2,1,0:T(8,128)(2,1)S(1)} all-to-all(bf16[4,128,256]{2,1,0:T(8,128)(2,1)S(1)} %bitcast.26), channel_id=1, replica_groups=mesh['quarter'=4,'row'=8,'y'=4,'z_hi'=2,'core'=2] {'quarter'}, dimensions={0} | all-to-all | bytes 524288 | tf_op jit(solution)/shard_map/all_to_all | solution.py:246
  (100 shorter events, 18.5 us)
Async XLA Ops:
  1.7 28.8 %collective-permute-start.1 = (bf16[1024,256]{1,0:T(8,128)(2,1)S(1)}, bf16[1024,256]{1,0:T(8,128)(2,1)S(1)}, u32[]{:S(2)}, u32[]{:S(2)}) collective-permute-start(bf16[1024,256]{1,0:T(8,128)(2,1)S(1)} %get-tuple-element.23), channel_id=1, source_target_pairs={{0,8},{4,12},{8,0},{12,4},{1,9},{5,13},{9,1},{13,5},{2,10},{6,14},... | collective-permute-start | bytes 1572872 | tf_op jit(solution)/shard_map/ppermute | solution.py:27
  6.8 23.7 %collective-permute-start = (bf16[1024,256]{1,0:T(8,128)(2,1)S(1)}, bf16[1024,256]{1,0:T(8,128)(2,1)S(1)}, u32[]{:S(2)}, u32[]{:S(2)}) collective-permute-start(bf16[1024,256]{1,0:T(8,128)(2,1)S(1)} %get-tuple-element.23), channel_id=1, source_target_pairs={{0,4},{4,8},{8,12},{12,0},{1,5},{5,9},{9,13},{13,1},{2,6},{6,10},{... | collective-permute-start | bytes 1572872 | tf_op jit(solution)/shard_map/ppermute | solution.py:27
  9.4 21.2 %collective-permute-start.2 = (bf16[1024,256]{1,0:T(8,128)(2,1)S(1)}, bf16[1024,256]{1,0:T(8,128)(2,1)S(1)}, u32[]{:S(2)}, u32[]{:S(2)}) collective-permute-start(bf16[1024,256]{1,0:T(8,128)(2,1)S(1)} %get-tuple-element.23), channel_id=1, source_target_pairs={{0,12},{4,0},{8,4},{12,8},{1,13},{5,1},{9,5},{13,9},{2,14},{6,2},{... | collective-permute-start | bytes 1572872 | tf_op jit(solution)/shard_map/ppermute | solution.py:27
  15.7 54.5 %collective-permute-start.4 = (bf16[640,256]{1,0:T(8,128)(2,1)S(1)}, bf16[640,256]{1,0:T(8,128)(2,1)S(1)}, u32[]{:S(2)}, u32[]{:S(2)}) collective-permute-start(bf16[640,256]{1,0:T(8,128)(2,1)S(1)} %pad_maximum_fusion.3), channel_id=1, source_target_pairs={{0,2},{2,0},{1,3},{3,1},{4,6},{6,4},{5,7},{7,5},{8,10},{10,8},{9,1... | collective-permute-start | bytes 983048 | tf_op jit(solution)/shard_map/ppermute | solution.py:222
  31.6 3.4 %copy-start.18 = (bf16[1,512,256]{2,1,0:T(8,128)(2,1)S(1)}, bf16[1,512,256]{2,1,0:T(8,128)(2,1)}, u32[]{:S(2)}) copy-start(bf16[1,512,256]{2,1,0:T(8,128)(2,1)} %param.7) | copy-start | bytes 786436
  33.1 96.3 %collective-permute-start.3 = (bf16[4,1024,256]{2,1,0:T(8,128)(2,1)S(1)}, bf16[4,1024,256]{2,1,0:T(8,128)(2,1)}, u32[]{:S(2)}, u32[]{:S(2)}) collective-permute-start(bf16[4,1024,256]{2,1,0:T(8,128)(2,1)S(1)} %pad_maximum_fusion.refs_0_), channel_id=1, source_target_pairs={{0,1},{1,0},{2,3},{3,2},{4,5},{5,4},{6,7},{7,6},{8,9},{9,8},{10,11... | collective-permute-start | bytes 6291464 | tf_op jit(solution)/shard_map/ppermute | solution.py:204
  35.0 29.3 %collective-permute-start.16 = (bf16[512,256]{1,0:T(8,128)(2,1)S(1)}, bf16[512,256]{1,0:T(8,128)(2,1)S(1)}, u32[]{:S(2)}, u32[]{:S(2)}) collective-permute-start(bf16[512,256]{1,0:T(8,128)(2,1)S(1)} %bitcast.33), channel_id=1, source_target_pairs={{16,0},{32,16},{48,32},{64,48},{80,64},{96,80},{112,96},{17,1},{33... | collective-permute-start | bytes 786440 | tf_op jit(solution)/shard_map/ppermute | solution.py:51
  37.9 29.8 %collective-permute-start.9 = (bf16[512,256]{1,0:T(8,128)(2,1)S(1)}, bf16[512,256]{1,0:T(8,128)(2,1)S(1)}, u32[]{:S(2)}, u32[]{:S(2)}) collective-permute-start(bf16[512,256]{1,0:T(8,128)(2,1)S(1)} %bitcast.34), channel_id=1, source_target_pairs={{0,16},{16,32},{32,48},{48,64},{64,80},{80,96},{96,112},{1,17},{17... | collective-permute-start | bytes 786440 | tf_op jit(solution)/shard_map/ppermute | solution.py:50
  64.3 22.7 %copy-start.19 = (bf16[512,256]{1,0:T(8,128)(2,1)}, bf16[512,256]{1,0:T(8,128)(2,1)S(1)}, u32[]{:S(2)}) copy-start(bf16[512,256]{1,0:T(8,128)(2,1)S(1)} %collective-permute-done.16.refs_12_) | copy-start | bytes 786436
  64.3 10.9 %collective-permute-start.17 = (bf16[512,256]{1,0:T(8,128)(2,1)S(1)}, bf16[512,256]{1,0:T(8,128)(2,1)S(1)}, u32[]{:S(2)}, u32[]{:S(2)}) collective-permute-start(bf16[512,256]{1,0:T(8,128)(2,1)S(1)} %collective-permute-done.16.refs_12_), channel_id=1, source_target_pairs={{16,0},{32,16},{48,32},{64,48},{80,64},{96,80},{112,96},{17,1},{33... | collective-permute-start | bytes 786440 | tf_op jit(solution)/shard_map/ppermute | solution.py:51
  67.8 19.2 %copy-start.20 = (bf16[512,256]{1,0:T(8,128)(2,1)}, bf16[512,256]{1,0:T(8,128)(2,1)S(1)}, u32[]{:S(2)}) copy-start(bf16[512,256]{1,0:T(8,128)(2,1)S(1)} %collective-permute-done.9.refs_5_) | copy-start | bytes 786436
  67.8 11.5 %collective-permute-start.10 = (bf16[512,256]{1,0:T(8,128)(2,1)S(1)}, bf16[512,256]{1,0:T(8,128)(2,1)S(1)}, u32[]{:S(2)}, u32[]{:S(2)}) collective-permute-start(bf16[512,256]{1,0:T(8,128)(2,1)S(1)} %collective-permute-done.9.refs_5_), channel_id=1, source_target_pairs={{0,16},{16,32},{32,48},{48,64},{64,80},{80,96},{96,112},{1,17},{17... | collective-permute-start | bytes 786440 | tf_op jit(solution)/shard_map/ppermute | solution.py:50
  70.3 12.6 %collective-permute-start.6 = (bf16[512,256]{1,0:T(8,128)(2,1)S(1)}, bf16[512,256]{1,0:T(8,128)(2,1)S(1)}, u32[]{:S(2)}, u32[]{:S(2)}) collective-permute-start(bf16[512,256]{1,0:T(8,128)(2,1)S(1)} %get-tuple-element.25), channel_id=1, source_target_pairs={{0,8},{4,12},{8,0},{12,4},{1,9},{5,13},{9,1},{13,5},{2,10},{6,14},... | collective-permute-start | bytes 786440 | tf_op jit(solution)/shard_map/ppermute | solution.py:27
  72.2 14.8 %collective-permute-start.5 = (bf16[512,256]{1,0:T(8,128)(2,1)S(1)}, bf16[512,256]{1,0:T(8,128)(2,1)S(1)}, u32[]{:S(2)}, u32[]{:S(2)}) collective-permute-start(bf16[512,256]{1,0:T(8,128)(2,1)S(1)} %get-tuple-element.25), channel_id=1, source_target_pairs={{0,4},{4,8},{8,12},{12,0},{1,5},{5,9},{9,13},{13,1},{2,6},{6,10},{... | collective-permute-start | bytes 786440 | tf_op jit(solution)/shard_map/ppermute | solution.py:27
  75.2 15.9 %copy-start.21 = (bf16[512,256]{1,0:T(8,128)(2,1)}, bf16[512,256]{1,0:T(8,128)(2,1)S(1)}, u32[]{:S(2)}) copy-start(bf16[512,256]{1,0:T(8,128)(2,1)S(1)} %collective-permute-done.17.refs_13_) | copy-start | bytes 786436
  75.3 11.7 %collective-permute-start.7 = (bf16[512,256]{1,0:T(8,128)(2,1)S(1)}, bf16[512,256]{1,0:T(8,128)(2,1)S(1)}, u32[]{:S(2)}, u32[]{:S(2)}) collective-permute-start(bf16[512,256]{1,0:T(8,128)(2,1)S(1)} %get-tuple-element.25), channel_id=1, source_target_pairs={{0,12},{4,0},{8,4},{12,8},{1,13},{5,1},{9,5},{13,9},{2,14},{6,2},{... | collective-permute-start | bytes 786440 | tf_op jit(solution)/shard_map/ppermute | solution.py:27
  79.3 14.9 %copy-start.22 = (bf16[512,256]{1,0:T(8,128)(2,1)}, bf16[512,256]{1,0:T(8,128)(2,1)S(1)}, u32[]{:S(2)}) copy-start(bf16[512,256]{1,0:T(8,128)(2,1)S(1)} %collective-permute-done.10.refs_6_) | copy-start | bytes 786436
  79.3 9.1 %collective-permute-start.18 = (bf16[512,256]{1,0:T(8,128)(2,1)S(1)}, bf16[512,256]{1,0:T(8,128)(2,1)S(1)}, u32[]{:S(2)}, u32[]{:S(2)}) collective-permute-start(bf16[512,256]{1,0:T(8,128)(2,1)S(1)} %collective-permute-done.17.refs_13_), channel_id=1, source_target_pairs={{16,0},{32,16},{48,32},{64,48},{80,64},{96,80},{112,96},{17,1},{33... | collective-permute-start | bytes 786440 | tf_op jit(solution)/shard_map/ppermute | solution.py:51
  82.9 8.3 %collective-permute-start.11 = (bf16[512,256]{1,0:T(8,128)(2,1)S(1)}, bf16[512,256]{1,0:T(8,128)(2,1)S(1)}, u32[]{:S(2)}, u32[]{:S(2)}) collective-permute-start(bf16[512,256]{1,0:T(8,128)(2,1)S(1)} %collective-permute-done.10.refs_6_), channel_id=1, source_target_pairs={{0,16},{16,32},{32,48},{48,64},{64,80},{80,96},{96,112},{1,17},{17... | collective-permute-start | bytes 786440 | tf_op jit(solution)/shard_map/ppermute | solution.py:50
  88.3 7.8 %copy-start.23 = (bf16[512,256]{1,0:T(8,128)(2,1)}, bf16[512,256]{1,0:T(8,128)(2,1)S(1)}, u32[]{:S(2)}) copy-start(bf16[512,256]{1,0:T(8,128)(2,1)S(1)} %collective-permute-done.18.refs_14_) | copy-start | bytes 786436
  88.4 8.9 %collective-permute-start.19 = (bf16[512,256]{1,0:T(8,128)(2,1)S(1)}, bf16[512,256]{1,0:T(8,128)(2,1)S(1)}, u32[]{:S(2)}, u32[]{:S(2)}) collective-permute-start(bf16[512,256]{1,0:T(8,128)(2,1)S(1)} %collective-permute-done.18.refs_14_), channel_id=1, source_target_pairs={{16,0},{32,16},{48,32},{64,48},{80,64},{96,80},{112,96},{17,1},{33... | collective-permute-start | bytes 786440 | tf_op jit(solution)/shard_map/ppermute | solution.py:51
  91.1 6.2 %copy-start.24 = (bf16[512,256]{1,0:T(8,128)(2,1)}, bf16[512,256]{1,0:T(8,128)(2,1)S(1)}, u32[]{:S(2)}) copy-start(bf16[512,256]{1,0:T(8,128)(2,1)S(1)} %collective-permute-done.11.refs_7_) | copy-start | bytes 786436
  91.1 8.4 %collective-permute-start.12 = (bf16[512,256]{1,0:T(8,128)(2,1)S(1)}, bf16[512,256]{1,0:T(8,128)(2,1)S(1)}, u32[]{:S(2)}, u32[]{:S(2)}) collective-permute-start(bf16[512,256]{1,0:T(8,128)(2,1)S(1)} %collective-permute-done.11.refs_7_), channel_id=1, source_target_pairs={{0,16},{16,32},{32,48},{48,64},{64,80},{80,96},{96,112},{1,17},{17... | collective-permute-start | bytes 786440 | tf_op jit(solution)/shard_map/ppermute | solution.py:50
  94.2 35.1 %collective-permute-start.8 = (bf16[4,512,256]{2,1,0:T(8,128)(2,1)S(1)}, bf16[4,512,256]{2,1,0:T(8,128)(2,1)}, u32[]{:S(2)}, u32[]{:S(2)}) collective-permute-start(bf16[4,512,256]{2,1,0:T(8,128)(2,1)S(1)} %pad_maximum_fusion.1.refs_2_), channel_id=1, source_target_pairs={{0,1},{1,0},{2,3},{3,2},{4,5},{5,4},{6,7},{7,6},{8,9},{9,8},{10,11... | collective-permute-start | bytes 3145736 | tf_op jit(solution)/shard_map/ppermute | solution.py:204
  97.3 9.5 %collective-permute-start.20 = (bf16[512,256]{1,0:T(8,128)(2,1)S(1)}, bf16[512,256]{1,0:T(8,128)(2,1)S(1)}, u32[]{:S(2)}, u32[]{:S(2)}) collective-permute-start(bf16[512,256]{1,0:T(8,128)(2,1)S(1)} %collective-permute-done.19.refs_15_), channel_id=1, source_target_pairs={{16,0},{32,16},{48,32},{64,48},{80,64},{96,80},{112,96},{17,1},{33... | collective-permute-start | bytes 786440 | tf_op jit(solution)/shard_map/ppermute | solution.py:51
  99.5 7.3 %copy-start.26 = (bf16[512,256]{1,0:T(8,128)(2,1)}, bf16[512,256]{1,0:T(8,128)(2,1)S(1)}, u32[]{:S(2)}) copy-start(bf16[512,256]{1,0:T(8,128)(2,1)S(1)} %collective-permute-done.12.refs_8_) | copy-start | bytes 786436
  99.5 10.1 %collective-permute-start.13 = (bf16[512,256]{1,0:T(8,128)(2,1)S(1)}, bf16[512,256]{1,0:T(8,128)(2,1)S(1)}, u32[]{:S(2)}, u32[]{:S(2)}) collective-permute-start(bf16[512,256]{1,0:T(8,128)(2,1)S(1)} %collective-permute-done.12.refs_8_), channel_id=1, source_target_pairs={{0,16},{16,32},{32,48},{48,64},{64,80},{80,96},{96,112},{1,17},{17... | collective-permute-start | bytes 786440 | tf_op jit(solution)/shard_map/ppermute | solution.py:50
  106.8 10.9 %collective-permute-start.21 = (bf16[512,256]{1,0:T(8,128)(2,1)S(1)}, bf16[512,256]{1,0:T(8,128)(2,1)}, u32[]{:S(2)}, u32[]{:S(2)}) collective-permute-start(bf16[512,256]{1,0:T(8,128)(2,1)S(1)} %collective-permute-done.20.refs_16_), channel_id=1, source_target_pairs={{16,0},{32,16},{48,32},{64,48},{80,64},{96,80},{112,96},{17,1},{33... | collective-permute-start | bytes 786440 | tf_op jit(solution)/shard_map/ppermute | solution.py:51
  109.6 8.1 %copy-start.28 = (bf16[512,256]{1,0:T(8,128)(2,1)}, bf16[512,256]{1,0:T(8,128)(2,1)S(1)}, u32[]{:S(2)}) copy-start(bf16[512,256]{1,0:T(8,128)(2,1)S(1)} %collective-permute-done.13.refs_9_) | copy-start | bytes 786436
  109.6 10.0 %collective-permute-start.14 = (bf16[512,256]{1,0:T(8,128)(2,1)S(1)}, bf16[512,256]{1,0:T(8,128)(2,1)}, u32[]{:S(2)}, u32[]{:S(2)}) collective-permute-start(bf16[512,256]{1,0:T(8,128)(2,1)S(1)} %collective-permute-done.13.refs_9_), channel_id=1, source_target_pairs={{0,16},{16,32},{32,48},{48,64},{64,80},{80,96},{96,112},{1,17},{17... | collective-permute-start | bytes 786440 | tf_op jit(solution)/shard_map/ppermute | solution.py:50
  117.7 11.6 %collective-permute-start.22 = (bf16[512,256]{1,0:T(8,128)(2,1)}, bf16[512,256]{1,0:T(8,128)(2,1)}, u32[]{:S(2)}, u32[]{:S(2)}) collective-permute-start(bf16[512,256]{1,0:T(8,128)(2,1)} %collective-permute-done.21.refs_17_), channel_id=1, source_target_pairs={{16,0},{32,16},{48,32},{64,48},{80,64},{96,80},{112,96},{17,1},{33... | collective-permute-start | bytes 786440 | tf_op jit(solution)/shard_map/ppermute | solution.py:51
  119.6 9.7 %collective-permute-start.15 = (bf16[512,256]{1,0:T(8,128)(2,1)}, bf16[512,256]{1,0:T(8,128)(2,1)}, u32[]{:S(2)}, u32[]{:S(2)}) collective-permute-start(bf16[512,256]{1,0:T(8,128)(2,1)} %collective-permute-done.14.refs_10_), channel_id=1, source_target_pairs={{0,16},{16,32},{32,48},{48,64},{64,80},{80,96},{96,112},{1,17},{17... | collective-permute-start | bytes 786440 | tf_op jit(solution)/shard_map/ppermute | solution.py:50
  124.9 11.9 %all-to-all-start = ((bf16[4,128,256]{2,1,0:T(8,128)(2,1)}), bf16[4,128,256]{2,1,0:T(8,128)(2,1)}, u32[]{:S(2)}, u32[]{:S(2)}) async-start(bf16[4,128,256]{2,1,0:T(8,128)(2,1)} %broadcast_in_dim.6), calls=%async_computation | async-start | bytes 524288 | tf_op jit(solution)/shard_map/all_to_all | solution.py:21
  136.8 19.5 %copy-start.15 = (bf16[512,128]{1,0:T(8,128)(2,1)S(1)}, bf16[512,128]{1,0:T(8,128)(2,1)}, u32[]{:S(2)}) copy-start(bf16[512,128]{1,0:T(8,128)(2,1)} %copy-done.14) | copy-start | bytes 393220
  136.8 45.0 %copy-start.13 = (bf16[512,128]{1,0:T(8,128)(2,1)S(1)}, bf16[512,128]{1,0:T(8,128)(2,1)}, u32[]{:S(2)}) copy-start(bf16[512,128]{1,0:T(8,128)(2,1)} %copy-done.12) | copy-start | bytes 393220
  154.4 67.4 %collective-permute-start.23 = (bf16[4,512,256]{2,1,0:T(8,128)(2,1)S(1)}, bf16[4,512,256]{2,1,0:T(8,128)(2,1)S(1)}, u32[]{:S(2)}, u32[]{:S(2)}) collective-permute-start(bf16[4,512,256]{2,1,0:T(8,128)(2,1)S(1)} %all_to_all.15.refs_2_), channel_id=1, source_target_pairs={{0,1},{1,0},{2,3},{3,2},{4,5},{5,4},{6,7},{7,6},{8,9},{9,8},{10,11... | collective-permute-start | bytes 3145736 | tf_op jit(solution)/shard_map/ppermute | solution.py:204
  156.3 25.5 %collective-permute-start.24 = (bf16[512,128]{1,0:T(8,128)(2,1)S(1)}, bf16[512,128]{1,0:T(8,128)(2,1)S(1)}, u32[]{:S(2)}, u32[]{:S(2)}) collective-permute-start(bf16[512,128]{1,0:T(8,128)(2,1)S(1)} %copy-done.15), channel_id=1, source_target_pairs={{0,64},{16,80},{32,96},{48,112},{64,0},{80,16},{96,32},{112,48},{1... | collective-permute-start | bytes 393224 | tf_op jit(solution)/shard_map/ppermute | solution.py:39
  163.8 41.7 %collective-permute-start.34 = (bf16[512,256]{1,0:T(8,128)(2,1)S(1)}, bf16[512,256]{1,0:T(8,128)(2,1)S(1)}, u32[]{:S(2)}, u32[]{:S(2)}) collective-permute-start(bf16[512,256]{1,0:T(8,128)(2,1)S(1)} %get-tuple-element.19.refs_4_), channel_id=1, source_target_pairs={{0,48},{16,0},{32,16},{48,32},{64,112},{80,64},{96,80},{112,96},{1... | collective-permute-start | bytes 786440 | tf_op jit(solution)/shard_map/ppermute | solution.py:34
  168.2 39.9 %collective-permute-start.33 = (bf16[512,256]{1,0:T(8,128)(2,1)S(1)}, bf16[512,256]{1,0:T(8,128)(2,1)S(1)}, u32[]{:S(2)}, u32[]{:S(2)}) collective-permute-start(bf16[512,256]{1,0:T(8,128)(2,1)S(1)} %get-tuple-element.19.refs_4_), channel_id=1, source_target_pairs={{0,32},{16,48},{32,0},{48,16},{64,96},{80,112},{96,64},{112,80},{1... | collective-permute-start | bytes 786440 | tf_op jit(solution)/shard_map/ppermute | solution.py:34
  170.1 42.6 %collective-permute-start.32 = (bf16[512,256]{1,0:T(8,128)(2,1)S(1)}, bf16[512,256]{1,0:T(8,128)(2,1)S(1)}, u32[]{:S(2)}, u32[]{:S(2)}) collective-permute-start(bf16[512,256]{1,0:T(8,128)(2,1)S(1)} %get-tuple-element.19.refs_4_), channel_id=1, source_target_pairs={{0,16},{16,32},{32,48},{48,0},{64,80},{80,96},{96,112},{112,64},{1... | collective-permute-start | bytes 786440 | tf_op jit(solution)/shard_map/ppermute | solution.py:34
  181.8 21.8 %collective-permute-start.28 = (bf16[512,128]{1,0:T(8,128)(2,1)S(1)}, bf16[512,128]{1,0:T(8,128)(2,1)}, u32[]{:S(2)}, u32[]{:S(2)}) collective-permute-start(bf16[512,128]{1,0:T(8,128)(2,1)S(1)} %copy-done.13), channel_id=1, source_target_pairs={{0,64},{16,80},{32,96},{48,112},{64,0},{80,16},{96,32},{112,48},{1... | collective-permute-start | bytes 393224 | tf_op jit(solution)/shard_map/ppermute | solution.py:39
  203.6 13.3 %collective-permute-start.27 = (bf16[512,128]{1,0:T(8,128)(2,1)S(1)}, bf16[512,128]{1,0:T(8,128)(2,1)S(1)}, u32[]{:S(2)}, u32[]{:S(2)}) collective-permute-start(bf16[512,128]{1,0:T(8,128)(2,1)S(1)} %collective-permute-done.24.refs_4_), channel_id=1, source_target_pairs={{0,48},{16,0},{32,16},{48,32},{64,112},{80,64},{96,80},{112,96},{1... | collective-permute-start | bytes 393224 | tf_op jit(solution)/shard_map/ppermute | solution.py:34
  206.2 28.5 %collective-permute-start.26 = (bf16[512,128]{1,0:T(8,128)(2,1)S(1)}, bf16[512,128]{1,0:T(8,128)(2,1)}, u32[]{:S(2)}, u32[]{:S(2)}) collective-permute-start(bf16[512,128]{1,0:T(8,128)(2,1)S(1)} %collective-permute-done.24.refs_4_), channel_id=1, source_target_pairs={{0,32},{16,48},{32,0},{48,16},{64,96},{80,112},{96,64},{112,80},{1... | collective-permute-start | bytes 393224 | tf_op jit(solution)/shard_map/ppermute | solution.py:34
  208.8 25.9 %collective-permute-start.25 = (bf16[512,128]{1,0:T(8,128)(2,1)S(1)}, bf16[512,128]{1,0:T(8,128)(2,1)}, u32[]{:S(2)}, u32[]{:S(2)}) collective-permute-start(bf16[512,128]{1,0:T(8,128)(2,1)S(1)} %collective-permute-done.24.refs_4_), channel_id=1, source_target_pairs={{0,16},{16,32},{32,48},{48,0},{64,80},{80,96},{96,112},{112,64},{1... | collective-permute-start | bytes 393224 | tf_op jit(solution)/shard_map/ppermute | solution.py:34
  213.5 21.2 %collective-permute-start.31 = (bf16[512,128]{1,0:T(8,128)(2,1)}, bf16[512,128]{1,0:T(8,128)(2,1)}, u32[]{:S(2)}, u32[]{:S(2)}) collective-permute-start(bf16[512,128]{1,0:T(8,128)(2,1)} %collective-permute-done.28.refs_8_), channel_id=1, source_target_pairs={{0,48},{16,0},{32,16},{48,32},{64,112},{80,64},{96,80},{112,96},{1... | collective-permute-start | bytes 393224 | tf_op jit(solution)/shard_map/ppermute | solution.py:34
  217.5 17.2 %collective-permute-start.30 = (bf16[512,128]{1,0:T(8,128)(2,1)}, bf16[512,128]{1,0:T(8,128)(2,1)}, u32[]{:S(2)}, u32[]{:S(2)}) collective-permute-start(bf16[512,128]{1,0:T(8,128)(2,1)} %collective-permute-done.28.refs_8_), channel_id=1, source_target_pairs={{0,32},{16,48},{32,0},{48,16},{64,96},{80,112},{96,64},{112,80},{1... | collective-permute-start | bytes 393224 | tf_op jit(solution)/shard_map/ppermute | solution.py:34
  222.7 12.0 %collective-permute-start.29 = (bf16[512,128]{1,0:T(8,128)(2,1)}, bf16[512,128]{1,0:T(8,128)(2,1)}, u32[]{:S(2)}, u32[]{:S(2)}) collective-permute-start(bf16[512,128]{1,0:T(8,128)(2,1)} %collective-permute-done.28.refs_8_), channel_id=1, source_target_pairs={{0,16},{16,32},{32,48},{48,0},{64,80},{80,96},{96,112},{112,64},{1... | collective-permute-start | bytes 393224 | tf_op jit(solution)/shard_map/ppermute | solution.py:34
  231.8 2.9 %copy-start.11 = (bf16[512,128]{1,0:T(8,128)(2,1)S(1)}, bf16[512,128]{1,0:T(8,128)(2,1)}, u32[]{:S(2)}) copy-start(bf16[512,128]{1,0:T(8,128)(2,1)} %copy-done.10) | copy-start | bytes 393220
  (17 other events, 21.7 us)

commit v9 on v7

--- a/solution.py
+++ b/solution.py
@@ -19,6 +19,13 @@
     n = lax.axis_size(axis)
     spread = jnp.broadcast_to(piece[None], (n, *piece.shape))
     return lax.all_to_all(spread, axis, 0, 0, tiled=True)
+
+
+def y_slots(piece):
+    n = lax.axis_size("y")
+    return jnp.stack(
+        [piece] + [lax.ppermute(piece, "y", [(i, (i + by) % n) for i in range(n)]) for by in range(1, n)]
+    )
 
 
 def turn(piece, by):
@@ -50,6 +57,8 @@
         rows = jnp.where(odd == n // 2, even, other)
         back = 2 * step + (odd if n < 2 else 1 - odd)
         at = place[3] + (turned + 2 * CUBE - back) % CUBE // 2
+        if n < 2:
+            at = (place[4] + CUBE - at) % CUBE
         block = piece[at, at_rows[n] * 2 * depth : (at_rows[n] + 1) * 2 * depth, :]
         part = jnp.dot(block, rows, preferred_element_type=jnp.float32)
         total = part if total is None else total + part
@@ -98,6 +107,8 @@
         first = 2 * (half if n < 2 else 1 - half) + (core if n % 2 == 0 else 1 - core)
         rights.append(b_ref[pl.ds(pl.multiple_of(first * depth, depth), depth), :])
         at = place[3] + pl.program_id(0) if piece.shape[0] > 1 else 0
+        if n < 2:
+            at = (place[4] + CUBE - at) % CUBE
         start = at_rows[n] * 2 * depth if piece.shape[1] > 2 * depth else 0
         lefts.append(piece[at, start : start + 2 * depth, :])
     total = jnp.dot(
@@ -163,9 +174,10 @@
 def per_device(grad, left_root, right_root, momentum, weights):
     half, core, row = (lax.axis_index(a).astype(jnp.int32) for a in ("z_hi", "core", "row"))
     upper = row // CUBE
-    every = jnp.stack((half, core, row % CUBE, 0 * upper))
-    near = jnp.stack((half, core, row % CUBE, 2 * upper))
-    far = jnp.stack((half, core, row % CUBE, 2 - 2 * upper))
+    y = lax.axis_index("y").astype(jnp.int32)
+    every = jnp.stack((half, core, row % CUBE, 0 * upper, y))
+    near = jnp.stack((half, core, row % CUBE, 2 * upper, y))
+    far = jnp.stack((half, core, row % CUBE, 2 - 2 * upper, y))
     quarter = lax.axis_index("quarter")
     quarters = lax.axis_size("quarter")
     rows, depth = left_root.shape
@@ -174,13 +186,19 @@
 
     right_panel = lax.all_gather(right_root, "row", axis=0, tiled=True)
     left_part = lax.dynamic_slice_in_dim(left_root, quarter * part, part, 0)
-    cut = (rows + part) // 2
-    top = lax.ppermute(grad[:cut], "z_hi", SWAP)
-    bottom = lax.ppermute(jnp.concatenate((grad[cut:], left_part)), "z_hi", SWAP)
-    mine = with_partner(copies_to_all(jnp.concatenate((grad, left_root)), "y"))
-    grad_theirs = copies_to_all(jnp.concatenate((top, bottom[: rows - cut])), "y")
+    cuts = (0, 3 * rows // 8, 3 * rows // 4, rows)
+    crossed = []
+    for start, end in zip(cuts[:-1], cuts[1:], strict=True):
+        piece = grad[start:end]
+        if end == rows:
+            piece = jnp.concatenate((piece, left_part))
+        crossed.append(lax.ppermute(piece, "z_hi", SWAP))
+    crossed = jnp.concatenate(crossed)
+    mine = y_slots(jnp.concatenate((grad, left_root)))
+    mine = with_partner(mine)
+    grad_theirs = copies_to_all(crossed[:rows], "y")
     panel = mine + with_partner(grad_theirs)
-    _, left_part = lax.optimization_barrier((grad_theirs, bottom[rows - cut :]))
+    _, left_part = lax.optimization_barrier((grad_theirs, crossed[rows:]))
     left_other = copies_to_all(left_part, "quarter").reshape(rows, depth)
 
     mixed, *parts = mix(every, panel, (0, 0, 0, 0), right_panel, jnp.bfloat16, 2)

time: 212 us -> 231 us (1.090)
  starting transfers between devices: 69.5 us -> 82.5 us
    ppermute x2 -> x6, starting transfers between devices: 16.7 us -> 41.9 us  [the longest x3 31.6 us: per_device(): crossed.append(lax.ppermute(piece, 'z_hi', SWAP))]
    ppermute x2, waiting for transfers between devices: 19.8 us -> 26.8 us  [across(): return lax.ppermute(piece, 'row', [(i, i ^ CUBE) for i in range(rows)])]
    all_gather x1, waiting for transfers between devices: 6.88 us -> 0.02 us  [per_device(): right_panel = lax.all_gather(right_root, 'row', axis=0, tiled=True)]
    ppermute x6, starting transfers between devices: 23.8 us -> 17.4 us  [turn(): return lax.ppermute(piece, 'row', pairs)]
    all_to_all x3 -> x2, starting transfers between devices: 13.4 us -> 7.66 us  [copies_to_all(): return lax.all_to_all(spread, axis, 0, 0, tiled=True)]
    ppermute x2 -> x6, waiting for transfers between devices: 28.9 us -> 33.1 us  [the longest x3 27 us: per_device(): crossed.append(lax.ppermute(piece, 'z_hi', SWAP))]
    all_to_all x3 -> x2, waiting for transfers between devices: 19.9 us -> 15.8 us  [copies_to_all(): return lax.all_to_all(spread, axis, 0, 0, tiled=True)]
    all_to_all x1, blocking collectives: 15.2 us -> 17.9 us  [copies_to_all(): return lax.all_to_all(spread, axis, 0, 0, tiled=True)]
  transfers between devices with their start and end apart: 18 -> 21, of which waited for: 8 -> 9; matrix products, arithmetic and copies ran while one was open for 1% -> 2% of each run, Pallas kernels for 4% -> 4%
where the time goes in v9:
time: 231 us; the launch traced here: 230 us
  starting transfers between devices  82.5 us (36%)
  waiting for transfers between devices  80.2 us (35%)
  blocking collectives  28.4 us (12%)
  between operations  14.3 us (6%)
  Pallas kernels  13.1 us (6%)
  local copies, waits for them, and re-layouts  8.47 us (4%)
  other arithmetic  2.63 us (1%)
    ppermute x3, starting transfers between devices, per_device(): crossed.append(lax.ppermute(piece, 'z_hi', SWAP))  31.6 us
    ppermute x3, waiting for transfers between devices, per_device(): crossed.append(lax.ppermute(piece, 'z_hi', SWAP))  27 us
    ppermute x2, waiting for transfers between devices, across(): return lax.ppermute(piece, 'row', [(i, i ^ CUBE) for i in range(rows)])  26.8 us
    all_to_all x1, blocking collectives, copies_to_all(): return lax.all_to_all(spread, axis, 0, 0, tiled=True)  17.9 us
    ppermute x6, starting transfers between devices, turn(): return lax.ppermute(piece, 'row', pairs)  17.4 us
    all_to_all x2, waiting for transfers between devices, copies_to_all(): return lax.all_to_all(spread, axis, 0, 0, tiled=True)  15.8 us
    all_to_all x1, blocking collectives, per_device(): lax.all_to_all(updated.reshape(quarters, part, depth), 'quarter', 0, 0, t...  10.5 us
    ppermute x3, starting transfers between devices, y_slots(): lax.ppermute(piece, 'y', [(i, (i + by) % n) for i in range(n)])  10.3 us
  transfers between devices with their start and end apart: 21, of which 9 were waited for; matrix products, arithmetic and copies ran while one was open for 2% of the time, Pallas kernels for 4%

profile of v9, /device:TPU:32, one launch (start us, length us, event | category | flops | bytes accessed | tf_op | source)
XLA Modules:
  0.0 229.7 jit_solution(12513682623765199673)
XLA Ops:
  7.2 0.7 all-gather.6.cloned.1.call-update
  7.9 1.1 fusion
  9.0 4.9 %collective-permute-start.2 = (bf16[1024,256]{1,0:T(8,128)(2,1)S(1)}, bf16[1024,256]{1,0:T(8,128)(2,1)S(1)}, u32[]{:S(2)}, u32[]{:S(2)}) collective-permute-start(bf16[1024,256]{1,0:T(8,128)(2,1)S(1)} %get-tuple-element.23), channel_id=1, source_target_pairs={{0,12},{4,0},{8,4},{12,8},{1,13},{5,1},{9,5},{13,9},{2,14},{6,2},{... | collective-permute-start | bytes 1572872 | tf_op jit(solution)/shard_map/ppermute | solution.py:27
  13.9 2.5 %collective-permute-start.1 = (bf16[1024,256]{1,0:T(8,128)(2,1)S(1)}, bf16[1024,256]{1,0:T(8,128)(2,1)S(1)}, u32[]{:S(2)}, u32[]{:S(2)}) collective-permute-start(bf16[1024,256]{1,0:T(8,128)(2,1)S(1)} %get-tuple-element.23), channel_id=1, source_target_pairs={{0,8},{4,12},{8,0},{12,4},{1,9},{5,13},{9,1},{13,5},{2,10},{6,14},... | collective-permute-start | bytes 1572872 | tf_op jit(solution)/shard_map/ppermute | solution.py:27
  16.5 2.9 %collective-permute-start = (bf16[1024,256]{1,0:T(8,128)(2,1)S(1)}, bf16[1024,256]{1,0:T(8,128)(2,1)S(1)}, u32[]{:S(2)}, u32[]{:S(2)}) collective-permute-start(bf16[1024,256]{1,0:T(8,128)(2,1)S(1)} %get-tuple-element.23), channel_id=1, source_target_pairs={{0,4},{4,8},{8,12},{12,0},{1,5},{5,9},{9,13},{13,1},{2,6},{6,10},{... | collective-permute-start | bytes 1572872 | tf_op jit(solution)/shard_map/ppermute | solution.py:27
  19.4 0.8 constant_dynamic-slice_fusion
  20.2 0.8 slice_bitcast_fusion.2
  21.1 14.8 %collective-permute-start.6 = (bf16[256,256]{1,0:T(8,128)(2,1)S(1)}, bf16[256,256]{1,0:T(8,128)(2,1)S(1)}, u32[]{:S(2)}, u32[]{:S(2)}) collective-permute-start(bf16[256,256]{1,0:T(8,128)(2,1)S(1)} %pad_maximum_fusion.4), channel_id=1, source_target_pairs={{0,2},{2,0},{1,3},{3,1},{4,6},{6,4},{5,7},{7,5},{8,10},{10,8},{9,1... | collective-permute-start | bytes 393224 | tf_op jit(solution)/shard_map/ppermute | solution.py:195
  35.9 0.4 collective-permute-done.2
  36.3 5.6 %collective-permute-done = bf16[1024,256]{1,0:T(8,128)(2,1)S(1)} collective-permute-done((bf16[1024,256]{1,0:T(8,128)(2,1)S(1)}, bf16[1024,256]{1,0:T(8,128)(2,1)S(1)}, u32[]{:S(2)}, u32[]{:S(2)}) %collective-permute-start) | collective-permute-done | bytes 524320 | tf_op jit(solution)/shard_map/ppermute | solution.py:27
  42.0 0.8 copy-done.6
  42.7 1.5 pad_maximum_fusion.a0.refs_0_
  44.2 1.9 collective-permute-start.3
  46.2 14.8 %collective-permute-start.5 = (bf16[192,256]{1,0:T(8,128)(2,1)S(1)}, bf16[192,256]{1,0:T(8,128)(2,1)S(1)}, u32[]{:S(2)}, u32[]{:S(2)}) collective-permute-start(bf16[192,256]{1,0:T(8,128)(2,1)S(1)} %get-tuple-element.25), channel_id=1, source_target_pairs={{0,2},{2,0},{1,3},{3,1},{4,6},{6,4},{5,7},{7,5},{8,10},{10,8},{9,1... | collective-permute-start | bytes 294920 | tf_op jit(solution)/shard_map/ppermute | solution.py:195
  61.1 1.9 collective-permute-start.4
  63.0 13.4 %collective-permute-done.5 = bf16[192,256]{1,0:T(8,128)(2,1)S(1)} collective-permute-done((bf16[192,256]{1,0:T(8,128)(2,1)S(1)}, bf16[192,256]{1,0:T(8,128)(2,1)S(1)}, u32[]{:S(2)}, u32[]{:S(2)}) %collective-permute-start.5) | collective-permute-done | bytes 98336 | tf_op jit(solution)/shard_map/ppermute | solution.py:195
  76.4 13.6 %collective-permute-done.4 = bf16[192,256]{1,0:T(8,128)(2,1)S(1)} collective-permute-done((bf16[192,256]{1,0:T(8,128)(2,1)S(1)}, bf16[192,256]{1,0:T(8,128)(2,1)S(1)}, u32[]{:S(2)}, u32[]{:S(2)}) %collective-permute-start.4) | collective-permute-done | bytes 98336 | tf_op jit(solution)/shard_map/ppermute | solution.py:195
  90.1 17.9 %all_to_all.20.a2 = bf16[4,512,256]{2,1,0:T(8,128)(2,1)S(1)} all-to-all(bf16[4,512,256]{2,1,0:T(8,128)(2,1)S(1)} %broadcast_in_dim.8), channel_id=1, replica_groups=mesh['quarter'=4,'row'=8,'y'=4,'z_hi'=2,'core'=2] {'y'}, dimensions={0} | all-to-all | bytes 2097152 | tf_op jit(solution)/shard_map/all_to_all | solution.py:21
  108.0 1.9 collective-permute-start.7
  110.0 0.7 broadcast_in_dim.9
  110.7 4.1 %all-to-all-start.1 = ((bf16[4,128,256]{2,1,0:T(8,128)(2,1)}), bf16[4,128,256]{2,1,0:T(8,128)(2,1)}, u32[]{:S(2)}, u32[]{:S(2)}) async-start(bf16[4,128,256]{2,1,0:T(8,128)(2,1)} %broadcast_in_dim.9), calls=%async_computation.1 | async-start | bytes 524288 | tf_op jit(solution)/shard_map/all_to_all | solution.py:21
  114.8 0.1 stack.61.place
  115.0 5.9 %shard_map.68 = (bf16[512,256]{1,0:T(8,128)(2,1)}, bf16[512,128]{1,0:T(8,128)(2,1)S(1)}, bf16[512,128]{1,0:T(8,128)(2,1)}) custom-call(s32[5]{0:T(128)S(1)} %stack.61.place, bf16[4,1024,256]{2,1,0:T(8,128)(2,1)S(1)} %pad_maximum_fusion.a0.refs_0_, bf16[4,1024,256]{2,1,0:T(8,128)(2,1)} %collective-permute-done.3.a1.refs_1_, ...), custom_call_target="tpu_custom_call" | custom-call | flops 1073741824 | bytes 6291456 | tf_op jit(solution)/shard_map/pallas_call | solution.py:147
  120.9 1.5 all-to-all-done.1
  122.4 2.0 broadcast_in_dim.10
  124.4 3.5 %all-to-all-start.2 = ((bf16[4,512,256]{2,1,0:T(8,128)(2,1)}), bf16[4,512,256]{2,1,0:T(8,128)(2,1)S(1)}, u32[]{:S(2)}, u32[]{:S(2)}) async-start(bf16[4,512,256]{2,1,0:T(8,128)(2,1)} %broadcast_in_dim.10), calls=%async_computation.2 | async-start | bytes 2097152 | tf_op jit(solution)/shard_map/all_to_all | solution.py:21
  128.0 0.7 all-gather.4.cloned.1.call-update
  128.7 14.2 %all-to-all-done.2.a2.refs_2_ = bf16[4,512,256]{2,1,0:T(8,128)(2,1)S(1)} async-done(((bf16[4,512,256]{2,1,0:T(8,128)(2,1)}), bf16[4,512,256]{2,1,0:T(8,128)(2,1)S(1)}, u32[]{:S(2)}, u32[]{:S(2)}) %all-to-all-start.2) | async-done | bytes 1048608 | tf_op jit(solution)/shard_map/all_to_all | solution.py:21
  142.9 1.9 collective-permute-start.8
  144.8 1.9 collective-permute-start.9
  146.8 7.8 %collective-permute-start.13 = (bf16[512,128]{1,0:T(8,128)(2,1)}, bf16[512,128]{1,0:T(8,128)(2,1)S(1)}, u32[]{:S(2)}, u32[]{:S(2)}) collective-permute-start(bf16[512,128]{1,0:T(8,128)(2,1)} %get-tuple-element.18), channel_id=1, source_target_pairs={{0,64},{16,80},{32,96},{48,112},{64,0},{80,16},{96,32},{112,48},{1... | collective-permute-start | bytes 393224 | tf_op jit(solution)/shard_map/ppermute | solution.py:39
  154.6 25.8 %collective-permute-done.9.refs_4_ = bf16[512,128]{1,0:T(8,128)(2,1)S(1)} collective-permute-done((bf16[512,128]{1,0:T(8,128)(2,1)S(1)}, bf16[512,128]{1,0:T(8,128)(2,1)S(1)}, u32[]{:S(2)}, u32[]{:S(2)}) %collective-permute-start.9) | collective-permute-done | bytes 131104 | tf_op jit(solution)/shard_map/ppermute | solution.py:39
  180.4 1.9 collective-permute-start.10
  182.3 1.9 collective-permute-start.11
  184.3 3.9 %collective-permute-start.12 = (bf16[512,128]{1,0:T(8,128)(2,1)S(1)}, bf16[512,128]{1,0:T(8,128)(2,1)}, u32[]{:S(2)}, u32[]{:S(2)}) collective-permute-start(bf16[512,128]{1,0:T(8,128)(2,1)S(1)} %collective-permute-done.9.refs_4_), channel_id=1, source_target_pairs={{0,48},{16,0},{32,16},{48,32},{64,112},{80,64},{96,80},{112,96},{1... | collective-permute-start | bytes 393224 | tf_op jit(solution)/shard_map/ppermute | solution.py:34
  188.2 1.0 collective-permute-done.13.refs_8_
  189.2 2.4 %collective-permute-start.14 = (bf16[512,128]{1,0:T(8,128)(2,1)S(1)}, bf16[512,128]{1,0:T(8,128)(2,1)}, u32[]{:S(2)}, u32[]{:S(2)}) collective-permute-start(bf16[512,128]{1,0:T(8,128)(2,1)S(1)} %collective-permute-done.13.refs_8_), channel_id=1, source_target_pairs={{0,16},{16,32},{32,48},{48,0},{64,80},{80,96},{96,112},{112,64},{1... | collective-permute-start | bytes 393224 | tf_op jit(solution)/shard_map/ppermute | solution.py:34
  191.6 5.2 %collective-permute-start.15 = (bf16[512,128]{1,0:T(8,128)(2,1)S(1)}, bf16[512,128]{1,0:T(8,128)(2,1)}, u32[]{:S(2)}, u32[]{:S(2)}) collective-permute-start(bf16[512,128]{1,0:T(8,128)(2,1)S(1)} %collective-permute-done.13.refs_8_), channel_id=1, source_target_pairs={{0,32},{16,48},{32,0},{48,16},{64,96},{80,112},{96,64},{112,80},{1... | collective-permute-start | bytes 393224 | tf_op jit(solution)/shard_map/ppermute | solution.py:34
  196.8 1.0 copy-done
  197.8 2.1 collective-permute-start.16
  199.9 0.1 stack.55.place
  200.0 0.1 stack.63.place
  200.1 1.2 copy-done.1
  201.3 3.3 %shard_map.69.refs_12_ = f32[512,256]{1,0:T(8,128)S(1)} custom-call(s32[5]{0:T(128)S(1)} %stack.63.place, bf16[4,1024,256]{2,1,0:T(8,128)(2,1)S(1)} %pad_maximum_fusion.a0.refs_0_, bf16[4,1024,256]{2,1,0:T(8,128)(2,1)} %collective-permute-done.3.a1.refs_1_, bf16[4,512,256]{2,1,0:T(8,128)(2,1)S(1)} %all-to-all-done.2.a2.refs_2_, ...), custom_call_target="tpu_custom_call" | custom-call | flops 536870912 | bytes 3145728 | tf_op jit(solution)/shard_map/pallas_call | solution.py:147
  204.7 3.1 %collective-permute-done.16.refs_11_ = bf16[512,128]{1,0:T(8,128)(2,1)} collective-permute-done((bf16[512,128]{1,0:T(8,128)(2,1)S(1)}, bf16[512,128]{1,0:T(8,128)(2,1)}, u32[]{:S(2)}, u32[]{:S(2)}) %collective-permute-start.16) | collective-permute-done | bytes 131104 | tf_op jit(solution)/shard_map/ppermute | solution.py:34
  207.8 3.8 %update.1 = (f32[512,256]{1,0:T(8,128)}, bf16[512,256]{1,0:T(8,128)(2,1)S(1)}) custom-call(s32[5]{0:T(128)S(1)} %stack.55.place, bf16[4,1024,256]{2,1,0:T(8,128)(2,1)S(1)} %pad_maximum_fusion.a0.refs_0_, bf16[4,1024,256]{2,1,0:T(8,128)(2,1)} %collective-permute-done.3.a1.refs_1_, bf16[4,512,256]{2,1,0:T(8,128)(2,1)S(1)} %all-to-all-done.2.a2.refs_2_, ...), custom_call_target="tpu_custom_call" | custom-call | flops 536870912 | bytes 4980736 | tf_op jit(solution)/shard_map/update/pallas_call | solution.py:84
  211.6 10.5 %all_to_all.21 = bf16[4,128,256]{2,1,0:T(8,128)(2,1)S(1)} all-to-all(bf16[4,128,256]{2,1,0:T(8,128)(2,1)S(1)} %bitcast.26), channel_id=1, replica_groups=mesh['quarter'=4,'row'=8,'y'=4,'z_hi'=2,'core'=2] {'quarter'}, dimensions={0} | all-to-all | bytes 524288 | tf_op jit(solution)/shard_map/all_to_all | solution.py:218
  222.1 0.7 copy.8
  (30 shorter events, 0.3 us)
Async XLA Ops:
  7.2 107.8 %all-gather.6.cloned.1.call-start = ((), (), s32[]{:S(2)}) async-start(), calls=%async_computation.5 | async-start | bytes 2359296 | tf_op jit(solution)/shard_map/all_gather | solution.py:187
  9.0 27.3 %collective-permute-start.2 = (bf16[1024,256]{1,0:T(8,128)(2,1)S(1)}, bf16[1024,256]{1,0:T(8,128)(2,1)S(1)}, u32[]{:S(2)}, u32[]{:S(2)}) collective-permute-start(bf16[1024,256]{1,0:T(8,128)(2,1)S(1)} %get-tuple-element.23), channel_id=1, source_target_pairs={{0,12},{4,0},{8,4},{12,8},{1,13},{5,1},{9,5},{13,9},{2,14},{6,2},{... | collective-permute-start | bytes 1572872 | tf_op jit(solution)/shard_map/ppermute | solution.py:27
  13.9 22.4 %collective-permute-start.1 = (bf16[1024,256]{1,0:T(8,128)(2,1)S(1)}, bf16[1024,256]{1,0:T(8,128)(2,1)S(1)}, u32[]{:S(2)}, u32[]{:S(2)}) collective-permute-start(bf16[1024,256]{1,0:T(8,128)(2,1)S(1)} %get-tuple-element.23), channel_id=1, source_target_pairs={{0,8},{4,12},{8,0},{12,4},{1,9},{5,13},{9,1},{13,5},{2,10},{6,14},... | collective-permute-start | bytes 1572872 | tf_op jit(solution)/shard_map/ppermute | solution.py:27
  16.5 25.5 %collective-permute-start = (bf16[1024,256]{1,0:T(8,128)(2,1)S(1)}, bf16[1024,256]{1,0:T(8,128)(2,1)S(1)}, u32[]{:S(2)}, u32[]{:S(2)}) collective-permute-start(bf16[1024,256]{1,0:T(8,128)(2,1)S(1)} %get-tuple-element.23), channel_id=1, source_target_pairs={{0,4},{4,8},{8,12},{12,0},{1,5},{5,9},{9,13},{13,1},{2,6},{6,10},{... | collective-permute-start | bytes 1572872 | tf_op jit(solution)/shard_map/ppermute | solution.py:27
  21.1 69.0 %collective-permute-start.6 = (bf16[256,256]{1,0:T(8,128)(2,1)S(1)}, bf16[256,256]{1,0:T(8,128)(2,1)S(1)}, u32[]{:S(2)}, u32[]{:S(2)}) collective-permute-start(bf16[256,256]{1,0:T(8,128)(2,1)S(1)} %pad_maximum_fusion.4), channel_id=1, source_target_pairs={{0,2},{2,0},{1,3},{3,1},{4,6},{6,4},{5,7},{7,5},{8,10},{10,8},{9,1... | collective-permute-start | bytes 393224 | tf_op jit(solution)/shard_map/ppermute | solution.py:195
  36.3 5.6 %copy-start.5 = (bf16[1024,256]{1,0:T(8,128)(2,1)}, bf16[1024,256]{1,0:T(8,128)(2,1)S(1)}, u32[]{:S(2)}) copy-start(bf16[1024,256]{1,0:T(8,128)(2,1)S(1)} %collective-permute-done.1) | copy-start | bytes 1572868
  41.9 0.8 copy-start.6
  42.7 3.4 %copy-start.4 = (bf16[1,512,256]{2,1,0:T(8,128)(2,1)S(1)}, bf16[1,512,256]{2,1,0:T(8,128)(2,1)}, u32[]{:S(2)}) copy-start(bf16[1,512,256]{2,1,0:T(8,128)(2,1)} %param.5) | copy-start | bytes 786436
  44.2 70.7 %collective-permute-start.3 = (bf16[4,1024,256]{2,1,0:T(8,128)(2,1)S(1)}, bf16[4,1024,256]{2,1,0:T(8,128)(2,1)}, u32[]{:S(2)}, u32[]{:S(2)}) collective-permute-start(bf16[4,1024,256]{2,1,0:T(8,128)(2,1)S(1)} %pad_maximum_fusion.a0.refs_0_), channel_id=1, source_target_pairs={{0,1},{1,0},{2,3},{3,2},{4,5},{5,4},{6,7},{7,6},{8,9},{9,8},{10,11... | collective-permute-start | bytes 6291464 | tf_op jit(solution)/shard_map/ppermute | solution.py:171
  46.2 30.2 %collective-permute-start.5 = (bf16[192,256]{1,0:T(8,128)(2,1)S(1)}, bf16[192,256]{1,0:T(8,128)(2,1)S(1)}, u32[]{:S(2)}, u32[]{:S(2)}) collective-permute-start(bf16[192,256]{1,0:T(8,128)(2,1)S(1)} %get-tuple-element.25), channel_id=1, source_target_pairs={{0,2},{2,0},{1,3},{3,1},{4,6},{6,4},{5,7},{7,5},{8,10},{10,8},{9,1... | collective-permute-start | bytes 294920 | tf_op jit(solution)/shard_map/ppermute | solution.py:195
  61.1 29.0 %collective-permute-start.4 = (bf16[192,256]{1,0:T(8,128)(2,1)S(1)}, bf16[192,256]{1,0:T(8,128)(2,1)S(1)}, u32[]{:S(2)}, u32[]{:S(2)}) collective-permute-start(bf16[192,256]{1,0:T(8,128)(2,1)S(1)} %get-tuple-element.24), channel_id=1, source_target_pairs={{0,2},{2,0},{1,3},{3,1},{4,6},{6,4},{5,7},{7,5},{8,10},{10,8},{9,1... | collective-permute-start | bytes 294920 | tf_op jit(solution)/shard_map/ppermute | solution.py:195
  108.0 6.9 %collective-permute-start.7 = (bf16[4,512,256]{2,1,0:T(8,128)(2,1)S(1)}, bf16[4,512,256]{2,1,0:T(8,128)(2,1)}, u32[]{:S(2)}, u32[]{:S(2)}) collective-permute-start(bf16[4,512,256]{2,1,0:T(8,128)(2,1)S(1)} %all_to_all.20.a2), channel_id=1, source_target_pairs={{0,1},{1,0},{2,3},{3,2},{4,5},{5,4},{6,7},{7,6},{8,9},{9,8},{10,11... | collective-permute-start | bytes 3145736 | tf_op jit(solution)/shard_map/ppermute | solution.py:171
  110.7 11.7 %all-to-all-start.1 = ((bf16[4,128,256]{2,1,0:T(8,128)(2,1)}), bf16[4,128,256]{2,1,0:T(8,128)(2,1)}, u32[]{:S(2)}, u32[]{:S(2)}) async-start(bf16[4,128,256]{2,1,0:T(8,128)(2,1)} %broadcast_in_dim.9), calls=%async_computation.1 | async-start | bytes 524288 | tf_op jit(solution)/shard_map/all_to_all | solution.py:21
  124.4 18.5 %all-to-all-start.2 = ((bf16[4,512,256]{2,1,0:T(8,128)(2,1)}), bf16[4,512,256]{2,1,0:T(8,128)(2,1)S(1)}, u32[]{:S(2)}, u32[]{:S(2)}) async-start(bf16[4,512,256]{2,1,0:T(8,128)(2,1)} %broadcast_in_dim.10), calls=%async_computation.2 | async-start | bytes 2097152 | tf_op jit(solution)/shard_map/all_to_all | solution.py:21
  127.9 72.2 %all-gather.4.cloned.1.call-start = ((), (), s32[]{:S(2)}) async-start(), calls=%async_computation.4 | async-start | bytes 1310720 | tf_op jit(solution)/shard_map/all_gather | solution.py:207
  142.9 53.9 %collective-permute-start.8 = (bf16[4,512,256]{2,1,0:T(8,128)(2,1)S(1)}, bf16[4,512,256]{2,1,0:T(8,128)(2,1)S(1)}, u32[]{:S(2)}, u32[]{:S(2)}) collective-permute-start(bf16[4,512,256]{2,1,0:T(8,128)(2,1)S(1)} %all-to-all-done.2.a2.refs_2_), channel_id=1, source_target_pairs={{0,1},{1,0},{2,3},{3,2},{4,5},{5,4},{6,7},{7,6},{8,9},{9,8},{10,11... | collective-permute-start | bytes 3145736 | tf_op jit(solution)/shard_map/ppermute | solution.py:171
  144.8 35.6 %collective-permute-start.9 = (bf16[512,128]{1,0:T(8,128)(2,1)S(1)}, bf16[512,128]{1,0:T(8,128)(2,1)S(1)}, u32[]{:S(2)}, u32[]{:S(2)}) collective-permute-start(bf16[512,128]{1,0:T(8,128)(2,1)S(1)} %get-tuple-element.17), channel_id=1, source_target_pairs={{0,64},{16,80},{32,96},{48,112},{64,0},{80,16},{96,32},{112,48},{1... | collective-permute-start | bytes 393224 | tf_op jit(solution)/shard_map/ppermute | solution.py:39
  146.8 42.5 %collective-permute-start.13 = (bf16[512,128]{1,0:T(8,128)(2,1)}, bf16[512,128]{1,0:T(8,128)(2,1)S(1)}, u32[]{:S(2)}, u32[]{:S(2)}) collective-permute-start(bf16[512,128]{1,0:T(8,128)(2,1)} %get-tuple-element.18), channel_id=1, source_target_pairs={{0,64},{16,80},{32,96},{48,112},{64,0},{80,16},{96,32},{112,48},{1... | collective-permute-start | bytes 393224 | tf_op jit(solution)/shard_map/ppermute | solution.py:39
  180.4 11.2 %collective-permute-start.10 = (bf16[512,128]{1,0:T(8,128)(2,1)S(1)}, bf16[512,128]{1,0:T(8,128)(2,1)S(1)}, u32[]{:S(2)}, u32[]{:S(2)}) collective-permute-start(bf16[512,128]{1,0:T(8,128)(2,1)S(1)} %collective-permute-done.9.refs_4_), channel_id=1, source_target_pairs={{0,16},{16,32},{32,48},{48,0},{64,80},{80,96},{96,112},{112,64},{1... | collective-permute-start | bytes 393224 | tf_op jit(solution)/shard_map/ppermute | solution.py:34
  182.3 22.3 %collective-permute-start.11 = (bf16[512,128]{1,0:T(8,128)(2,1)S(1)}, bf16[512,128]{1,0:T(8,128)(2,1)}, u32[]{:S(2)}, u32[]{:S(2)}) collective-permute-start(bf16[512,128]{1,0:T(8,128)(2,1)S(1)} %collective-permute-done.9.refs_4_), channel_id=1, source_target_pairs={{0,32},{16,48},{32,0},{48,16},{64,96},{80,112},{96,64},{112,80},{1... | collective-permute-start | bytes 393224 | tf_op jit(solution)/shard_map/ppermute | solution.py:34
  184.3 20.4 %collective-permute-start.12 = (bf16[512,128]{1,0:T(8,128)(2,1)S(1)}, bf16[512,128]{1,0:T(8,128)(2,1)}, u32[]{:S(2)}, u32[]{:S(2)}) collective-permute-start(bf16[512,128]{1,0:T(8,128)(2,1)S(1)} %collective-permute-done.9.refs_4_), channel_id=1, source_target_pairs={{0,48},{16,0},{32,16},{48,32},{64,112},{80,64},{96,80},{112,96},{1... | collective-permute-start | bytes 393224 | tf_op jit(solution)/shard_map/ppermute | solution.py:34
  189.2 15.5 %collective-permute-start.14 = (bf16[512,128]{1,0:T(8,128)(2,1)S(1)}, bf16[512,128]{1,0:T(8,128)(2,1)}, u32[]{:S(2)}, u32[]{:S(2)}) collective-permute-start(bf16[512,128]{1,0:T(8,128)(2,1)S(1)} %collective-permute-done.13.refs_8_), channel_id=1, source_target_pairs={{0,16},{16,32},{32,48},{48,0},{64,80},{80,96},{96,112},{112,64},{1... | collective-permute-start | bytes 393224 | tf_op jit(solution)/shard_map/ppermute | solution.py:34
  191.6 13.1 %collective-permute-start.15 = (bf16[512,128]{1,0:T(8,128)(2,1)S(1)}, bf16[512,128]{1,0:T(8,128)(2,1)}, u32[]{:S(2)}, u32[]{:S(2)}) collective-permute-start(bf16[512,128]{1,0:T(8,128)(2,1)S(1)} %collective-permute-done.13.refs_8_), channel_id=1, source_target_pairs={{0,32},{16,48},{32,0},{48,16},{64,96},{80,112},{96,64},{112,80},{1... | collective-permute-start | bytes 393224 | tf_op jit(solution)/shard_map/ppermute | solution.py:34
  196.8 1.0 copy-start
  197.8 10.0 %collective-permute-start.16 = (bf16[512,128]{1,0:T(8,128)(2,1)S(1)}, bf16[512,128]{1,0:T(8,128)(2,1)}, u32[]{:S(2)}, u32[]{:S(2)}) collective-permute-start(bf16[512,128]{1,0:T(8,128)(2,1)S(1)} %collective-permute-done.13.refs_8_), channel_id=1, source_target_pairs={{0,48},{16,0},{32,16},{48,32},{64,112},{80,64},{96,80},{112,96},{1... | collective-permute-start | bytes 393224 | tf_op jit(solution)/shard_map/ppermute | solution.py:34
  200.1 1.2 copy-start.1
  201.3 6.5 %copy-start.2 = (f32[1,512,256]{2,1,0:T(8,128)S(1)}, f32[1,512,256]{2,1,0:T(8,128)}, u32[]{:S(2)}) copy-start(f32[1,512,256]{2,1,0:T(8,128)} %param.8) | copy-start | bytes 1572868
  201.3 6.5 %copy-start.3 = (bf16[1,512,256]{2,1,0:T(8,128)(2,1)S(1)}, bf16[1,512,256]{2,1,0:T(8,128)(2,1)}, u32[]{:S(2)}) copy-start(bf16[1,512,256]{2,1,0:T(8,128)(2,1)} %param.9) | copy-start | bytes 786436
Sparse Core Ops, SparseCore 0:
  10.0 92.4 all-gather.5
  131.4 47.9 all-gather.3

commit v10 on v7

--- a/solution.py
+++ b/solution.py
@@ -43,10 +43,7 @@
     total = None
     for n, piece in enumerate(pieces):
         first = pl.multiple_of(depth * (core if n % 2 == 0 else 1 - core), depth)
-        even, other = (
-            jnp.concatenate([part[pl.ds(first, depth), :] for part in slot], axis=1)
-            for slot in slots[2 * step : 2 * step + 2]
-        )
+        even, other = (slot[pl.ds(first, depth), :] for slot in slots[2 * step : 2 * step + 2])
         rows = jnp.where(odd == n // 2, even, other)
         back = 2 * step + (odd if n < 2 else 1 - odd)
         at = place[3] + (turned + 2 * CUBE - back) % CUBE // 2
@@ -57,8 +54,7 @@
 
 
 def update_kernel(at_rows, place, *refs):
-    pieces, parts, (p_ref, m_ref, w_ref, mo_ref, wo_ref) = refs[:4], refs[4 : 4 + 2 * CUBE], refs[4 + 2 * CUBE :]
-    slots = list(zip(parts[:CUBE], parts[CUBE:], strict=True))
+    pieces, slots, (p_ref, m_ref, w_ref, mo_ref, wo_ref) = refs[:4], refs[4 : 4 + CUBE], refs[4 + CUBE :]
     product = p_ref[...]
     for step in range(CUBE // 2):
         product += accumulate(place, step, pieces, at_rows, slots)
@@ -67,10 +63,10 @@
     wo_ref[...] = (w_ref[...].astype(jnp.float32) - step_rate * renewed).astype(wo_ref.dtype)
 
 
-def update(place, pieces, at_rows, low, high, begun, momentum, weights):
+def update(place, pieces, at_rows, slots, begun, momentum, weights):
     depth = pieces[0].shape[-1]
     rows, columns = momentum.shape
-    given = in_vmem([*pieces, *low, *high, begun, momentum, weights])
+    given = in_vmem([*pieces, *slots, begun, momentum, weights])
     moved = 4 * CUBE * rows * depth + 2 * CUBE * rows * columns + 14 * rows * columns
     return pl.pallas_call(
         functools.partial(update_kernel, at_rows),
@@ -174,29 +170,23 @@
 
     right_panel = lax.all_gather(right_root, "row", axis=0, tiled=True)
     left_part = lax.dynamic_slice_in_dim(left_root, quarter * part, part, 0)
-    cut = (rows + part) // 2
-    top = lax.ppermute(grad[:cut], "z_hi", SWAP)
-    bottom = lax.ppermute(jnp.concatenate((grad[cut:], left_part)), "z_hi", SWAP)
+    crossed = lax.ppermute(jnp.concatenate((grad, left_part)), "z_hi", SWAP)
     mine = with_partner(copies_to_all(jnp.concatenate((grad, left_root)), "y"))
-    grad_theirs = copies_to_all(jnp.concatenate((top, bottom[: rows - cut])), "y")
+    grad_theirs = copies_to_all(crossed[:rows], "y")
     panel = mine + with_partner(grad_theirs)
-    _, left_part = lax.optimization_barrier((grad_theirs, bottom[rows - cut :]))
+    _, left_part = lax.optimization_barrier((grad_theirs, crossed[rows:]))
     left_other = copies_to_all(left_part, "quarter").reshape(rows, depth)
 
-    mixed, *parts = mix(every, panel, (0, 0, 0, 0), right_panel, jnp.bfloat16, 2)
-    mixed, parts, left_other = lax.optimization_barrier((mixed, parts, left_other))
+    (mixed,) = mix(every, panel, (0, 0, 0, 0), right_panel, jnp.bfloat16, 0)
+    mixed, left_other = lax.optimization_barrier((mixed, left_other))
     runs = [list(range(i, i + CUBE)) for i in range(0, lax.axis_size("row"), CUBE)]
     near_panel = lax.all_gather(mixed, "row", axis=0, tiled=True, axis_index_groups=runs)
-    others = []
-    for piece in parts:
-        others.append(across(piece))
+    mixed_far = across(mixed)
     left_theirs = copies_to_all(left_other, "y")
     panel = mine + with_partner(left_theirs)
-    slots = []
-    for piece in others:
-        slots.append(far_slots(piece))
+    slots = far_slots(mixed_far)
     (begun,) = mix(near, panel, (1, 1, 0, 0), near_panel, jnp.float32, 0, (3,))
-    renewed, updated = update(far, panel, (1, 1, 0, 0), *slots, begun, momentum[0], weights[0])
+    renewed, updated = update(far, panel, (1, 1, 0, 0), slots, begun, momentum[0], weights[0])
     spread = lax.all_to_all(updated.reshape(quarters, part, depth), "quarter", 0, 0, tiled=True)
     return renewed[None], spread
 

time: 212 us -> 220 us (1.038)
  the two profiles are of different devices: /device:TPU:32 before, /device:TPU:1 now
where the time goes in v10:
time: 220 us; the launch traced here: 219 us
  waiting for transfers between devices  81.3 us (37%)
  starting transfers between devices  78.5 us (36%)
  blocking collectives  25.5 us (12%)
  between operations  14.2 us (6%)
  Pallas kernels  13.5 us (6%)
  local copies, waits for them, and re-layouts  4.88 us (2%)
    ppermute x3, starting transfers between devices, turn(): return lax.ppermute(piece, 'row', pairs)  25.1 us
    ppermute x3, starting transfers between devices, with_partner(): return [mine, lax.ppermute(mine, 'core', SWAP)]  22.5 us
    all_gather x1, waiting for transfers between devices, per_device(): right_panel = lax.all_gather(right_root, 'row', axis=0, tiled=True)  21.6 us
    ppermute x1, waiting for transfers between devices, across(): return lax.ppermute(piece, 'row', [(i, i ^ CUBE) for i in range(rows)])  20.2 us
    all_to_all x1, blocking collectives, copies_to_all(): return lax.all_to_all(spread, axis, 0, 0, tiled=True)  15.9 us
    ppermute x1, starting transfers between devices, per_device(): crossed = lax.ppermute(jnp.concatenate((grad, left_part)), 'z_hi', SWAP)  15.4 us
    ppermute x3, waiting for transfers between devices, turn(): return lax.ppermute(piece, 'row', pairs)  15.1 us
    all_to_all x3, waiting for transfers between devices, copies_to_all(): return lax.all_to_all(spread, axis, 0, 0, tiled=True)  14.7 us
  transfers between devices with their start and end apart: 13, of which 6 were waited for; matrix products, arithmetic and copies ran while one was open for 2% of the time, Pallas kernels for 4%

profile of v10, /device:TPU:1, one launch (start us, length us, event | category | flops | bytes accessed | tf_op | source)
XLA Modules:
  0.0 219.1 jit_solution(9728528967612466805)
XLA Ops:
  7.2 0.0 all-gather.6.cloned.1.call-start
  7.2 0.7 all-gather.6.cloned.1.call-update
  7.9 1.1 pad_maximum_fusion
  9.0 1.5 broadcast_in_dim.10
  10.4 0.0 copy-start.2
  10.4 5.1 %all-to-all-start = ((bf16[4,1024,256]{2,1,0:T(8,128)(2,1)}), bf16[4,1024,256]{2,1,0:T(8,128)(2,1)S(1)}, u32[]{:S(2)}, u32[]{:S(2)}) async-start(bf16[4,1024,256]{2,1,0:T(8,128)(2,1)} %broadcast_in_dim.10), calls=%async_computation | async-start | bytes 4194304 | tf_op jit(solution)/shard_map/all_to_all | solution.py:21
  15.6 0.8 constant_dynamic-slice_fusion
  16.4 0.0 copy-done.2
  16.4 15.4 %collective-permute-start.1 = (bf16[640,256]{1,0:T(8,128)(2,1)S(1)}, bf16[640,256]{1,0:T(8,128)(2,1)S(1)}, u32[]{:S(2)}, u32[]{:S(2)}) collective-permute-start(bf16[640,256]{1,0:T(8,128)(2,1)S(1)} %pad_maximum_fusion.1), channel_id=1, source_target_pairs={{0,2},{2,0},{1,3},{3,1},{4,6},{6,4},{5,7},{7,5},{8,10},{10,8},{9,1... | collective-permute-start | bytes 983048 | tf_op jit(solution)/shard_map/ppermute | solution.py:173
  31.9 4.7 %all-to-all-done.a0.refs_0_ = bf16[4,1024,256]{2,1,0:T(8,128)(2,1)S(1)} async-done(((bf16[4,1024,256]{2,1,0:T(8,128)(2,1)}), bf16[4,1024,256]{2,1,0:T(8,128)(2,1)S(1)}, u32[]{:S(2)}, u32[]{:S(2)}) %all-to-all-start) | async-done | bytes 2097184 | tf_op jit(solution)/shard_map/all_to_all | solution.py:21
  36.6 8.2 %collective-permute-start = (bf16[4,1024,256]{2,1,0:T(8,128)(2,1)S(1)}, bf16[4,1024,256]{2,1,0:T(8,128)(2,1)}, u32[]{:S(2)}, u32[]{:S(2)}) collective-permute-start(bf16[4,1024,256]{2,1,0:T(8,128)(2,1)S(1)} %all-to-all-done.a0.refs_0_), channel_id=1, source_target_pairs={{0,1},{1,0},{2,3},{3,2},{4,5},{5,4},{6,7},{7,6},{8,9},{9,8},{10,11... | collective-permute-start | bytes 6291464 | tf_op jit(solution)/shard_map/ppermute | solution.py:156
  44.8 8.2 %collective-permute-done.1 = bf16[640,256]{1,0:T(8,128)(2,1)S(1)} collective-permute-done((bf16[640,256]{1,0:T(8,128)(2,1)S(1)}, bf16[640,256]{1,0:T(8,128)(2,1)S(1)}, u32[]{:S(2)}, u32[]{:S(2)}) %collective-permute-start.1) | collective-permute-done | bytes 327712 | tf_op jit(solution)/shard_map/ppermute | solution.py:173
  53.0 0.1 broadcast_in_dim.11
  53.1 15.9 %all_to_all.25.a2 = bf16[4,512,256]{2,1,0:T(8,128)(2,1)S(1)} all-to-all(bf16[4,512,256]{2,1,0:T(8,128)(2,1)S(1)} %broadcast_in_dim.11), channel_id=1, replica_groups=mesh['quarter'=4,'row'=8,'y'=4,'z_hi'=2,'core'=2] {'y'}, dimensions={0} | all-to-all | bytes 2097152 | tf_op jit(solution)/shard_map/all_to_all | solution.py:21
  69.0 7.2 %collective-permute-start.2 = (bf16[4,512,256]{2,1,0:T(8,128)(2,1)S(1)}, bf16[4,512,256]{2,1,0:T(8,128)(2,1)}, u32[]{:S(2)}, u32[]{:S(2)}) collective-permute-start(bf16[4,512,256]{2,1,0:T(8,128)(2,1)S(1)} %all_to_all.25.a2), channel_id=1, source_target_pairs={{0,1},{1,0},{2,3},{3,2},{4,5},{5,4},{6,7},{7,6},{8,9},{9,8},{10,11... | collective-permute-start | bytes 3145736 | tf_op jit(solution)/shard_map/ppermute | solution.py:156
  76.2 0.1 pad_add_fusion.3
  76.3 0.7 broadcast_in_dim.12
  77.0 4.0 %all-to-all-start.2 = ((bf16[4,128,256]{2,1,0:T(8,128)(2,1)}), bf16[4,128,256]{2,1,0:T(8,128)(2,1)S(1)}, u32[]{:S(2)}, u32[]{:S(2)}) async-start(bf16[4,128,256]{2,1,0:T(8,128)(2,1)} %broadcast_in_dim.12), calls=%async_computation.2 | async-start | bytes 524288 | tf_op jit(solution)/shard_map/all_to_all | solution.py:21
  81.0 0.1 pad_add_fusion.2
  81.1 0.0 collective-permute-done.2.a3
  81.1 21.6 %all-gather.6.cloned.1.call-done = bf16[1,4096,256]{2,1,0:T(8,128)(2,1)} async-done(((bf16[1,512,256]{2,1,0:T(8,128)(2,1)}), bf16[1,4096,256]{2,1,0:T(8,128)(2,1)}) %all-gather.6.cloned.1.call-update) | async-done | bytes 2097168 | tf_op jit(solution)/shard_map/all_gather | solution.py:171
  102.7 0.0 collective-permute-done.a1.refs_1_
  102.7 5.9 %shard_map.68 = bf16[512,256]{1,0:T(8,128)(2,1)} custom-call(s32[4]{0:T(128)S(1)} %get-tuple-element.14.place, bf16[4,1024,256]{2,1,0:T(8,128)(2,1)S(1)} %all-to-all-done.a0.refs_0_, bf16[4,1024,256]{2,1,0:T(8,128)(2,1)} %collective-permute-done.a1.refs_1_, bf16[4,512,256]{2,1,0:T(8,128)(2,1)S(1)} %all_to_all.25.a2, ...), custom_call_target="tpu_custom_call" | custom-call | flops 1073741824 | bytes 6291456 | tf_op jit(solution)/shard_map/pallas_call | solution.py:132
  108.5 0.0 all-to-all-done.2
  108.5 1.0 broadcast_in_dim.13
  109.6 4.2 %all-to-all-start.3 = ((bf16[4,512,256]{2,1,0:T(8,128)(2,1)}), bf16[4,512,256]{2,1,0:T(8,128)(2,1)S(1)}, u32[]{:S(2)}, u32[]{:S(2)}) async-start(bf16[4,512,256]{2,1,0:T(8,128)(2,1)} %broadcast_in_dim.13), calls=%async_computation.3 | async-start | bytes 2097152 | tf_op jit(solution)/shard_map/all_to_all | solution.py:21
  113.8 0.0 all-gather.4.cloned.1.call-start
  113.8 0.7 all-gather.4.cloned.1.call-update
  114.5 10.0 %all-to-all-done.3.a2.refs_2_ = bf16[4,512,256]{2,1,0:T(8,128)(2,1)S(1)} async-done(((bf16[4,512,256]{2,1,0:T(8,128)(2,1)}), bf16[4,512,256]{2,1,0:T(8,128)(2,1)S(1)}, u32[]{:S(2)}, u32[]{:S(2)}) %all-to-all-start.3) | async-done | bytes 1048608 | tf_op jit(solution)/shard_map/all_to_all | solution.py:21
  124.5 7.2 %collective-permute-start.3 = (bf16[4,512,256]{2,1,0:T(8,128)(2,1)S(1)}, bf16[4,512,256]{2,1,0:T(8,128)(2,1)}, u32[]{:S(2)}, u32[]{:S(2)}) collective-permute-start(bf16[4,512,256]{2,1,0:T(8,128)(2,1)S(1)} %all-to-all-done.3.a2.refs_2_), channel_id=1, source_target_pairs={{0,1},{1,0},{2,3},{3,2},{4,5},{5,4},{6,7},{7,6},{8,9},{9,8},{10,11... | collective-permute-start | bytes 3145736 | tf_op jit(solution)/shard_map/ppermute | solution.py:156
  131.7 2.1 collective-permute-start.4
  133.8 20.2 %collective-permute-done.4.refs_4_ = bf16[512,256]{1,0:T(8,128)(2,1)S(1)} collective-permute-done((bf16[512,256]{1,0:T(8,128)(2,1)}, bf16[512,256]{1,0:T(8,128)(2,1)S(1)}, u32[]{:S(2)}, u32[]{:S(2)}) %collective-permute-start.4) | collective-permute-done | bytes 262176 | tf_op jit(solution)/shard_map/ppermute | solution.py:32
  154.0 1.9 collective-permute-start.7
  155.9 19.9 %collective-permute-start.6 = (bf16[512,256]{1,0:T(8,128)(2,1)S(1)}, bf16[512,256]{1,0:T(8,128)(2,1)}, u32[]{:S(2)}, u32[]{:S(2)}) collective-permute-start(bf16[512,256]{1,0:T(8,128)(2,1)S(1)} %collective-permute-done.4.refs_4_), channel_id=1, source_target_pairs={{0,32},{16,48},{32,0},{48,16},{64,96},{80,112},{96,64},{112,80},{1... | collective-permute-start | bytes 786440 | tf_op jit(solution)/shard_map/ppermute | solution.py:27
  175.8 3.4 %collective-permute-start.5 = (bf16[512,256]{1,0:T(8,128)(2,1)S(1)}, bf16[512,256]{1,0:T(8,128)(2,1)}, u32[]{:S(2)}, u32[]{:S(2)}) collective-permute-start(bf16[512,256]{1,0:T(8,128)(2,1)S(1)} %collective-permute-done.4.refs_4_), channel_id=1, source_target_pairs={{0,16},{16,32},{32,48},{48,0},{64,80},{80,96},{96,112},{112,64},{1... | collective-permute-start | bytes 786440 | tf_op jit(solution)/shard_map/ppermute | solution.py:27
  179.2 0.0 all-gather.4.cloned.1.call-done.b_ref
  179.2 0.0 collective-permute-done.3.a3.refs_3_
  179.2 0.0 copy-start
  179.2 0.0 copy-start.1
  179.2 3.5 %shard_map.69.refs_8_ = f32[512,256]{1,0:T(8,128)S(1)} custom-call(s32[4]{0:T(128)S(1)} %get-tuple-element.12.place, bf16[4,1024,256]{2,1,0:T(8,128)(2,1)S(1)} %all-to-all-done.a0.refs_0_, bf16[4,1024,256]{2,1,0:T(8,128)(2,1)} %collective-permute-done.a1.refs_1_, bf16[4,512,256]{2,1,0:T(8,128)(2,1)S(1)} %all-to-all-done.3.a2.refs_2_, ...), custom_call_target="tpu_custom_call" | custom-call | flops 536870912 | bytes 3145728 | tf_op jit(solution)/shard_map/pallas_call | solution.py:132
  182.7 0.0 collective-permute-done.7.refs_7_
  182.7 15.1 %collective-permute-done.6.refs_6_ = bf16[512,256]{1,0:T(8,128)(2,1)} collective-permute-done((bf16[512,256]{1,0:T(8,128)(2,1)S(1)}, bf16[512,256]{1,0:T(8,128)(2,1)}, u32[]{:S(2)}, u32[]{:S(2)}) %collective-permute-start.6) | collective-permute-done | bytes 262176 | tf_op jit(solution)/shard_map/ppermute | solution.py:27
  197.8 0.0 collective-permute-done.5.refs_5_
  197.8 0.0 copy-done
  197.8 0.0 copy-done.1
  197.8 4.1 %update.1 = (f32[512,256]{1,0:T(8,128)}, bf16[512,256]{1,0:T(8,128)(2,1)S(1)}) custom-call(s32[4]{0:T(128)S(1)} %get-tuple-element.15.place, bf16[4,1024,256]{2,1,0:T(8,128)(2,1)S(1)} %all-to-all-done.a0.refs_0_, bf16[4,1024,256]{2,1,0:T(8,128)(2,1)} %collective-permute-done.a1.refs_1_, bf16[4,512,256]{2,1,0:T(8,128)(2,1)S(1)} %all-to-all-done.3.a2.refs_2_, ...), custom_call_target="tpu_custom_call" | custom-call | flops 536870912 | bytes 4980736 | tf_op jit(solution)/shard_map/update/pallas_call | solution.py:71
  201.9 9.6 %all_to_all.26 = bf16[4,128,256]{2,1,0:T(8,128)(2,1)S(1)} all-to-all(bf16[4,128,256]{2,1,0:T(8,128)(2,1)S(1)} %bitcast.14), channel_id=1, replica_groups=mesh['quarter'=4,'row'=8,'y'=4,'z_hi'=2,'core'=2] {'quarter'}, dimensions={0} | all-to-all | bytes 524288 | tf_op jit(solution)/shard_map/all_to_all | solution.py:190
  211.5 0.7 copy.8
  (3 shorter events, 0.0 us)
Async XLA Ops:
  7.2 95.5 %all-gather.6.cloned.1.call-start = ((), (), s32[]{:S(2)}) async-start(), calls=%async_computation.6 | async-start | bytes 2359296 | tf_op jit(solution)/shard_map/all_gather | solution.py:171
  10.4 6.0 %copy-start.2 = (bf16[1,512,256]{2,1,0:T(8,128)(2,1)S(1)}, bf16[1,512,256]{2,1,0:T(8,128)(2,1)}, u32[]{:S(2)}) copy-start(bf16[1,512,256]{2,1,0:T(8,128)(2,1)} %param.5) | copy-start | bytes 786436
  10.4 26.1 %all-to-all-start = ((bf16[4,1024,256]{2,1,0:T(8,128)(2,1)}), bf16[4,1024,256]{2,1,0:T(8,128)(2,1)S(1)}, u32[]{:S(2)}, u32[]{:S(2)}) async-start(bf16[4,1024,256]{2,1,0:T(8,128)(2,1)} %broadcast_in_dim.10), calls=%async_computation | async-start | bytes 4194304 | tf_op jit(solution)/shard_map/all_to_all | solution.py:21
  16.4 36.5 %collective-permute-start.1 = (bf16[640,256]{1,0:T(8,128)(2,1)S(1)}, bf16[640,256]{1,0:T(8,128)(2,1)S(1)}, u32[]{:S(2)}, u32[]{:S(2)}) collective-permute-start(bf16[640,256]{1,0:T(8,128)(2,1)S(1)} %pad_maximum_fusion.1), channel_id=1, source_target_pairs={{0,2},{2,0},{1,3},{3,1},{4,6},{6,4},{5,7},{7,5},{8,10},{10,8},{9,1... | collective-permute-start | bytes 983048 | tf_op jit(solution)/shard_map/ppermute | solution.py:173
  36.6 66.1 %collective-permute-start = (bf16[4,1024,256]{2,1,0:T(8,128)(2,1)S(1)}, bf16[4,1024,256]{2,1,0:T(8,128)(2,1)}, u32[]{:S(2)}, u32[]{:S(2)}) collective-permute-start(bf16[4,1024,256]{2,1,0:T(8,128)(2,1)S(1)} %all-to-all-done.a0.refs_0_), channel_id=1, source_target_pairs={{0,1},{1,0},{2,3},{3,2},{4,5},{5,4},{6,7},{7,6},{8,9},{9,8},{10,11... | collective-permute-start | bytes 6291464 | tf_op jit(solution)/shard_map/ppermute | solution.py:156
  69.0 12.1 %collective-permute-start.2 = (bf16[4,512,256]{2,1,0:T(8,128)(2,1)S(1)}, bf16[4,512,256]{2,1,0:T(8,128)(2,1)}, u32[]{:S(2)}, u32[]{:S(2)}) collective-permute-start(bf16[4,512,256]{2,1,0:T(8,128)(2,1)S(1)} %all_to_all.25.a2), channel_id=1, source_target_pairs={{0,1},{1,0},{2,3},{3,2},{4,5},{5,4},{6,7},{7,6},{8,9},{9,8},{10,11... | collective-permute-start | bytes 3145736 | tf_op jit(solution)/shard_map/ppermute | solution.py:156
  77.0 31.5 %all-to-all-start.2 = ((bf16[4,128,256]{2,1,0:T(8,128)(2,1)}), bf16[4,128,256]{2,1,0:T(8,128)(2,1)S(1)}, u32[]{:S(2)}, u32[]{:S(2)}) async-start(bf16[4,128,256]{2,1,0:T(8,128)(2,1)} %broadcast_in_dim.12), calls=%async_computation.2 | async-start | bytes 524288 | tf_op jit(solution)/shard_map/all_to_all | solution.py:21
  109.6 15.0 %all-to-all-start.3 = ((bf16[4,512,256]{2,1,0:T(8,128)(2,1)}), bf16[4,512,256]{2,1,0:T(8,128)(2,1)S(1)}, u32[]{:S(2)}, u32[]{:S(2)}) async-start(bf16[4,512,256]{2,1,0:T(8,128)(2,1)} %broadcast_in_dim.13), calls=%async_computation.3 | async-start | bytes 2097152 | tf_op jit(solution)/shard_map/all_to_all | solution.py:21
  113.8 65.4 %all-gather.4.cloned.1.call-start = ((), (), s32[]{:S(2)}) async-start(), calls=%async_computation.5 | async-start | bytes 1310720 | tf_op jit(solution)/shard_map/all_gather | solution.py:183
  124.5 54.7 %collective-permute-start.3 = (bf16[4,512,256]{2,1,0:T(8,128)(2,1)S(1)}, bf16[4,512,256]{2,1,0:T(8,128)(2,1)}, u32[]{:S(2)}, u32[]{:S(2)}) collective-permute-start(bf16[4,512,256]{2,1,0:T(8,128)(2,1)S(1)} %all-to-all-done.3.a2.refs_2_), channel_id=1, source_target_pairs={{0,1},{1,0},{2,3},{3,2},{4,5},{5,4},{6,7},{7,6},{8,9},{9,8},{10,11... | collective-permute-start | bytes 3145736 | tf_op jit(solution)/shard_map/ppermute | solution.py:156
  131.7 22.3 %collective-permute-start.4 = (bf16[512,256]{1,0:T(8,128)(2,1)}, bf16[512,256]{1,0:T(8,128)(2,1)S(1)}, u32[]{:S(2)}, u32[]{:S(2)}) collective-permute-start(bf16[512,256]{1,0:T(8,128)(2,1)} %shard_map.68), channel_id=1, source_target_pairs={{0,64},{16,80},{32,96},{48,112},{64,0},{80,16},{96,32},{112,48},{1... | collective-permute-start | bytes 786440 | tf_op jit(solution)/shard_map/ppermute | solution.py:32
  154.0 28.7 %collective-permute-start.7 = (bf16[512,256]{1,0:T(8,128)(2,1)S(1)}, bf16[512,256]{1,0:T(8,128)(2,1)}, u32[]{:S(2)}, u32[]{:S(2)}) collective-permute-start(bf16[512,256]{1,0:T(8,128)(2,1)S(1)} %collective-permute-done.4.refs_4_), channel_id=1, source_target_pairs={{0,48},{16,0},{32,16},{48,32},{64,112},{80,64},{96,80},{112,96},{1... | collective-permute-start | bytes 786440 | tf_op jit(solution)/shard_map/ppermute | solution.py:27
  155.9 41.9 %collective-permute-start.6 = (bf16[512,256]{1,0:T(8,128)(2,1)S(1)}, bf16[512,256]{1,0:T(8,128)(2,1)}, u32[]{:S(2)}, u32[]{:S(2)}) collective-permute-start(bf16[512,256]{1,0:T(8,128)(2,1)S(1)} %collective-permute-done.4.refs_4_), channel_id=1, source_target_pairs={{0,32},{16,48},{32,0},{48,16},{64,96},{80,112},{96,64},{112,80},{1... | collective-permute-start | bytes 786440 | tf_op jit(solution)/shard_map/ppermute | solution.py:27
  175.8 22.0 %collective-permute-start.5 = (bf16[512,256]{1,0:T(8,128)(2,1)S(1)}, bf16[512,256]{1,0:T(8,128)(2,1)}, u32[]{:S(2)}, u32[]{:S(2)}) collective-permute-start(bf16[512,256]{1,0:T(8,128)(2,1)S(1)} %collective-permute-done.4.refs_4_), channel_id=1, source_target_pairs={{0,16},{16,32},{32,48},{48,0},{64,80},{80,96},{96,112},{112,64},{1... | collective-permute-start | bytes 786440 | tf_op jit(solution)/shard_map/ppermute | solution.py:27
  179.2 18.6 %copy-start = (f32[1,512,256]{2,1,0:T(8,128)S(1)}, f32[1,512,256]{2,1,0:T(8,128)}, u32[]{:S(2)}) copy-start(f32[1,512,256]{2,1,0:T(8,128)} %param.8) | copy-start | bytes 1572868
  179.2 18.6 %copy-start.1 = (bf16[1,512,256]{2,1,0:T(8,128)(2,1)S(1)}, bf16[1,512,256]{2,1,0:T(8,128)(2,1)}, u32[]{:S(2)}) copy-start(bf16[1,512,256]{2,1,0:T(8,128)(2,1)} %param.9) | copy-start | bytes 786436
Sparse Core Ops, SparseCore 0:
  10.0 92.5 all-gather.5
  117.2 57.8 all-gather.3

commit v11 on v7

--- a/solution.py
+++ b/solution.py
@@ -41,17 +41,21 @@
     depth = pieces[0].shape[-1]
     odd = (turned + half) % 2
     total = None
-    for n, piece in enumerate(pieces):
-        first = pl.multiple_of(depth * (core if n % 2 == 0 else 1 - core), depth)
-        even, other = (
-            jnp.concatenate([part[pl.ds(first, depth), :] for part in slot], axis=1)
-            for slot in slots[2 * step : 2 * step + 2]
+    for theirs in range(2):
+        back = 2 * step + (1 - odd if theirs else odd)
+        at = place[3] + (turned + 2 * CUBE - back) % CUBE // 2
+        lefts, rights = [], []
+        for n in range(2 * theirs, 2 * theirs + 2):
+            first = pl.multiple_of(depth * (core if n % 2 == 0 else 1 - core), depth)
+            even, other = (
+                jnp.concatenate([part[pl.ds(first, depth), :] for part in slot], axis=1)
+                for slot in slots[2 * step : 2 * step + 2]
+            )
+            rights.append(jnp.where(odd == theirs, even, other))
+            lefts.append(pieces[n][at, at_rows[n] * 2 * depth : (at_rows[n] + 1) * 2 * depth, :])
+        part = jnp.dot(
+            jnp.concatenate(lefts, axis=1), jnp.concatenate(rights, axis=0), preferred_element_type=jnp.float32
         )
-        rows = jnp.where(odd == n // 2, even, other)
-        back = 2 * step + (odd if n < 2 else 1 - odd)
-        at = place[3] + (turned + 2 * CUBE - back) % CUBE // 2
-        block = piece[at, at_rows[n] * 2 * depth : (at_rows[n] + 1) * 2 * depth, :]
-        part = jnp.dot(block, rows, preferred_element_type=jnp.float32)
         total = part if total is None else total + part
     return total
 
@@ -94,12 +98,15 @@
     depth = a0.shape[-1]
     parts, acc_ref = refs[:-1], refs[-1]
     lefts, rights = [], []
-    for n, piece in enumerate((a0, a1, a2, a3)):
-        first = 2 * (half if n < 2 else 1 - half) + (core if n % 2 == 0 else 1 - core)
-        rights.append(b_ref[pl.ds(pl.multiple_of(first * depth, depth), depth), :])
-        at = place[3] + pl.program_id(0) if piece.shape[0] > 1 else 0
-        start = at_rows[n] * 2 * depth if piece.shape[1] > 2 * depth else 0
-        lefts.append(piece[at, start : start + 2 * depth, :])
+    per_step = b_ref.shape[0] // (4 * depth)
+    for group in range(per_step):
+        for n, piece in enumerate((a0, a1, a2, a3)):
+            first = 4 * group + 2 * (half if n < 2 else 1 - half) + (core if n % 2 == 0 else 1 - core)
+            rights.append(b_ref[pl.ds(pl.multiple_of(first * depth, depth), depth), :])
+            streamed = piece.shape[0] == 1
+            at = 0 if streamed else place[3] + per_step * pl.program_id(0) + group
+            start = 0 if streamed else at_rows[n] * 2 * depth
+            lefts.append(piece[at, start : start + 2 * depth, :])
     total = jnp.dot(
         jnp.concatenate(lefts, axis=1), jnp.concatenate(rights, axis=0), preferred_element_type=jnp.float32
     )
@@ -124,7 +131,9 @@
 def mix(place, pieces, at_rows, right, kind, split, streamed=()):
     depth = pieces[0].shape[-1]
     columns = right.shape[1]
-    steps, rows = right.shape[0] // (4 * depth), 2 * depth
+    rows = 2 * depth
+    steps = right.shape[0] // (4 * depth if streamed else 8 * depth)
+    height = right.shape[0] // steps
 
     def piece_spec(n):
         if n in streamed:
@@ -139,13 +148,13 @@
         grid_spec=pltpu.PrefetchScalarGridSpec(
             num_scalar_prefetch=1,
             grid=(steps,),
-            in_specs=[piece_spec(n) for n in range(4)] + [pl.BlockSpec((4 * depth, columns), lambda i, place: (i, 0))],
+            in_specs=[piece_spec(n) for n in range(4)] + [pl.BlockSpec((height, columns), lambda i, place: (i, 0))],
             out_specs=[pl.BlockSpec((rows, width), lambda i, place: (0, 0)) for width in widths],
             scratch_shapes=[pltpu.VMEM((rows, columns), jnp.float32)],
         ),
         cost_estimate=pl.CostEstimate(
             flops=2 * rows * right.size,
-            bytes_accessed=2 * (4 * steps * rows * depth + right.size),
+            bytes_accessed=2 * (right.shape[0] * rows + right.size),
             transcendentals=0,
         ),
         compiler_params=pltpu.CompilerParams(vmem_limit_bytes=KERNEL_VMEM),

time: 212 us -> 211 us (level)
  no operation moved by 1% of the time
where the time goes in v11:
time: 211 us
  waiting for transfers between devices  79.6 us (38%)
  starting transfers between devices  69.5 us (33%)
  blocking collectives  26.6 us (13%)
  between operations  14.3 us (7%)
  Pallas kernels  12.3 us (6%)
  local copies, waits for them, and re-layouts  7.1 us (3%)
    ppermute x6, starting transfers between devices, turn(): return lax.ppermute(piece, 'row', pairs)  23.8 us
    all_to_all x3, waiting for transfers between devices, copies_to_all(): return lax.all_to_all(spread, axis, 0, 0, tiled=True)  19.9 us
    ppermute x2, waiting for transfers between devices, across(): return lax.ppermute(piece, 'row', [(i, i ^ CUBE) for i in range(rows)])  19.8 us
    ppermute x1, waiting for transfers between devices, per_device(): top = lax.ppermute(grad[:cut], 'z_hi', SWAP)  15.4 us
    all_to_all x1, blocking collectives, copies_to_all(): return lax.all_to_all(spread, axis, 0, 0, tiled=True)  15.2 us
    ppermute x1, starting transfers between devices, per_device(): lax.ppermute(jnp.concatenate((grad[cut:], left_part)), 'z_hi', SWAP)  14.8 us
    ppermute x1, waiting for transfers between devices, per_device(): lax.ppermute(jnp.concatenate((grad[cut:], left_part)), 'z_hi', SWAP)  13.6 us
    all_to_all x3, starting transfers between devices, copies_to_all(): return lax.all_to_all(spread, axis, 0, 0, tiled=True)  13.4 us
  transfers between devices with their start and end apart: 18, of which 8 were waited for; matrix products, arithmetic and copies ran while one was open for 1% of the time, Pallas kernels for 4%

profile of v11, /device:TPU:32, one launch (start us, length us, event | category | flops | bytes accessed | tf_op | source)
XLA Modules:
  0.0 210.5 jit_solution(4268572017559450240)
XLA Ops:
  7.2 1.1 pad_maximum_fusion
  8.2 1.5 broadcast_in_dim.10
  9.7 4.6 %all-to-all-start = ((bf16[4,1024,256]{2,1,0:T(8,128)(2,1)}), bf16[4,1024,256]{2,1,0:T(8,128)(2,1)S(1)}, u32[]{:S(2)}, u32[]{:S(2)}) async-start(bf16[4,1024,256]{2,1,0:T(8,128)(2,1)} %broadcast_in_dim.10), calls=%async_computation | async-start | bytes 4194304 | tf_op jit(solution)/shard_map/all_to_all | solution.py:21
  14.3 0.7 all-gather.6.cloned.1.call-update
  15.0 0.8 constant_dynamic-slice_fusion
  15.9 14.8 %collective-permute-start.2 = (bf16[320,256]{1,0:T(8,128)(2,1)S(1)}, bf16[320,256]{1,0:T(8,128)(2,1)S(1)}, u32[]{:S(2)}, u32[]{:S(2)}) collective-permute-start(bf16[320,256]{1,0:T(8,128)(2,1)S(1)} %pad_maximum_fusion.2), channel_id=1, source_target_pairs={{0,2},{2,0},{1,3},{3,1},{4,6},{6,4},{5,7},{7,5},{8,10},{10,8},{9,1... | collective-permute-start | bytes 491528 | tf_op jit(solution)/shard_map/ppermute | solution.py:188
  30.8 1.9 collective-permute-start.1
  32.7 7.9 %all-to-all-done.a0.refs_0_ = bf16[4,1024,256]{2,1,0:T(8,128)(2,1)S(1)} async-done(((bf16[4,1024,256]{2,1,0:T(8,128)(2,1)}), bf16[4,1024,256]{2,1,0:T(8,128)(2,1)S(1)}, u32[]{:S(2)}, u32[]{:S(2)}) %all-to-all-start) | async-done | bytes 2097184 | tf_op jit(solution)/shard_map/all_to_all | solution.py:21
  40.7 1.9 collective-permute-start
  42.6 13.6 %collective-permute-done.2 = bf16[320,256]{1,0:T(8,128)(2,1)S(1)} collective-permute-done((bf16[320,256]{1,0:T(8,128)(2,1)S(1)}, bf16[320,256]{1,0:T(8,128)(2,1)S(1)}, u32[]{:S(2)}, u32[]{:S(2)}) %collective-permute-start.2) | collective-permute-done | bytes 163872 | tf_op jit(solution)/shard_map/ppermute | solution.py:188
  56.2 15.4 %collective-permute-done.1 = bf16[320,256]{1,0:T(8,128)(2,1)S(1)} collective-permute-done((bf16[320,256]{1,0:T(8,128)(2,1)S(1)}, bf16[320,256]{1,0:T(8,128)(2,1)S(1)}, u32[]{:S(2)}, u32[]{:S(2)}) %collective-permute-start.1) | collective-permute-done | bytes 163872 | tf_op jit(solution)/shard_map/ppermute | solution.py:187
  71.5 0.1 broadcast_in_dim.11
  71.6 15.2 %all_to_all.25.a2 = bf16[4,512,256]{2,1,0:T(8,128)(2,1)S(1)} all-to-all(bf16[4,512,256]{2,1,0:T(8,128)(2,1)S(1)} %broadcast_in_dim.11), channel_id=1, replica_groups=mesh['quarter'=4,'row'=8,'y'=4,'z_hi'=2,'core'=2] {'y'}, dimensions={0} | all-to-all | bytes 2097152 | tf_op jit(solution)/shard_map/all_to_all | solution.py:21
  86.8 1.9 collective-permute-start.3
  88.8 0.1 pad_add_fusion.3
  88.8 0.7 broadcast_in_dim.12
  89.6 4.3 %all-to-all-start.2 = ((bf16[4,128,256]{2,1,0:T(8,128)(2,1)}), bf16[4,128,256]{2,1,0:T(8,128)(2,1)S(1)}, u32[]{:S(2)}, u32[]{:S(2)}) async-start(bf16[4,128,256]{2,1,0:T(8,128)(2,1)} %broadcast_in_dim.12), calls=%async_computation.2 | async-start | bytes 524288 | tf_op jit(solution)/shard_map/all_to_all | solution.py:21
  93.9 0.1 pad_add_fusion.2
  93.9 0.0 collective-permute-done.3.a3
  93.9 0.0 collective-permute-done.a1.refs_1_
  93.9 6.9 %all-gather.6.cloned.1.call-done = bf16[1,4096,256]{2,1,0:T(8,128)(2,1)} async-done(((bf16[1,512,256]{2,1,0:T(8,128)(2,1)}), bf16[1,4096,256]{2,1,0:T(8,128)(2,1)}) %all-gather.6.cloned.1.call-update) | async-done | bytes 2097168 | tf_op jit(solution)/shard_map/all_gather | solution.py:184
  100.8 5.0 %shard_map.68 = (bf16[512,256]{1,0:T(8,128)(2,1)}, bf16[512,128]{1,0:T(8,128)(2,1)S(1)}, bf16[512,128]{1,0:T(8,128)(2,1)}) custom-call(s32[4]{0:T(128)S(1)} %get-tuple-element.24.place, bf16[4,1024,256]{2,1,0:T(8,128)(2,1)S(1)} %all-to-all-done.a0.refs_0_, bf16[4,1024,256]{2,1,0:T(8,128)(2,1)} %collective-permute-done.a1.refs_1_, ...), custom_call_target="tpu_custom_call" | custom-call | flops 1073741824 | bytes 6291456 | tf_op jit(solution)/shard_map/pallas_call | solution.py:145
  105.9 0.0 all-to-all-done.2
  105.9 1.0 broadcast_in_dim.13
  106.9 4.5 %all-to-all-start.3 = ((bf16[4,512,256]{2,1,0:T(8,128)(2,1)}), bf16[4,512,256]{2,1,0:T(8,128)(2,1)S(1)}, u32[]{:S(2)}, u32[]{:S(2)}) async-start(bf16[4,512,256]{2,1,0:T(8,128)(2,1)} %broadcast_in_dim.13), calls=%async_computation.3 | async-start | bytes 2097152 | tf_op jit(solution)/shard_map/all_to_all | solution.py:21
  111.4 0.7 all-gather.4.cloned.1.call-update
  112.2 12.0 %all-to-all-done.3.a2.refs_2_ = bf16[4,512,256]{2,1,0:T(8,128)(2,1)S(1)} async-done(((bf16[4,512,256]{2,1,0:T(8,128)(2,1)}), bf16[4,512,256]{2,1,0:T(8,128)(2,1)S(1)}, u32[]{:S(2)}, u32[]{:S(2)}) %all-to-all-start.3) | async-done | bytes 1048608 | tf_op jit(solution)/shard_map/all_to_all | solution.py:21
  124.1 1.9 collective-permute-start.4
  126.1 3.6 %collective-permute-start.5 = (bf16[512,128]{1,0:T(8,128)(2,1)S(1)}, bf16[512,128]{1,0:T(8,128)(2,1)S(1)}, u32[]{:S(2)}, u32[]{:S(2)}) collective-permute-start(bf16[512,128]{1,0:T(8,128)(2,1)S(1)} %get-tuple-element.17), channel_id=1, source_target_pairs={{0,64},{16,80},{32,96},{48,112},{64,0},{80,16},{96,32},{112,48},{1... | collective-permute-start | bytes 393224 | tf_op jit(solution)/shard_map/ppermute | solution.py:32
  129.6 6.2 %collective-permute-start.9 = (bf16[512,128]{1,0:T(8,128)(2,1)}, bf16[512,128]{1,0:T(8,128)(2,1)S(1)}, u32[]{:S(2)}, u32[]{:S(2)}) collective-permute-start(bf16[512,128]{1,0:T(8,128)(2,1)} %get-tuple-element.18), channel_id=1, source_target_pairs={{0,64},{16,80},{32,96},{48,112},{64,0},{80,16},{96,32},{112,48},{1... | collective-permute-start | bytes 393224 | tf_op jit(solution)/shard_map/ppermute | solution.py:32
  135.8 19.5 %collective-permute-done.5.refs_4_ = bf16[512,128]{1,0:T(8,128)(2,1)S(1)} collective-permute-done((bf16[512,128]{1,0:T(8,128)(2,1)S(1)}, bf16[512,128]{1,0:T(8,128)(2,1)S(1)}, u32[]{:S(2)}, u32[]{:S(2)}) %collective-permute-start.5) | collective-permute-done | bytes 131104 | tf_op jit(solution)/shard_map/ppermute | solution.py:32
  155.3 1.9 collective-permute-start.6
  157.2 1.9 collective-permute-start.7
  159.1 3.9 %collective-permute-start.8 = (bf16[512,128]{1,0:T(8,128)(2,1)S(1)}, bf16[512,128]{1,0:T(8,128)(2,1)}, u32[]{:S(2)}, u32[]{:S(2)}) collective-permute-start(bf16[512,128]{1,0:T(8,128)(2,1)S(1)} %collective-permute-done.5.refs_4_), channel_id=1, source_target_pairs={{0,48},{16,0},{32,16},{48,32},{64,112},{80,64},{96,80},{112,96},{1... | collective-permute-start | bytes 393224 | tf_op jit(solution)/shard_map/ppermute | solution.py:27
  163.1 0.3 collective-permute-done.9.refs_8_
  163.4 3.0 %collective-permute-start.10 = (bf16[512,128]{1,0:T(8,128)(2,1)S(1)}, bf16[512,128]{1,0:T(8,128)(2,1)}, u32[]{:S(2)}, u32[]{:S(2)}) collective-permute-start(bf16[512,128]{1,0:T(8,128)(2,1)S(1)} %collective-permute-done.9.refs_8_), channel_id=1, source_target_pairs={{0,16},{16,32},{32,48},{48,0},{64,80},{80,96},{96,112},{112,64},{1... | collective-permute-start | bytes 393224 | tf_op jit(solution)/shard_map/ppermute | solution.py:27
  166.5 11.1 %collective-permute-start.11 = (bf16[512,128]{1,0:T(8,128)(2,1)S(1)}, bf16[512,128]{1,0:T(8,128)(2,1)}, u32[]{:S(2)}, u32[]{:S(2)}) collective-permute-start(bf16[512,128]{1,0:T(8,128)(2,1)S(1)} %collective-permute-done.9.refs_8_), channel_id=1, source_target_pairs={{0,32},{16,48},{32,0},{48,16},{64,96},{80,112},{96,64},{112,80},{1... | collective-permute-start | bytes 393224 | tf_op jit(solution)/shard_map/ppermute | solution.py:27
  177.6 1.0 copy-done
  178.6 1.9 collective-permute-start.12
  180.5 0.0 all-gather.4.cloned.1.call-done.b_ref
  180.5 1.2 copy-done.1
  181.8 3.4 %shard_map.69.refs_12_ = f32[512,256]{1,0:T(8,128)S(1)} custom-call(s32[4]{0:T(128)S(1)} %get-tuple-element.22.place, bf16[4,1024,256]{2,1,0:T(8,128)(2,1)S(1)} %all-to-all-done.a0.refs_0_, bf16[4,1024,256]{2,1,0:T(8,128)(2,1)} %collective-permute-done.a1.refs_1_, bf16[4,512,256]{2,1,0:T(8,128)(2,1)S(1)} %all-to-all-done.3.a2.refs_2_, ...), custom_call_target="tpu_custom_call" | custom-call | flops 536870912 | bytes 3145728 | tf_op jit(solution)/shard_map/pallas_call | solution.py:145
  185.1 0.0 collective-permute-done.8.refs_7_
  185.2 0.0 collective-permute-done.10.refs_9_
  185.2 2.6 %collective-permute-done.12.refs_11_ = bf16[512,128]{1,0:T(8,128)(2,1)} collective-permute-done((bf16[512,128]{1,0:T(8,128)(2,1)S(1)}, bf16[512,128]{1,0:T(8,128)(2,1)}, u32[]{:S(2)}, u32[]{:S(2)}) %collective-permute-start.12) | collective-permute-done | bytes 131104 | tf_op jit(solution)/shard_map/ppermute | solution.py:27
  187.8 3.9 %update.1 = (f32[512,256]{1,0:T(8,128)}, bf16[512,256]{1,0:T(8,128)(2,1)S(1)}) custom-call(s32[4]{0:T(128)S(1)} %get-tuple-element.25.place, bf16[4,1024,256]{2,1,0:T(8,128)(2,1)S(1)} %all-to-all-done.a0.refs_0_, bf16[4,1024,256]{2,1,0:T(8,128)(2,1)} %collective-permute-done.a1.refs_1_, bf16[4,512,256]{2,1,0:T(8,128)(2,1)S(1)} %all-to-all-done.3.a2.refs_2_, ...), custom_call_target="tpu_custom_call" | custom-call | flops 536870912 | bytes 4980736 | tf_op jit(solution)/shard_map/update/pallas_call | solution.py:79
  191.6 11.4 %all_to_all.26 = bf16[4,128,256]{2,1,0:T(8,128)(2,1)S(1)} all-to-all(bf16[4,128,256]{2,1,0:T(8,128)(2,1)S(1)} %bitcast.18), channel_id=1, replica_groups=mesh['quarter'=4,'row'=8,'y'=4,'z_hi'=2,'core'=2] {'quarter'}, dimensions={0} | all-to-all | bytes 524288 | tf_op jit(solution)/shard_map/all_to_all | solution.py:209
  203.0 0.7 copy.8
  (20 shorter events, 0.1 us)
Async XLA Ops:
  9.7 6.2 %copy-start.4 = (bf16[1,512,256]{2,1,0:T(8,128)(2,1)S(1)}, bf16[1,512,256]{2,1,0:T(8,128)(2,1)}, u32[]{:S(2)}) copy-start(bf16[1,512,256]{2,1,0:T(8,128)(2,1)} %param.5) | copy-start | bytes 786436
  9.7 30.9 %all-to-all-start = ((bf16[4,1024,256]{2,1,0:T(8,128)(2,1)}), bf16[4,1024,256]{2,1,0:T(8,128)(2,1)S(1)}, u32[]{:S(2)}, u32[]{:S(2)}) async-start(bf16[4,1024,256]{2,1,0:T(8,128)(2,1)} %broadcast_in_dim.10), calls=%async_computation | async-start | bytes 4194304 | tf_op jit(solution)/shard_map/all_to_all | solution.py:21
  14.3 86.5 %all-gather.6.cloned.1.call-start = ((), (), s32[]{:S(2)}) async-start(), calls=%async_computation.6 | async-start | bytes 2359296 | tf_op jit(solution)/shard_map/all_gather | solution.py:184
  15.9 40.2 %collective-permute-start.2 = (bf16[320,256]{1,0:T(8,128)(2,1)S(1)}, bf16[320,256]{1,0:T(8,128)(2,1)S(1)}, u32[]{:S(2)}, u32[]{:S(2)}) collective-permute-start(bf16[320,256]{1,0:T(8,128)(2,1)S(1)} %pad_maximum_fusion.2), channel_id=1, source_target_pairs={{0,2},{2,0},{1,3},{3,1},{4,6},{6,4},{5,7},{7,5},{8,10},{10,8},{9,1... | collective-permute-start | bytes 491528 | tf_op jit(solution)/shard_map/ppermute | solution.py:188
  30.8 40.7 %collective-permute-start.1 = (bf16[320,256]{1,0:T(8,128)(2,1)S(1)}, bf16[320,256]{1,0:T(8,128)(2,1)S(1)}, u32[]{:S(2)}, u32[]{:S(2)}) collective-permute-start(bf16[320,256]{1,0:T(8,128)(2,1)S(1)} %slice_bitcast_fusion), channel_id=1, source_target_pairs={{0,2},{2,0},{1,3},{3,1},{4,6},{6,4},{5,7},{7,5},{8,10},{10,8},{9,1... | collective-permute-start | bytes 491528 | tf_op jit(solution)/shard_map/ppermute | solution.py:187
  40.7 53.3 %collective-permute-start = (bf16[4,1024,256]{2,1,0:T(8,128)(2,1)S(1)}, bf16[4,1024,256]{2,1,0:T(8,128)(2,1)}, u32[]{:S(2)}, u32[]{:S(2)}) collective-permute-start(bf16[4,1024,256]{2,1,0:T(8,128)(2,1)S(1)} %all-to-all-done.a0.refs_0_), channel_id=1, source_target_pairs={{0,1},{1,0},{2,3},{3,2},{4,5},{5,4},{6,7},{7,6},{8,9},{9,8},{10,11... | collective-permute-start | bytes 6291464 | tf_op jit(solution)/shard_map/ppermute | solution.py:169
  86.8 7.1 %collective-permute-start.3 = (bf16[4,512,256]{2,1,0:T(8,128)(2,1)S(1)}, bf16[4,512,256]{2,1,0:T(8,128)(2,1)}, u32[]{:S(2)}, u32[]{:S(2)}) collective-permute-start(bf16[4,512,256]{2,1,0:T(8,128)(2,1)S(1)} %all_to_all.25.a2), channel_id=1, source_target_pairs={{0,1},{1,0},{2,3},{3,2},{4,5},{5,4},{6,7},{7,6},{8,9},{9,8},{10,11... | collective-permute-start | bytes 3145736 | tf_op jit(solution)/shard_map/ppermute | solution.py:169
  89.6 16.3 %all-to-all-start.2 = ((bf16[4,128,256]{2,1,0:T(8,128)(2,1)}), bf16[4,128,256]{2,1,0:T(8,128)(2,1)S(1)}, u32[]{:S(2)}, u32[]{:S(2)}) async-start(bf16[4,128,256]{2,1,0:T(8,128)(2,1)} %broadcast_in_dim.12), calls=%async_computation.2 | async-start | bytes 524288 | tf_op jit(solution)/shard_map/all_to_all | solution.py:21
  106.9 17.2 %all-to-all-start.3 = ((bf16[4,512,256]{2,1,0:T(8,128)(2,1)}), bf16[4,512,256]{2,1,0:T(8,128)(2,1)S(1)}, u32[]{:S(2)}, u32[]{:S(2)}) async-start(bf16[4,512,256]{2,1,0:T(8,128)(2,1)} %broadcast_in_dim.13), calls=%async_computation.3 | async-start | bytes 2097152 | tf_op jit(solution)/shard_map/all_to_all | solution.py:21
  111.4 69.1 %all-gather.4.cloned.1.call-start = ((), (), s32[]{:S(2)}) async-start(), calls=%async_computation.5 | async-start | bytes 1310720 | tf_op jit(solution)/shard_map/all_gather | solution.py:198
  124.1 53.5 %collective-permute-start.4 = (bf16[4,512,256]{2,1,0:T(8,128)(2,1)S(1)}, bf16[4,512,256]{2,1,0:T(8,128)(2,1)S(1)}, u32[]{:S(2)}, u32[]{:S(2)}) collective-permute-start(bf16[4,512,256]{2,1,0:T(8,128)(2,1)S(1)} %all-to-all-done.3.a2.refs_2_), channel_id=1, source_target_pairs={{0,1},{1,0},{2,3},{3,2},{4,5},{5,4},{6,7},{7,6},{8,9},{9,8},{10,11... | collective-permute-start | bytes 3145736 | tf_op jit(solution)/shard_map/ppermute | solution.py:169
  126.1 29.2 %collective-permute-start.5 = (bf16[512,128]{1,0:T(8,128)(2,1)S(1)}, bf16[512,128]{1,0:T(8,128)(2,1)S(1)}, u32[]{:S(2)}, u32[]{:S(2)}) collective-permute-start(bf16[512,128]{1,0:T(8,128)(2,1)S(1)} %get-tuple-element.17), channel_id=1, source_target_pairs={{0,64},{16,80},{32,96},{48,112},{64,0},{80,16},{96,32},{112,48},{1... | collective-permute-start | bytes 393224 | tf_op jit(solution)/shard_map/ppermute | solution.py:32
  129.6 33.8 %collective-permute-start.9 = (bf16[512,128]{1,0:T(8,128)(2,1)}, bf16[512,128]{1,0:T(8,128)(2,1)S(1)}, u32[]{:S(2)}, u32[]{:S(2)}) collective-permute-start(bf16[512,128]{1,0:T(8,128)(2,1)} %get-tuple-element.18), channel_id=1, source_target_pairs={{0,64},{16,80},{32,96},{48,112},{64,0},{80,16},{96,32},{112,48},{1... | collective-permute-start | bytes 393224 | tf_op jit(solution)/shard_map/ppermute | solution.py:32
  155.3 11.2 %collective-permute-start.6 = (bf16[512,128]{1,0:T(8,128)(2,1)S(1)}, bf16[512,128]{1,0:T(8,128)(2,1)S(1)}, u32[]{:S(2)}, u32[]{:S(2)}) collective-permute-start(bf16[512,128]{1,0:T(8,128)(2,1)S(1)} %collective-permute-done.5.refs_4_), channel_id=1, source_target_pairs={{0,16},{16,32},{32,48},{48,0},{64,80},{80,96},{96,112},{112,64},{1... | collective-permute-start | bytes 393224 | tf_op jit(solution)/shard_map/ppermute | solution.py:27
  157.2 27.9 %collective-permute-start.7 = (bf16[512,128]{1,0:T(8,128)(2,1)S(1)}, bf16[512,128]{1,0:T(8,128)(2,1)}, u32[]{:S(2)}, u32[]{:S(2)}) collective-permute-start(bf16[512,128]{1,0:T(8,128)(2,1)S(1)} %collective-permute-done.5.refs_4_), channel_id=1, source_target_pairs={{0,32},{16,48},{32,0},{48,16},{64,96},{80,112},{96,64},{112,80},{1... | collective-permute-start | bytes 393224 | tf_op jit(solution)/shard_map/ppermute | solution.py:27
  159.1 26.0 %collective-permute-start.8 = (bf16[512,128]{1,0:T(8,128)(2,1)S(1)}, bf16[512,128]{1,0:T(8,128)(2,1)}, u32[]{:S(2)}, u32[]{:S(2)}) collective-permute-start(bf16[512,128]{1,0:T(8,128)(2,1)S(1)} %collective-permute-done.5.refs_4_), channel_id=1, source_target_pairs={{0,48},{16,0},{32,16},{48,32},{64,112},{80,64},{96,80},{112,96},{1... | collective-permute-start | bytes 393224 | tf_op jit(solution)/shard_map/ppermute | solution.py:27
  163.4 21.7 %collective-permute-start.10 = (bf16[512,128]{1,0:T(8,128)(2,1)S(1)}, bf16[512,128]{1,0:T(8,128)(2,1)}, u32[]{:S(2)}, u32[]{:S(2)}) collective-permute-start(bf16[512,128]{1,0:T(8,128)(2,1)S(1)} %collective-permute-done.9.refs_8_), channel_id=1, source_target_pairs={{0,16},{16,32},{32,48},{48,0},{64,80},{80,96},{96,112},{112,64},{1... | collective-permute-start | bytes 393224 | tf_op jit(solution)/shard_map/ppermute | solution.py:27
  166.5 18.7 %collective-permute-start.11 = (bf16[512,128]{1,0:T(8,128)(2,1)S(1)}, bf16[512,128]{1,0:T(8,128)(2,1)}, u32[]{:S(2)}, u32[]{:S(2)}) collective-permute-start(bf16[512,128]{1,0:T(8,128)(2,1)S(1)} %collective-permute-done.9.refs_8_), channel_id=1, source_target_pairs={{0,32},{16,48},{32,0},{48,16},{64,96},{80,112},{96,64},{112,80},{1... | collective-permute-start | bytes 393224 | tf_op jit(solution)/shard_map/ppermute | solution.py:27
  177.6 1.0 copy-start
  178.6 9.2 %collective-permute-start.12 = (bf16[512,128]{1,0:T(8,128)(2,1)S(1)}, bf16[512,128]{1,0:T(8,128)(2,1)}, u32[]{:S(2)}, u32[]{:S(2)}) collective-permute-start(bf16[512,128]{1,0:T(8,128)(2,1)S(1)} %collective-permute-done.9.refs_8_), channel_id=1, source_target_pairs={{0,48},{16,0},{32,16},{48,32},{64,112},{80,64},{96,80},{112,96},{1... | collective-permute-start | bytes 393224 | tf_op jit(solution)/shard_map/ppermute | solution.py:27
  180.5 1.2 copy-start.1
  181.8 6.0 %copy-start.2 = (f32[1,512,256]{2,1,0:T(8,128)S(1)}, f32[1,512,256]{2,1,0:T(8,128)}, u32[]{:S(2)}) copy-start(f32[1,512,256]{2,1,0:T(8,128)} %param.8) | copy-start | bytes 1572868
  181.8 6.0 %copy-start.3 = (bf16[1,512,256]{2,1,0:T(8,128)(2,1)S(1)}, bf16[1,512,256]{2,1,0:T(8,128)(2,1)}, u32[]{:S(2)}) copy-start(bf16[1,512,256]{2,1,0:T(8,128)(2,1)} %param.9) | copy-start | bytes 786436
Sparse Core Ops, SparseCore 0:
  17.2 83.5 all-gather.5
  114.9 56.3 all-gather.3
